TPU v7x, 32 devices: a whole 2x2x4 slice. The times are simulated.
32 devices in a mesh: dp: 2 (over x), seq: 4 (over z), tensor: 4 (over y, core).
Axes of the slice: x: 2, y: 2, z: 4, core: 2. Of those that a mesh axis runs over, the one named last changes fastest.
Arguments:
- tokens: bfloat16 [2, 4, 32, 196, 768], P(None, 'dp', 'seq', 'tensor'), may hold values from -6 to 6
- out_grad: bfloat16 [2, 4, 32, 196, 768], P(None, 'dp', 'seq', 'tensor'), may hold values from -6 to 6
- slot_window: int32 [2, 4, 32], P(None, 'dp', 'seq'), may hold values from 0 to 31, each once within a row
- first_gain: float32 [768], replicated, may hold values from 0.5 to 1.5
- first_shift: float32 [768], replicated, may hold values from -0.3 to 0.3
- triple_weight: bfloat16 [768, 2304], P('tensor'), may hold values from -0.21875 to 0.21875
- triple_bias: float32 [2304], replicated, may hold values from -0.3 to 0.3
- height_table: float32 [27, 64], replicated, may hold values from -0.2 to 0.2
- width_table: float32 [27, 64], replicated, may hold values from -0.2 to 0.2
- output_weight: bfloat16 [768, 768], P('tensor'), may hold values from -1.25 to 1.25
- output_bias: float32 [768], replicated, may hold values from -0.3 to 0.3
- second_gain: float32 [768], replicated, may hold values from 0.5 to 1.5
- second_shift: float32 [768], replicated, may hold values from -0.3 to 0.3
- expand_weight: bfloat16 [768, 3072], P('tensor'), may hold values from -0.21875 to 0.21875
- expand_bias: float32 [3072], replicated, may hold values from -0.3 to 0.3
- shrink_weight: bfloat16 [3072, 768], P('tensor'), may hold values from -0.109375 to 0.109375
- shrink_bias: float32 [768], replicated, may hold values from -0.3 to 0.3
Outputs:
- result: bfloat16 [2, 4, 32, 196, 768], P(None, 'dp', 'seq', 'tensor')
- tokens_gradient: bfloat16 [2, 4, 32, 196, 768], P(None, 'dp', 'seq', 'tensor')
- first_gain_gradient: float32 [768], replicated
- first_shift_gradient: float32 [768], replicated
- triple_weight_gradient: float32 [768, 2304], P('tensor')
- triple_bias_gradient: float32 [2304], replicated
- height_table_gradient: float32 [27, 64], replicated
- width_table_gradient: float32 [27, 64], replicated
- output_weight_gradient: float32 [768, 768], P('tensor')
- output_bias_gradient: float32 [768], replicated
- second_gain_gradient: float32 [768], replicated
- second_shift_gradient: float32 [768], replicated
- expand_weight_gradient: float32 [768, 3072], P('tensor')
- expand_bias_gradient: float32 [3072], replicated
- shrink_weight_gradient: float32 [3072, 768], P('tensor')
- shrink_bias_gradient: float32 [768], replicated
Inputs may be any that keep to these rules, and one draw needn't show every extreme that they name: For each micro-batch and image, slot_window is a permutation of 0 to 31; a value w below 25 names the window in row w // 5 and column w % 5 of the grid padded to 70 tokens a side, larger values mark empty slots.
All inputs are finite; a program needn't handle non-finite values.
Results may differ from a plain program's by a relative error of at most 0.015.
Values may be sent and summed in bfloat16 or wider, within the bound.
No kernel may reach another device: no remote copies, remote signals or barrier semaphores. Data moves between devices by JAX's collectives and lax.ppermute only.
A program may use at most 320 MiB of HBM per device.

v0:
```python
import jax
import jax.numpy as jnp
import numpy as np
from jax import lax
from jax.sharding import PartitionSpec as P

HEADS = 12
HD = 64
WIN = 14
GRID = 64
WGRID = 5


EPSILON = 1e-06
MASKED_SCORE = -1000000000.0
PRECISE = lax.Precision.HIGHEST


def layer_norm(values, gain, shift):
    centre = jnp.mean(values, axis=-1, keepdims=True)
    spread = values - centre
    variance = jnp.mean(spread * spread, axis=-1, keepdims=True)
    return spread * lax.rsqrt(variance + EPSILON) * gain + shift


def smooth_gate(values):
    return 0.5 * values * (1.0 + jax.scipy.special.erf(values * 0.7071067811865476))


def window_valid(slot_window, window, grid, across):
    position = jnp.arange(window * window, dtype=jnp.int32)
    window_id = slot_window[..., None]
    inside = (
        (window_id < across * across)
        & (window_id // across * window + position // window < grid)
        & (window_id % across * window + position % window < grid)
    )
    return jnp.where(inside, 1.0, 0.0).astype(jnp.float32)


def offset_table(window):
    first_index = np.arange(window)[:, None, None]
    second = np.arange(window)[None, :, None]
    offset = np.arange(2 * window - 1)[None, None, :]
    return jnp.asarray((first_index - second + window - 1 == offset).astype(np.float32))


def key_expanders(window):
    positions = np.arange(window * window)[None, :]
    sides = np.arange(window)[:, None]
    by_height = jnp.asarray((positions // window == sides).astype(np.float32))
    by_width = jnp.asarray((positions % window == sides).astype(np.float32))
    return (by_height, by_width)


def contract_rows(left, right):
    return lax.dot_general(
        left, right, (((0,), (0,)), ((), ())), preferred_element_type=jnp.float32
    )


def times_transposed(left, weight):
    return lax.dot_general(
        left, weight, (((1,), (1,)), ((), ())), preferred_element_type=jnp.float32
    )


def scores_of(query_rows, key_rows, height_full, width_full, valid_keys):
    slab_count, full_rows, heads_dev, head_dim = query_rows.shape
    window = height_full.shape[0]
    by_height, by_width = key_expanders(window)
    raw_scores = jnp.einsum(
        "sqhc,skhc->shqk", query_rows, key_rows, preferred_element_type=jnp.float32
    ) * head_dim ** (-0.5)
    grid_query = query_rows.astype(jnp.float32).reshape(
        slab_count, window, window, heads_dev, head_dim
    )
    along_height = jnp.einsum("sijhc,ikc->shijk", grid_query, height_full, precision=PRECISE)
    along_width = jnp.einsum("sijhc,jlc->shijl", grid_query, width_full, precision=PRECISE)
    along_height = along_height.reshape(slab_count, heads_dev, full_rows, window)
    along_width = along_width.reshape(slab_count, heads_dev, full_rows, window)
    height_bias = jnp.einsum("shqk,kc->shqc", along_height, by_height, precision=PRECISE)
    width_bias = jnp.einsum("shql,lc->shqc", along_width, by_width, precision=PRECISE)
    summed = raw_scores + height_bias + width_bias
    return (jnp.where(valid_keys[:, None, None, :] > 0, summed, MASKED_SCORE), grid_query)


def attend(heads, valid_full, height_full, width_full):
    masked, grid_query = scores_of(
        heads[:, :, 0], heads[:, :, 1], height_full, width_full, valid_full
    )
    maxima = jnp.max(masked, axis=-1, keepdims=True)
    exponent = jnp.exp(masked - maxima)
    summed = jnp.sum(exponent, axis=-1, keepdims=True)
    soft_low = (exponent / summed).astype(jnp.bfloat16)
    mixed_rows = jnp.einsum(
        "shqk,skhc->sqhc", soft_low, heads[:, :, 2], preferred_element_type=jnp.float32
    )
    mixed_rows = mixed_rows * valid_full[:, :, None, None]
    slab_count, full_rows, heads_dev, head_dim = mixed_rows.shape
    packed_rows = mixed_rows.astype(jnp.bfloat16).reshape(
        slab_count, full_rows, 1, heads_dev * head_dim
    )
    return (packed_rows, maxima + jnp.log(summed))


def attend_back(heads, valid_full, height_full, width_full, offsets, log_total, grad_mixed):
    query_rows = heads[:, :, 0]
    key_rows = heads[:, :, 1]
    value_rows = heads[:, :, 2]
    slab_count, full_rows, heads_dev, head_dim = query_rows.shape
    window = height_full.shape[0]
    by_height, by_width = key_expanders(window)
    masked, grid_query = scores_of(query_rows, key_rows, height_full, width_full, valid_full)
    soft_weights = jnp.exp(masked - log_total)
    soft_low = soft_weights.astype(jnp.bfloat16)
    grad_out = grad_mixed * valid_full[:, :, None, None].astype(jnp.bfloat16)
    grad_values = jnp.einsum(
        "shqk,sqhc->skhc", soft_low, grad_out, preferred_element_type=jnp.float32
    )
    grad_soft = jnp.einsum(
        "sqhc,skhc->shqk", grad_out, value_rows, preferred_element_type=jnp.float32
    )
    grad_scores = soft_weights * (
        grad_soft - jnp.sum(soft_weights * grad_soft, axis=-1, keepdims=True)
    )
    grad_scores = jnp.where(valid_full[:, None, None, :] > 0, grad_scores, 0.0).astype(jnp.bfloat16)
    score_scale = head_dim ** (-0.5)
    grad_queries = (
        jnp.einsum("shqk,skhc->sqhc", grad_scores, key_rows, preferred_element_type=jnp.float32)
        * score_scale
    )
    grad_keys = (
        jnp.einsum("shqk,sqhc->skhc", grad_scores, query_rows, preferred_element_type=jnp.float32)
        * score_scale
    )
    grad_wide = grad_scores.astype(jnp.float32)
    grad_height = jnp.einsum("shqc,kc->shqk", grad_wide, by_height, precision=PRECISE)
    grad_width = jnp.einsum("shqc,lc->shql", grad_wide, by_width, precision=PRECISE)
    grad_height = grad_height.reshape(slab_count, heads_dev, window, window, window)
    grad_width = grad_width.reshape(slab_count, heads_dev, window, window, window)
    grid_query_grad = jnp.einsum("shijk,ikc->sijhc", grad_height, height_full, precision=PRECISE)
    grid_query_grad = grid_query_grad + jnp.einsum(
        "shijl,jlc->sijhc", grad_width, width_full, precision=PRECISE
    )
    grad_queries = grad_queries + grid_query_grad.reshape(
        slab_count, full_rows, heads_dev, head_dim
    )
    height_expanded = jnp.einsum("shijk,sijhc->ikc", grad_height, grid_query, precision=PRECISE)
    width_expanded = jnp.einsum("shijl,sijhc->jlc", grad_width, grid_query, precision=PRECISE)
    height_grad = jnp.einsum("ikr,ikc->rc", offsets, height_expanded, precision=PRECISE)
    width_grad = jnp.einsum("ikr,ikc->rc", offsets, width_expanded, precision=PRECISE)
    grad_heads = jnp.stack((grad_queries, grad_keys, grad_values), axis=2).astype(jnp.bfloat16)
    return (
        grad_heads.reshape(slab_count, full_rows, 3, 1, heads_dev * head_dim),
        height_grad,
        width_grad,
    )


def local(
    tokens,
    out_grad,
    slot_window,
    first_gain,
    first_shift,
    triple_weight,
    triple_bias,
    height_table,
    width_table,
    output_weight,
    output_bias,
    second_gain,
    second_shift,
    expand_weight,
    expand_bias,
    shrink_weight,
    shrink_bias,
):
    micro_count, images, slot_dev, rows_dev, model_width = tokens.shape
    tensor_parts = lax.axis_size("tensor")
    heads_dev = HEADS // tensor_parts
    head_width = heads_dev * HD
    full_rows = rows_dev * tensor_parts
    slab_count = images * slot_dev
    row_count = slab_count * rows_dev
    offsets = offset_table(WIN)
    height_full = jnp.einsum("ikr,rc->ikc", offsets, height_table, precision=PRECISE)
    width_full = jnp.einsum("ikr,rc->ikc", offsets, width_table, precision=PRECISE)
    triple_full, output_full, expand_full, shrink_full = (
        lax.all_gather(triple_weight, "tensor", axis=0, tiled=True),
        lax.all_gather(output_weight, "tensor", axis=0, tiled=True),
        lax.all_gather(expand_weight, "tensor", axis=0, tiled=True),
        lax.all_gather(shrink_weight, "tensor", axis=0, tiled=True),
    )
    first_row = lax.axis_index("tensor") * rows_dev
    sums = [
        jnp.zeros(item.shape, jnp.float32)
        for item in (
            first_gain,
            first_shift,
            triple_full,
            triple_bias,
            height_table,
            width_table,
            output_full,
            output_bias,
            second_gain,
            second_shift,
            expand_full,
            expand_bias,
            shrink_full,
            shrink_bias,
        )
    ]
    results = []
    input_grads = []
    for micro_step in range(micro_count):
        valid_full = window_valid(slot_window[micro_step], WIN, GRID, WGRID).reshape(
            slab_count, full_rows
        )
        valid_local = lax.dynamic_slice_in_dim(valid_full, first_row, rows_dev, axis=1).reshape(
            row_count, 1
        )
        row_values = tokens[micro_step].astype(jnp.float32).reshape(row_count, model_width)
        normed = layer_norm(row_values, first_gain, first_shift).astype(jnp.bfloat16)
        triple = (
            jnp.dot(normed, triple_full, preferred_element_type=jnp.float32) + triple_bias
        ).astype(jnp.bfloat16)
        triple = triple.reshape(slab_count, rows_dev, 3, tensor_parts, head_width)
        heads = lax.all_to_all(triple, "tensor", split_axis=3, concat_axis=1, tiled=True)
        heads = heads.reshape(slab_count, full_rows, 3, heads_dev, HD)
        mixed_rows, log_total = attend(heads, valid_full, height_full, width_full)
        attended = lax.all_to_all(
            mixed_rows, "tensor", split_axis=1, concat_axis=2, tiled=True
        ).reshape(row_count, model_width)
        middle = (
            row_values
            + jnp.dot(attended, output_full, preferred_element_type=jnp.float32)
            + output_bias
        )
        normed2 = layer_norm(middle, second_gain, second_shift).astype(jnp.bfloat16)
        hidden = jnp.dot(normed2, expand_full, preferred_element_type=jnp.float32) + expand_bias
        active = smooth_gate(hidden).astype(jnp.bfloat16)
        output_rows = (
            middle + jnp.dot(active, shrink_full, preferred_element_type=jnp.float32) + shrink_bias
        )
        results.append(
            output_rows.astype(jnp.bfloat16).reshape(images, slot_dev, rows_dev, model_width)
        )
        grad_result = (
            out_grad[micro_step].astype(jnp.float32).reshape(row_count, model_width) * valid_local
        )
        grad_branch = grad_result.astype(jnp.bfloat16)
        sums[12] = sums[12] + contract_rows(active, grad_branch)
        sums[13] = sums[13] + jnp.sum(grad_branch, axis=0, dtype=jnp.float32)
        grad_active = times_transposed(grad_branch, shrink_full)
        unused_value, gate_back = jax.vjp(smooth_gate, hidden)
        grad_hidden = gate_back(grad_active)[0].astype(jnp.bfloat16)
        sums[10] = sums[10] + contract_rows(normed2, grad_hidden)
        sums[11] = sums[11] + jnp.sum(grad_hidden, axis=0, dtype=jnp.float32)
        grad_normed2 = times_transposed(grad_hidden, expand_full)
        unused_value, second_back = jax.vjp(layer_norm, middle, second_gain, second_shift)
        grad_middle, grad_gain, grad_shift = second_back(grad_normed2)
        sums[8] = sums[8] + grad_gain
        sums[9] = sums[9] + grad_shift
        grad_middle = grad_result + grad_middle
        grad_output = grad_middle.astype(jnp.bfloat16)
        sums[6] = sums[6] + contract_rows(attended, grad_output)
        sums[7] = sums[7] + jnp.sum(grad_output, axis=0, dtype=jnp.float32)
        grad_attended = times_transposed(grad_output, output_full).astype(jnp.bfloat16)
        grad_attended = grad_attended.reshape(slab_count, rows_dev, tensor_parts, head_width)
        grad_mixed = lax.all_to_all(
            grad_attended, "tensor", split_axis=2, concat_axis=1, tiled=True
        )
        grad_mixed = grad_mixed.reshape(slab_count, full_rows, heads_dev, HD)
        grad_heads, height_grad, width_grad = attend_back(
            heads, valid_full, height_full, width_full, offsets, log_total, grad_mixed
        )
        sums[4] = sums[4] + height_grad
        sums[5] = sums[5] + width_grad
        grad_triple = lax.all_to_all(
            grad_heads, "tensor", split_axis=1, concat_axis=3, tiled=True
        ).reshape(row_count, 3 * model_width)
        sums[2] = sums[2] + contract_rows(normed, grad_triple)
        sums[3] = sums[3] + jnp.sum(grad_triple, axis=0, dtype=jnp.float32)
        grad_normed = times_transposed(grad_triple, triple_full)
        unused_value, first_back = jax.vjp(layer_norm, row_values, first_gain, first_shift)
        grad_rows, grad_gain, grad_shift = first_back(grad_normed)
        sums[0] = sums[0] + grad_gain
        sums[1] = sums[1] + grad_shift
        grad_input = (grad_middle + grad_rows).astype(jnp.bfloat16)
        input_grads.append(grad_input.reshape(images, slot_dev, rows_dev, model_width))
    shares = (
        lax.psum_scatter(
            sums[2].astype(jnp.bfloat16), "tensor", scatter_dimension=0, tiled=True
        ).astype(jnp.float32),
        lax.psum_scatter(
            sums[6].astype(jnp.bfloat16), "tensor", scatter_dimension=0, tiled=True
        ).astype(jnp.float32),
        lax.psum_scatter(
            sums[10].astype(jnp.bfloat16), "tensor", scatter_dimension=0, tiled=True
        ).astype(jnp.float32),
        lax.psum_scatter(
            sums[12].astype(jnp.bfloat16), "tensor", scatter_dimension=0, tiled=True
        ).astype(jnp.float32),
    )
    blocks = lax.psum((shares[0], shares[1], shares[2], shares[3]), ("dp", "seq"))
    triple_gradient = blocks[0]
    output_gradient = blocks[1]
    expand_gradient = blocks[2]
    shrink_gradient = blocks[3]
    small = lax.psum(
        (
            sums[0],
            sums[1],
            sums[3],
            sums[4],
            sums[5],
            sums[7],
            sums[8],
            sums[9],
            sums[11],
            sums[13],
        ),
        ("dp", "seq", "tensor"),
    )
    result = jnp.stack(results, axis=0)
    tokens_gradient = jnp.stack(input_grads, axis=0)
    return (
        result,
        tokens_gradient,
        small[0],
        small[1],
        triple_gradient,
        small[2],
        small[3],
        small[4],
        output_gradient,
        small[5],
        small[6],
        small[7],
        expand_gradient,
        small[8],
        shrink_gradient,
        small[9],
    )


def solution(mesh):
    return jax.shard_map(
        local,
        mesh=mesh,
        in_specs=(
            P(None, "dp", "seq", "tensor", None),
            P(None, "dp", "seq", "tensor", None),
            P(None, "dp", "seq"),
            P(),
            P(),
            P("tensor", None),
            P(),
            P(),
            P(),
            P("tensor", None),
            P(),
            P(),
            P(),
            P("tensor", None),
            P(),
            P("tensor", None),
            P(),
        ),
        out_specs=(
            P(None, "dp", "seq", "tensor", None),
            P(None, "dp", "seq", "tensor", None),
            P(),
            P(),
            P("tensor", None),
            P(),
            P(),
            P(),
            P("tensor", None),
            P(),
            P(),
            P(),
            P("tensor", None),
            P(),
            P("tensor", None),
            P(),
        ),
        check_vma=False,
    )
```

profile of v0, /device:TPU:0, one launch (start us, length us, event | category | flops | bytes accessed | tf_op | source)
XLA Modules:
  0.0 1685.7 jit_solution(17513940450612606039)
XLA Ops:
  17.8 25.3 %all-gather.5.cloned.1.call-done = bf16[768,2304]{1,0:T(8,128)(2,1)} async-done(((bf16[192,2304]{1,0:T(8,128)(2,1)}), bf16[768,2304]{1,0:T(8,128)(2,1)}) %all-gather.5.cloned.1.call-update) | async-done | bytes 3538960 | tf_op jit(solution)/shard_map/all_gather | solution.py:191
  100.4 63.5 %all-to-all-done = bf16[16,49,3,4,192]{4,0,2,1,3:T(8,128)(2,1)} async-done(((bf16[16,49,3,4,192]{4,0,2,1,3:T(8,128)(2,1)}), bf16[16,49,3,4,192]{4,0,2,1,3:T(8,128)(2,1)}, u32[]{:S(2)}, u32[]{:S(2)}) %all-to-all-start) | async-done | bytes 3612704 | tf_op jit(solution)/shard_map/all_to_all | solution.py:231
  171.0 18.2 %reshape.1102 = bf16[16,196,3,3,64]{4,3,0,2,1:T(4,128)(2,1)} reshape(bf16[16,4,49,3,1,192]{5,0,3,2,1,4:T(8,128)(2,1)} %bitcast.1) | data formatting | bytes 7225344 | tf_op jit(solution)/shard_map/reshape | solution.py:232
  208.0 20.2 %all-to-all-done.2 = bf16[16,49,3,4,192]{4,0,2,1,3:T(8,128)(2,1)} async-done(((bf16[16,49,3,4,192]{4,0,2,1,3:T(8,128)(2,1)}), bf16[16,49,3,4,192]{4,0,2,1,3:T(8,128)(2,1)}, u32[]{:S(2)}, u32[]{:S(2)}) %all-to-all-start.2) | async-done | bytes 3612704 | tf_op jit(solution)/shard_map/all_to_all | solution.py:231
  228.2 18.2 %reshape.1104 = bf16[16,196,3,3,64]{4,3,0,2,1:T(4,128)(2,1)} reshape(bf16[16,4,49,3,1,192]{5,0,3,2,1,4:T(8,128)(2,1)} %bitcast.25) | data formatting | bytes 7225344 | tf_op jit(solution)/shard_map/reshape | solution.py:232
  265.8 19.1 %fusion.52 = f32[16,3,14,14,14]{0,4,1,2,3:T(8,128)} fusion(bf16[16,14,14,3,64]{4,0,3,2,1:T(8,128)(2,1)S(1)} %bitcast.281, f32[14,14,64]{2,1,0:T(8,128)S(1)} %fusion.128), kind=kOutput, calls=%fused_computation.124 | convolution fusion | flops 101154816 | bytes 1781248 | tf_op jit(solution)/shard_map/sijhc,jlc->shijl/dot_general | solution.py:79
  284.8 19.2 %fusion.170 = f32[14,14,16,14,3]{2,1,4,3,0:T(8,128)} fusion(f32[14,14,64,1,1]{2,1,4,3,0:T(8,128)S(1)} %convolution_bitcast_fusion, bf16[16,14,14,3,64]{4,0,3,2,1:T(8,128)(2,1)S(1)} %bitcast.282), kind=kOutput, calls=%fused_computation.272 | convolution fusion | flops 101154816 | bytes 1781248 | tf_op jit(solution)/shard_map/sijhc,ikc->shijk/dot_general | solution.py:78
  304.0 19.1 %fusion.55 = f32[16,3,14,14,14]{0,4,1,2,3:T(8,128)} fusion(bf16[16,14,14,3,64]{4,0,3,2,1:T(8,128)(2,1)S(1)} %bitcast.285, f32[14,14,64]{2,1,0:T(8,128)S(1)} %fusion.128), kind=kOutput, calls=%fused_computation.125 | convolution fusion | flops 101154816 | bytes 1781248 | tf_op jit(solution)/shard_map/sijhc,jlc->shijl/dot_general | solution.py:79
  323.1 19.2 %fusion.173 = f32[14,14,16,14,3]{2,1,4,3,0:T(8,128)} fusion(f32[14,14,64,1,1]{2,1,4,3,0:T(8,128)S(1)} %convolution_bitcast_fusion, bf16[16,14,14,3,64]{4,0,3,2,1:T(8,128)(2,1)S(1)} %bitcast.286), kind=kOutput, calls=%fused_computation.275 | convolution fusion | flops 101154816 | bytes 1781248 | tf_op jit(solution)/shard_map/sijhc,ikc->shijk/dot_general | solution.py:78
  408.0 12.1 copy.353
  431.4 12.0 copy.357
  454.7 12.2 copy.333
  478.2 12.1 copy.337
  496.9 12.1 copy.350
  526.3 26.2 %fusion.164 = (f32[16,3,196]{0,2,1:T(8,128)S(1)}, f32[16,3,196,196]{3,0,2,1:T(8,128)}, f32[16,3,196]{0,2,1:T(8,128)S(1)}, f32[16,3,196,196]{3,0,2,1:T(8,128)}) fusion(f32[16,3,196,196]{3,0,2,1:T(8,128)} %copy.337, f32[16,3,196,196]{3,0,2,1:T(8,128)} %copy.333, f32[16,3,196,196]{3,0,2,1:T(8,128)} %copy.330, pred[16,196]{1,0:T(8,128)(4,1)S(1)} %get-tuple-element.166, ...), kind=kLoop, calls=%fused_computation.266 | loop fusion | flops 18420864 | bytes 59088512 | tf_op jit(solution)/shard_map/reduce_max | solution.py:92
  655.1 14.5 convert_reduce_fusion
  687.4 15.2 convert_reduce_fusion.1
  824.5 12.7 copy.365
  837.1 62.2 %select_convert_fusion.1 = bf16[16,3,196,196]{3,0,2,1:T(8,128)(2,1)S(1)} fusion(f32[16,3,196,196]{3,0,2,1:T(8,128)} %copy.365, f32[16,3,196,196]{3,0,2,1:T(8,128)} %get-tuple-element.125, f32[16,3,196]{0,2,1:T(8,128)S(1)} %copy-done.65, pred[16,196]{1,0:T(8,128)(4,1)S(1)} %copy-done.88), kind=kOutput, calls=%fused_computation.11 | output fusion | flops 12917379 | bytes 18480448 | tf_op jit(solution)/shard_map/sub | solution.py:125
  1027.9 12.1 copy.385
  1040.0 62.0 %select_convert_fusion = bf16[16,3,196,196]{3,0,2,1:T(8,128)(2,1)S(1)} fusion(f32[16,3,196,196]{3,0,2,1:T(8,128)} %copy.385, f32[16,3,196,196]{3,0,2,1:T(8,128)} %get-tuple-element.192, f32[16,3,196]{0,2,1:T(8,128)S(1)} %copy-done.63, pred[16,196]{1,0:T(8,128)(4,1)S(1)} %copy-done.86), kind=kOutput, calls=%fused_computation.6 | output fusion | flops 12917379 | bytes 18480448 | tf_op jit(solution)/shard_map/sub | solution.py:125
  1239.5 12.8 all-to-all-done.7
  1359.6 41.9 %all-reduce = (f32[768]{0:T(1024)}, f32[768]{0:T(1024)}, f32[2304]{0:T(1024)}, f32[27,64]{1,0:T(8,128)}, f32[27,64]{1,0:T(8,128)}, /*index=5*/f32[768]{0:T(1024)...) all-reduce(f32[768]{0:T(1024)S(1)} %add.540, ...), channel_id=1, replica_groups=mesh['dp'=2,'seq'=4,'tensor'=4] {'dp','seq','tensor'}, use_global_device_ids=true, to_apply=%region_24.25 | all-reduce | flops 13440 | bytes 107520 | tf_op jit(solution)/shard_map/psum | solution.py:313
  1401.5 277.1 %all-reduce.3 = (f32[192,2304]{1,0:T(8,128)}, f32[192,768]{1,0:T(8,128)}, f32[192,3072]{1,0:T(8,128)}, f32[768,768]{1,0:T(8,128)}) all-reduce(bf16[192,2304]{1,0:T(8,128)(2,1)} %reduce-scatter.5.cloned.1.call-done, bf16[192,768]{1,0:T(8,128)(2,1)S(1)} %copy-done.76, ...), channel_id=1, replica_groups=mesh['dp'=2,'seq'=4,'tensor'=4] {'dp','seq'}, use_global_device_ids=true, to_apply=%region_29.30 | all-reduce | flops 1769472 | bytes 10616832 | tf_op jit(solution)/shard_map/psum | solution.py:308
  (537 shorter events, 850.3 us)
Async XLA Ops:
  7.2 162.4 %copy-start = (f32[27,64]{1,0:T(8,128)S(1)}, f32[27,64]{1,0:T(8,128)}, u32[]{:S(2)}) copy-start(f32[27,64]{1,0:T(8,128)} %param.37) | copy-start | bytes 20740
  7.2 35.9 %all-gather.5.cloned.1.call-start = ((), (), s32[]{:S(2)}) async-start(), calls=%async_computation.12 | async-start | bytes 4423680 | tf_op jit(solution)/shard_map/all_gather | solution.py:191
  7.9 628.7 %all-gather.7.cloned.1.call-start = ((), (), s32[]{:S(2)}) async-start(), calls=%async_computation.13 | async-start | bytes 1474560 | tf_op jit(solution)/shard_map/all_gather | solution.py:192
  8.7 635.4 %all-gather.9.cloned.1.call-start = ((), (), s32[]{:S(2)}) async-start(), calls=%async_computation.14 | async-start | bytes 5898240 | tf_op jit(solution)/shard_map/all_gather | solution.py:193
  66.2 97.7 %all-to-all-start = ((bf16[16,49,3,4,192]{4,0,2,1,3:T(8,128)(2,1)}), bf16[16,49,3,4,192]{4,0,2,1,3:T(8,128)(2,1)}, u32[]{:S(2)}, u32[]{:S(2)}) async-start(bf16[16,49,3,4,192]{4,0,2,1,3:T(8,128)(2,1)} %copy.325), calls=%async_computation | async-start | bytes 9633792 | tf_op jit(solution)/shard_map/all_to_all | solution.py:231
  71.2 583.8 %all-gather.11.cloned.1.call-start = ((), (), s32[]{:S(2)}) async-start(), calls=%async_computation.15 | async-start | bytes 5898240 | tf_op jit(solution)/shard_map/all_gather | solution.py:194
  163.9 64.3 %all-to-all-start.2 = ((bf16[16,49,3,4,192]{4,0,2,1,3:T(8,128)(2,1)}), bf16[16,49,3,4,192]{4,0,2,1,3:T(8,128)(2,1)}, u32[]{:S(2)}, u32[]{:S(2)}) async-start(bf16[16,49,3,4,192]{4,0,2,1,3:T(8,128)(2,1)} %copy.345), calls=%async_computation.2 | async-start | bytes 9633792 | tf_op jit(solution)/shard_map/all_to_all | solution.py:231
  169.9 153.2 %copy-start.58 = (f32[14,14,64,1,1]{2,1,4,3,0:T(8,128)}, f32[14,14,64,1,1]{2,1,4,3,0:T(8,128)S(1)}, u32[]{:S(2)}) copy-start(f32[14,14,64,1,1]{2,1,4,3,0:T(8,128)S(1)} %convolution_bitcast_fusion) | copy-start | bytes 150532
  170.0 356.3 %copy-start.85 = (pred[16,196]{1,0:T(8,128)(4,1)}, pred[16,196]{1,0:T(8,128)(4,1)S(1)}, u32[]{:S(2)}) copy-start(pred[16,196]{1,0:T(8,128)(4,1)S(1)} %get-tuple-element.167) | copy-start | bytes 9412
  170.0 356.2 %copy-start.87 = (pred[16,196]{1,0:T(8,128)(4,1)}, pred[16,196]{1,0:T(8,128)(4,1)S(1)}, u32[]{:S(2)}) copy-start(pred[16,196]{1,0:T(8,128)(4,1)S(1)} %get-tuple-element.166) | copy-start | bytes 9412
  171.0 133.1 %copy-start.60 = (f32[14,14,64]{2,1,0:T(8,128)}, f32[14,14,64]{2,1,0:T(8,128)S(1)}, u32[]{:S(2)}) copy-start(f32[14,14,64]{2,1,0:T(8,128)S(1)} %fusion.128) | copy-start | bytes 150532
  347.2 161.8 %copy-start.19 = (bf16[16,196,1,3,64]{1,4,3,0,2:T(8,128)(2,1)}, bf16[16,196,1,3,64]{1,4,3,0,2:T(8,128)(2,1)S(1)}, u32[]{:S(2)}) copy-start(bf16[16,196,1,3,64]{1,4,3,0,2:T(8,128)(2,1)S(1)} %copy.442) | copy-start | bytes 3612676
  377.0 113.3 %copy-start.17 = (bf16[16,196,1,3,64]{1,4,3,0,2:T(8,128)(2,1)}, bf16[16,196,1,3,64]{1,4,3,0,2:T(8,128)(2,1)S(1)}, u32[]{:S(2)}) copy-start(bf16[16,196,1,3,64]{1,4,3,0,2:T(8,128)(2,1)S(1)} %copy.445) | copy-start | bytes 3612676
  571.3 32.8 %all-to-all-start.3 = ((bf16[16,196,1,192]{3,0,2,1:T(8,128)(2,1)}), bf16[16,196,1,192]{3,0,2,1:T(8,128)(2,1)}, u32[]{:S(2)}, u32[]{:S(2)}) async-start(bf16[16,196,1,192]{3,0,2,1:T(8,128)(2,1)} %copy.359), calls=%async_computation.3 | async-start | bytes 3211264 | tf_op jit(solution)/shard_map/all_to_all | solution.py:234
  604.1 25.0 %all-to-all-start.1 = ((bf16[16,196,1,192]{3,0,2,1:T(8,128)(2,1)}), bf16[16,196,1,192]{3,0,2,1:T(8,128)(2,1)}, u32[]{:S(2)}, u32[]{:S(2)}) async-start(bf16[16,196,1,192]{3,0,2,1:T(8,128)(2,1)} %copy.339), calls=%async_computation.1 | async-start | bytes 3211264 | tf_op jit(solution)/shard_map/all_to_all | solution.py:234
  608.6 720.5 %reduce-scatter.7.cloned.1.call-start = ((), (), s32[]{:S(2)}) async-start(), calls=%async_computation.17 | async-start | bytes 1474560 | tf_op jit(solution)/shard_map/reduce_scatter | solution.py:298
  722.5 679.0 %reduce-scatter.9.cloned.1.call-start = ((), (), s32[]{:S(2)}) async-start(), calls=%async_computation.18 | async-start | bytes 5898240 | tf_op jit(solution)/shard_map/reduce_scatter | solution.py:301
  761.8 39.6 %all-to-all-start.4 = ((bf16[16,49,4,192]{3,0,1,2:T(8,128)(2,1)}), bf16[16,49,4,192]{3,0,1,2:T(8,128)(2,1)}, u32[]{:S(2)}, u32[]{:S(2)}) async-start(bf16[16,49,4,192]{3,0,1,2:T(8,128)(2,1)} %copy.362), calls=%async_computation.4 | async-start | bytes 3211264 | tf_op jit(solution)/shard_map/all_to_all | solution.py:273
  766.1 635.4 %reduce-scatter.11.cloned.1.call-start = ((), (), s32[]{:S(2)}) async-start(), calls=%async_computation.19 | async-start | bytes 5898240 | tf_op jit(solution)/shard_map/reduce_scatter | solution.py:304
  801.4 115.9 %all-to-all-start.6 = ((bf16[16,49,4,192]{3,0,1,2:T(8,128)(2,1)}), bf16[16,49,4,192]{3,0,1,2:T(8,128)(2,1)S(1)}, u32[]{:S(2)}, u32[]{:S(2)}) async-start(bf16[16,49,4,192]{3,0,1,2:T(8,128)(2,1)} %copy.382), calls=%async_computation.6 | async-start | bytes 3211264 | tf_op jit(solution)/shard_map/all_to_all | solution.py:273
  1022.9 169.4 %all-to-all-start.5 = ((bf16[16,196,3,1,192]{4,0,2,3,1:T(8,128)(2,1)}), bf16[16,196,3,1,192]{4,0,2,3,1:T(8,128)(2,1)}, u32[]{:S(2)}, u32[]{:S(2)}) async-start(bf16[16,196,3,1,192]{4,0,2,3,1:T(8,128)(2,1)} %pad_maximum_fusion), calls=%async_computation.5 | async-start | bytes 9633792 | tf_op jit(solution)/shard_map/all_to_all | solution.py:282
  1192.2 60.0 %all-to-all-start.7 = ((bf16[16,196,3,1,192]{4,0,2,3,1:T(8,128)(2,1)}), bf16[16,196,3,1,192]{4,0,2,3,1:T(8,128)(2,1)}, u32[]{:S(2)}, u32[]{:S(2)}) async-start(bf16[16,196,3,1,192]{4,0,2,3,1:T(8,128)(2,1)} %pad_maximum_fusion.1), calls=%async_computation.7 | async-start | bytes 9633792 | tf_op jit(solution)/shard_map/all_to_all | solution.py:282
  1197.4 204.1 %reduce-scatter.5.cloned.1.call-start = ((), (), s32[]{:S(2)}) async-start(), calls=%async_computation.16 | async-start | bytes 4423680 | tf_op jit(solution)/shard_map/reduce_scatter | solution.py:295
  1357.7 320.9 %copy-start.1 = (f32[27,64]{1,0:T(8,128)S(1)}, f32[27,64]{1,0:T(8,128)}, u32[]{:S(2)}) copy-start(f32[27,64]{1,0:T(8,128)} %param.37) | copy-start | bytes 20740
  (128 other events, 1363.9 us)
Sparse Core Ops, SparseCore 0:
  9.6 33.4 all-gather.4
  44.7 17.4 all-gather.6
  63.7 62.7 all-gather.8
  127.9 54.3 all-gather.10
  722.7 25.7 reduce-scatter.6
  751.0 65.5 reduce-scatter.8
  819.1 47.8 reduce-scatter.10
  1280.3 40.5 reduce-scatter.4
where the time goes:
time: 1700 us; the launch traced here: 1690 us
  local copies, waits for them, and re-layouts  507 us (30%)
  matrix products  448 us (26%)
  blocking collectives  319 us (19%)
  other arithmetic  219 us (13%)
  waiting for transfers between devices  140 us (8%)
  starting transfers between devices  37.6 us (2%)
    psum x1, blocking collectives, local(): lax.psum((shares[0], shares[1], shares[2], shares[3]), ('dp', 'seq'))  277 us
    sub x2, other arithmetic, attend_back(): grad_soft - jnp.sum(soft_weights * grad_soft, axis=-1, keepdims=True)  124 us
    all_to_all x2, waiting for transfers between devices, local(): lax.all_to_all(triple, 'tensor', split_axis=3, concat_axis=1, tiled=True)  83.6 us
    dot_general x8, matrix products, times_transposed(): lax.dot_general(left, weight, (((1,), (1,)), ((), ())), preferred_element...  62.2 us
    dot_general x8, matrix products, contract_rows(): lax.dot_general(left, right, (((0,), (0,)), ((), ())), preferred_element_...  48 us
    unnamed x280, local copies, waits for them, and re-layouts  45.6 us
    reshape x6, local copies, waits for them, and re-layouts, attend_back(): grad_width.reshape(slab_count, heads_dev, window, window, window)  45 us
    psum x1, blocking collectives, local(): lax.psum((sums[0], sums[1], sums[3], sums[4], sums[5], sums[7], sums[8],...  41.9 us
  transfers between devices with their start and end apart: 16, of which 6 were waited for; matrix products, arithmetic and copies ran while one was open for 65% of the time, Pallas kernels for 0%

commit v1 on v0

v1 whole, which is shorter than its diff:
```python
import functools

import jax
import jax.numpy as jnp
import numpy as np
from jax import lax
from jax.experimental import pallas as pl
from jax.experimental.pallas import tpu as pltpu
from jax.sharding import PartitionSpec as P

HEADS = 12
HD = 64
WIN = 14
GRID = 64
WGRID = 5
WROWS = WIN * WIN
ROWS = 200
QUAD = 4
LANES = 128
SEG = 32
EPSILON = 1e-06
PENALTY = -1e9

F32 = jnp.float32
BF16 = jnp.bfloat16
VMEM_LIMIT = 58 * 1024 * 1024


def dot(left, right):
    return lax.dot_general(left, right, (((1,), (0,)), ((), ())), preferred_element_type=F32)


def dot_t(left, right):
    return lax.dot_general(left, right, (((1,), (1,)), ((), ())), preferred_element_type=F32)


def dot_rows(left, right):
    return lax.dot_general(left, right, (((0,), (0,)), ((), ())), preferred_element_type=F32)


def key_selectors(mirrored):
    out = np.zeros((QUAD, ROWS, LANES), np.float32)
    for head in range(QUAD):
        for key in range(WROWS):
            high, wide = key // WIN, key % WIN
            if mirrored:
                high, wide = WIN - 1 - high, WIN - 1 - wide
            out[head, key, SEG * head + high] = 1.0
            out[head, key, SEG * head + 16 + wide] = 1.0
    return jnp.asarray(out, BF16)


def block_diagonal(table):
    padded = jnp.pad(table.T, ((0, 0), (0, SEG - table.shape[0])))
    rows = []
    for head in range(QUAD):
        rows.append(jnp.pad(padded, ((0, 0), (SEG * head, LANES - SEG * (head + 1)))))
    return jnp.concatenate(rows, axis=0)


def forward_tables(height_table, width_table):
    high = jnp.roll(block_diagonal(height_table[::-1]), 1 - WIN, axis=1)
    wide = jnp.roll(block_diagonal(width_table[::-1]), 17 - WIN, axis=1)
    return jnp.concatenate([high, wide], axis=1).astype(BF16)


def backward_tables(height_table, width_table):
    high = block_diagonal(height_table)
    wide = jnp.roll(block_diagonal(width_table), 16, axis=1)
    return jnp.concatenate([high, wide], axis=1).astype(BF16)


def table_gradients(summed, count):
    high = summed[:, :LANES]
    wide = jnp.roll(summed[:, LANES:], -16, axis=1)
    out = []
    for part in (high, wide):
        total = 0.0
        for head in range(QUAD):
            total = total + part[HD * head : HD * (head + 1), SEG * head : SEG * head + count]
        out.append(total.T)
    return out


def valid_rows(high_limit, wide_limit):
    row = lax.broadcasted_iota(jnp.int32, (ROWS, 1), 0)
    high = (row * 4682) >> 16
    wide = row - high * WIN
    return (high < high_limit) & (wide < wide_limit) & (row < WROWS)


def roll_rows(values, by_width):
    sub = lax.broadcasted_iota(jnp.int32, (8, LANES), 0)
    pieces = []
    for start in range(0, ROWS, 8):
        piece = values[start : start + 8]
        first = start // WIN
        crossing = (first + 1) * WIN - start
        shifts = (first, first + 1)
        if by_width:
            one = pltpu.roll(piece, start - first * WIN, 1, stride=1, stride_axis=0)
        else:
            one = pltpu.roll(piece, first, 1) if first else piece
        if crossing < 8:
            if by_width:
                two = pltpu.roll(piece, LANES - crossing, 1)
                two = pltpu.roll(two, 0, 1, stride=1, stride_axis=0)
            else:
                two = pltpu.roll(piece, shifts[1], 1)
            one = jnp.where(sub < crossing, one, two)
        pieces.append(one)
    return jnp.concatenate(pieces, axis=0)


def normalize(values):
    centre = jnp.mean(values, axis=-1, keepdims=True)
    spread = values - centre
    variance = jnp.mean(spread * spread, axis=-1, keepdims=True)
    scale = lax.rsqrt(variance + EPSILON)
    return spread * scale, scale


def normalize_back(unit, scale, grad, gain):
    scaled = grad * gain
    mean_grad = jnp.mean(scaled, axis=-1, keepdims=True)
    mean_both = jnp.mean(scaled * unit, axis=-1, keepdims=True)
    return (scaled - mean_grad - unit * mean_both) * scale


def load_shards(shards, order_ref, target, sems, columns=None):
    copies = []
    for index, shard in enumerate(shards):
        source = shard if columns is None else shard.at[:, columns]
        height = shard.shape[0]
        start = pl.multiple_of(order_ref[index] * height, 16)
        copies.append(
            pltpu.make_async_copy(source, target.at[pl.ds(start, height), :], sems.at[index])
        )
    for copy in copies:
        copy.start()
    for copy in copies:
        copy.wait()


def gather_quarters(block, target, slabs, fill_tail):
    parts, rows = block.shape[0], block.shape[2]
    for slab in range(slabs):
        for part in range(parts):
            target[slab, part * rows : (part + 1) * rows, :] = block[part, slab].astype(F32)
        if fill_tail:
            target[slab, parts * rows :, :] = jnp.zeros(
                (ROWS - parts * rows, target.shape[2]), F32
            )


def attend_kernel(
    slabs,
    lims,
    order,
    tokens,
    gain,
    shift,
    bias,
    tables,
    selectors,
    w0,
    w1,
    w2,
    w3,
    *rest,
):
    rows_out, normed_out, triple_out, probs_out, attended_out, full, weight, masked_keys, sems = (
        rest[-9:]
    )
    step = pl.program_id(0)

    @pl.when(step == 0)
    def _():
        load_shards((w0, w1, w2, w3), order, weight, sems)

    width = full.shape[2]
    gather_quarters(tokens, full, slabs, True)
    rows = full[...].reshape(slabs * ROWS, width)
    unit, _ = normalize(rows)
    normed = (unit * gain[...] + shift[...]).astype(BF16)
    rows_out[...] = rows.astype(BF16).reshape(slabs, ROWS, width)
    normed_out[...] = normed.reshape(slabs, ROWS, width)
    for part in range(3):
        columns = slice(part * width, (part + 1) * width)
        triple = dot(normed, weight[:, columns]) + bias[:, columns]
        triple_out[:, :, columns] = triple.astype(BF16).reshape(slabs, ROWS, width)

    lane = lax.broadcasted_iota(jnp.int32, (ROWS, LANES), 1)
    within = lane & (SEG - 1)
    upper = lane >= HD
    quads = HEADS // QUAD
    for slab in range(slabs):
        which = step * slabs + slab
        allowed = valid_rows(lims[which, 0], lims[which, 1])
        penalty = jnp.where((lane == WIN) & jnp.logical_not(allowed), PENALTY, 0.0).astype(BF16)
        for head in range(QUAD):
            masked_keys[slab, head] = selectors[head] + penalty

    def one_quad(index, carry):
        slab = index // quads
        quad = index - slab * quads
        which = step * slabs + slab
        allowed = valid_rows(lims[which, 0], lims[which, 1])
        base = pl.multiple_of(quad * QUAD * HD, LANES)
        queries = triple_out[slab, :, pl.ds(base, QUAD * HD)]
        keys = triple_out[slab, :, pl.ds(pl.multiple_of(base + width, LANES), QUAD * HD)]
        values = triple_out[slab, :, pl.ds(pl.multiple_of(base + 2 * width, LANES), QUAD * HD)]
        terms = dot(queries, tables[...])
        high = roll_rows(terms[:, :LANES], False)
        wide = roll_rows(terms[:, LANES:], True)
        constant = jnp.where(lane == WIN, 1.0, 0.0)
        relative = jnp.where(
            within < WIN, high, jnp.where((within >= 16) & (within < 16 + WIN), wide, constant)
        ).astype(BF16)
        queries = queries * jnp.asarray(HD**-0.5, BF16)
        outs = []
        for pair in range(QUAD // 2):
            columns = slice(pair * LANES, (pair + 1) * LANES)
            left = jnp.concatenate([queries[:, columns], relative], axis=1)
            total = None
            for side in range(2):
                head = 2 * pair + side
                mine = upper if side else jnp.logical_not(upper)
                zero = jnp.zeros((ROWS, LANES), BF16)
                right = jnp.concatenate(
                    [jnp.where(mine, keys[:, columns], zero), masked_keys[slab, head]], axis=1
                )
                scores = dot_t(left, right)
                maxima = jnp.max(scores, axis=-1, keepdims=True)
                exponent = jnp.exp(scores - maxima)
                summed = jnp.sum(exponent, axis=-1, keepdims=True)
                probs = (exponent * (1.0 / summed)).astype(BF16)
                probs_out[slab, quad * QUAD + head] = probs
                part = dot(probs, jnp.where(mine, values[:, columns], zero))
                total = part if total is None else total + part
            outs.append(total)
        mixed = jnp.concatenate(outs, axis=1)
        mixed = jnp.where(allowed, mixed, 0.0)
        attended_out[slab, :, pl.ds(base, QUAD * HD)] = mixed.astype(BF16)
        return carry

    lax.fori_loop(0, slabs * quads, one_quad, 0)


def attend(micro, slabs_all, lims, order, tokens, gain, shift, bias, tables, selectors, shards, kept):
    parts, slabs_here, rows_dev, width = tokens.shape
    slabs = 2 if slabs_here % 2 == 0 else 1
    steps = slabs_here // slabs
    here = micro * steps
    triple_width = shards[0].shape[1]
    block3 = lambda columns: pl.BlockSpec((slabs, ROWS, columns), lambda i, *_: (i + here, 0, 0))
    whole = lambda *shape: pl.BlockSpec(shape, lambda i, *_: (0,) * len(shape))
    anywhere = pl.BlockSpec(memory_space=pl.ANY)
    out_shape = (
        jax.ShapeDtypeStruct((slabs_all, ROWS, width), BF16),
        jax.ShapeDtypeStruct((slabs_all, ROWS, width), BF16),
        jax.ShapeDtypeStruct((slabs_all, ROWS, triple_width), BF16),
        jax.ShapeDtypeStruct((slabs_all, HEADS, ROWS, ROWS), BF16),
        jax.ShapeDtypeStruct((slabs_all, ROWS, width), BF16),
    )
    in_specs = [
        pl.BlockSpec((parts, slabs, rows_dev, width), lambda i, *_: (0, i, 0, 0)),
        whole(1, width),
        whole(1, width),
        whole(1, triple_width),
        whole(2 * LANES, 2 * LANES),
        whole(QUAD, ROWS, LANES),
    ] + [anywhere] * 4
    aliases = {}
    if kept is not None:
        aliases = {2 + len(in_specs) + n: n for n in range(len(kept))}
        in_specs = in_specs + [anywhere] * len(kept)
    rows = slabs_here * ROWS
    flops = 2 * rows * width * triple_width + slabs_here * HEADS * 2 * 2 * ROWS * ROWS * 256
    return pl.pallas_call(
        functools.partial(attend_kernel, slabs),
        out_shape=out_shape,
        grid_spec=pltpu.PrefetchScalarGridSpec(
            num_scalar_prefetch=2,
            grid=(steps,),
            in_specs=in_specs,
            out_specs=(
                block3(width),
                block3(width),
                block3(triple_width),
                pl.BlockSpec((slabs, HEADS, ROWS, ROWS), lambda i, *_: (i + here, 0, 0, 0)),
                block3(width),
            ),
            scratch_shapes=[
                pltpu.VMEM((slabs, ROWS, width), F32),
                pltpu.VMEM((width, triple_width), BF16),
                pltpu.VMEM((slabs, QUAD, ROWS, LANES), BF16),
                pltpu.SemaphoreType.DMA((4,)),
            ],
        ),
        input_output_aliases=aliases,
        compiler_params=pltpu.CompilerParams(vmem_limit_bytes=VMEM_LIMIT),
        cost_estimate=pl.CostEstimate(
            flops=flops,
            bytes_accessed=rows * (width * 8 + triple_width * 2 + HEADS * 512) + width * 4608,
            transcendentals=slabs_here * HEADS * ROWS * ROWS,
        ),
        name="attend",
    )(lims, order, tokens, gain, shift, bias, tables, selectors, *shards, *(kept or ()))


def project_kernel(
    slabs, lims, order, attended, rows_in, grads, bias, gain, shift, w0, w1, w2, w3,
    middle_out, normed_out, branch_out, shrink_bias_out, full, weight, sems,
):
    step = pl.program_id(0)

    @pl.when(step == 0)
    def _():
        load_shards((w0, w1, w2, w3), order, weight, sems)
        shrink_bias_out[...] = jnp.zeros_like(shrink_bias_out)

    width = full.shape[2]
    count = slabs * ROWS
    middle = (
        rows_in[...].reshape(count, width).astype(F32)
        + dot(attended[...].reshape(count, width), weight[...])
        + bias[...]
    )
    unit, _ = normalize(middle)
    middle_out[...] = middle.reshape(slabs, ROWS, width)
    normed_out[...] = (unit * gain[...] + shift[...]).astype(BF16).reshape(slabs, ROWS, width)
    gather_quarters(grads.at[0], full, slabs, True)
    for slab in range(slabs):
        which = step * slabs + slab
        allowed = valid_rows(lims[which, 0], lims[which, 1])
        branch = jnp.where(allowed, full[slab], 0.0)
        branch_out[slab] = branch.astype(BF16)
        shrink_bias_out[...] += jnp.sum(branch, axis=0, keepdims=True)


def project(lims, order, attended, rows_in, grads, bias, gain, shift, shards):
    slabs_all, _, width = attended.shape
    micros, parts, slabs_here, rows_dev, _ = grads.shape
    slabs = 2 if slabs_here % 2 == 0 else 1
    per = slabs_here // slabs
    block = pl.BlockSpec((slabs, ROWS, width), lambda i, *_: (i, 0, 0))
    vector = pl.BlockSpec((1, width), lambda i, *_: (0, 0))
    anywhere = pl.BlockSpec(memory_space=pl.ANY)
    rows = slabs_all * ROWS
    return pl.pallas_call(
        functools.partial(project_kernel, slabs),
        out_shape=(
            jax.ShapeDtypeStruct((slabs_all, ROWS, width), F32),
            jax.ShapeDtypeStruct((slabs_all, ROWS, width), BF16),
            jax.ShapeDtypeStruct((slabs_all, ROWS, width), BF16),
            jax.ShapeDtypeStruct((1, width), F32),
        ),
        grid_spec=pltpu.PrefetchScalarGridSpec(
            num_scalar_prefetch=2,
            grid=(micros * per,),
            in_specs=[
                block,
                block,
                pl.BlockSpec(
                    (1, parts, slabs, rows_dev, width), lambda i, *_: (i // per, 0, i % per, 0, 0)
                ),
                vector,
                vector,
                vector,
            ]
            + [anywhere] * 4,
            out_specs=(block, block, block, vector),
            scratch_shapes=[
                pltpu.VMEM((slabs, ROWS, width), F32),
                pltpu.VMEM((width, width), BF16),
                pltpu.SemaphoreType.DMA((4,)),
            ],
        ),
        compiler_params=pltpu.CompilerParams(vmem_limit_bytes=VMEM_LIMIT),
        cost_estimate=pl.CostEstimate(
            flops=2 * rows * width * width, bytes_accessed=rows * width * 14, transcendentals=0
        ),
        name="project",
    )(lims, order, attended, rows_in, grads, bias, gain, shift, *shards)


def gate_both(hidden):
    half = 0.5 * (1.0 + lax.erf(hidden * 0.7071067811865476))
    density = jnp.exp(hidden * hidden * -0.5) * 0.3989422804014327
    return hidden * half, half + hidden * density


def feed_kernel(
    relative, first, tile, lims, order, normed, branch, bias, shrink, e0, e1, e2, e3, *rest,
):
    if not first:
        out_in, grad_in = rest[:2]
    (out_acc, grad_acc, expand_grad, shrink_grad, bias_grad, expand, acc_e, acc_s, sems) = rest[-9:]
    step = pl.program_id(0)
    last = pl.num_programs(0) - 1
    chunk = shrink.shape[0]
    width = shrink.shape[1]

    @pl.when(step == 0)
    def _():
        start = pl.multiple_of(order[relative] * chunk, LANES)
        load_shards((e0, e1, e2, e3), order, expand, sems, pl.ds(start, chunk))
        acc_e[...] = jnp.zeros_like(acc_e)
        acc_s[...] = jnp.zeros_like(acc_s)
        bias_grad[...] = jnp.zeros_like(bias_grad)

    rows = normed[...]
    grads = branch[...]
    total_out = None
    total_grad = None
    for start in range(0, chunk, tile):
        columns = slice(start, start + tile)
        hidden = dot(rows, expand[:, columns]) + bias[0, :, columns]
        active, slope = gate_both(hidden)
        active = active.astype(BF16)
        part = dot(active, shrink[columns, :])
        total_out = part if total_out is None else total_out + part
        back = (dot_t(grads, shrink[columns, :]) * slope).astype(BF16)
        acc_s[columns, :] += dot_rows(active, grads)
        acc_e[:, columns] += dot_rows(rows, back)
        bias_grad[:, columns] += jnp.sum(back.astype(F32), axis=0, keepdims=True)
        part = dot_t(back, expand[:, columns])
        total_grad = part if total_grad is None else total_grad + part
    if first:
        out_acc[...] = total_out
        grad_acc[...] = total_grad
    else:
        out_acc[...] = out_in[...] + total_out
        grad_acc[...] = grad_in[...] + total_grad

    @pl.when(step == last)
    def _():
        shrink_grad[...] = acc_s[...].astype(BF16)
        parts, height = expand_grad.shape[0], expand_grad.shape[1]
        for part in range(parts):
            start = pl.multiple_of(order[part] * height, 16)
            expand_grad[part] = acc_e[pl.ds(start, height), :].astype(BF16)


def feed(relative, lims, order, normed, branch, bias, shrink, shards, kept):
    rows, width = normed.shape
    chunk = shrink.shape[0]
    parts = len(shards)
    height = shards[0].shape[0]
    block_rows = 2 * ROWS
    block = pl.BlockSpec((block_rows, width), lambda i, *_: (i, 0))
    anywhere = pl.BlockSpec(memory_space=pl.ANY)
    in_specs = [
        block,
        block,
        pl.BlockSpec((1, 1, chunk), lambda i, lims, order: (order[relative], 0, 0)),
        pl.BlockSpec((chunk, width), lambda i, *_: (0, 0)),
    ] + [anywhere] * parts
    aliases = {}
    if kept is not None:
        aliases = {2 + len(in_specs) + n: n for n in range(2)}
        in_specs = in_specs + [block, block]
    else:
        kept = ()
    return pl.pallas_call(
        functools.partial(feed_kernel, relative, not kept, 256),
        out_shape=(
            jax.ShapeDtypeStruct((rows, width), F32),
            jax.ShapeDtypeStruct((rows, width), F32),
            jax.ShapeDtypeStruct((parts, height, chunk), BF16),
            jax.ShapeDtypeStruct((chunk, width), BF16),
            jax.ShapeDtypeStruct((1, chunk), F32),
        ),
        grid_spec=pltpu.PrefetchScalarGridSpec(
            num_scalar_prefetch=2,
            grid=(rows // block_rows,),
            in_specs=in_specs,
            out_specs=(
                block,
                block,
                pl.BlockSpec((parts, height, chunk), lambda i, *_: (0, 0, 0)),
                pl.BlockSpec((chunk, width), lambda i, *_: (0, 0)),
                pl.BlockSpec((1, chunk), lambda i, *_: (0, 0)),
            ),
            scratch_shapes=[
                pltpu.VMEM((width, chunk), BF16),
                pltpu.VMEM((width, chunk), F32),
                pltpu.VMEM((chunk, width), F32),
                pltpu.SemaphoreType.DMA((parts,)),
            ],
        ),
        input_output_aliases=aliases,
        compiler_params=pltpu.CompilerParams(vmem_limit_bytes=VMEM_LIMIT),
        cost_estimate=pl.CostEstimate(
            flops=12 * rows * width * chunk,
            bytes_accessed=rows * width * 20 + width * chunk * 8,
            transcendentals=2 * rows * chunk,
        ),
        name="feed",
    )(lims, order, normed, branch, bias, shrink, *shards, *kept)


def middle_kernel(
    slabs, lims, order, middle, out_acc, grad_acc, branch, attended, bias, gain, w0, w1, w2, w3,
    result_out, d_middle_out, d_attended_out, weight_grad, output_bias_grad, gain_grad, shift_grad,
    full, weight, acc, sems,
):
    step = pl.program_id(0)
    last = pl.num_programs(0) - 1

    @pl.when(step == 0)
    def _():
        load_shards((w0, w1, w2, w3), order, weight, sems)
        acc[...] = jnp.zeros_like(acc)
        output_bias_grad[...] = jnp.zeros_like(output_bias_grad)
        gain_grad[...] = jnp.zeros_like(gain_grad)
        shift_grad[...] = jnp.zeros_like(shift_grad)

    width = full.shape[2]
    count = slabs * ROWS
    rows = middle[...].reshape(count, width)
    full[...] = (rows + out_acc[...] + bias[...]).reshape(slabs, ROWS, width)
    parts, rows_dev = result_out.shape[1], result_out.shape[3]
    for slab in range(slabs):
        for part in range(parts):
            result_out[0, part, slab] = full[
                slab, part * rows_dev : (part + 1) * rows_dev, :
            ].astype(BF16)
    unit, scale = normalize(rows)
    grad = grad_acc[...]
    gain_grad[...] += jnp.sum(grad * unit, axis=0, keepdims=True)
    shift_grad[...] += jnp.sum(grad, axis=0, keepdims=True)
    d_middle = branch[...].reshape(count, width).astype(F32) + normalize_back(
        unit, scale, grad, gain[...]
    )
    d_middle_out[...] = d_middle.reshape(slabs, ROWS, width)
    d_output = d_middle.astype(BF16)
    output_bias_grad[...] += jnp.sum(d_output.astype(F32), axis=0, keepdims=True)
    acc[...] += dot_rows(attended[...].reshape(count, width), d_output)
    d_attended = dot_t(d_output, weight[...]).astype(BF16)
    d_attended_out[...] = d_attended.reshape(slabs, ROWS, width)
    for slab in range(slabs):
        which = step * slabs + slab
        allowed = valid_rows(lims[which, 0], lims[which, 1])
        mine = d_attended_out[slab]
        d_attended_out[slab] = jnp.where(allowed, mine, jnp.zeros_like(mine))

    @pl.when(step == last)
    def _():
        height = weight_grad.shape[1]
        for part in range(weight_grad.shape[0]):
            start = pl.multiple_of(order[part] * height, 16)
            weight_grad[part] = acc[pl.ds(start, height), :].astype(BF16)


def middle_back(micros, parts, lims, order, middle, out_acc, grad_acc, branch, attended, bias, gain, shards):
    slabs_all, _, width = attended.shape
    slabs_here = slabs_all // micros
    rows_dev = WROWS // parts
    slabs = 2 if slabs_here % 2 == 0 else 1
    per = slabs_here // slabs
    height = shards[0].shape[0]
    block = pl.BlockSpec((slabs, ROWS, width), lambda i, *_: (i, 0, 0))
    flat = pl.BlockSpec((slabs * ROWS, width), lambda i, *_: (i, 0))
    vector = pl.BlockSpec((1, width), lambda i, *_: (0, 0))
    anywhere = pl.BlockSpec(memory_space=pl.ANY)
    rows = slabs_all * ROWS
    vec = jax.ShapeDtypeStruct((1, width), F32)
    return pl.pallas_call(
        functools.partial(middle_kernel, slabs),
        out_shape=(
            jax.ShapeDtypeStruct((micros, parts, slabs_here, rows_dev, width), BF16),
            jax.ShapeDtypeStruct((slabs_all, ROWS, width), F32),
            jax.ShapeDtypeStruct((slabs_all, ROWS, width), BF16),
            jax.ShapeDtypeStruct((len(shards), height, width), BF16),
            vec,
            vec,
            vec,
        ),
        grid_spec=pltpu.PrefetchScalarGridSpec(
            num_scalar_prefetch=2,
            grid=(micros * per,),
            in_specs=[block, flat, flat, block, block, vector, vector] + [anywhere] * len(shards),
            out_specs=(
                pl.BlockSpec(
                    (1, parts, slabs, rows_dev, width), lambda i, *_: (i // per, 0, i % per, 0, 0)
                ),
                block,
                block,
                pl.BlockSpec((len(shards), height, width), lambda i, *_: (0, 0, 0)),
                vector,
                vector,
                vector,
            ),
            scratch_shapes=[
                pltpu.VMEM((slabs, ROWS, width), F32),
                pltpu.VMEM((width, width), BF16),
                pltpu.VMEM((width, width), F32),
                pltpu.SemaphoreType.DMA((len(shards),)),
            ],
        ),
        compiler_params=pltpu.CompilerParams(vmem_limit_bytes=VMEM_LIMIT),
        cost_estimate=pl.CostEstimate(
            flops=4 * rows * width * width, bytes_accessed=rows * width * 24, transcendentals=0
        ),
        name="middle",
    )(lims, order, middle, out_acc, grad_acc, branch, attended, bias, gain, *shards)


def attend_back_kernel(
    slabs, order, normed, queries_in, keys_in, values_in, probs_in, d_mixed_in, mixed_in,
    tables, selectors, sums,
    d_queries, d_keys, d_values, weight_grad, bias_grad, table_grad, grads, acc,
):
    step = pl.program_id(0)
    last = pl.num_programs(0) - 1
    wide4 = QUAD * HD

    @pl.when(step == 0)
    def _():
        acc[...] = jnp.zeros_like(acc)
        bias_grad[...] = jnp.zeros_like(bias_grad)
        table_grad[...] = jnp.zeros_like(table_grad)

    lane = lax.broadcasted_iota(jnp.int32, (ROWS, LANES), 1)
    within = lane & (SEG - 1)
    upper = lane >= HD
    zero = jnp.zeros((ROWS, LANES), BF16)

    def one_slab(slab, carry):
        queries, keys, values = queries_in[slab], keys_in[slab], values_in[slab]
        d_mixed = d_mixed_in[slab]
        product = d_mixed.astype(F32) * mixed_in[slab].astype(F32)
        product_high = product.astype(BF16)
        product_low = (product - product_high.astype(F32)).astype(BF16)
        inner = dot(product_high, sums[...]) + dot(product_low, sums[...])
        inner_high = inner.astype(BF16)
        inner_low = (inner - inner_high.astype(F32)).astype(BF16)
        inner = jnp.where((lane & 1) == 0, inner_high, inner_low)
        d_relative = None
        dq, dk, dv = [], [], []
        for pair in range(QUAD // 2):
            columns = slice(pair * LANES, (pair + 1) * LANES)
            left = jnp.concatenate([d_mixed[:, columns], inner], axis=1)
            dq_pair = dk_pair = dv_pair = None
            for side in range(2):
                head = 2 * pair + side
                mine = upper if side else jnp.logical_not(upper)
                minus = jnp.where((lane == 2 * head) | (lane == 2 * head + 1), -1.0, 0.0)
                right = jnp.concatenate(
                    [jnp.where(mine, values[:, columns], zero), minus.astype(BF16)], axis=1
                )
                d_probs = dot_t(left, right)
                probs = probs_in[slab, head]
                d_scores = (probs.astype(F32) * d_probs).astype(BF16)
                back = dot(
                    d_scores,
                    jnp.concatenate(
                        [jnp.where(mine, keys[:, columns], zero), selectors[head]], axis=1
                    ),
                )
                part_k = dot_rows(d_scores, jnp.where(mine, queries[:, columns], zero))
                part_v = dot_rows(probs, jnp.where(mine, d_mixed[:, columns], zero))
                if dq_pair is None:
                    dq_pair, dk_pair, dv_pair = back[:, :LANES], part_k, part_v
                else:
                    dq_pair = dq_pair + back[:, :LANES]
                    dk_pair = dk_pair + part_k
                    dv_pair = dv_pair + part_v
                d_relative = back[:, LANES:] if d_relative is None else d_relative + back[:, LANES:]
            dq.append(dq_pair)
            dk.append(dk_pair)
            dv.append(dv_pair)
        high = roll_rows(jnp.where(within < WIN, d_relative, 0.0), False)
        wide = roll_rows(
            jnp.where((within >= 16) & (within < 16 + WIN), d_relative, 0.0), True
        )
        d_terms = jnp.concatenate([high, wide], axis=1).astype(BF16)
        scale = HD**-0.5
        dq = jnp.concatenate(dq, axis=1) * scale + dot_t(d_terms, tables[...])
        table_grad[...] += dot_rows(queries, d_terms)
        dq = dq.astype(BF16)
        dk = (jnp.concatenate(dk, axis=1) * scale).astype(BF16)
        dv = jnp.concatenate(dv, axis=1).astype(BF16)
        d_queries[slab] = dq
        d_keys[slab] = dk
        d_values[slab] = dv
        grads[slab] = jnp.concatenate([dq, dk, dv], axis=1)
        return carry

    lax.fori_loop(0, slabs, one_slab, 0)
    width = normed.shape[2]
    both = grads[...].reshape(slabs * ROWS, 3 * wide4)
    bias_grad[...] += jnp.sum(both.astype(F32), axis=0, keepdims=True)
    acc[...] += dot_rows(normed[...].reshape(slabs * ROWS, width), both)

    @pl.when(step == last)
    def _():
        height = weight_grad.shape[1]
        for part in range(weight_grad.shape[0]):
            start = pl.multiple_of(order[part] * height, 16)
            weight_grad[part] = acc[pl.ds(start, height), :].astype(BF16)


def attend_back(quad, parts, order, normed, triple, probs, d_mixed, mixed, tables, selectors, sums):
    slabs_all, _, width = normed.shape
    slabs = 2 if slabs_all % 2 == 0 else 1
    wide4 = QUAD * HD
    quads = HEADS // QUAD
    column = lambda where: pl.BlockSpec((slabs, ROWS, wide4), lambda i, *_: (i, 0, where))
    whole = lambda *shape: pl.BlockSpec(shape, lambda i, *_: (0,) * len(shape))
    narrow = jax.ShapeDtypeStruct((slabs_all, ROWS, wide4), BF16)
    out_block = pl.BlockSpec((slabs, ROWS, wide4), lambda i, *_: (i, 0, 0))
    rows = slabs_all * ROWS
    return pl.pallas_call(
        functools.partial(attend_back_kernel, slabs),
        out_shape=(
            narrow,
            narrow,
            narrow,
            jax.ShapeDtypeStruct((parts, width // parts, 3 * wide4), BF16),
            jax.ShapeDtypeStruct((1, 3 * wide4), F32),
            jax.ShapeDtypeStruct((wide4, 2 * LANES), F32),
        ),
        grid_spec=pltpu.PrefetchScalarGridSpec(
            num_scalar_prefetch=1,
            grid=(slabs_all // slabs,),
            in_specs=[
                pl.BlockSpec((slabs, ROWS, width), lambda i, *_: (i, 0, 0)),
                column(quad),
                column(quads + quad),
                column(2 * quads + quad),
                pl.BlockSpec((slabs, QUAD, ROWS, ROWS), lambda i, *_: (i, quad, 0, 0)),
                column(quad),
                column(quad),
                whole(wide4, 2 * LANES),
                whole(QUAD, ROWS, LANES),
                whole(wide4, LANES),
            ],
            out_specs=(
                out_block,
                out_block,
                out_block,
                whole(parts, width // parts, 3 * wide4),
                whole(1, 3 * wide4),
                whole(wide4, 2 * LANES),
            ),
            scratch_shapes=[
                pltpu.VMEM((slabs, ROWS, 3 * wide4), BF16),
                pltpu.VMEM((width, 3 * wide4), F32),
            ],
        ),
        compiler_params=pltpu.CompilerParams(vmem_limit_bytes=VMEM_LIMIT),
        cost_estimate=pl.CostEstimate(
            flops=2 * rows * width * 3 * wide4 + slabs_all * QUAD * 2 * 4 * ROWS * ROWS * 256,
            bytes_accessed=rows * (width * 2 + wide4 * 16 + QUAD * 512),
            transcendentals=0,
        ),
        name="attend_back",
    )(order, normed, triple, triple, triple, probs, d_mixed, mixed, tables, selectors, sums)


def first_kernel(slabs, order, rows_in, d_middle, gain, *rest):
    grads, (w0, w1, w2, w3) = rest[:9], rest[9:13]
    out, gain_grad, shift_grad, full, weight, sems = rest[13:]
    step = pl.program_id(0)

    @pl.when(step == 0)
    def _():
        load_shards((w0, w1, w2, w3), order, weight, sems)
        gain_grad[...] = jnp.zeros_like(gain_grad)
        shift_grad[...] = jnp.zeros_like(shift_grad)

    width = full.shape[2]
    count = slabs * ROWS
    total = None
    wide4 = QUAD * HD
    for index, grad in enumerate(grads):
        part = dot_t(
            grad[...].reshape(count, wide4), weight[:, index * wide4 : (index + 1) * wide4]
        )
        total = part if total is None else total + part
    unit, scale = normalize(rows_in[...].reshape(count, width).astype(F32))
    gain_grad[...] += jnp.sum(total * unit, axis=0, keepdims=True)
    shift_grad[...] += jnp.sum(total, axis=0, keepdims=True)
    back = normalize_back(unit, scale, total, gain[...])
    full[...] = d_middle[...] + back.reshape(slabs, ROWS, width)
    parts, rows_dev = out.shape[0], out.shape[2]
    for slab in range(slabs):
        for part in range(parts):
            out[part, slab] = full[slab, part * rows_dev : (part + 1) * rows_dev, :].astype(BF16)


def first_back(micro, micros, parts, order, rows_in, d_middle, gain, grads, shards):
    slabs_all, _, width = rows_in.shape
    slabs_here = slabs_all // micros
    slabs = 2 if slabs_here % 2 == 0 else 1
    steps = slabs_here // slabs
    here = micro * steps
    rows_dev = WROWS // parts
    wide4 = QUAD * HD
    block = pl.BlockSpec((slabs, ROWS, width), lambda i, *_: (i + here, 0, 0))
    narrow = pl.BlockSpec((slabs, ROWS, wide4), lambda i, *_: (i + here, 0, 0))
    vector = pl.BlockSpec((1, width), lambda i, *_: (0, 0))
    anywhere = pl.BlockSpec(memory_space=pl.ANY)
    rows = slabs_here * ROWS
    return pl.pallas_call(
        functools.partial(first_kernel, slabs),
        out_shape=(
            jax.ShapeDtypeStruct((parts, slabs_here, rows_dev, width), BF16),
            jax.ShapeDtypeStruct((1, width), F32),
            jax.ShapeDtypeStruct((1, width), F32),
        ),
        grid_spec=pltpu.PrefetchScalarGridSpec(
            num_scalar_prefetch=1,
            grid=(steps,),
            in_specs=[block, block, vector] + [narrow] * len(grads) + [anywhere] * len(shards),
            out_specs=(
                pl.BlockSpec((parts, slabs, rows_dev, width), lambda i, *_: (0, i, 0, 0)),
                vector,
                vector,
            ),
            scratch_shapes=[
                pltpu.VMEM((slabs, ROWS, width), F32),
                pltpu.VMEM((width, 3 * width), BF16),
                pltpu.SemaphoreType.DMA((len(shards),)),
            ],
        ),
        compiler_params=pltpu.CompilerParams(vmem_limit_bytes=VMEM_LIMIT),
        cost_estimate=pl.CostEstimate(
            flops=6 * rows * width * width, bytes_accessed=rows * width * 14, transcendentals=0
        ),
        name="first_back",
    )(order, rows_in, d_middle, gain, *grads, *shards)


def exchange(values, bit):
    count = lax.axis_size("tensor")
    return lax.ppermute(values, "tensor", [(n, n ^ bit) for n in range(count)])


def gather_shards(shard):
    far = exchange(shard, 2)
    near = exchange(shard, 1)
    return (shard, near, far, exchange(far, 1))


def swap_windows(values, axis):
    return lax.all_to_all(values, "tensor", split_axis=axis, concat_axis=axis, tiled=True)


def reduce_group(pieces):
    mine = lax.axis_index("tensor")
    out = []
    for piece in pieces:
        ordered = jnp.take(piece, jnp.arange(piece.shape[0]) ^ mine, axis=0)
        share = lax.psum_scatter(ordered, "tensor", scatter_dimension=0, tiled=True)
        share = share.reshape(piece.shape[1:])
        part = lax.psum_scatter(share, ("dp", "seq"), scatter_dimension=0, tiled=True)
        out.append(lax.all_gather(part, ("dp", "seq"), axis=0, tiled=True))
    return out


def local(
    tokens,
    out_grad,
    slot_window,
    first_gain,
    first_shift,
    triple_weight,
    triple_bias,
    height_table,
    width_table,
    output_weight,
    output_bias,
    second_gain,
    second_shift,
    expand_weight,
    expand_bias,
    shrink_weight,
    shrink_bias,
):
    micros, images, slots, rows_dev, width = tokens.shape
    parts = lax.axis_size("tensor")
    mine = lax.axis_index("tensor")
    slabs_here = images * slots // parts
    slabs_all = micros * slabs_here
    rows = slabs_all * ROWS
    order = mine ^ jnp.arange(parts, dtype=jnp.int32)
    vector = lambda item: item.reshape(1, -1)

    windows = slot_window.reshape(micros, parts, slabs_here)
    windows = lax.dynamic_index_in_dim(windows, mine, axis=1, keepdims=False).reshape(-1)
    limits = jnp.stack([GRID - windows // WGRID * WIN, GRID - windows % WGRID * WIN], axis=1)
    limits = jnp.where((windows < WGRID * WGRID)[:, None], limits, 0).astype(jnp.int32)

    rows_in = [
        swap_windows(tokens[m].reshape(parts, slabs_here, rows_dev, width), 0)
        for m in range(micros)
    ]
    triple_shards = gather_shards(triple_weight)
    output_shards = gather_shards(output_weight)
    expand_shards = gather_shards(expand_weight)
    shrink_shards = gather_shards(shrink_weight)
    grads_in = swap_windows(out_grad.reshape(micros, parts, slabs_here, rows_dev, width), 1)

    ahead = forward_tables(height_table, width_table)
    behind = backward_tables(height_table, width_table)
    selectors = key_selectors(False)
    mirrored = key_selectors(True)
    sums = np.zeros((QUAD * HD, LANES), np.float32)
    for head in range(QUAD):
        sums[head * HD : (head + 1) * HD, 2 * head : 2 * head + 2] = 1.0
    sums = jnp.asarray(sums, BF16)

    kept = None
    for m in range(micros):
        kept = attend(
            m, slabs_all, limits[m * slabs_here : (m + 1) * slabs_here], order, rows_in[m],
            vector(first_gain), vector(first_shift), vector(triple_bias), ahead, selectors,
            triple_shards, kept,
        )
    full_rows, normed, triple, probs, attended = kept

    middle, normed2, branch, shrink_bias_grad = project(
        limits, order, attended, full_rows, grads_in, vector(output_bias), vector(second_gain),
        vector(second_shift), output_shards,
    )
    flat_normed2 = normed2.reshape(rows, width)
    flat_branch = branch.reshape(rows, width)
    bias_chunks = expand_bias.reshape(parts, 1, -1)
    sums_kept = None
    expand_grads, shrink_grads, expand_bias_grads = [], [], []
    for relative in range(parts):
        out_acc, grad_acc, expand_grad, shrink_grad, bias_grad = feed(
            relative, limits, order, flat_normed2, flat_branch, bias_chunks,
            shrink_shards[relative], expand_shards, sums_kept,
        )
        sums_kept = (out_acc, grad_acc)
        expand_grads.append(expand_grad)
        shrink_grads.append(shrink_grad)
        expand_bias_grads.append(bias_grad)

    result, d_middle, d_attended, output_grad, output_bias_grad, gain2_grad, shift2_grad = (
        middle_back(
            micros, parts, limits, order, middle, out_acc, grad_acc, branch, attended,
            vector(shrink_bias), vector(second_gain), output_shards,
        )
    )
    result = swap_windows(result, 1).reshape(tokens.shape)

    expand_grads = jnp.take(jnp.stack(expand_grads), order, axis=0)
    expand_grads = jnp.moveaxis(expand_grads, 0, 2).reshape(parts, width // parts, -1)
    shrink_grads = jnp.stack(shrink_grads)

    quad_grads, triple_grads, triple_bias_grads, table_sum = [], [], [], 0.0
    for quad in range(HEADS // QUAD):
        dq, dk, dv, weight_grad, bias_grad, table_grad = attend_back(
            quad, parts, order, normed, triple, probs, d_attended, attended, behind, mirrored, sums
        )
        quad_grads.append((dq, dk, dv))
        triple_grads.append(weight_grad)
        triple_bias_grads.append(bias_grad)
        table_sum = table_sum + table_grad
    wide4 = QUAD * HD
    grads9 = [quad_grads[quad][part] for part in range(3) for quad in range(HEADS // QUAD)]
    by_part = lambda items: jnp.concatenate(
        [
            item[..., part * wide4 : (part + 1) * wide4]
            for part in range(3)
            for item in items
        ],
        axis=-1,
    )
    triple_grads = by_part(triple_grads)
    triple_bias_grad = by_part(triple_bias_grads)

    token_grads, gain1_grad, shift1_grad = [], 0.0, 0.0
    for m in range(micros):
        token_grad, gain_grad, shift_grad = first_back(
            m, micros, parts, order, full_rows, d_middle, vector(first_gain), grads9, triple_shards
        )
        token_grads.append(swap_windows(token_grad, 0))
        gain1_grad = gain1_grad + gain_grad
        shift1_grad = shift1_grad + shift_grad
    tokens_gradient = jnp.stack(token_grads).reshape(tokens.shape)

    shrink_gradient, expand_gradient, output_gradient, triple_gradient = (
        item.astype(F32)
        for item in reduce_group((shrink_grads, expand_grads, output_grad, triple_grads))
    )
    expand_bias_grad = jnp.take(
        jnp.stack(expand_bias_grads).reshape(parts, -1), order, axis=0
    ).reshape(1, -1)
    height_grad, width_grad = table_gradients(table_sum, height_table.shape[0])
    small = [
        gain1_grad, shift1_grad, triple_bias_grad, height_grad, width_grad, output_bias_grad,
        gain2_grad, shift2_grad, expand_bias_grad, shrink_bias_grad,
    ]
    packed = jnp.concatenate([item.reshape(-1) for item in small])
    packed = lax.psum(packed, ("dp", "seq", "tensor"))
    outs, start = [], 0
    for item, like in zip(
        small,
        (
            first_gain, first_shift, triple_bias, height_table, width_table, output_bias,
            second_gain, second_shift, expand_bias, shrink_bias,
        ),
    ):
        outs.append(packed[start : start + item.size].reshape(like.shape))
        start += item.size
    return (
        result,
        tokens_gradient,
        outs[0],
        outs[1],
        triple_gradient,
        outs[2],
        outs[3],
        outs[4],
        output_gradient,
        outs[5],
        outs[6],
        outs[7],
        expand_gradient,
        outs[8],
        shrink_gradient,
        outs[9],
    )


def solution(mesh):
    split = P(None, "dp", "seq", "tensor", None)
    rows = P("tensor", None)
    return jax.shard_map(
        local,
        mesh=mesh,
        in_specs=(
            split, split, P(None, "dp", "seq"), P(), P(), rows, P(), P(), P(), rows, P(), P(), P(),
            rows, P(), rows, P(),
        ),
        out_specs=(
            split, split, P(), P(), rows, P(), P(), P(), rows, P(), P(), P(), rows, P(), rows, P(),
        ),
        check_vma=False,
    )
```

time: 1700 us -> 819 us (0.48)
  matrix products: 448 us -> 0 us
  local copies, waits for them, and re-layouts: 507 us -> 103 us
  Pallas kernels: 0 us -> 242 us
  blocking collectives: 319 us -> 109 us
  other arithmetic: 219 us -> 36.5 us
  waiting for transfers between devices: 140 us -> 278 us
    dot_general x62 -> x0, matrix products: 448 us -> none  [the longest x8 62.2 us: times_transposed(): lax.dot_general(left, weight, (((1,), (1,)), ((), ())), preferred_element...]
    psum x2 -> x1, blocking collectives: 319 us -> 40.7 us  [local(): packed = lax.psum(packed, ('dp', 'seq', 'tensor'))]
    reshape x38 -> x14, local copies, waits for them, and re-layouts: 256 us -> 10.9 us  [the longest x7 4.09 us: local(): vector = lambda item: item.reshape(1, -1)]
    pallas_call x0 -> x13, Pallas kernels: none -> 242 us  [the longest x4 90.9 us: feed(): pl.pallas_call(functools.partial(feed_kernel, relative, not kept, 256), o...]
    reduce_scatter x4 -> x8, waiting for transfers between devices: 0.03 us -> 163 us  [the longest x4 104 us: reduce_group(): lax.psum_scatter(share, ('dp', 'seq'), scatter_dimension=0, tiled=True)]
    sub x2 -> x1, other arithmetic: 124 us -> 0.01 us  [local(): GRID - windows // WGRID * WIN]
    dot_general x10 -> x0, local copies, waits for them, and re-layouts: 99 us -> none  [the longest x2 24.8 us: attend_back(): jnp.einsum('sqhc,skhc->shqk', grad_out, value_rows, preferred_element_typ...]
    all_to_all x8 -> x6, waiting for transfers between devices: 112 us -> 27.4 us  [swap_windows(): lax.all_to_all(values, 'tensor', split_axis=axis, concat_axis=axis, tiled...]
  transfers between devices with their start and end apart: 16 -> 28, of which waited for: 6 -> 13; matrix products, arithmetic and copies ran while one was open for 65% -> 13% of each run, Pallas kernels for 0% -> 27%
where the time goes in v1:
time: 819 us; the launch traced here: 812 us
  waiting for transfers between devices  278 us (34%)
  Pallas kernels  242 us (30%)
  blocking collectives  109 us (13%)
  local copies, waits for them, and re-layouts  103 us (13%)
  other arithmetic  36.5 us (4%)
  starting transfers between devices  28.1 us (3%)
  between operations  15.4 us (2%)
    reduce_scatter x4, waiting for transfers between devices, reduce_group(): lax.psum_scatter(share, ('dp', 'seq'), scatter_dimension=0, tiled=True)  104 us
    pallas_call x4, Pallas kernels, feed(): pl.pallas_call(functools.partial(feed_kernel, relative, not kept, 256), o...  90.9 us
    all_gather x2, blocking collectives, reduce_group(): out.append(lax.all_gather(part, ('dp', 'seq'), axis=0, tiled=True))  68.6 us
    reduce_scatter x4, waiting for transfers between devices, reduce_group(): share = lax.psum_scatter(ordered, 'tensor', scatter_dimension=0, tiled=True)  58.2 us
    pallas_call x3, Pallas kernels, attend_back(): pl.pallas_call(functools.partial(attend_back_kernel, slabs), out_shape=(n...  53.4 us
    pallas_call x2, Pallas kernels, attend(): pl.pallas_call(functools.partial(attend_kernel, slabs), out_shape=out_sha...  46.6 us
    all_gather x2, waiting for transfers between devices, reduce_group(): out.append(lax.all_gather(part, ('dp', 'seq'), axis=0, tiled=True))  46.3 us
    psum x1, blocking collectives, local(): packed = lax.psum(packed, ('dp', 'seq', 'tensor'))  40.7 us
  transfers between devices with their start and end apart: 28, of which 13 were waited for; matrix products, arithmetic and copies ran while one was open for 13% of the time, Pallas kernels for 27%

profile of v1, /device:TPU:0, one launch (start us, length us, event | category | flops | bytes accessed | tf_op | source)
XLA Modules:
  0.0 811.5 jit_solution(8671694501500194654)
XLA Ops:
  57.2 14.2 %collective-permute-done.1.w2.rest_11_ = bf16[192,2304]{1,0:T(8,128)(2,1)} collective-permute-done((bf16[192,2304]{1,0:T(8,128)(2,1)S(1)}, bf16[192,2304]{1,0:T(8,128)(2,1)}, u32[]{:S(2)}, u32[]{:S(2)}) %collective-permute-start.1) | collective-permute-done | bytes 884768 | tf_op jit(solution)/shard_map/ppermute | solution.py:840
  77.7 25.3 %collective-permute-done.9.e2 = bf16[192,3072]{1,0:T(8,128)(2,1)} collective-permute-done((bf16[192,3072]{1,0:T(8,128)(2,1)}, bf16[192,3072]{1,0:T(8,128)(2,1)}, u32[]{:S(2)}, u32[]{:S(2)}) %collective-permute-start.9) | collective-permute-done | bytes 1179680 | tf_op jit(solution)/shard_map/ppermute | solution.py:840
  108.2 23.4 %attend.2 = (bf16[8,200,768]{2,1,0:T(8,128)(2,1)}, bf16[8,200,768]{2,1,0:T(8,128)(2,1)}, bf16[8,200,2304]{2,1,0:T(8,128)(2,1)}, bf16[8,12,200,200]{3,2,1,0:T(8,128)(2,1)}, bf16[8,200,768]{2,1,0:T(8,128)(2,1)}) custom-call(s32[4,2]{1,0:T(4,128)} %get-tuple-element.210.lims, s32[4]{0:T(128)} %iota_xor_fusion.order, bf16[4,4,49,768]{3,2,1,0:T(8,128)(2,1)} %copy.105.tokens, ...), custom_call_target="tpu_custom_call" | custom-call | flops 4797235200 | bytes 17055744 | tf_op jit(solution)/shard_map/attend/pallas_call | solution.py:280
  131.6 23.2 %attend.3 = (bf16[8,200,768]{2,1,0:T(8,128)(2,1)}, bf16[8,200,768]{2,1,0:T(8,128)(2,1)}, bf16[8,200,2304]{2,1,0:T(8,128)(2,1)}, bf16[8,12,200,200]{3,2,1,0:T(8,128)(2,1)}, bf16[8,200,768]{2,1,0:T(8,128)(2,1)}) custom-call(s32[4,2]{1,0:T(4,128)} %get-tuple-element.211.lims, ...), custom_call_target="tpu_custom_call", output_to_operand_aliasing={{0}: (12, {}), {1}: (13, {}), {2}: (14, {}), {3}: (15, {}),... | custom-call | flops 4797235200 | bytes 17055744 | tf_op jit(solution)/shard_map/attend/pallas_call | solution.py:280
  168.7 21.7 %feed.4 = (f32[1600,768]{1,0:T(8,128)}, f32[1600,768]{1,0:T(8,128)}, bf16[4,192,768]{2,1,0:T(8,128)(2,1)}, bf16[768,768]{1,0:T(8,128)(2,1)}, f32[1,768]{1,0:T(1,128)}) custom-call(s32[8,2]{1,0:T(8,128)} %copy-done.25, s32[4]{0:T(128)} %iota_xor_fusion.order, bf16[1600,768]{1,0:T(8,128)(2,1)} %bitcast.82, bf16[1600,768]{1,0:T(8,128)(2,1)} %bitcast.55, ...), custom_call_target="tpu_custom_call" | custom-call | flops 11324620800 | bytes 29294592 | tf_op jit(solution)/shard_map/feed/pallas_call | solution.py:466
  191.5 23.2 %feed.5 = (f32[1600,768]{1,0:T(8,128)}, f32[1600,768]{1,0:T(8,128)}, bf16[4,192,768]{2,1,0:T(8,128)(2,1)}, bf16[768,768]{1,0:T(8,128)(2,1)}, f32[1,768]{1,0:T(1,128)}) custom-call(s32[8,2]{1,0:T(8,128)} %copy-done.25, s32[4]{0:T(128)} %iota_xor_fusion.order, bf16[1600,768]{1,0:T(8,128)(2,1)} %bitcast.83, ...), custom_call_target="tpu_custom_call", output_to_operand_aliasing={{0}: (10, {}), {1}: (11, {})} | custom-call | flops 11324620800 | bytes 29294592 | tf_op jit(solution)/shard_map/feed/pallas_call | solution.py:466
  214.7 22.8 %feed.6 = (f32[1600,768]{1,0:T(8,128)}, f32[1600,768]{1,0:T(8,128)}, bf16[4,192,768]{2,1,0:T(8,128)(2,1)}, bf16[768,768]{1,0:T(8,128)(2,1)}, f32[1,768]{1,0:T(1,128)}) custom-call(s32[8,2]{1,0:T(8,128)} %copy-done.25, s32[4]{0:T(128)} %iota_xor_fusion.order, bf16[1600,768]{1,0:T(8,128)(2,1)} %bitcast.84, ...), custom_call_target="tpu_custom_call", output_to_operand_aliasing={{0}: (10, {}), {1}: (11, {})} | custom-call | flops 11324620800 | bytes 29294592 | tf_op jit(solution)/shard_map/feed/pallas_call | solution.py:466
  238.6 23.1 %feed.7 = (f32[1600,768]{1,0:T(8,128)}, f32[1600,768]{1,0:T(8,128)}, bf16[4,192,768]{2,1,0:T(8,128)(2,1)}, bf16[768,768]{1,0:T(8,128)(2,1)}, f32[1,768]{1,0:T(1,128)}) custom-call(s32[8,2]{1,0:T(8,128)} %copy-done.25, s32[4]{0:T(128)} %iota_xor_fusion.order, bf16[1600,768]{1,0:T(8,128)(2,1)} %bitcast.85, ...), custom_call_target="tpu_custom_call", output_to_operand_aliasing={{0}: (10, {}), {1}: (11, {})} | custom-call | flops 11324620800 | bytes 29294592 | tf_op jit(solution)/shard_map/feed/pallas_call | solution.py:466
  306.4 18.1 %middle.1 = (bf16[2,4,4,49,768]{4,3,2,1,0:T(8,128)(2,1)}, f32[8,200,768]{2,1,0:T(8,128)}, bf16[8,200,768]{2,1,0:T(8,128)(2,1)}, bf16[4,192,768]{2,1,0:T(8,128)(2...) custom-call(s32[8,2]{1,0:T(8,128)} %copy-done.25, s32[4]{0:T(128)} %iota_xor_fusion.order, ...), custom_call_target="tpu_custom_call" | custom-call | flops 3774873600 | bytes 29491200 | tf_op jit(solution)/shard_map/middle/pallas_call | solution.py:570
  326.5 17.6 %attend_back.3 = (bf16[8,200,256]{2,1,0:T(8,128)(2,1)}, bf16[8,200,256]{2,1,0:T(8,128)(2,1)}, bf16[8,200,256]{2,1,0:T(8,128)(2,1)}, bf16[4,192,768]{2,1,0:T(8,12...) custom-call(s32[4]{0:T(128)} %iota_xor_fusion.order, bf16[8,200,768]{2,1,0:T(8,128)(2,1)} %get-tuple-element.101.normed, ...), custom_call_target="tpu_custom_call" | custom-call | flops 4508876800 | bytes 12288000 | tf_op jit(solution)/shard_map/attend_back/pallas_call | solution.py:716
  346.0 17.9 %attend_back.4 = (bf16[8,200,256]{2,1,0:T(8,128)(2,1)}, bf16[8,200,256]{2,1,0:T(8,128)(2,1)}, bf16[8,200,256]{2,1,0:T(8,128)(2,1)}, bf16[4,192,768]{2,1,0:T(8,12...) custom-call(s32[4]{0:T(128)} %iota_xor_fusion.order, bf16[8,200,768]{2,1,0:T(8,128)(2,1)} %get-tuple-element.101.normed, ...), custom_call_target="tpu_custom_call" | custom-call | flops 4508876800 | bytes 12288000 | tf_op jit(solution)/shard_map/attend_back/pallas_call | solution.py:716
  365.8 17.8 %attend_back.5 = (bf16[8,200,256]{2,1,0:T(8,128)(2,1)}, bf16[8,200,256]{2,1,0:T(8,128)(2,1)}, bf16[8,200,256]{2,1,0:T(8,128)(2,1)}, bf16[4,192,768]{2,1,0:T(8,12...) custom-call(s32[4]{0:T(128)} %iota_xor_fusion.order, bf16[8,200,768]{2,1,0:T(8,128)(2,1)} %get-tuple-element.101.normed, ...), custom_call_target="tpu_custom_call" | custom-call | flops 4508876800 | bytes 12288000 | tf_op jit(solution)/shard_map/attend_back/pallas_call | solution.py:716
  398.4 15.2 %reduce-scatter.13.cloned.1.call-done = bf16[1,192,768]{2,1,0:T(8,128)(2,1)} async-done(((bf16[4,192,768]{2,1,0:T(8,128)(2,1)}), bf16[1,192,768]{2,1,0:T(8,128)(2,1)}) %reduce-scatter.13.cloned.1.call-update) | async-done | bytes 294928 | tf_op jit(solution)/shard_map/reduce_scatter | solution.py:858
  413.7 43.0 %reduce-scatter.9.cloned.1.call-done = bf16[1,192,2304]{2,1,0:T(8,128)(2,1)} async-done(((bf16[4,192,2304]{2,1,0:T(8,128)(2,1)}), bf16[1,192,2304]{2,1,0:T(8,128)(2,1)}) %reduce-scatter.9.cloned.1.call-update) | async-done | bytes 884752 | tf_op jit(solution)/shard_map/reduce_scatter | solution.py:858
  456.7 11.2 %first_back.2 = (bf16[4,4,49,768]{3,2,1,0:T(8,128)(2,1)}, f32[1,768]{1,0:T(1,128)}, f32[1,768]{1,0:T(1,128)}) custom-call(s32[4]{0:T(128)} %iota_xor_fusion.order, bf16[8,200,768]{2,1,0:T(8,128)(2,1)} %get-tuple-element.87.rows_in, f32[8,200,768]{2,1,0:T(8,128)} %get-tuple-element.100.d_middle, f32[1,768]{1,0:T(1,128)} %reshape.262.gain, ...), custom_call_target="tpu_custom_call" | custom-call | flops 2831155200 | bytes 8601600 | tf_op jit(solution)/shard_map/first_back/pallas_call | solution.py:808
  474.6 49.3 %reduce-scatter.23.cloned.1.call-done = bf16[96,768]{1,0:T(8,128)(2,1)} async-done(((bf16[768,768]{1,0:T(8,128)(2,1)}), bf16[96,768]{1,0:T(8,128)(2,1)}) %reduce-scatter.23.cloned.1.call-update) | async-done | bytes 147472 | tf_op jit(solution)/shard_map/reduce_scatter | solution.py:860
  524.9 10.9 %first_back.3 = (bf16[4,4,49,768]{3,2,1,0:T(8,128)(2,1)}, f32[1,768]{1,0:T(1,128)}, f32[1,768]{1,0:T(1,128)}) custom-call(s32[4]{0:T(128)} %iota_xor_fusion.order, bf16[8,200,768]{2,1,0:T(8,128)(2,1)} %get-tuple-element.87.rows_in, f32[8,200,768]{2,1,0:T(8,128)} %get-tuple-element.100.d_middle, f32[1,768]{1,0:T(1,128)} %reshape.262.gain, ...), custom_call_target="tpu_custom_call" | custom-call | flops 2831155200 | bytes 8601600 | tf_op jit(solution)/shard_map/first_back/pallas_call | solution.py:808
  547.1 11.4 %all-to-all-done.5 = bf16[4,4,49,768]{3,1,2,0:T(4,128)(2,1)S(1)} async-done(((bf16[4,4,49,768]{3,1,2,0:T(4,128)(2,1)}), bf16[4,4,49,768]{3,1,2,0:T(4,128)(2,1)S(1)}, u32[]{:S(2)}, u32[]{:S(2)}) %all-to-all-start.5) | async-done | bytes 1204256 | tf_op jit(solution)/shard_map/all_to_all | solution.py:850
  563.2 26.9 %reduce-scatter.19.cloned.1.call-done = bf16[24,3072]{1,0:T(8,128)(2,1)} async-done(((bf16[192,3072]{1,0:T(8,128)(2,1)}), bf16[24,3072]{1,0:T(8,128)(2,1)}) %reduce-scatter.19.cloned.1.call-update) | async-done | bytes 147472 | tf_op jit(solution)/shard_map/reduce_scatter | solution.py:860
  590.5 40.7 %psum.7 = f32[13440]{0:T(1024)S(1)} all-reduce(f32[13440]{0:T(1024)S(1)} %concatenate.51), channel_id=1, replica_groups=mesh['dp'=2,'seq'=4,'tensor'=4] {'dp','seq','tensor'}, use_global_device_ids=true, to_apply=%region_0.1 | all-reduce | flops 13440 | bytes 107520 | tf_op jit(solution)/shard_map/psum | solution.py:1002
  653.3 32.0 %all_gather.13 = bf16[192,768]{1,0:T(8,128)(2,1)S(1)} all-gather(bf16[24,768]{1,0:T(8,128)(2,1)} %reduce-scatter.15.cloned.1.call-done), channel_id=1, replica_groups=mesh['dp'=2,'seq'=4,'tensor'=4] {'dp','seq'}, dimensions={0}, use_global_device_ids=true | all-gather | bytes 331776 | tf_op jit(solution)/shard_map/all_gather | solution.py:861
  686.2 28.2 %reduce-scatter.11.cloned.1.call-done = bf16[24,2304]{1,0:T(8,128)(2,1)} async-done(((bf16[192,2304]{1,0:T(8,128)(2,1)}), bf16[24,2304]{1,0:T(8,128)(2,1)}) %reduce-scatter.11.cloned.1.call-update) | async-done | bytes 110608 | tf_op jit(solution)/shard_map/reduce_scatter | solution.py:860
  714.4 36.5 %all_gather.12 = bf16[192,2304]{1,0:T(8,128)(2,1)S(1)} all-gather(bf16[24,2304]{1,0:T(8,128)(2,1)} %reduce-scatter.11.cloned.1.call-done), channel_id=1, replica_groups=mesh['dp'=2,'seq'=4,'tensor'=4] {'dp','seq'}, dimensions={0}, use_global_device_ids=true | all-gather | bytes 995328 | tf_op jit(solution)/shard_map/all_gather | solution.py:861
  762.6 38.9 %all-gather.3.cloned.1.call-done = bf16[192,3072]{1,0:T(8,128)(2,1)} async-done(((bf16[24,3072]{1,0:T(8,128)(2,1)}), bf16[192,3072]{1,0:T(8,128)(2,1)}) %all-gather.3.cloned.1.call-update) | async-done | bytes 1179664 | tf_op jit(solution)/shard_map/all_gather | solution.py:861
  (297 shorter events, 203.6 us)
Async XLA Ops:
  35.8 35.6 %collective-permute-start.1 = (bf16[192,2304]{1,0:T(8,128)(2,1)S(1)}, bf16[192,2304]{1,0:T(8,128)(2,1)}, u32[]{:S(2)}, u32[]{:S(2)}) collective-permute-start(bf16[192,2304]{1,0:T(8,128)(2,1)S(1)} %copy-done), channel_id=1, source_target_pairs={{0,2},{1,3},{2,0},{3,1},{4,6},{5,7},{6,4},{7,5},{8,10},{9,11},{10,... | collective-permute-start | bytes 2654216 | tf_op jit(solution)/shard_map/ppermute | solution.py:840
  37.8 69.0 %collective-permute-start = (bf16[192,2304]{1,0:T(8,128)(2,1)S(1)}, bf16[192,2304]{1,0:T(8,128)(2,1)}, u32[]{:S(2)}, u32[]{:S(2)}) collective-permute-start(bf16[192,2304]{1,0:T(8,128)(2,1)S(1)} %copy-done), channel_id=1, source_target_pairs={{0,1},{1,0},{2,3},{3,2},{4,5},{5,4},{6,7},{7,6},{8,9},{9,8},{10,11... | collective-permute-start | bytes 2654216 | tf_op jit(solution)/shard_map/ppermute | solution.py:840
  37.8 40.0 %collective-permute-start.4 = (bf16[192,768]{1,0:T(8,128)(2,1)}, bf16[192,768]{1,0:T(8,128)(2,1)}, u32[]{:S(2)}, u32[]{:S(2)}) collective-permute-start(bf16[192,768]{1,0:T(8,128)(2,1)} %w0.7), channel_id=1, source_target_pairs={{0,2},{1,3},{2,0},{3,1},{4,6},{5,7},{6,4},{7,5},{8,10},{9,11},{10,... | collective-permute-start | bytes 884744 | tf_op jit(solution)/shard_map/ppermute | solution.py:840
  38.0 65.0 %collective-permute-start.9 = (bf16[192,3072]{1,0:T(8,128)(2,1)}, bf16[192,3072]{1,0:T(8,128)(2,1)}, u32[]{:S(2)}, u32[]{:S(2)}) collective-permute-start(bf16[192,3072]{1,0:T(8,128)(2,1)} %e0.7), channel_id=1, source_target_pairs={{0,2},{1,3},{2,0},{3,1},{4,6},{5,7},{6,4},{7,5},{8,10},{9,11},{10,... | collective-permute-start | bytes 3538952 | tf_op jit(solution)/shard_map/ppermute | solution.py:840
  39.8 117.1 %collective-permute-start.6 = (bf16[768,768]{1,0:T(8,128)(2,1)}, bf16[768,768]{1,0:T(8,128)(2,1)}, u32[]{:S(2)}, u32[]{:S(2)}) collective-permute-start(bf16[768,768]{1,0:T(8,128)(2,1)} %shrink.1), channel_id=1, source_target_pairs={{0,2},{1,3},{2,0},{3,1},{4,6},{5,7},{6,4},{7,5},{8,10},{9,11},{10,... | collective-permute-start | bytes 3538952 | tf_op jit(solution)/shard_map/ppermute | solution.py:840
  53.4 101.5 %all-to-all-start.2 = ((bf16[2,4,4,49,768]{4,2,3,0,1:T(4,128)(2,1)}), bf16[2,4,4,49,768]{4,2,3,0,1:T(4,128)(2,1)S(1)}, u32[]{:S(2)}, u32[]{:S(2)}) async-start(bf16[2,4,4,49,768]{4,2,3,0,1:T(4,128)(2,1)} %copy.108), calls=%async_computation.2 | async-start | bytes 4816896 | tf_op jit(solution)/shard_map/all_to_all | solution.py:850
  57.0 340.3 %reduce-scatter.21.cloned.1.call-start = ((), (), s32[]{:S(2)}) async-start(), calls=%async_computation.21 | async-start | bytes 5898240 | tf_op jit(solution)/shard_map/reduce_scatter | solution.py:858
  71.4 35.9 %collective-permute-start.2 = (bf16[192,2304]{1,0:T(8,128)(2,1)}, bf16[192,2304]{1,0:T(8,128)(2,1)S(1)}, u32[]{:S(2)}, u32[]{:S(2)}) collective-permute-start(bf16[192,2304]{1,0:T(8,128)(2,1)} %collective-permute-done.1.w2.rest_11_), channel_id=1, source_target_pairs={{0,1},{1,0},{2,3},{3,2},{4,5},{5,4},{6,7},{7,6},{8,9},{9,8},{10,11... | collective-permute-start | bytes 2654216 | tf_op jit(solution)/shard_map/ppermute | solution.py:840
  77.7 91.0 %collective-permute-start.8 = (bf16[192,3072]{1,0:T(8,128)(2,1)}, bf16[192,3072]{1,0:T(8,128)(2,1)}, u32[]{:S(2)}, u32[]{:S(2)}) collective-permute-start(bf16[192,3072]{1,0:T(8,128)(2,1)} %e0.7), channel_id=1, source_target_pairs={{0,1},{1,0},{2,3},{3,2},{4,5},{5,4},{6,7},{7,6},{8,9},{9,8},{10,11... | collective-permute-start | bytes 3538952 | tf_op jit(solution)/shard_map/ppermute | solution.py:840
  103.0 65.7 %collective-permute-start.10 = (bf16[192,3072]{1,0:T(8,128)(2,1)}, bf16[192,3072]{1,0:T(8,128)(2,1)}, u32[]{:S(2)}, u32[]{:S(2)}) collective-permute-start(bf16[192,3072]{1,0:T(8,128)(2,1)} %collective-permute-done.9.e2), channel_id=1, source_target_pairs={{0,1},{1,0},{2,3},{3,2},{4,5},{5,4},{6,7},{7,6},{8,9},{9,8},{10,11... | collective-permute-start | bytes 3538952 | tf_op jit(solution)/shard_map/ppermute | solution.py:840
  106.8 50.0 %collective-permute-start.3 = (bf16[192,768]{1,0:T(8,128)(2,1)}, bf16[192,768]{1,0:T(8,128)(2,1)S(1)}, u32[]{:S(2)}, u32[]{:S(2)}) collective-permute-start(bf16[192,768]{1,0:T(8,128)(2,1)} %w0.7), channel_id=1, source_target_pairs={{0,1},{1,0},{2,3},{3,2},{4,5},{5,4},{6,7},{7,6},{8,9},{9,8},{10,11... | collective-permute-start | bytes 884744 | tf_op jit(solution)/shard_map/ppermute | solution.py:840
  107.3 50.1 %collective-permute-start.5 = (bf16[192,768]{1,0:T(8,128)(2,1)}, bf16[192,768]{1,0:T(8,128)(2,1)S(1)}, u32[]{:S(2)}, u32[]{:S(2)}) collective-permute-start(bf16[192,768]{1,0:T(8,128)(2,1)} %collective-permute-done.4.w2), channel_id=1, source_target_pairs={{0,1},{1,0},{2,3},{3,2},{4,5},{5,4},{6,7},{7,6},{8,9},{9,8},{10,11... | collective-permute-start | bytes 884744 | tf_op jit(solution)/shard_map/ppermute | solution.py:840
  156.9 80.7 %collective-permute-start.7 = (bf16[768,768]{1,0:T(8,128)(2,1)}, bf16[768,768]{1,0:T(8,128)(2,1)S(1)}, u32[]{:S(2)}, u32[]{:S(2)}) collective-permute-start(bf16[768,768]{1,0:T(8,128)(2,1)} %collective-permute-done.6.shrink), channel_id=1, source_target_pairs={{0,1},{1,0},{2,3},{3,2},{4,5},{5,4},{6,7},{7,6},{8,9},{9,8},{10,11... | collective-permute-start | bytes 3538952 | tf_op jit(solution)/shard_map/ppermute | solution.py:840
  276.0 121.9 %reduce-scatter.17.cloned.1.call-start = ((), (), s32[]{:S(2)}) async-start(), calls=%async_computation.18 | async-start | bytes 5898240 | tf_op jit(solution)/shard_map/reduce_scatter | solution.py:858
  304.2 109.4 %reduce-scatter.13.cloned.1.call-start = ((), (), s32[]{:S(2)}) async-start(), calls=%async_computation.16 | async-start | bytes 1474560 | tf_op jit(solution)/shard_map/reduce_scatter | solution.py:858
  386.8 69.9 %reduce-scatter.9.cloned.1.call-start = ((), (), s32[]{:S(2)}) async-start(), calls=%async_computation.14 | async-start | bytes 4423680 | tf_op jit(solution)/shard_map/reduce_scatter | solution.py:858
  397.2 126.7 %reduce-scatter.23.cloned.1.call-start = ((), (), s32[]{:S(2)}) async-start(), calls=%async_computation.22 | async-start | bytes 1327104 | tf_op jit(solution)/shard_map/reduce_scatter | solution.py:860
  397.8 192.3 %reduce-scatter.19.cloned.1.call-start = ((), (), s32[]{:S(2)}) async-start(), calls=%async_computation.19 | async-start | bytes 1327104 | tf_op jit(solution)/shard_map/reduce_scatter | solution.py:860
  398.4 255.0 %reduce-scatter.15.cloned.1.call-start = ((), (), s32[]{:S(2)}) async-start(), calls=%async_computation.17 | async-start | bytes 331776 | tf_op jit(solution)/shard_map/reduce_scatter | solution.py:860
  413.6 300.8 %reduce-scatter.11.cloned.1.call-start = ((), (), s32[]{:S(2)}) async-start(), calls=%async_computation.15 | async-start | bytes 995328 | tf_op jit(solution)/shard_map/reduce_scatter | solution.py:860
  470.8 68.0 %all-to-all-start.4 = ((bf16[4,4,49,768]{3,1,2,0:T(4,128)(2,1)}), bf16[4,4,49,768]{3,1,2,0:T(4,128)(2,1)S(1)}, u32[]{:S(2)}, u32[]{:S(2)}) async-start(bf16[4,4,49,768]{3,1,2,0:T(4,128)(2,1)} %copy.114), calls=%async_computation.4 | async-start | bytes 2408448 | tf_op jit(solution)/shard_map/all_to_all | solution.py:850
  474.5 285.2 %all-gather.5.cloned.1.call-start = ((), (), s32[]{:S(2)}) async-start(), calls=%async_computation.23 | async-start | bytes 1327104 | tf_op jit(solution)/shard_map/all_gather | solution.py:861
  559.5 90.2 %all-to-all-start.3 = ((bf16[2,4,4,49,768]{4,2,3,0,1:T(4,128)(2,1)}), bf16[2,4,4,49,768]{4,2,3,0,1:T(4,128)(2,1)S(1)}, u32[]{:S(2)}, u32[]{:S(2)}) async-start(bf16[2,4,4,49,768]{4,2,3,0,1:T(4,128)(2,1)} %copy.110), calls=%async_computation.3 | async-start | bytes 4816896 | tf_op jit(solution)/shard_map/all_to_all | solution.py:850
  563.2 238.3 %all-gather.3.cloned.1.call-start = ((), (), s32[]{:S(2)}) async-start(), calls=%async_computation.20 | async-start | bytes 1327104 | tf_op jit(solution)/shard_map/all_gather | solution.py:861
  (63 other events, 1649.0 us)
Sparse Core Ops, SparseCore 0:
  276.1 48.8 reduce-scatter.20
  327.7 47.8 reduce-scatter.16
  386.9 26.6 reduce-scatter.12
  416.2 40.4 reduce-scatter.8
  459.9 63.9 reduce-scatter.22
  527.1 62.9 reduce-scatter.18
  593.4 57.3 reduce-scatter.14
  654.2 60.1 reduce-scatter.10
  716.5 43.1 all-gather.4
  761.7 39.7 all-gather.2

commit v2 on v1

v2 whole, which is shorter than its diff:
```python
import functools

import jax
import jax.numpy as jnp
import numpy as np
from jax import lax
from jax.experimental import pallas as pl
from jax.experimental.pallas import tpu as pltpu
from jax.sharding import PartitionSpec as P

HEADS = 12
HD = 64
WIN = 14
GRID = 64
WGRID = 5
WROWS = WIN * WIN
ROWS = 200
QUAD = 4
LANES = 128
REL = 2 * WIN - 1
SEG = 32
EPSILON = 1e-06
PENALTY = -1e9

F32 = jnp.float32
BF16 = jnp.bfloat16
FIRST_GAIN, FIRST_SHIFT, OUTPUT_BIAS, SECOND_GAIN, SECOND_SHIFT, SHRINK_BIAS = range(6)
TRIPLE_BIAS, EXPAND_BIAS, TABLES = 6, 9, 13
VMEM_LIMIT = 58 * 1024 * 1024


def dot(left, right):
    return lax.dot_general(left, right, (((1,), (0,)), ((), ())), preferred_element_type=F32)


def dot_t(left, right):
    return lax.dot_general(left, right, (((1,), (1,)), ((), ())), preferred_element_type=F32)


def dot_rows(left, right):
    return lax.dot_general(left, right, (((0,), (0,)), ((), ())), preferred_element_type=F32)


def key_selectors(mirrored):
    out = np.zeros((QUAD, ROWS, LANES), np.float32)
    for head in range(QUAD):
        for key in range(WROWS):
            high, wide = key // WIN, key % WIN
            if mirrored:
                high, wide = WIN - 1 - high, WIN - 1 - wide
            out[head, key, SEG * head + high] = 1.0
            out[head, key, SEG * head + 16 + wide] = 1.0
    return jnp.asarray(out, BF16)


def table_places(mirrored):
    out = np.zeros((2, REL, 2 * LANES), np.float32)
    for head in range(QUAD):
        for row in range(REL):
            if mirrored:
                out[0, row, SEG * head + row] = 1.0
                out[1, row, LANES + (SEG * head + 16 + row) % LANES] = 1.0
            else:
                out[0, REL - 1 - row, (SEG * head + row - 13) % LANES] = 1.0
                out[1, REL - 1 - row, LANES + (SEG * head + row + 3) % LANES] = 1.0
    return jnp.asarray(out, BF16)


def head_blocks(mirrored):
    out = np.zeros((QUAD * HD, 2 * LANES), np.float32)
    for head in range(QUAD):
        rows = slice(head * HD, (head + 1) * HD)
        for row in range(REL):
            if mirrored:
                out[rows, SEG * head + row] = 1.0
                out[rows, LANES + (SEG * head + 16 + row) % LANES] = 1.0
            else:
                out[rows, (SEG * head + row - 13) % LANES] = 1.0
                out[rows, LANES + (SEG * head + row + 3) % LANES] = 1.0
    return jnp.asarray(out, BF16)


def valid_rows(window):
    high_place = (window * 13) >> 6
    wide_place = window - high_place * WGRID
    inside = window < WGRID * WGRID
    row = lax.broadcasted_iota(jnp.int32, (ROWS, 1), 0)
    high = (row * 4682) >> 16
    wide = row - high * WIN
    high_limit = jnp.where(inside, GRID - high_place * WIN, 0)
    return (high < high_limit) & (wide < GRID - wide_place * WIN) & (row < WROWS)


def build_tables(height, width, places, blocks):
    both = dot_rows(height[...].astype(BF16), places[0]) + dot_rows(
        width[...].astype(BF16), places[1]
    )
    both = both.astype(BF16)
    return jnp.concatenate([both] * QUAD, axis=0) * blocks[...]


def roll_rows(values, by_width):
    sub = lax.broadcasted_iota(jnp.int32, (8, LANES), 0)
    pieces = []
    for start in range(0, ROWS, 8):
        piece = values[start : start + 8]
        first = start // WIN
        crossing = (first + 1) * WIN - start
        shifts = (first, first + 1)
        if by_width:
            one = pltpu.roll(piece, start - first * WIN, 1, stride=1, stride_axis=0)
        else:
            one = pltpu.roll(piece, first, 1) if first else piece
        if crossing < 8:
            if by_width:
                two = pltpu.roll(piece, LANES - crossing, 1)
                two = pltpu.roll(two, 0, 1, stride=1, stride_axis=0)
            else:
                two = pltpu.roll(piece, shifts[1], 1)
            one = jnp.where(sub < crossing, one, two)
        pieces.append(one)
    return jnp.concatenate(pieces, axis=0)


def normalize(values):
    centre = jnp.mean(values, axis=-1, keepdims=True)
    spread = values - centre
    variance = jnp.mean(spread * spread, axis=-1, keepdims=True)
    scale = lax.rsqrt(variance + EPSILON)
    return spread * scale, scale


def normalize_back(unit, scale, grad, gain):
    scaled = grad * gain
    mean_grad = jnp.mean(scaled, axis=-1, keepdims=True)
    mean_both = jnp.mean(scaled * unit, axis=-1, keepdims=True)
    return (scaled - mean_grad - unit * mean_both) * scale


def weight_places(meta, pieces):
    own, near, far0, far1, cross0, cross1 = pieces
    mine, bit = meta[0], meta[1]
    return [
        (own, 0, 2 * mine),
        (own, 1, 2 * mine + 1),
        (near, 0, 2 * (mine ^ 1)),
        (near, 1, 2 * (mine ^ 1) + 1),
        (far0, None, 2 * (mine ^ 2) + bit),
        (far1, None, 2 * (mine ^ 2) + 1 - bit),
        (cross0, None, 2 * (mine ^ 3) + bit),
        (cross1, None, 2 * (mine ^ 3) + 1 - bit),
    ]


def start_copies(pairs, sems):
    copies = []
    for number, (source, target) in enumerate(pairs):
        copies.append(pltpu.make_async_copy(source, target, sems.at[number]))
    for copy in copies:
        copy.start()
    return copies


def wait_all(copies):
    for copy in copies:
        copy.wait()


def load_rows(meta, pieces, target, sems, first=0):
    height = target.shape[0] // 8
    pairs = []
    for source, half, place in weight_places(meta, pieces):
        source = source if half is None else source.at[half]
        start = pl.multiple_of(place * height, 16)
        pairs.append(
            (source.at[pl.ds(first, height), :], target.at[pl.ds(start, height), :])
        )
    return start_copies(pairs, sems)


def gather_quarters(first, block, staged, target, base, slabs):
    parts, rows, slots, width = block.shape
    lanes = width // LANES

    @pl.when(first)
    def _():
        for part in range(parts):
            values = block[part].astype(F32).reshape(rows * slots, width)
            for piece in range(lanes):
                staged[part * lanes + piece] = values[:, piece * LANES : (piece + 1) * LANES]
        target[:, parts * rows :, :] = jnp.zeros((slabs, ROWS - parts * rows, width), F32)

    for slab in range(slabs):
        for part in range(parts):
            for piece in range(lanes):
                target[
                    slab, part * rows : (part + 1) * rows, piece * LANES : (piece + 1) * LANES
                ] = staged[part * lanes + piece, pl.ds(base + slab, rows, stride=slots), :]


def scatter_quarters(last, full, staged, block, base, slabs):
    parts, rows, slots, width = block.shape
    lanes = width // LANES
    for slab in range(slabs):
        for part in range(parts):
            for piece in range(lanes):
                staged[part * lanes + piece, pl.ds(base + slab, rows, stride=slots), :] = full[
                    slab, part * rows : (part + 1) * rows, piece * LANES : (piece + 1) * LANES
                ]

    @pl.when(last)
    def _():
        for part in range(parts):
            for piece in range(lanes):
                values = staged[part * lanes + piece].reshape(rows, slots, LANES)
                block[part, :, :, piece * LANES : (piece + 1) * LANES] = values.astype(BF16)


def write_owned(source, meta, keep, send):
    height = keep.shape[1]
    for index in range(4):
        start = pl.multiple_of((meta[0] ^ index) * height, 16)
        target = send if index & 1 else keep
        target[index >> 1] = source[pl.ds(start, height), :].astype(BF16)


ANY = pl.BlockSpec(memory_space=pl.ANY)


def whole(*shape):
    return pl.BlockSpec(shape, lambda *_: (0,) * len(shape))


def like(shape, dtype):
    return jax.ShapeDtypeStruct(shape, dtype)


def call(kernel, name, steps, scalars, ins, outs, scratch, cost, aliases=None):
    flops, moved, transcendentals = cost
    return pl.pallas_call(
        kernel,
        out_shape=tuple(item for item, _ in outs),
        grid_spec=pltpu.PrefetchScalarGridSpec(
            num_scalar_prefetch=len(scalars),
            grid=(steps,),
            in_specs=[spec for _, spec in ins],
            out_specs=tuple(spec for _, spec in outs),
            scratch_shapes=scratch,
        ),
        input_output_aliases={len(scalars) + k: v for k, v in (aliases or {}).items()},
        compiler_params=pltpu.CompilerParams(vmem_limit_bytes=VMEM_LIMIT),
        cost_estimate=pl.CostEstimate(
            flops=int(flops), bytes_accessed=int(moved), transcendentals=int(transcendentals)
        ),
        name=name,
    )(*scalars, *[item for item, _ in ins])


def group(count):
    return 2 if count % 2 == 0 else 1


def prepare_kernel(chunks, *refs):
    items, (output, expand, shrink), (vectors, packed) = refs[:8], refs[8:11], refs[11:]
    width = vectors.shape[1]
    row = 0
    for item in items:
        for start in range(0, item.shape[0], width):
            vectors[row : row + 1, :] = item[pl.ds(start, width)].reshape(1, width)
            row += 1
    half = output.shape[0] // 2
    blocks = expand.shape[1] // width
    tall = shrink.shape[0] // (2 * chunks)
    for upper in range(2):
        rows = slice(upper * half, (upper + 1) * half)
        packed[upper, :half, :] = output[rows, :]
        for block in range(blocks):
            start = (1 + block) * half
            packed[upper, start : start + half, :] = expand[
                rows, block * width : (block + 1) * width
            ]
        for number in range(chunks):
            start = (1 + blocks) * half + number * tall
            source = (2 * number + upper) * tall
            packed[upper, start : start + tall, :] = shrink[source : source + tall, :]


def prepare(chunks, items, weights):
    width = weights[0].shape[1]
    count = sum(item.shape[0] for item in items) // width
    total = sum(item.shape[0] * item.shape[1] for item in weights) // (2 * width)
    return call(
        functools.partial(prepare_kernel, chunks),
        "prepare",
        1,
        (),
        [(item, whole(*item.shape)) for item in (*items, *weights)],
        [
            (like((count, width), F32), whole(count, width)),
            (like((2, total, width), BF16), whole(2, total, width)),
        ],
        [],
        (0, 8 * total * width, 0),
    )


def collect_kernel(*refs):
    out = refs[-1]
    width = out.shape[1]
    singles, triples, expands, tables = refs[:6], refs[6:9], refs[9:12], refs[12:-1]
    out[...] = jnp.zeros_like(out)
    for row, item in enumerate(singles):
        out[row : row + 1, :] = item[...]
    size = width // 3
    for number, item in enumerate(triples):
        for part in range(3):
            row = TRIPLE_BIAS + part
            out[row : row + 1, number * size : (number + 1) * size] = item[
                :, part * size : (part + 1) * size
            ]
    for number, item in enumerate(expands):
        for part in range(item.shape[1] // size):
            row = EXPAND_BIAS + part
            out[row : row + 1, number * size : (number + 1) * size] = item[
                :, part * size : (part + 1) * size
            ]
    total = tables[0][...]
    for item in tables[1:]:
        total = total + item[...]
    for piece in range(3):
        out[TABLES : TABLES + 9, piece * LANES : (piece + 1) * LANES] = total[
            9 * piece : 9 * piece + 9, :
        ]


def collect(singles, triples, expands, tables):
    width = singles[0].shape[1]
    items = (*singles, *triples, *expands, *tables)
    return call(
        collect_kernel,
        "collect",
        1,
        (),
        [(item, whole(*item.shape)) for item in items],
        [(like((24, width), F32), whole(24, width))],
        [],
        (0, 16 * 24 * width, 0),
    )[0]


def attend_kernel(
    slabs, before, meta, windows, tokens, vectors, height, width_table, places, blocks, selectors,
    p0, p1, p2, p3, p4, p5, *rest,
):
    (
        rows_out, normed_out, triple_out, probs_out, attended_out,
        full, staged, weight, tables, masked_keys, sems,
    ) = rest[-11:]
    step = pl.program_id(0)
    base_slab = (step + before) * slabs
    width = full.shape[2]

    @pl.when(step == 0)
    def _():
        copies = load_rows(meta, (p0, p1, p2, p3, p4, p5), weight, sems)
        tables[...] = build_tables(height, width_table, places, blocks)
        wait_all(copies)

    gather_quarters(step == 0, tokens, staged, full, base_slab, slabs)
    rows = full[...].reshape(slabs * ROWS, width)
    unit, _ = normalize(rows)
    normed = unit * vectors[FIRST_GAIN : FIRST_GAIN + 1] + vectors[FIRST_SHIFT : FIRST_SHIFT + 1]
    normed = normed.astype(BF16)
    rows_out[...] = rows.astype(BF16).reshape(slabs, ROWS, width)
    normed_out[...] = normed.reshape(slabs, ROWS, width)
    for part in range(3):
        columns = slice(part * width, (part + 1) * width)
        bias = vectors[TRIPLE_BIAS + part : TRIPLE_BIAS + part + 1]
        triple = dot(normed, weight[:, columns]) + bias
        triple_out[:, :, columns] = triple.astype(BF16).reshape(slabs, ROWS, width)

    lane = lax.broadcasted_iota(jnp.int32, (ROWS, LANES), 1)
    within = lane & (SEG - 1)
    upper = lane >= HD
    quads = HEADS // QUAD
    for slab in range(slabs):
        allowed = valid_rows(windows[meta[0], base_slab + slab])
        penalty = jnp.where((lane == WIN) & jnp.logical_not(allowed), PENALTY, 0.0).astype(BF16)
        for head in range(QUAD):
            masked_keys[slab, head] = selectors[head] + penalty

    def one_quad(index, carry):
        slab = index // quads
        quad = index - slab * quads
        allowed = valid_rows(windows[meta[0], base_slab + slab])
        base = pl.multiple_of(quad * QUAD * HD, LANES)
        queries = triple_out[slab, :, pl.ds(base, QUAD * HD)]
        keys = triple_out[slab, :, pl.ds(pl.multiple_of(base + width, LANES), QUAD * HD)]
        values = triple_out[slab, :, pl.ds(pl.multiple_of(base + 2 * width, LANES), QUAD * HD)]
        terms = dot(queries, tables[...])
        high = roll_rows(terms[:, :LANES], False)
        wide = roll_rows(terms[:, LANES:], True)
        constant = jnp.where(lane == WIN, 1.0, 0.0)
        relative = jnp.where(
            within < WIN, high, jnp.where((within >= 16) & (within < 16 + WIN), wide, constant)
        ).astype(BF16)
        queries = queries * jnp.asarray(HD**-0.5, BF16)
        outs = []
        for pair in range(QUAD // 2):
            columns = slice(pair * LANES, (pair + 1) * LANES)
            left = jnp.concatenate([queries[:, columns], relative], axis=1)
            total = None
            for side in range(2):
                head = 2 * pair + side
                mine = upper if side else jnp.logical_not(upper)
                zero = jnp.zeros((ROWS, LANES), BF16)
                right = jnp.concatenate(
                    [jnp.where(mine, keys[:, columns], zero), masked_keys[slab, head]], axis=1
                )
                scores = dot_t(left, right)
                maxima = jnp.max(scores, axis=-1, keepdims=True)
                exponent = jnp.exp(scores - maxima)
                summed = jnp.sum(exponent, axis=-1, keepdims=True)
                probs = (exponent * (1.0 / summed)).astype(BF16)
                probs_out[slab, quad * QUAD + head] = probs
                part = dot(probs, jnp.where(mine, values[:, columns], zero))
                total = part if total is None else total + part
            outs.append(total)
        mixed = jnp.concatenate(outs, axis=1)
        mixed = jnp.where(allowed, mixed, 0.0)
        attended_out[slab, :, pl.ds(base, QUAD * HD)] = mixed.astype(BF16)
        return carry

    lax.fori_loop(0, slabs * quads, one_quad, 0)


def attend(before, steps, meta, windows, tokens, vectors, tables, selectors, pieces, kept):
    parts, rows_dev, slots, width = tokens.shape
    slabs = group(slots)
    block3 = lambda columns: pl.BlockSpec((slabs, ROWS, columns), lambda i, *_: (i + before, 0, 0))
    rows = steps * slabs * ROWS
    ins = [(item, whole(*item.shape)) for item in (tokens, vectors, *tables, selectors)]
    ins += [(item, ANY) for item in pieces]
    aliases = {}
    if kept is not None:
        aliases = {len(ins) + n: n for n in range(len(kept))}
        ins += [(item, ANY) for item in kept]
    return call(
        functools.partial(attend_kernel, slabs, before),
        "attend",
        steps,
        (meta, windows),
        ins,
        [
            (like((slots, ROWS, width), BF16), block3(width)),
            (like((slots, ROWS, width), BF16), block3(width)),
            (like((slots, ROWS, 3 * width), BF16), block3(3 * width)),
            (
                like((slots, HEADS, ROWS, ROWS), BF16),
                pl.BlockSpec((slabs, HEADS, ROWS, ROWS), lambda i, *_: (i + before, 0, 0, 0)),
            ),
            (like((slots, ROWS, width), BF16), block3(width)),
        ],
        [
            pltpu.VMEM((slabs, ROWS, width), F32),
            pltpu.VMEM((parts * width // LANES, rows_dev * slots, LANES), F32),
            pltpu.VMEM((width, 3 * width), BF16),
            pltpu.VMEM((2 * LANES, 2 * LANES), BF16),
            pltpu.VMEM((slabs, QUAD, ROWS, LANES), BF16),
            pltpu.SemaphoreType.DMA((8,)),
        ],
        (
            6 * rows * width * width + steps * slabs * HEADS * 4 * ROWS * ROWS * 256,
            rows * (width * 16 + HEADS * 512) + width * width * 6,
            steps * slabs * HEADS * ROWS * ROWS,
        ),
        aliases,
    )


def project_kernel(
    slabs, meta, windows, attended, rows_in, grads, vectors, p0, p1, p2, p3, p4, p5,
    middle_out, normed_out, branch_out, shrink_bias_out, full, staged, weight, sems,
):
    step = pl.program_id(0)

    @pl.when(step == 0)
    def _():
        wait_all(load_rows(meta, (p0, p1, p2, p3, p4, p5), weight, sems))
        shrink_bias_out[...] = jnp.zeros_like(shrink_bias_out)

    width = full.shape[2]
    count = slabs * ROWS
    middle = (
        rows_in[...].reshape(count, width).astype(F32)
        + dot(attended[...].reshape(count, width), weight[...])
        + vectors[OUTPUT_BIAS : OUTPUT_BIAS + 1]
    )
    unit, _ = normalize(middle)
    middle_out[...] = middle
    normed = unit * vectors[SECOND_GAIN : SECOND_GAIN + 1] + vectors[SECOND_SHIFT : SECOND_SHIFT + 1]
    normed_out[...] = normed.astype(BF16)
    gather_quarters(step == 0, grads, staged, full, step * slabs, slabs)
    for slab in range(slabs):
        allowed = valid_rows(windows[meta[0], step * slabs + slab])
        branch = jnp.where(allowed, full[slab], 0.0)
        branch_out[slab * ROWS : (slab + 1) * ROWS, :] = branch.astype(BF16)
        shrink_bias_out[...] += jnp.sum(branch, axis=0, keepdims=True)


def project(meta, windows, attended, rows_in, grads, vectors, pieces):
    parts, rows_dev, slots, width = grads.shape
    slabs = group(slots)
    block = pl.BlockSpec((slabs, ROWS, width), lambda i, *_: (i, 0, 0))
    flat = pl.BlockSpec((slabs * ROWS, width), lambda i, *_: (i, 0))
    rows = slots * ROWS
    return call(
        functools.partial(project_kernel, slabs),
        "project",
        slots // slabs,
        (meta, windows),
        [(attended, block), (rows_in, block)]
        + [(item, whole(*item.shape)) for item in (grads, vectors)]
        + [(item, ANY) for item in pieces],
        [
            (like((rows, width), F32), flat),
            (like((rows, width), BF16), flat),
            (like((rows, width), BF16), flat),
            (like((1, width), F32), whole(1, width)),
        ],
        [
            pltpu.VMEM((slabs, ROWS, width), F32),
            pltpu.VMEM((parts * width // LANES, rows_dev * slots, LANES), F32),
            pltpu.VMEM((width, width), BF16),
            pltpu.SemaphoreType.DMA((8,)),
        ],
        (2 * rows * width * width, rows * width * 14, 0),
    )


def gate_both(hidden):
    half = 0.5 * (1.0 + lax.erf(hidden * 0.7071067811865476))
    density = jnp.exp(hidden * hidden * -0.5) * 0.3989422804014327
    return hidden * half, half + hidden * density


def feed_kernel(number, first, unit, meta, normed, branch, vectors, *rest):
    pieces, rest = rest[:6], rest[6:]
    if not first:
        out_in, grad_in = rest[:2]
    out_acc, grad_acc, keep, send, bias_grad, expand, shrink, acc_e, acc_s, sems = rest[-10:]
    step = pl.program_id(0)
    last = pl.num_programs(0) - 1
    width, chunk = expand.shape
    blocks = chunk // unit

    @pl.when(step == 0)
    def _():
        pairs = []
        height = width // 8
        tall = chunk // 8
        for source, half, place in weight_places(meta, pieces):
            source = source if half is None else source.at[half]
            start = pl.multiple_of(place * height, 16)
            for block in range(blocks):
                pairs.append(
                    (
                        source.at[
                            pl.ds((1 + block) * height, height), pl.ds(number * unit, unit)
                        ],
                        expand.at[pl.ds(start, height), pl.ds(block * unit, unit)],
                    )
                )
            start = pl.multiple_of(place * tall, 16)
            first_row = (1 + blocks) * height + number * tall
            pairs.append((source.at[pl.ds(first_row, tall), :], shrink.at[pl.ds(start, tall), :]))
        copies = start_copies(pairs, sems)
        acc_e[...] = jnp.zeros_like(acc_e)
        acc_s[...] = jnp.zeros_like(acc_s)
        bias_grad[...] = jnp.zeros_like(bias_grad)
        wait_all(copies)

    rows = normed[...]
    grads = branch[...]
    total_out = None
    total_grad = None
    for block in range(blocks):
        columns = slice(block * unit, (block + 1) * unit)
        bias = vectors[
            EXPAND_BIAS + block : EXPAND_BIAS + block + 1, number * unit : (number + 1) * unit
        ]
        hidden = dot(rows, expand[:, columns]) + bias
        active, slope = gate_both(hidden)
        active = active.astype(BF16)
        part = dot(active, shrink[columns, :])
        total_out = part if total_out is None else total_out + part
        back = (dot_t(grads, shrink[columns, :]) * slope).astype(BF16)
        acc_s[columns, :] += dot_rows(active, grads)
        acc_e[:, columns] += dot_rows(rows, back)
        bias_grad[:, columns] += jnp.sum(back.astype(F32), axis=0, keepdims=True)
        part = dot_t(back, expand[:, columns])
        total_grad = part if total_grad is None else total_grad + part
    if first:
        out_acc[...] = total_out
        grad_acc[...] = total_grad
    else:
        out_acc[...] = out_in[...] + total_out
        grad_acc[...] = grad_in[...] + total_grad

    @pl.when(step == last)
    def _():
        height = width // 4
        third = height // 3
        for index in range(4):
            target = (send if index & 1 else keep).at[index >> 1]
            start = pl.multiple_of((meta[0] ^ index) * unit, 16)
            target[:unit, :] = acc_s[pl.ds(start, unit), :].astype(BF16)
            start = pl.multiple_of((meta[0] ^ index) * height, 16)
            target[unit : unit + height, :] = acc_e[pl.ds(start, height), :width].astype(BF16)
            for piece in range(3):
                here = pl.multiple_of(start + piece * third, 16)
                target[unit + height :, piece * unit : (piece + 1) * unit] = acc_e[
                    pl.ds(here, third), width:
                ].astype(BF16)


def feed(number, count, meta, normed, branch, vectors, pieces, kept):
    rows, width = normed.shape
    chunk = 4 * width // count
    unit = chunk // 4
    block_rows = 2 * ROWS
    block = pl.BlockSpec((block_rows, width), lambda i, *_: (i, 0))
    ins = [(normed, block), (branch, block), (vectors, whole(*vectors.shape))]
    ins += [(item, ANY) for item in pieces]
    aliases = {}
    if kept is not None:
        aliases = {len(ins) + n: n for n in range(2)}
        ins += [(item, block) for item in kept]
    payload = (2, unit + unit, width)
    return call(
        functools.partial(feed_kernel, number, kept is None, unit),
        "feed",
        rows // block_rows,
        (meta,),
        ins,
        [
            (like((rows, width), F32), block),
            (like((rows, width), F32), block),
            (like(payload, BF16), whole(*payload)),
            (like(payload, BF16), whole(*payload)),
            (like((1, chunk), F32), whole(1, chunk)),
        ],
        [
            pltpu.VMEM((width, chunk), BF16),
            pltpu.VMEM((chunk, width), BF16),
            pltpu.VMEM((width, chunk), F32),
            pltpu.VMEM((chunk, width), F32),
            pltpu.SemaphoreType.DMA((40,)),
        ],
        (12 * rows * width * chunk, rows * width * 20 + width * chunk * 8, 2 * rows * chunk),
        aliases,
    )


def middle_kernel(
    slabs, meta, windows, middle, out_acc, grad_acc, branch, attended, vectors,
    p0, p1, p2, p3, p4, p5,
    result_out, d_middle_out, d_attended_out, keep, send, output_bias_grad, gain_grad,
    shift_grad, full, staged, weight, acc, sems,
):
    step = pl.program_id(0)
    last = pl.num_programs(0) - 1

    @pl.when(step == 0)
    def _():
        copies = load_rows(meta, (p0, p1, p2, p3, p4, p5), weight, sems)
        acc[...] = jnp.zeros_like(acc)
        output_bias_grad[...] = jnp.zeros_like(output_bias_grad)
        gain_grad[...] = jnp.zeros_like(gain_grad)
        shift_grad[...] = jnp.zeros_like(shift_grad)
        wait_all(copies)

    width = full.shape[2]
    count = slabs * ROWS
    rows = middle[...]
    result = rows + out_acc[...] + vectors[SHRINK_BIAS : SHRINK_BIAS + 1]
    full[...] = result.reshape(slabs, ROWS, width)
    scatter_quarters(step == last, full, staged, result_out, step * slabs, slabs)
    unit, scale = normalize(rows)
    grad = grad_acc[...]
    gain_grad[...] += jnp.sum(grad * unit, axis=0, keepdims=True)
    shift_grad[...] += jnp.sum(grad, axis=0, keepdims=True)
    d_middle = branch[...].astype(F32) + normalize_back(
        unit, scale, grad, vectors[SECOND_GAIN : SECOND_GAIN + 1]
    )
    d_middle_out[...] = d_middle
    d_output = d_middle.astype(BF16)
    output_bias_grad[...] += jnp.sum(d_output.astype(F32), axis=0, keepdims=True)
    acc[...] += dot_rows(attended[...].reshape(count, width), d_output)
    d_attended = dot_t(d_output, weight[...]).reshape(slabs, ROWS, width)
    for slab in range(slabs):
        allowed = valid_rows(windows[meta[0], step * slabs + slab])
        d_attended_out[slab] = jnp.where(allowed, d_attended[slab], 0.0).astype(BF16)

    @pl.when(step == last)
    def _():
        write_owned(acc, meta, keep, send)


def middle_back(meta, windows, rows_dev, middle, out_acc, grad_acc, branch, attended, vectors, pieces):
    slots, _, width = attended.shape
    parts = WROWS // rows_dev
    slabs = group(slots)
    block = pl.BlockSpec((slabs, ROWS, width), lambda i, *_: (i, 0, 0))
    flat = pl.BlockSpec((slabs * ROWS, width), lambda i, *_: (i, 0))
    rows = slots * ROWS
    vec = (like((1, width), F32), whole(1, width))
    payload = (2, width // 4, width)
    quarter = (parts, rows_dev, slots, width)
    return call(
        functools.partial(middle_kernel, slabs),
        "middle",
        slots // slabs,
        (meta, windows),
        [
            (middle, flat), (out_acc, flat), (grad_acc, flat), (branch, flat), (attended, block),
            (vectors, whole(*vectors.shape)),
        ]
        + [(item, ANY) for item in pieces],
        [
            (like(quarter, BF16), whole(*quarter)),
            (like((rows, width), F32), flat),
            (like((slots, ROWS, width), BF16), block),
            (like(payload, BF16), whole(*payload)),
            (like(payload, BF16), whole(*payload)),
            vec,
            vec,
            vec,
        ],
        [
            pltpu.VMEM((slabs, ROWS, width), F32),
            pltpu.VMEM((parts * width // LANES, rows_dev * slots, LANES), F32),
            pltpu.VMEM((width, width), BF16),
            pltpu.VMEM((width, width), F32),
            pltpu.SemaphoreType.DMA((8,)),
        ],
        (4 * rows * width * width, rows * width * 24, 0),
    )


def attend_back_kernel(
    slabs, meta, normed, queries_in, keys_in, values_in, probs_in, d_mixed_in, mixed_in,
    height, width_table, places, blocks, selectors, sums,
    d_queries, d_keys, d_values, keep, send, bias_grad, table_out, grads, acc, tables, table_grad,
):
    step = pl.program_id(0)
    last = pl.num_programs(0) - 1
    wide4 = QUAD * HD

    @pl.when(step == 0)
    def _():
        acc[...] = jnp.zeros_like(acc)
        bias_grad[...] = jnp.zeros_like(bias_grad)
        table_grad[...] = jnp.zeros_like(table_grad)
        tables[...] = build_tables(height, width_table, places, blocks)

    lane = lax.broadcasted_iota(jnp.int32, (ROWS, LANES), 1)
    within = lane & (SEG - 1)
    upper = lane >= HD
    zero = jnp.zeros((ROWS, LANES), BF16)

    def one_slab(slab, carry):
        queries, keys, values = queries_in[slab], keys_in[slab], values_in[slab]
        d_mixed = d_mixed_in[slab]
        product = d_mixed.astype(F32) * mixed_in[slab].astype(F32)
        product_high = product.astype(BF16)
        product_low = (product - product_high.astype(F32)).astype(BF16)
        inner = dot(product_high, sums[...]) + dot(product_low, sums[...])
        inner_high = inner.astype(BF16)
        inner_low = (inner - inner_high.astype(F32)).astype(BF16)
        inner = jnp.where((lane & 1) == 0, inner_high, inner_low)
        d_relative = None
        dq, dk, dv = [], [], []
        for pair in range(QUAD // 2):
            columns = slice(pair * LANES, (pair + 1) * LANES)
            left = jnp.concatenate([d_mixed[:, columns], inner], axis=1)
            dq_pair = dk_pair = dv_pair = None
            for side in range(2):
                head = 2 * pair + side
                mine = upper if side else jnp.logical_not(upper)
                minus = jnp.where((lane == 2 * head) | (lane == 2 * head + 1), -1.0, 0.0)
                right = jnp.concatenate(
                    [jnp.where(mine, values[:, columns], zero), minus.astype(BF16)], axis=1
                )
                d_probs = dot_t(left, right)
                probs = probs_in[slab, head]
                d_scores = (probs.astype(F32) * d_probs).astype(BF16)
                back = dot(
                    d_scores,
                    jnp.concatenate(
                        [jnp.where(mine, keys[:, columns], zero), selectors[head]], axis=1
                    ),
                )
                part_k = dot_rows(d_scores, jnp.where(mine, queries[:, columns], zero))
                part_v = dot_rows(probs, jnp.where(mine, d_mixed[:, columns], zero))
                if dq_pair is None:
                    dq_pair, dk_pair, dv_pair = back[:, :LANES], part_k, part_v
                else:
                    dq_pair = dq_pair + back[:, :LANES]
                    dk_pair = dk_pair + part_k
                    dv_pair = dv_pair + part_v
                d_relative = back[:, LANES:] if d_relative is None else d_relative + back[:, LANES:]
            dq.append(dq_pair)
            dk.append(dk_pair)
            dv.append(dv_pair)
        high = roll_rows(jnp.where(within < WIN, d_relative, 0.0), False)
        wide = roll_rows(
            jnp.where((within >= 16) & (within < 16 + WIN), d_relative, 0.0), True
        )
        d_terms = jnp.concatenate([high, wide], axis=1).astype(BF16)
        scale = HD**-0.5
        dq = jnp.concatenate(dq, axis=1) * scale + dot_t(d_terms, tables[...])
        table_grad[...] += dot_rows(queries, d_terms)
        dq = dq.astype(BF16)
        dk = (jnp.concatenate(dk, axis=1) * scale).astype(BF16)
        dv = jnp.concatenate(dv, axis=1).astype(BF16)
        d_queries[slab] = dq
        d_keys[slab] = dk
        d_values[slab] = dv
        grads[slab] = jnp.concatenate([dq, dk, dv], axis=1)
        return carry

    lax.fori_loop(0, slabs, one_slab, 0)
    width = normed.shape[2]
    both = grads[...].reshape(slabs * ROWS, 3 * wide4)
    bias_grad[...] += jnp.sum(both.astype(F32), axis=0, keepdims=True)
    acc[...] += dot_rows(normed[...].reshape(slabs * ROWS, width), both)

    @pl.when(step == last)
    def _():
        write_owned(acc, meta, keep, send)
        masked = table_grad[...] * blocks[...].astype(F32)
        folded = masked[:HD]
        for head in range(1, QUAD):
            folded = folded + masked[head * HD : (head + 1) * HD]
        high = folded.astype(BF16)
        low = (folded - high.astype(F32)).astype(BF16)
        for which in range(2):
            table_out[:, which * HD : (which + 1) * HD] = dot_t(places[which], high) + dot_t(
                places[which], low
            )


def attend_back(quad, meta, normed, triple, probs, d_mixed, mixed, tables, selectors, sums):
    slots, _, width = normed.shape
    slabs = group(slots)
    wide4 = QUAD * HD
    quads = HEADS // QUAD
    column = lambda where: pl.BlockSpec((slabs, ROWS, wide4), lambda i, *_: (i, 0, where))
    narrow = (
        like((slots, ROWS, wide4), BF16),
        pl.BlockSpec((slabs, ROWS, wide4), lambda i, *_: (i, 0, 0)),
    )
    rows = slots * ROWS
    payload = (2, width // 4, 3 * wide4)
    return call(
        functools.partial(attend_back_kernel, slabs),
        "attend_back",
        slots // slabs,
        (meta,),
        [
            (normed, pl.BlockSpec((slabs, ROWS, width), lambda i, *_: (i, 0, 0))),
            (triple, column(quad)),
            (triple, column(quads + quad)),
            (triple, column(2 * quads + quad)),
            (probs, pl.BlockSpec((slabs, QUAD, ROWS, ROWS), lambda i, *_: (i, quad, 0, 0))),
            (d_mixed, column(quad)),
            (mixed, column(quad)),
        ]
        + [(item, whole(*item.shape)) for item in (*tables, selectors, sums)],
        [
            narrow,
            narrow,
            narrow,
            (like(payload, BF16), whole(*payload)),
            (like(payload, BF16), whole(*payload)),
            (like((1, 3 * wide4), F32), whole(1, 3 * wide4)),
            (like((REL, 2 * HD), F32), whole(REL, 2 * HD)),
        ],
        [
            pltpu.VMEM((slabs, ROWS, 3 * wide4), BF16),
            pltpu.VMEM((width, 3 * wide4), F32),
            pltpu.VMEM((2 * LANES, 2 * LANES), BF16),
            pltpu.VMEM((2 * LANES, 2 * LANES), F32),
        ],
        (
            2 * rows * width * 3 * wide4 + slots * QUAD * 8 * ROWS * ROWS * 256,
            rows * (width * 2 + wide4 * 16 + QUAD * 512),
            0,
        ),
    )


def first_kernel(slabs, meta, rows_in, d_middle, vectors, *rest):
    grads, pieces = rest[:9], rest[9:15]
    tokens_out, gain_grad, shift_grad, full, staged, weight, sems = rest[15:]
    step = pl.program_id(0)
    last = pl.num_programs(0) - 1

    @pl.when(step == 0)
    def _():
        copies = load_rows(meta, pieces, weight, sems)
        gain_grad[...] = jnp.zeros_like(gain_grad)
        shift_grad[...] = jnp.zeros_like(shift_grad)
        wait_all(copies)

    width = full.shape[2]
    count = slabs * ROWS
    total = None
    wide4 = QUAD * HD
    for index, grad in enumerate(grads):
        part = dot_t(
            grad[...].reshape(count, wide4), weight[:, index * wide4 : (index + 1) * wide4]
        )
        total = part if total is None else total + part
    unit, scale = normalize(rows_in[...].reshape(count, width).astype(F32))
    gain_grad[...] += jnp.sum(total * unit, axis=0, keepdims=True)
    shift_grad[...] += jnp.sum(total, axis=0, keepdims=True)
    back = normalize_back(unit, scale, total, vectors[FIRST_GAIN : FIRST_GAIN + 1])
    full[...] = (d_middle[...] + back).reshape(slabs, ROWS, width)
    scatter_quarters(step == last, full, staged, tokens_out, step * slabs, slabs)


def first_back(before, steps, meta, rows_dev, rows_in, d_middle, vectors, grads, pieces):
    slots, _, width = rows_in.shape
    parts = WROWS // rows_dev
    slabs = group(slots)
    wide4 = QUAD * HD
    block = pl.BlockSpec((slabs, ROWS, width), lambda i, *_: (i + before, 0, 0))
    flat = pl.BlockSpec((slabs * ROWS, width), lambda i, *_: (i + before, 0))
    narrow = pl.BlockSpec((slabs, ROWS, wide4), lambda i, *_: (i + before, 0, 0))
    rows = steps * slabs * ROWS
    quarter = (parts, rows_dev, steps * slabs, width)
    return call(
        functools.partial(first_kernel, slabs),
        "first_back",
        steps,
        (meta,),
        [(rows_in, block), (d_middle, flat), (vectors, whole(*vectors.shape))]
        + [(item, narrow) for item in grads]
        + [(item, ANY) for item in pieces],
        [(like(quarter, BF16), whole(*quarter))] + [(like((1, width), F32), whole(1, width))] * 2,
        [
            pltpu.VMEM((slabs, ROWS, width), F32),
            pltpu.VMEM((parts * width // LANES, rows_dev * steps * slabs, LANES), F32),
            pltpu.VMEM((width, 3 * width), BF16),
            pltpu.SemaphoreType.DMA((8,)),
        ],
        (6 * rows * width * width, rows * width * 14, 0),
    )


def finish_kernel(unit, pairs, meta, *refs):
    items, small, refs = refs[: 2 * pairs], refs[2 * pairs], refs[2 * pairs + 1 :]
    (triple_out, output_out, expand_out, shrink_out), refs = refs[:4], refs[4:]
    vectors, tables, staged = refs[:8], refs[8:10], refs[10:]
    upper = meta[1] > 0
    for number, both in enumerate(staged):
        mine, other = items[2 * number], items[2 * number + 1]
        half = mine.shape[0]

        @pl.when(upper)
        def _():
            both[:half] = other[...]
            both[half:] = mine[...]

        @pl.when(jnp.logical_not(upper))
        def _():
            both[:half] = mine[...]
            both[half:] = other[...]

    shard, width = output_out.shape
    third = shard // 3
    parts = width // shard
    for number, both in enumerate(staged[:3]):
        here = number * unit
        shrink_out[here : here + unit, :] = both[:unit, :].astype(F32)
        for block in range(parts - 1):
            start = block * width + here
            expand_out[:, start : start + unit] = both[
                unit : unit + shard, block * unit : (block + 1) * unit
            ].astype(F32)
        start = (parts - 1) * width + here
        for piece in range(3):
            expand_out[piece * third : (piece + 1) * third, start : start + unit] = both[
                unit + shard :, piece * unit : (piece + 1) * unit
            ].astype(F32)
    output_out[...] = staged[3][:shard, :].astype(F32)
    wide4 = QUAD * HD
    for quad, both in enumerate(staged[3:]):
        values = both[shard:, :] if quad == 0 else both[...]
        for part in range(3):
            start = part * width + quad * wide4
            triple_out[:, start : start + wide4] = values[
                :, part * wide4 : (part + 1) * wide4
            ].astype(F32)
    row = 0
    for item in vectors:
        for start in range(0, item.shape[0], width):
            item[pl.ds(start, width)] = small[row : row + 1, :].reshape(width)
            row += 1
    for which, item in enumerate(tables):
        for piece in range(3):
            start = piece * LANES + which * HD
            item[9 * piece : 9 * piece + 9, :] = small[TABLES : TABLES + 9, start : start + HD]


def finish(meta, shares, small, matrices, vectors, tables, unit):
    items = [item for pair in shares for item in pair]
    outs = [item.shape for item in (*matrices, *vectors, *tables)]
    return call(
        functools.partial(finish_kernel, unit, len(shares)),
        "finish",
        1,
        (meta,),
        [(item, whole(*item.shape)) for item in (*items, small)],
        [(like(shape, F32), whole(*shape)) for shape in outs],
        [pltpu.VMEM((2 * mine.shape[0], mine.shape[1]), BF16) for mine, _ in shares],
        (0, sum(6 * item.size for item in items), 0),
    )


def swap(values, axis, bits):
    count = lax.axis_size(axis)
    return lax.ppermute(values, axis, [(n, n ^ bits) for n in range(count)])


def exchange_windows(values):
    return lax.all_to_all(values, "tensor", split_axis=0, concat_axis=0, tiled=True)


def after(values, *others):
    return lax.optimization_barrier((values, *others))[0]


def far_half(packed):
    bit = lax.axis_index("dp") & 1
    mine = lax.dynamic_index_in_dim(packed, bit, axis=0, keepdims=False)
    return swap(mine, "tensor", 2)


def add(*items):
    total = items[0].astype(F32)
    for item in items[1:]:
        total = total + item.astype(F32)
    return total.astype(BF16)


def halves(axis):
    out, bit = [], 1
    while bit < lax.axis_size(axis):
        out.append(bit)
        bit *= 2
    return out


def reduce_stages(payloads):
    totals = []
    while True:
        keep, send, more = payloads.pop(0)
        (far,) = yield [(send, "tensor", 1)]
        totals.append(add(keep, far))
        if not more:
            break
    total = totals[0] if len(totals) == 1 else jnp.concatenate(totals, axis=1)
    spot = lax.axis_index("dp")
    for bit in halves("dp"):
        size = total.shape[1] // 2
        upper = (spot & bit) > 0
        far = jnp.where(upper, total[:, :size], total[:, size:])
        near = jnp.where(upper, total[:, size:], total[:, :size])
        (far,) = yield [(far, "dp", bit)]
        total = add(near, far)
    (far,) = yield [(total[1], "tensor", 2)]
    total = add(total[0], far)
    for bit in halves("seq"):
        (far,) = yield [(total, "seq", bit)]
        total = add(total, far)
    for bit in reversed(halves("dp")):
        upper = (spot & bit) > 0
        (far,) = yield [(total, "dp", bit)]
        if bit > 1:
            total = jnp.concatenate(
                [jnp.where(upper, far, total), jnp.where(upper, total, far)], axis=0
            )
    return total, far


def sum_stages(values):
    for axis in ("tensor", "dp", "seq"):
        for bit in halves(axis):
            (far,) = yield [(values, axis, bit)]
            values = values + far
    return (values,)


class Exchanges:
    def __init__(self):
        self.running = []
        self.done = {}

    def begin(self, name, stages):
        self.running.append([name, stages, None])

    def step(self, token, meta, *extra):
        asked, ended = [], []
        arrived = [item for entry in self.running for item in (entry[2] or ())]
        if token is not None and arrived:
            token, *arrived = lax.optimization_barrier((token, *arrived))
        arrived = iter(arrived)
        for entry in list(self.running):
            name, stages, waiting = entry
            mine = None if waiting is None else [next(arrived) for _ in waiting]
            try:
                asked.append((entry, stages.send(mine)))
            except StopIteration as stop:
                ended.append((name, stop.value))
                self.running.remove(entry)
        values = [item[0] for _, wanted in asked for item in wanted]
        finished = [item for _, pair in ended for item in pair]
        if meta is not None:
            count = len(values)
            meta, *rest = lax.optimization_barrier((meta, *values, *finished, *extra))
            values = rest[:count]
            finished = rest[count : count + len(finished)]
            extra = rest[count + len(finished) :]
        values, finished = iter(values), iter(finished)
        for entry, wanted in asked:
            entry[2] = [swap(next(values), axis, bits) for _, axis, bits in wanted]
        for name, pair in ended:
            self.done[name] = tuple(next(finished) for _ in pair)
        return (token, meta, *extra)

    def finish(self):
        while self.running:
            self.step(None, None)


def local(
    tokens,
    out_grad,
    slot_window,
    first_gain,
    first_shift,
    triple_weight,
    triple_bias,
    height_table,
    width_table,
    output_weight,
    output_bias,
    second_gain,
    second_shift,
    expand_weight,
    expand_bias,
    shrink_weight,
    shrink_bias,
):
    micros, images, slots, rows_dev, width = tokens.shape
    parts = lax.axis_size("tensor")
    mine = lax.axis_index("tensor")
    shard = width // parts
    chunks = 3
    unit = width // chunks
    bit = lax.axis_index("dp") & 1
    meta = jnp.where(jnp.arange(2) == 0, mine, bit).astype(jnp.int32)

    by_image = lambda values: jnp.swapaxes(values, 2, 3).reshape(parts, rows_dev, slots, width)
    to_image = lambda values: jnp.swapaxes(
        values.reshape(micros, images, rows_dev, slots, width), 2, 3
    )
    windows = slot_window.reshape(parts, slots)

    packed = triple_weight.reshape(2, shard // 2, -1)
    far = far_half(packed)
    rows_in = exchange_windows(by_image(tokens))
    near = swap(packed, "tensor", 1)
    vectors, packed_rest = prepare(
        chunks,
        (
            first_gain, first_shift, output_bias, second_gain, second_shift, shrink_bias,
            triple_bias, expand_bias,
        ),
        (output_weight, expand_weight, shrink_weight),
    )
    sums = np.zeros((QUAD * HD, LANES), np.float32)
    for head in range(QUAD):
        sums[head * HD : (head + 1) * HD, 2 * head : 2 * head + 2] = 1.0
    sums = jnp.asarray(sums, BF16)
    ahead = (height_table, width_table, table_places(False), head_blocks(False))
    behind = (height_table, width_table, table_places(True), head_blocks(True))
    far, vectors, packed_rest, meta = lax.optimization_barrier((far, vectors, packed_rest, meta))
    other = swap(far, "dp", 1)
    triple_pieces = (
        packed, near, far, other, swap(far, "tensor", 1), swap(other, "tensor", 1),
    )

    packed = after(packed_rest, rows_in, far)
    far = far_half(packed)
    near = swap(packed, "tensor", 1)
    steps = slots // group(slots)
    early = max(1, steps // 2)
    selectors = key_selectors(False)
    kept = attend(
        0, early, meta, windows, rows_in, vectors, ahead, selectors, triple_pieces, None
    )
    kept = list(kept)
    kept[4], far, own_grads = lax.optimization_barrier((kept[4], far, by_image(out_grad)))
    meta, far, own_grads = lax.optimization_barrier((meta, far, own_grads))
    other = swap(far, "dp", 1)
    crossed = swap(far, "tensor", 1)
    grads_in = exchange_windows(own_grads)
    if early < steps:
        kept = attend(
            early, steps - early, meta, windows, rows_in, vectors, ahead, selectors,
            triple_pieces, kept,
        )
    full_rows, normed, triple, probs, attended = kept
    attended, other = lax.optimization_barrier((attended, other))
    rest_pieces = (packed, near, far, other, crossed, swap(other, "tensor", 1))

    middle, normed2, branch, shrink_bias_grad = project(
        meta, windows, attended, full_rows, grads_in, vectors, rest_pieces
    )
    exchanges = Exchanges()
    kept = None
    expand_bias_grads = []
    for number in range(chunks):
        *kept, keep, send, bias_grad = feed(
            number, chunks, meta, normed2, branch, vectors, rest_pieces, kept
        )
        exchanges.begin(("feed", number), reduce_stages([(keep, send, False)]))
        bias_grad, meta = exchanges.step(bias_grad, meta)
        expand_bias_grads.append(bias_grad)

    result, d_middle, d_attended, keep, send, output_bias_grad, gain2_grad, shift2_grad = (
        middle_back(
            meta, windows, rows_dev, middle, *kept, branch, attended, vectors, rest_pieces
        )
    )
    payloads = [(keep, send, True)]
    exchanges.begin(("rest", 0), reduce_stages(payloads))
    output_bias_grad, meta = exchanges.step(output_bias_grad, meta)
    result = exchange_windows(result)

    quad_grads, triple_bias_grads, table_grads = [], [], []
    for quad in range(HEADS // QUAD):
        dq, dk, dv, keep, send, bias_grad, table_grad = attend_back(
            quad, meta, normed, triple, probs, d_attended, attended, behind, key_selectors(True), sums
        )
        if quad == 0:
            payloads.append((keep, send, False))
        else:
            exchanges.begin(("rest", quad), reduce_stages([(keep, send, False)]))
        if quad == 1:
            bias_grad, meta, result = exchanges.step(bias_grad, meta, result)
        else:
            bias_grad, meta = exchanges.step(bias_grad, meta)
        quad_grads.append((dq, dk, dv))
        triple_bias_grads.append(bias_grad)
        table_grads.append(table_grad)
    wide4 = QUAD * HD
    grads9 = [quad_grads[quad][part] for part in range(3) for quad in range(HEADS // QUAD)]
    token_grad, gain1_grad, shift1_grad = first_back(
        0, steps, meta, rows_dev, full_rows, d_middle, vectors, grads9, triple_pieces
    )
    tokens_gradient = to_image(exchange_windows(token_grad))
    result = to_image(result)
    gain1_grad, _ = exchanges.step(gain1_grad, None)
    small = collect(
        (gain1_grad, shift1_grad, output_bias_grad, gain2_grad, shift2_grad, shrink_bias_grad),
        triple_bias_grads,
        expand_bias_grads,
        table_grads,
    )
    exchanges.begin("small", sum_stages(small))
    exchanges.finish()
    shares = [exchanges.done["feed", number] for number in range(chunks)]
    shares += [exchanges.done["rest", number] for number in range(HEADS // QUAD)]
    (
        triple_gradient, output_gradient, expand_gradient, shrink_gradient, *outs, high, wide,
    ) = finish(
        meta,
        shares,
        exchanges.done["small"][0],
        (triple_weight, output_weight, expand_weight, shrink_weight),
        (
            first_gain, first_shift, output_bias, second_gain, second_shift, shrink_bias,
            triple_bias, expand_bias,
        ),
        (height_table, width_table),
        unit,
    )
    return (
        result,
        tokens_gradient,
        outs[0],
        outs[1],
        triple_gradient,
        outs[6],
        high,
        wide,
        output_gradient,
        outs[2],
        outs[3],
        outs[4],
        expand_gradient,
        outs[7],
        shrink_gradient,
        outs[5],
    )


def solution(mesh):
    split = P(None, "dp", "seq", "tensor", None)
    rows = P("tensor", None)
    return jax.shard_map(
        local,
        mesh=mesh,
        in_specs=(
            split, split, P(None, "dp", "seq"), P(), P(), rows, P(), P(), P(), rows, P(), P(), P(),
            rows, P(), rows, P(),
        ),
        out_specs=(
            split, split, P(), P(), rows, P(), P(), P(), rows, P(), P(), P(), rows, P(), rows, P(),
        ),
        check_vma=False,
    )
```

time: 819 us -> 467 us (0.57)
  waiting for transfers between devices: 278 us -> 114 us
  blocking collectives: 109 us -> 0 us
  local copies, waits for them, and re-layouts: 103 us -> 15.9 us
  starting transfers between devices: 28.1 us -> 63.7 us
  other arithmetic: 36.5 us -> 18.7 us
  between operations: 15.4 us -> 1.63 us
    reduce_scatter x8 -> x0, waiting for transfers between devices: 163 us -> none  [the longest x4 104 us: reduce_group(): lax.psum_scatter(share, ('dp', 'seq'), scatter_dimension=0, tiled=True)]
    ppermute x12 -> x52, waiting for transfers between devices: 40.1 us -> 110 us  [swap(): return lax.ppermute(values, axis, [(n, n ^ bits) for n in range(count)])]
    all_gather x2 -> x0, blocking collectives: 68.6 us -> none  [reduce_group(): out.append(lax.all_gather(part, ('dp', 'seq'), axis=0, tiled=True))]
    all_gather x2 -> x0, waiting for transfers between devices: 46.3 us -> none  [reduce_group(): out.append(lax.all_gather(part, ('dp', 'seq'), axis=0, tiled=True))]
    ppermute x12 -> x52, starting transfers between devices: 5.44 us -> 46.5 us  [swap(): return lax.ppermute(values, axis, [(n, n ^ bits) for n in range(count)])]
    psum x1 -> x0, blocking collectives: 40.7 us -> none  [local(): packed = lax.psum(packed, ('dp', 'seq', 'tensor'))]
    all_to_all x6 -> x4, waiting for transfers between devices: 27.4 us -> 4.02 us  [exchange_windows(): lax.all_to_all(values, 'tensor', split_axis=0, concat_axis=0, tiled=True)]
    gather x6 -> x0, local copies, waits for them, and re-layouts: 23 us -> none  [the longest x4 16 us: reduce_group(): ordered = jnp.take(piece, jnp.arange(piece.shape[0]) ^ mine, axis=0)]
  transfers between devices with their start and end apart: 28 -> 56, of which waited for: 13 -> 13; matrix products, arithmetic and copies ran while one was open for 13% -> 3% of each run, Pallas kernels for 27% -> 45%
where the time goes in v2:
time: 467 us; the launch traced here: 462 us
  Pallas kernels  248 us (53%)
  waiting for transfers between devices  114 us (24%)
  starting transfers between devices  63.7 us (14%)
  other arithmetic  18.7 us (4%)
  local copies, waits for them, and re-layouts  15.9 us (3%)
    pallas_call x14, Pallas kernels, call(): pl.pallas_call(kernel, out_shape=tuple((item for item, _ in outs)), grid_...  248 us
    ppermute x52, waiting for transfers between devices, swap(): return lax.ppermute(values, axis, [(n, n ^ bits) for n in range(count)])  110 us
    ppermute x52, starting transfers between devices, swap(): return lax.ppermute(values, axis, [(n, n ^ bits) for n in range(count)])  46.5 us
    all_to_all x4, starting transfers between devices, exchange_windows(): lax.all_to_all(values, 'tensor', split_axis=0, concat_axis=0, tiled=True)  17.2 us
    convert_element_type x28, other arithmetic, add(): return total.astype(BF16)  14.5 us
    unnamed x58, local copies, waits for them, and re-layouts  11.3 us
  transfers between devices with their start and end apart: 56, of which 13 were waited for; matrix products, arithmetic and copies ran while one was open for 3% of the time, Pallas kernels for 45%

profile of v2, /device:TPU:0, one launch (start us, length us, event | category | flops | bytes accessed | tf_op | source)
XLA Modules:
  0.0 462.1 jit_solution(9119328152887701152)
XLA Ops:
  0.7 4.4 all-to-all-start
  12.2 31.4 %collective-permute-done.p2.rest_11_ = bf16[96,2304]{1,0:T(8,128)(2,1)} collective-permute-done((bf16[96,2304]{1,0:T(8,128)(2,1)}, bf16[96,2304]{1,0:T(8,128)(2,1)}, u32[]{:S(2)}, u32[]{:S(2)}) %collective-permute-start) | collective-permute-done | bytes 442400 | tf_op jit(solution)/shard_map/ppermute | solution.py:1035
  48.7 7.6 %collective-permute-done.2.p3.rest_12_ = bf16[96,2304]{1,0:T(8,128)(2,1)} collective-permute-done((bf16[96,2304]{1,0:T(8,128)(2,1)}, bf16[96,2304]{1,0:T(8,128)(2,1)}, u32[]{:S(2)}, u32[]{:S(2)}) %collective-permute-start.2) | collective-permute-done | bytes 442400 | tf_op jit(solution)/shard_map/ppermute | solution.py:1035
  59.0 24.5 %attend.2 = (bf16[8,200,768]{2,1,0:T(8,128)(2,1)}, bf16[8,200,768]{2,1,0:T(8,128)(2,1)}, bf16[8,200,2304]{2,1,0:T(8,128)(2,1)}, bf16[8,12,200,200]{3,2,1,0:T(8,128)(2,1)}, bf16[8,200,768]{2,1,0:T(8,128)(2,1)}) custom-call(s32[2]{0:T(128)} %compare_select_fusion.meta, s32[4,8]{1,0:T(4,128)} %bitcast.68, bf16[4,49,8,768]{3,2,1,0:T(8,128)(2,1)} %copy-done.1, ...), custom_call_target="tpu_custom_call" | custom-call | flops 4797235200 | bytes 18284544 | tf_op jit(solution)/shard_map/attend/pallas_call | solution.py:240
  85.3 4.7 %all-to-all-start.1 = ((bf16[4,49,8,768]{3,2,1,0:T(8,128)(2,1)}), bf16[4,49,8,768]{3,2,1,0:T(8,128)(2,1)}, u32[]{:S(2)}, u32[]{:S(2)}) async-start(bf16[4,49,8,768]{3,2,1,0:T(8,128)(2,1)} %bitcast.62), calls=%async_computation.1 | async-start | bytes 4816896 | tf_op jit(solution)/shard_map/all_to_all | solution.py:1039
  90.6 24.3 %attend.3 = (bf16[8,200,768]{2,1,0:T(8,128)(2,1)}, bf16[8,200,768]{2,1,0:T(8,128)(2,1)}, bf16[8,200,2304]{2,1,0:T(8,128)(2,1)}, bf16[8,12,200,200]{3,2,1,0:T(8,128)(2,1)}, bf16[8,200,768]{2,1,0:T(8,128)(2,1)}) custom-call(s32[2]{0:T(128)} %compare_select_fusion.meta, ...), custom_call_target="tpu_custom_call", output_to_operand_aliasing={{0}: (15, {}), {1}: (16, {}), {2}: (17, {}), {3}: (18, {}),... | custom-call | flops 4797235200 | bytes 18284544 | tf_op jit(solution)/shard_map/attend/pallas_call | solution.py:240
  115.1 4.0 all-to-all-done.1.grads
  119.1 11.9 %project.1 = (f32[1600,768]{1,0:T(8,128)}, bf16[1600,768]{1,0:T(8,128)(2,1)}, bf16[1600,768]{1,0:T(8,128)(2,1)}, f32[1,768]{1,0:T(1,128)}) custom-call(s32[2]{0:T(128)} %compare_select_fusion.meta, s32[4,8]{1,0:T(4,128)} %bitcast.70, bf16[8,200,768]{2,1,0:T(8,128)(2,1)} %get-tuple-element.189.attended.mixed_in, ...), custom_call_target="tpu_custom_call" | custom-call | flops 1887436800 | bytes 17203200 | tf_op jit(solution)/shard_map/project/pallas_call | solution.py:240
  131.0 27.6 %feed.3 = (f32[1600,768]{1,0:T(8,128)}, f32[1600,768]{1,0:T(8,128)}, bf16[2,512,768]{2,1,0:T(8,128)(2,1)}, bf16[2,512,768]{2,1,0:T(8,128)(2,1)}, f32[1,1024]{1,0:T(1,128)}) custom-call(s32[2]{0:T(128)} %compare_select_fusion.meta, bf16[1600,768]{1,0:T(8,128)(2,1)} %get-tuple-element.193.normed, bf16[1600,768]{1,0:T(8,128)(2,1)} %get-tuple-element.194.branch, ...), custom_call_target="tpu_custom_call" | custom-call | flops 15099494400 | bytes 30867456 | tf_op jit(solution)/shard_map/feed/pallas_call | solution.py:240
  158.7 29.2 %feed.4 = (f32[1600,768]{1,0:T(8,128)}, f32[1600,768]{1,0:T(8,128)}, bf16[2,512,768]{2,1,0:T(8,128)(2,1)}, bf16[2,512,768]{2,1,0:T(8,128)(2,1)}, f32[1,1024]{1,0:T(1,128)}) custom-call(s32[2]{0:T(128)} %compare_select_fusion.meta, bf16[1600,768]{1,0:T(8,128)(2,1)} %get-tuple-element.193.normed, ...), custom_call_target="tpu_custom_call", output_to_operand_aliasing={{0}: (10, {}), {1}: (11, {})} | custom-call | flops 15099494400 | bytes 30867456 | tf_op jit(solution)/shard_map/feed/pallas_call | solution.py:240
  190.0 28.8 %feed.5 = (f32[1600,768]{1,0:T(8,128)}, f32[1600,768]{1,0:T(8,128)}, bf16[2,512,768]{2,1,0:T(8,128)(2,1)}, bf16[2,512,768]{2,1,0:T(8,128)(2,1)}, f32[1,1024]{1,0:T(1,128)}) custom-call(s32[2]{0:T(128)} %compare_select_fusion.meta, bf16[1600,768]{1,0:T(8,128)(2,1)} %get-tuple-element.193.normed, ...), custom_call_target="tpu_custom_call", output_to_operand_aliasing={{0}: (10, {}), {1}: (11, {})} | custom-call | flops 15099494400 | bytes 30867456 | tf_op jit(solution)/shard_map/feed/pallas_call | solution.py:240
  222.7 19.5 %middle.1 = (bf16[4,49,8,768]{3,2,1,0:T(8,128)(2,1)}, f32[1600,768]{1,0:T(8,128)}, bf16[8,200,768]{2,1,0:T(8,128)(2,1)}, bf16[2,192,768]{2,1,0:T(8,128)(2,1)}, b...) custom-call(s32[2]{0:T(128)} %compare_select_fusion.meta, ...), custom_call_target="tpu_custom_call" | custom-call | flops 3774873600 | bytes 29491200 | tf_op jit(solution)/shard_map/middle/pallas_call | solution.py:240
  248.7 4.5 all-to-all-start.2
  256.8 17.9 %attend_back.3 = (bf16[8,200,256]{2,1,0:T(8,128)(2,1)}, bf16[8,200,256]{2,1,0:T(8,128)(2,1)}, bf16[8,200,256]{2,1,0:T(8,128)(2,1)}, bf16[2,192,768]{2,1,0:T(8,12...) custom-call(s32[2]{0:T(128)} %compare_select_fusion.meta, ...), custom_call_target="tpu_custom_call" | custom-call | flops 4508876800 | bytes 12288000 | tf_op jit(solution)/shard_map/attend_back/pallas_call | solution.py:240
  274.7 15.9 %collective-permute-done.17 = bf16[256,768]{1,0:T(8,128)(2,1)S(1)} collective-permute-done((bf16[256,768]{1,0:T(8,128)(2,1)}, bf16[256,768]{1,0:T(8,128)(2,1)S(1)}, u32[]{:S(2)}, u32[]{:S(2)}) %collective-permute-start.17) | collective-permute-done | bytes 393248 | tf_op jit(solution)/shard_map/ppermute | solution.py:1035
  296.9 18.0 %attend_back.4 = (bf16[8,200,256]{2,1,0:T(8,128)(2,1)}, bf16[8,200,256]{2,1,0:T(8,128)(2,1)}, bf16[8,200,256]{2,1,0:T(8,128)(2,1)}, bf16[2,192,768]{2,1,0:T(8,12...) custom-call(s32[2]{0:T(128)} %compare_select_fusion.meta, ...), custom_call_target="tpu_custom_call" | custom-call | flops 4508876800 | bytes 12288000 | tf_op jit(solution)/shard_map/attend_back/pallas_call | solution.py:240
  324.1 17.9 %attend_back.5 = (bf16[8,200,256]{2,1,0:T(8,128)(2,1)}, bf16[8,200,256]{2,1,0:T(8,128)(2,1)}, bf16[8,200,256]{2,1,0:T(8,128)(2,1)}, bf16[2,192,768]{2,1,0:T(8,12...) custom-call(s32[2]{0:T(128)} %compare_select_fusion.meta, ...), custom_call_target="tpu_custom_call" | custom-call | flops 4508876800 | bytes 12288000 | tf_op jit(solution)/shard_map/attend_back/pallas_call | solution.py:240
  351.3 17.5 %first_back.1 = (bf16[4,49,8,768]{3,2,1,0:T(8,128)(2,1)}, f32[1,768]{1,0:T(1,128)}, f32[1,768]{1,0:T(1,128)}) custom-call(s32[2]{0:T(128)} %compare_select_fusion.meta, bf16[8,200,768]{2,1,0:T(8,128)(2,1)} %get-tuple-element.190.rows_in, f32[1600,768]{1,0:T(8,128)} %get-tuple-element.272.d_middle, f32[13,768]{1,0:T(8,128)} %get-tuple-element.174.vectors, ...), custom_call_target="tpu_custom_call" | custom-call | flops 5662310400 | bytes 17203200 | tf_op jit(solution)/shard_map/first_back/pallas_call | solution.py:240
  368.8 3.6 all-to-all-start.3
  384.7 21.5 %collective-permute-done.48 = f32[24,768]{1,0:T(8,128)S(1)} collective-permute-done((f32[24,768]{1,0:T(8,128)S(1)}, f32[24,768]{1,0:T(8,128)S(1)}, u32[]{:S(2)}, u32[]{:S(2)}) %collective-permute-start.48) | collective-permute-done | bytes 73760 | tf_op jit(solution)/shard_map/ppermute | solution.py:1035
  418.2 15.1 %collective-permute-done.40 = bf16[96,768]{1,0:T(8,128)(2,1)S(1)} collective-permute-done((bf16[96,768]{1,0:T(8,128)(2,1)S(1)}, bf16[96,768]{1,0:T(8,128)(2,1)S(1)}, u32[]{:S(2)}, u32[]{:S(2)}) %collective-permute-start.40) | collective-permute-done | bytes 147488 | tf_op jit(solution)/shard_map/ppermute | solution.py:1035
  435.7 7.3 %collective-permute-done.45 = bf16[96,768]{1,0:T(8,128)(2,1)S(1)} collective-permute-done((bf16[96,768]{1,0:T(8,128)(2,1)S(1)}, bf16[96,768]{1,0:T(8,128)(2,1)S(1)}, u32[]{:S(2)}, u32[]{:S(2)}) %collective-permute-start.45) | collective-permute-done | bytes 147488 | tf_op jit(solution)/shard_map/ppermute | solution.py:1035
  443.8 5.3 %collective-permute-done.51 = f32[24,768]{1,0:T(8,128)S(1)} collective-permute-done((f32[24,768]{1,0:T(8,128)S(1)}, f32[24,768]{1,0:T(8,128)S(1)}, u32[]{:S(2)}, u32[]{:S(2)}) %collective-permute-start.51) | collective-permute-done | bytes 73760 | tf_op jit(solution)/shard_map/ppermute | solution.py:1035
  451.3 5.9 %finish.1 = (f32[192,2304]{1,0:T(8,128)}, f32[192,768]{1,0:T(8,128)}, f32[192,3072]{1,0:T(8,128)}, f32[768,768]{1,0:T(8,128)}, f32[768]{0:T(1024)}, /*index=5*/f...) custom-call(s32[2]{0:T(128)} %compare_select_fusion.meta, ...), custom_call_target="tpu_custom_call" | custom-call | bytes 10616832 | tf_op jit(solution)/shard_map/finish/pallas_call | solution.py:240
  (208 shorter events, 92.2 us)
Async XLA Ops:
  0.7 45.3 %all-to-all-start = ((bf16[4,49,8,768]{3,2,1,0:T(8,128)(2,1)}), bf16[4,49,8,768]{3,2,1,0:T(8,128)(2,1)S(1)}, u32[]{:S(2)}, u32[]{:S(2)}) async-start(bf16[4,49,8,768]{3,2,1,0:T(8,128)(2,1)} %bitcast.61), calls=%async_computation | async-start | bytes 4816896 | tf_op jit(solution)/shard_map/all_to_all | solution.py:1039
  5.8 37.8 %collective-permute-start = (bf16[96,2304]{1,0:T(8,128)(2,1)}, bf16[96,2304]{1,0:T(8,128)(2,1)}, u32[]{:S(2)}, u32[]{:S(2)}) collective-permute-start(bf16[96,2304]{1,0:T(8,128)(2,1)} %dynamic-slice_bitcast_fusion.1), channel_id=1, source_target_pairs={{0,2},{1,3},{2,0},{3,1},{4,6},{5,7},{6,4},{7,5},{8,10},{9,11},{10,... | collective-permute-start | bytes 1327112 | tf_op jit(solution)/shard_map/ppermute | solution.py:1035
  8.2 48.0 %collective-permute-start.1 = (bf16[2,96,2304]{2,1,0:T(8,128)(2,1)S(1)}, bf16[2,96,2304]{2,1,0:T(8,128)(2,1)}, u32[]{:S(2)}, u32[]{:S(2)}) collective-permute-start(bf16[2,96,2304]{2,1,0:T(8,128)(2,1)S(1)} %bitcast.67), channel_id=1, source_target_pairs={{0,1},{1,0},{2,3},{3,2},{4,5},{5,4},{6,7},{7,6},{8,9},{9,8},{10,11... | collective-permute-start | bytes 2654216 | tf_op jit(solution)/shard_map/ppermute | solution.py:1035
  48.3 35.3 %collective-permute-start.5 = (bf16[864,768]{1,0:T(8,128)(2,1)S(1)}, bf16[864,768]{1,0:T(8,128)(2,1)}, u32[]{:S(2)}, u32[]{:S(2)}) collective-permute-start(bf16[864,768]{1,0:T(8,128)(2,1)S(1)} %dynamic-slice_bitcast_fusion), channel_id=1, source_target_pairs={{0,2},{1,3},{2,0},{3,1},{4,6},{5,7},{6,4},{7,5},{8,10},{9,11},{10,... | collective-permute-start | bytes 3981320 | tf_op jit(solution)/shard_map/ppermute | solution.py:1035
  83.5 31.6 %collective-permute-start.6 = (bf16[864,768]{1,0:T(8,128)(2,1)}, bf16[864,768]{1,0:T(8,128)(2,1)}, u32[]{:S(2)}, u32[]{:S(2)}) collective-permute-start(bf16[864,768]{1,0:T(8,128)(2,1)} %collective-permute-done.5.p2.rest_2_), channel_id=1, source_target_pairs={{0,16},{16,0},{1,17},{17,1},{2,18},{18,2},{3,19},{19,3},{4,20},{20... | collective-permute-start | bytes 3981320 | tf_op jit(solution)/shard_map/ppermute | solution.py:1035
  85.3 29.8 %collective-permute-start.7 = (bf16[2,864,768]{2,1,0:T(8,128)(2,1)S(1)}, bf16[2,864,768]{2,1,0:T(8,128)(2,1)}, u32[]{:S(2)}, u32[]{:S(2)}) collective-permute-start(bf16[2,864,768]{2,1,0:T(8,128)(2,1)S(1)} %copy-done), channel_id=1, source_target_pairs={{0,1},{1,0},{2,3},{3,2},{4,5},{5,4},{6,7},{7,6},{8,9},{9,8},{10,11... | collective-permute-start | bytes 7962632 | tf_op jit(solution)/shard_map/ppermute | solution.py:1035
  85.3 33.8 %all-to-all-start.1 = ((bf16[4,49,8,768]{3,2,1,0:T(8,128)(2,1)}), bf16[4,49,8,768]{3,2,1,0:T(8,128)(2,1)}, u32[]{:S(2)}, u32[]{:S(2)}) async-start(bf16[4,49,8,768]{3,2,1,0:T(8,128)(2,1)} %bitcast.62), calls=%async_computation.1 | async-start | bytes 4816896 | tf_op jit(solution)/shard_map/all_to_all | solution.py:1039
  90.0 25.1 %collective-permute-start.8 = (bf16[864,768]{1,0:T(8,128)(2,1)}, bf16[864,768]{1,0:T(8,128)(2,1)}, u32[]{:S(2)}, u32[]{:S(2)}) collective-permute-start(bf16[864,768]{1,0:T(8,128)(2,1)} %collective-permute-done.5.p2.rest_2_), channel_id=1, source_target_pairs={{0,1},{1,0},{2,3},{3,2},{4,5},{5,4},{6,7},{7,6},{8,9},{9,8},{10,11... | collective-permute-start | bytes 3981320 | tf_op jit(solution)/shard_map/ppermute | solution.py:1035
  158.6 29.3 %collective-permute-start.10 = (bf16[2,512,768]{2,1,0:T(8,128)(2,1)}, bf16[2,512,768]{2,1,0:T(8,128)(2,1)S(1)}, u32[]{:S(2)}, u32[]{:S(2)}) collective-permute-start(bf16[2,512,768]{2,1,0:T(8,128)(2,1)} %get-tuple-element.201), channel_id=1, source_target_pairs={{0,1},{1,0},{2,3},{3,2},{4,5},{5,4},{6,7},{7,6},{8,9},{9,8},{10,11... | collective-permute-start | bytes 4718600 | tf_op jit(solution)/shard_map/ppermute | solution.py:1035
  188.3 30.4 %collective-permute-start.12 = (bf16[2,512,768]{2,1,0:T(8,128)(2,1)}, bf16[2,512,768]{2,1,0:T(8,128)(2,1)S(1)}, u32[]{:S(2)}, u32[]{:S(2)}) collective-permute-start(bf16[2,512,768]{2,1,0:T(8,128)(2,1)} %get-tuple-element.209), channel_id=1, source_target_pairs={{0,1},{1,0},{2,3},{3,2},{4,5},{5,4},{6,7},{7,6},{8,9},{9,8},{10,11... | collective-permute-start | bytes 4718600 | tf_op jit(solution)/shard_map/ppermute | solution.py:1035
  188.9 29.9 %collective-permute-start.11 = (bf16[2,256,768]{2,1,0:T(8,128)(2,1)S(1)}, bf16[2,256,768]{2,1,0:T(8,128)(2,1)S(1)}, u32[]{:S(2)}, u32[]{:S(2)}) collective-permute-start(bf16[2,256,768]{2,1,0:T(8,128)(2,1)S(1)} %broadcast_select_fusion.2), channel_id=1, source_target_pairs={{0,16},{16,0},{1,17},{17,1},{2,18},{18,2},{3,19},{19,3},{4,20},{20... | collective-permute-start | bytes 2359304 | tf_op jit(solution)/shard_map/ppermute | solution.py:1035
  247.9 42.7 %collective-permute-start.18 = (bf16[2,256,768]{2,1,0:T(8,128)(2,1)}, bf16[2,256,768]{2,1,0:T(8,128)(2,1)}, u32[]{:S(2)}, u32[]{:S(2)}) collective-permute-start(bf16[2,256,768]{2,1,0:T(8,128)(2,1)} %broadcast_select_fusion), channel_id=1, source_target_pairs={{0,16},{16,0},{1,17},{17,1},{2,18},{18,2},{3,19},{19,3},{4,20},{20... | collective-permute-start | bytes 2359304 | tf_op jit(solution)/shard_map/ppermute | solution.py:1035
  248.7 41.9 %collective-permute-start.19 = (bf16[2,192,768]{2,1,0:T(8,128)(2,1)}, bf16[2,192,768]{2,1,0:T(8,128)(2,1)S(1)}, u32[]{:S(2)}, u32[]{:S(2)}) collective-permute-start(bf16[2,192,768]{2,1,0:T(8,128)(2,1)} %get-tuple-element.236), channel_id=1, source_target_pairs={{0,1},{1,0},{2,3},{3,2},{4,5},{5,4},{6,7},{7,6},{8,9},{9,8},{10,11... | collective-permute-start | bytes 1769480 | tf_op jit(solution)/shard_map/ppermute | solution.py:1035
  248.7 71.0 %all-to-all-start.2 = ((bf16[4,49,8,768]{3,2,1,0:T(8,128)(2,1)}), bf16[4,49,8,768]{3,2,1,0:T(8,128)(2,1)}, u32[]{:S(2)}, u32[]{:S(2)}) async-start(bf16[4,49,8,768]{3,2,1,0:T(8,128)(2,1)} %get-tuple-element.255), calls=%async_computation.2 | async-start | bytes 4816896 | tf_op jit(solution)/shard_map/all_to_all | solution.py:1039
  254.8 35.8 %collective-permute-start.17 = (bf16[256,768]{1,0:T(8,128)(2,1)}, bf16[256,768]{1,0:T(8,128)(2,1)S(1)}, u32[]{:S(2)}, u32[]{:S(2)}) collective-permute-start(bf16[256,768]{1,0:T(8,128)(2,1)} %slice_bitcast_fusion.3), channel_id=1, source_target_pairs={{0,2},{1,3},{2,0},{3,1},{4,6},{5,7},{6,4},{7,5},{8,10},{9,11},{10,... | collective-permute-start | bytes 1179656 | tf_op jit(solution)/shard_map/ppermute | solution.py:1035
  347.2 25.3 %collective-permute-start.33 = (bf16[2,192,768]{2,1,0:T(8,128)(2,1)}, bf16[2,192,768]{2,1,0:T(8,128)(2,1)}, u32[]{:S(2)}, u32[]{:S(2)}) collective-permute-start(bf16[2,192,768]{2,1,0:T(8,128)(2,1)} %get-tuple-element.290), channel_id=1, source_target_pairs={{0,1},{1,0},{2,3},{3,2},{4,5},{5,4},{6,7},{7,6},{8,9},{9,8},{10,11... | collective-permute-start | bytes 1769480 | tf_op jit(solution)/shard_map/ppermute | solution.py:1035
  347.2 25.3 %collective-permute-start.31 = (bf16[192,768]{1,0:T(8,128)(2,1)}, bf16[192,768]{1,0:T(8,128)(2,1)}, u32[]{:S(2)}, u32[]{:S(2)}) collective-permute-start(bf16[192,768]{1,0:T(8,128)(2,1)} %slice_bitcast_fusion.7), channel_id=1, source_target_pairs={{0,2},{1,3},{2,0},{3,1},{4,6},{5,7},{6,4},{7,5},{8,10},{9,11},{10,... | collective-permute-start | bytes 884744 | tf_op jit(solution)/shard_map/ppermute | solution.py:1035
  368.8 88.4 %all-to-all-start.3 = ((bf16[4,49,8,768]{3,2,1,0:T(8,128)(2,1)}), bf16[4,49,8,768]{3,2,1,0:T(8,128)(2,1)S(1)}, u32[]{:S(2)}, u32[]{:S(2)}) async-start(bf16[4,49,8,768]{3,2,1,0:T(8,128)(2,1)} %get-tuple-element.282), calls=%async_computation.3 | async-start | bytes 4816896 | tf_op jit(solution)/shard_map/all_to_all | solution.py:1039
  377.0 30.6 %collective-permute-start.38 = (bf16[96,768]{1,0:T(8,128)(2,1)S(1)}, bf16[96,768]{1,0:T(8,128)(2,1)S(1)}, u32[]{:S(2)}, u32[]{:S(2)}) collective-permute-start(bf16[96,768]{1,0:T(8,128)(2,1)S(1)} %slice_bitcast_fusion.10), channel_id=1, source_target_pairs={{0,2},{1,3},{2,0},{3,1},{4,6},{5,7},{6,4},{7,5},{8,10},{9,11},{10,... | collective-permute-start | bytes 442376 | tf_op jit(solution)/shard_map/ppermute | solution.py:1035
  380.0 31.9 %collective-permute-start.42 = (bf16[2,96,768]{2,1,0:T(8,128)(2,1)S(1)}, bf16[2,96,768]{2,1,0:T(8,128)(2,1)S(1)}, u32[]{:S(2)}, u32[]{:S(2)}) collective-permute-start(bf16[2,96,768]{2,1,0:T(8,128)(2,1)S(1)} %broadcast_select_fusion.4), channel_id=1, source_target_pairs={{0,16},{16,0},{1,17},{17,1},{2,18},{18,2},{3,19},{19,3},{4,20},{20... | collective-permute-start | bytes 884744 | tf_op jit(solution)/shard_map/ppermute | solution.py:1035
  381.3 25.0 %collective-permute-start.48 = (f32[24,768]{1,0:T(8,128)S(1)}, f32[24,768]{1,0:T(8,128)S(1)}, u32[]{:S(2)}, u32[]{:S(2)}) collective-permute-start(f32[24,768]{1,0:T(8,128)S(1)} %add.146), channel_id=1, source_target_pairs={{0,2},{1,3},{2,0},{3,1},{4,6},{5,7},{6,4},{7,5},{8,10},{9,11},{10,... | collective-permute-start | bytes 221192 | tf_op jit(solution)/shard_map/ppermute | solution.py:1035
  382.7 29.8 %collective-permute-start.35 = (bf16[192,768]{1,0:T(8,128)(2,1)S(1)}, bf16[192,768]{1,0:T(8,128)(2,1)S(1)}, u32[]{:S(2)}, u32[]{:S(2)}) collective-permute-start(bf16[192,768]{1,0:T(8,128)(2,1)S(1)} %fusion.3), channel_id=1, source_target_pairs={{0,4},{4,0},{8,12},{12,8},{1,5},{5,1},{9,13},{13,9},{2,6},{6,2},{1... | collective-permute-start | bytes 884744 | tf_op jit(solution)/shard_map/ppermute | solution.py:1035
  384.0 65.8 %collective-permute-start.34 = (bf16[256,768]{1,0:T(8,128)(2,1)S(1)}, bf16[256,768]{1,0:T(8,128)(2,1)S(1)}, u32[]{:S(2)}, u32[]{:S(2)}) collective-permute-start(bf16[256,768]{1,0:T(8,128)(2,1)S(1)} %add_convert_fusion.11.refs_4_), channel_id=1, source_target_pairs={{0,16},{16,0},{1,17},{17,1},{2,18},{18,2},{3,19},{19,3},{4,20},{20... | collective-permute-start | bytes 1179656 | tf_op jit(solution)/shard_map/ppermute | solution.py:1035
  410.7 33.0 %collective-permute-start.50 = (f32[24,768]{1,0:T(8,128)S(1)}, f32[24,768]{1,0:T(8,128)S(1)}, u32[]{:S(2)}, u32[]{:S(2)}) collective-permute-start(f32[24,768]{1,0:T(8,128)S(1)} %add.148), channel_id=1, source_target_pairs={{0,4},{4,0},{8,12},{12,8},{1,5},{5,1},{9,13},{13,9},{2,6},{6,2},{1... | collective-permute-start | bytes 221192 | tf_op jit(solution)/shard_map/ppermute | solution.py:1035
  (60 other events, 667.2 us)

commit v3 on v2

--- a/solution.py
+++ b/solution.py
@@ -137,18 +137,10 @@
     return (scaled - mean_grad - unit * mean_both) * scale
 
 
-def weight_places(meta, pieces):
-    own, near, far0, far1, cross0, cross1 = pieces
-    mine, bit = meta[0], meta[1]
+def quarter_places(meta):
+    mine, quarter = meta[0], meta[2]
     return [
-        (own, 0, 2 * mine),
-        (own, 1, 2 * mine + 1),
-        (near, 0, 2 * (mine ^ 1)),
-        (near, 1, 2 * (mine ^ 1) + 1),
-        (far0, None, 2 * (mine ^ 2) + bit),
-        (far1, None, 2 * (mine ^ 2) + 1 - bit),
-        (cross0, None, 2 * (mine ^ 3) + bit),
-        (cross1, None, 2 * (mine ^ 3) + 1 - bit),
+        [4 * (mine ^ who) + (quarter ^ flip) for flip in (0, 2, 1, 3)] for who in (2, 3)
     ]
 
 
@@ -167,14 +159,19 @@
 
 
 def load_rows(meta, pieces, target, sems, first=0):
-    height = target.shape[0] // 8
+    own, near, *far = pieces
+    columns = target.shape[1]
+    quarter = target.shape[0] // 16
     pairs = []
-    for source, half, place in weight_places(meta, pieces):
-        source = source if half is None else source.at[half]
-        start = pl.multiple_of(place * height, 16)
-        pairs.append(
-            (source.at[pl.ds(first, height), :], target.at[pl.ds(start, height), :])
-        )
+    for source, who in ((own, 0), (near, 1)):
+        start = pl.multiple_of(4 * (meta[0] ^ who) * quarter, 16)
+        pairs.append((source, target.at[pl.ds(start, 4 * quarter), :]))
+    for sources, places in zip(far, quarter_places(meta)):
+        for index, place in enumerate(places):
+            start = pl.multiple_of(place * quarter, 16)
+            pairs.append(
+                (sources.at[index, :, pl.ds(first, columns)], target.at[pl.ds(start, quarter), :])
+            )
     return start_copies(pairs, sems)
 
 
@@ -216,12 +213,14 @@
                 block[part, :, :, piece * LANES : (piece + 1) * LANES] = values.astype(BF16)
 
 
-def write_owned(source, meta, keep, send):
+def write_owned(source, meta, keep, send, across):
     height = keep.shape[1]
     for index in range(4):
         start = pl.multiple_of((meta[0] ^ index) * height, 16)
-        target = send if index & 1 else keep
-        target[index >> 1] = source[pl.ds(start, height), :].astype(BF16)
+        target = send if index & across else keep
+        target[index >> 1 if across == 1 else index & 1] = source[
+            pl.ds(start, height), :
+        ].astype(BF16)
 
 
 ANY = pl.BlockSpec(memory_space=pl.ANY)
@@ -261,34 +260,33 @@
 
 
 def prepare_kernel(chunks, *refs):
-    items, (output, expand, shrink), (vectors, packed) = refs[:8], refs[8:11], refs[11:]
+    items, (expand, shrink), (vectors, packed) = refs[:8], refs[8:10], refs[10:]
     width = vectors.shape[1]
     row = 0
     for item in items:
         for start in range(0, item.shape[0], width):
             vectors[row : row + 1, :] = item[pl.ds(start, width)].reshape(1, width)
             row += 1
-    half = output.shape[0] // 2
+    quarter = expand.shape[0] // 4
     blocks = expand.shape[1] // width
-    tall = shrink.shape[0] // (2 * chunks)
-    for upper in range(2):
-        rows = slice(upper * half, (upper + 1) * half)
-        packed[upper, :half, :] = output[rows, :]
+    tall = shrink.shape[0] // (4 * chunks)
+    for index in range(4):
+        rows = slice(index * quarter, (index + 1) * quarter)
         for block in range(blocks):
-            start = (1 + block) * half
-            packed[upper, start : start + half, :] = expand[
+            start = block * quarter
+            packed[index, start : start + quarter, :] = expand[
                 rows, block * width : (block + 1) * width
             ]
         for number in range(chunks):
-            start = (1 + blocks) * half + number * tall
-            source = (2 * number + upper) * tall
-            packed[upper, start : start + tall, :] = shrink[source : source + tall, :]
+            start = blocks * quarter + number * tall
+            source = (4 * number + index) * tall
+            packed[index, start : start + tall, :] = shrink[source : source + tall, :]
 
 
 def prepare(chunks, items, weights):
-    width = weights[0].shape[1]
+    width = weights[1].shape[1]
     count = sum(item.shape[0] for item in items) // width
-    total = sum(item.shape[0] * item.shape[1] for item in weights) // (2 * width)
+    total = sum(item.shape[0] * item.shape[1] for item in weights) // (4 * width)
     return call(
         functools.partial(prepare_kernel, chunks),
         "prepare",
@@ -297,7 +295,7 @@
         [(item, whole(*item.shape)) for item in (*items, *weights)],
         [
             (like((count, width), F32), whole(count, width)),
-            (like((2, total, width), BF16), whole(2, total, width)),
+            (like((4, total, width), BF16), whole(4, total, width)),
         ],
         [],
         (0, 8 * total * width, 0),
@@ -350,19 +348,20 @@
 
 def attend_kernel(
     slabs, before, meta, windows, tokens, vectors, height, width_table, places, blocks, selectors,
-    p0, p1, p2, p3, p4, p5, *rest,
+    *rest,
 ):
     (
         rows_out, normed_out, triple_out, probs_out, attended_out,
         full, staged, weight, tables, masked_keys, sems,
     ) = rest[-11:]
+    pieces = rest[:4]
     step = pl.program_id(0)
     base_slab = (step + before) * slabs
     width = full.shape[2]
 
     @pl.when(step == 0)
     def _():
-        copies = load_rows(meta, (p0, p1, p2, p3, p4, p5), weight, sems)
+        copies = load_rows(meta, pieces, weight, sems)
         tables[...] = build_tables(height, width_table, places, blocks)
         wait_all(copies)
 
@@ -389,49 +388,62 @@
         for head in range(QUAD):
             masked_keys[slab, head] = selectors[head] + penalty
 
-    def one_quad(index, carry):
-        slab = index // quads
-        quad = index - slab * quads
-        allowed = valid_rows(windows[meta[0], base_slab + slab])
+    sides = (jnp.logical_not(upper), upper)
+    zero = jnp.zeros((ROWS, LANES), BF16)
+    halves_of = lambda values, head: jnp.where(
+        sides[head & 1], values[:, (head >> 1) * LANES : ((head >> 1) + 1) * LANES], zero
+    )
+    every = [(slab, head) for slab in range(slabs) for head in range(QUAD)]
+    constant = jnp.where(lane == WIN, 1.0, 0.0)
+
+    def one_quad(quad, carry):
         base = pl.multiple_of(quad * QUAD * HD, LANES)
-        queries = triple_out[slab, :, pl.ds(base, QUAD * HD)]
-        keys = triple_out[slab, :, pl.ds(pl.multiple_of(base + width, LANES), QUAD * HD)]
-        values = triple_out[slab, :, pl.ds(pl.multiple_of(base + 2 * width, LANES), QUAD * HD)]
-        terms = dot(queries, tables[...])
-        high = roll_rows(terms[:, :LANES], False)
-        wide = roll_rows(terms[:, LANES:], True)
-        constant = jnp.where(lane == WIN, 1.0, 0.0)
-        relative = jnp.where(
-            within < WIN, high, jnp.where((within >= 16) & (within < 16 + WIN), wide, constant)
-        ).astype(BF16)
-        queries = queries * jnp.asarray(HD**-0.5, BF16)
-        outs = []
-        for pair in range(QUAD // 2):
-            columns = slice(pair * LANES, (pair + 1) * LANES)
-            left = jnp.concatenate([queries[:, columns], relative], axis=1)
-            total = None
-            for side in range(2):
-                head = 2 * pair + side
-                mine = upper if side else jnp.logical_not(upper)
-                zero = jnp.zeros((ROWS, LANES), BF16)
-                right = jnp.concatenate(
-                    [jnp.where(mine, keys[:, columns], zero), masked_keys[slab, head]], axis=1
-                )
-                scores = dot_t(left, right)
-                maxima = jnp.max(scores, axis=-1, keepdims=True)
-                exponent = jnp.exp(scores - maxima)
-                summed = jnp.sum(exponent, axis=-1, keepdims=True)
-                probs = (exponent * (1.0 / summed)).astype(BF16)
-                probs_out[slab, quad * QUAD + head] = probs
-                part = dot(probs, jnp.where(mine, values[:, columns], zero))
-                total = part if total is None else total + part
-            outs.append(total)
-        mixed = jnp.concatenate(outs, axis=1)
-        mixed = jnp.where(allowed, mixed, 0.0)
-        attended_out[slab, :, pl.ds(base, QUAD * HD)] = mixed.astype(BF16)
+        near = pl.multiple_of(base + width, LANES)
+        far = pl.multiple_of(base + 2 * width, LANES)
+        queries = [triple_out[slab, :, pl.ds(base, QUAD * HD)] for slab in range(slabs)]
+        keys = [triple_out[slab, :, pl.ds(near, QUAD * HD)] for slab in range(slabs)]
+        values = [triple_out[slab, :, pl.ds(far, QUAD * HD)] for slab in range(slabs)]
+        terms = [dot(item, tables[...]) for item in queries]
+        lefts = []
+        for slab in range(slabs):
+            high = roll_rows(terms[slab][:, :LANES], False)
+            wide = roll_rows(terms[slab][:, LANES:], True)
+            relative = jnp.where(
+                within < WIN, high, jnp.where((within >= 16) & (within < 16 + WIN), wide, constant)
+            ).astype(BF16)
+            scaled = queries[slab] * jnp.asarray(HD**-0.5, BF16)
+            lefts.append(
+                [
+                    jnp.concatenate([scaled[:, pair * LANES : (pair + 1) * LANES], relative], axis=1)
+                    for pair in range(QUAD // 2)
+                ]
+            )
+        scores = [
+            dot_t(
+                lefts[slab][head >> 1],
+                jnp.concatenate([halves_of(keys[slab], head), masked_keys[slab, head]], axis=1),
+            )
+            for slab, head in every
+        ]
+        probs = []
+        for (slab, head), score in zip(every, scores):
+            maxima = jnp.max(score, axis=-1, keepdims=True)
+            exponent = jnp.exp(score - maxima)
+            summed = jnp.sum(exponent, axis=-1, keepdims=True)
+            probs.append((exponent * (1.0 / summed)).astype(BF16))
+            probs_out[slab, quad * QUAD + head] = probs[-1]
+        parts = [dot(prob, halves_of(values[slab], head)) for (slab, head), prob in zip(every, probs)]
+        for slab in range(slabs):
+            mine = parts[slab * QUAD : (slab + 1) * QUAD]
+            mixed = jnp.concatenate(
+                [mine[2 * pair] + mine[2 * pair + 1] for pair in range(QUAD // 2)], axis=1
+            )
+            allowed = valid_rows(windows[meta[0], base_slab + slab])
+            mixed = jnp.where(allowed, mixed, 0.0)
+            attended_out[slab, :, pl.ds(base, QUAD * HD)] = mixed.astype(BF16)
         return carry
 
-    lax.fori_loop(0, slabs * quads, one_quad, 0)
+    lax.fori_loop(0, quads, one_quad, 0, unroll=True)
 
 
 def attend(before, steps, meta, windows, tokens, vectors, tables, selectors, pieces, kept):
@@ -467,7 +479,7 @@
             pltpu.VMEM((width, 3 * width), BF16),
             pltpu.VMEM((2 * LANES, 2 * LANES), BF16),
             pltpu.VMEM((slabs, QUAD, ROWS, LANES), BF16),
-            pltpu.SemaphoreType.DMA((8,)),
+            pltpu.SemaphoreType.DMA((10,)),
         ],
         (
             6 * rows * width * width + steps * slabs * HEADS * 4 * ROWS * ROWS * 256,
@@ -479,14 +491,15 @@
 
 
 def project_kernel(
-    slabs, meta, windows, attended, rows_in, grads, vectors, p0, p1, p2, p3, p4, p5,
-    middle_out, normed_out, branch_out, shrink_bias_out, full, staged, weight, sems,
+    slabs, first, meta, windows, attended, rows_in, grads, vectors, *rest,
 ):
+    pieces = rest[:4]
+    middle_out, normed_out, branch_out, shrink_bias_out, full, staged, weight, sems = rest[4:]
     step = pl.program_id(0)
 
     @pl.when(step == 0)
     def _():
-        wait_all(load_rows(meta, (p0, p1, p2, p3, p4, p5), weight, sems))
+        wait_all(load_rows(meta, pieces, weight, sems, first))
         shrink_bias_out[...] = jnp.zeros_like(shrink_bias_out)
 
     width = full.shape[2]
@@ -515,7 +528,7 @@
     flat = pl.BlockSpec((slabs * ROWS, width), lambda i, *_: (i, 0))
     rows = slots * ROWS
     return call(
-        functools.partial(project_kernel, slabs),
+        functools.partial(project_kernel, slabs, 3 * width),
         "project",
         slots // slabs,
         (meta, windows),
@@ -532,7 +545,7 @@
             pltpu.VMEM((slabs, ROWS, width), F32),
             pltpu.VMEM((parts * width // LANES, rows_dev * slots, LANES), F32),
             pltpu.VMEM((width, width), BF16),
-            pltpu.SemaphoreType.DMA((8,)),
+            pltpu.SemaphoreType.DMA((10,)),
         ],
         (2 * rows * width * width, rows * width * 14, 0),
     )
@@ -545,35 +558,41 @@
 
 
 def feed_kernel(number, first, unit, meta, normed, branch, vectors, *rest):
-    pieces, rest = rest[:6], rest[6:]
+    pieces, rest = rest[:10], rest[10:]
     if not first:
         out_in, grad_in = rest[:2]
     out_acc, grad_acc, keep, send, bias_grad, expand, shrink, acc_e, acc_s, sems = rest[-10:]
     step = pl.program_id(0)
     last = pl.num_programs(0) - 1
-    width, chunk = expand.shape
+    width, chunk = acc_e.shape
     blocks = chunk // unit
 
     @pl.when(step == 0)
     def _():
         pairs = []
-        height = width // 8
-        tall = chunk // 8
-        for source, half, place in weight_places(meta, pieces):
-            source = source if half is None else source.at[half]
-            start = pl.multiple_of(place * height, 16)
+        quarter, tall = expand.shape[1], shrink.shape[1]
+        here = blocks * quarter + number * tall
+        columns = pl.ds(number * unit, unit)
+        for source, who in zip(pieces[:2], (0, 1)):
+            places = pl.ds(4 * (meta[0] ^ who), 4)
             for block in range(blocks):
                 pairs.append(
                     (
-                        source.at[
-                            pl.ds((1 + block) * height, height), pl.ds(number * unit, unit)
-                        ],
-                        expand.at[pl.ds(start, height), pl.ds(block * unit, unit)],
+                        source.at[:, pl.ds(block * quarter, quarter), columns],
+                        expand.at[places, :, pl.ds(block * unit, unit)],
                     )
                 )
-            start = pl.multiple_of(place * tall, 16)
-            first_row = (1 + blocks) * height + number * tall
-            pairs.append((source.at[pl.ds(first_row, tall), :], shrink.at[pl.ds(start, tall), :]))
+            pairs.append((source.at[:, pl.ds(here, tall), :], shrink.at[places]))
+        for fetched, places in zip((pieces[2:6], pieces[6:10]), quarter_places(meta)):
+            for source, place in zip(fetched, places):
+                for block in range(blocks):
+                    pairs.append(
+                        (
+                            source.at[pl.ds(block * quarter, quarter), columns],
+                            expand.at[place, :, pl.ds(block * unit, unit)],
+                        )
+                    )
+                pairs.append((source.at[pl.ds(here, tall), :], shrink.at[place]))
         copies = start_copies(pairs, sems)
         acc_e[...] = jnp.zeros_like(acc_e)
         acc_s[...] = jnp.zeros_like(acc_s)
@@ -582,30 +601,33 @@
 
     rows = normed[...]
     grads = branch[...]
-    total_out = None
-    total_grad = None
-    for block in range(blocks):
-        columns = slice(block * unit, (block + 1) * unit)
-        bias = vectors[
-            EXPAND_BIAS + block : EXPAND_BIAS + block + 1, number * unit : (number + 1) * unit
-        ]
-        hidden = dot(rows, expand[:, columns]) + bias
-        active, slope = gate_both(hidden)
-        active = active.astype(BF16)
-        part = dot(active, shrink[columns, :])
-        total_out = part if total_out is None else total_out + part
-        back = (dot_t(grads, shrink[columns, :]) * slope).astype(BF16)
-        acc_s[columns, :] += dot_rows(active, grads)
-        acc_e[:, columns] += dot_rows(rows, back)
-        bias_grad[:, columns] += jnp.sum(back.astype(F32), axis=0, keepdims=True)
-        part = dot_t(back, expand[:, columns])
-        total_grad = part if total_grad is None else total_grad + part
+    bias = jnp.concatenate(
+        [
+            vectors[
+                EXPAND_BIAS + block : EXPAND_BIAS + block + 1, number * unit : (number + 1) * unit
+            ]
+            for block in range(blocks)
+        ],
+        axis=1,
+    )
+    whole_expand = expand[...].reshape(width, chunk)
+    whole_shrink = shrink[...].reshape(chunk, width)
+    hidden = dot(rows, whole_expand) + bias
+    d_active = dot_t(grads, whole_shrink)
+    active, slope = gate_both(hidden)
+    active = active.astype(BF16)
+    back = (d_active * slope).astype(BF16)
+    bias_grad[...] += jnp.sum(back.astype(F32), axis=0, keepdims=True)
+    acc_s[...] += dot_rows(active, grads)
+    acc_e[...] += dot_rows(rows, back)
+    total_out = dot(active, whole_shrink)
+    total_grad = dot_t(back, whole_expand)
     if first:
-        out_acc[...] = total_out
-        grad_acc[...] = total_grad
+        out_acc[...] = total_out.astype(BF16)
+        grad_acc[...] = total_grad.astype(BF16)
     else:
-        out_acc[...] = out_in[...] + total_out
-        grad_acc[...] = grad_in[...] + total_grad
+        out_acc[...] = (out_in[...].astype(F32) + total_out).astype(BF16)
+        grad_acc[...] = (grad_in[...].astype(F32) + total_grad).astype(BF16)
 
     @pl.when(step == last)
     def _():
@@ -644,36 +666,39 @@
         (meta,),
         ins,
         [
-            (like((rows, width), F32), block),
-            (like((rows, width), F32), block),
+            (like((rows, width), BF16), block),
+            (like((rows, width), BF16), block),
             (like(payload, BF16), whole(*payload)),
             (like(payload, BF16), whole(*payload)),
             (like((1, chunk), F32), whole(1, chunk)),
         ],
         [
-            pltpu.VMEM((width, chunk), BF16),
-            pltpu.VMEM((chunk, width), BF16),
+            pltpu.VMEM((16, width // 16, chunk), BF16),
+            pltpu.VMEM((16, chunk // 16, width), BF16),
             pltpu.VMEM((width, chunk), F32),
             pltpu.VMEM((chunk, width), F32),
-            pltpu.SemaphoreType.DMA((40,)),
+            pltpu.SemaphoreType.DMA((64,)),
         ],
-        (12 * rows * width * chunk, rows * width * 20 + width * chunk * 8, 2 * rows * chunk),
+        (12 * rows * width * chunk, rows * width * 12 + width * chunk * 8, 2 * rows * chunk),
         aliases,
     )
 
 
 def middle_kernel(
-    slabs, meta, windows, middle, out_acc, grad_acc, branch, attended, vectors,
-    p0, p1, p2, p3, p4, p5,
-    result_out, d_middle_out, d_attended_out, keep, send, output_bias_grad, gain_grad,
-    shift_grad, full, staged, weight, acc, sems,
+    slabs, first, meta, windows, middle, out_acc, grad_acc, branch, attended, vectors,
+    *rest,
 ):
+    pieces = rest[:4]
+    (
+        result_out, d_middle_out, d_attended_out, keep, send, output_bias_grad, gain_grad,
+        shift_grad, full, staged, weight, acc, sems,
+    ) = rest[4:]
     step = pl.program_id(0)
     last = pl.num_programs(0) - 1
 
     @pl.when(step == 0)
     def _():
-        copies = load_rows(meta, (p0, p1, p2, p3, p4, p5), weight, sems)
+        copies = load_rows(meta, pieces, weight, sems, first)
         acc[...] = jnp.zeros_like(acc)
         output_bias_grad[...] = jnp.zeros_like(output_bias_grad)
         gain_grad[...] = jnp.zeros_like(gain_grad)
@@ -683,18 +708,18 @@
     width = full.shape[2]
     count = slabs * ROWS
     rows = middle[...]
-    result = rows + out_acc[...] + vectors[SHRINK_BIAS : SHRINK_BIAS + 1]
+    result = rows + out_acc[...].astype(F32) + vectors[SHRINK_BIAS : SHRINK_BIAS + 1]
     full[...] = result.reshape(slabs, ROWS, width)
     scatter_quarters(step == last, full, staged, result_out, step * slabs, slabs)
     unit, scale = normalize(rows)
-    grad = grad_acc[...]
+    grad = grad_acc[...].astype(F32)
     gain_grad[...] += jnp.sum(grad * unit, axis=0, keepdims=True)
     shift_grad[...] += jnp.sum(grad, axis=0, keepdims=True)
     d_middle = branch[...].astype(F32) + normalize_back(
         unit, scale, grad, vectors[SECOND_GAIN : SECOND_GAIN + 1]
     )
-    d_middle_out[...] = d_middle
     d_output = d_middle.astype(BF16)
+    d_middle_out[...] = d_output
     output_bias_grad[...] += jnp.sum(d_output.astype(F32), axis=0, keepdims=True)
     acc[...] += dot_rows(attended[...].reshape(count, width), d_output)
     d_attended = dot_t(d_output, weight[...]).reshape(slabs, ROWS, width)
@@ -704,7 +729,7 @@
 
     @pl.when(step == last)
     def _():
-        write_owned(acc, meta, keep, send)
+        write_owned(acc, meta, keep, send, 1)
 
 
 def middle_back(meta, windows, rows_dev, middle, out_acc, grad_acc, branch, attended, vectors, pieces):
@@ -718,7 +743,7 @@
     payload = (2, width // 4, width)
     quarter = (parts, rows_dev, slots, width)
     return call(
-        functools.partial(middle_kernel, slabs),
+        functools.partial(middle_kernel, slabs, 3 * width),
         "middle",
         slots // slabs,
         (meta, windows),
@@ -729,7 +754,7 @@
         + [(item, ANY) for item in pieces],
         [
             (like(quarter, BF16), whole(*quarter)),
-            (like((rows, width), F32), flat),
+            (like((rows, width), BF16), flat),
             (like((slots, ROWS, width), BF16), block),
             (like(payload, BF16), whole(*payload)),
             (like(payload, BF16), whole(*payload)),
@@ -742,14 +767,14 @@
             pltpu.VMEM((parts * width // LANES, rows_dev * slots, LANES), F32),
             pltpu.VMEM((width, width), BF16),
             pltpu.VMEM((width, width), F32),
-            pltpu.SemaphoreType.DMA((8,)),
+            pltpu.SemaphoreType.DMA((10,)),
         ],
-        (4 * rows * width * width, rows * width * 24, 0),
+        (4 * rows * width * width, rows * width * 18, 0),
     )
 
 
 def attend_back_kernel(
-    slabs, meta, normed, queries_in, keys_in, values_in, probs_in, d_mixed_in, mixed_in,
+    slabs, across, meta, normed, queries_in, keys_in, values_in, probs_in, d_mixed_in, mixed_in,
     height, width_table, places, blocks, selectors, sums,
     d_queries, d_keys, d_values, keep, send, bias_grad, table_out, grads, acc, tables, table_grad,
 ):
@@ -769,8 +794,17 @@
     upper = lane >= HD
     zero = jnp.zeros((ROWS, LANES), BF16)
 
-    def one_slab(slab, carry):
-        queries, keys, values = queries_in[slab], keys_in[slab], values_in[slab]
+    sides = (jnp.logical_not(upper), upper)
+    halves_of = lambda items, head: jnp.where(
+        sides[head & 1], items[:, (head >> 1) * LANES : ((head >> 1) + 1) * LANES], zero
+    )
+    minus = [
+        jnp.where((lane == 2 * head) | (lane == 2 * head + 1), -1.0, 0.0).astype(BF16)
+        for head in range(QUAD)
+    ]
+    every = [(slab, head) for slab in range(slabs) for head in range(QUAD)]
+    lefts = []
+    for slab in range(slabs):
         d_mixed = d_mixed_in[slab]
         product = d_mixed.astype(F32) * mixed_in[slab].astype(F32)
         product_high = product.astype(BF16)
@@ -779,58 +813,59 @@
         inner_high = inner.astype(BF16)
         inner_low = (inner - inner_high.astype(F32)).astype(BF16)
         inner = jnp.where((lane & 1) == 0, inner_high, inner_low)
-        d_relative = None
-        dq, dk, dv = [], [], []
-        for pair in range(QUAD // 2):
-            columns = slice(pair * LANES, (pair + 1) * LANES)
-            left = jnp.concatenate([d_mixed[:, columns], inner], axis=1)
-            dq_pair = dk_pair = dv_pair = None
-            for side in range(2):
-                head = 2 * pair + side
-                mine = upper if side else jnp.logical_not(upper)
-                minus = jnp.where((lane == 2 * head) | (lane == 2 * head + 1), -1.0, 0.0)
-                right = jnp.concatenate(
-                    [jnp.where(mine, values[:, columns], zero), minus.astype(BF16)], axis=1
-                )
-                d_probs = dot_t(left, right)
-                probs = probs_in[slab, head]
-                d_scores = (probs.astype(F32) * d_probs).astype(BF16)
-                back = dot(
-                    d_scores,
-                    jnp.concatenate(
-                        [jnp.where(mine, keys[:, columns], zero), selectors[head]], axis=1
-                    ),
-                )
-                part_k = dot_rows(d_scores, jnp.where(mine, queries[:, columns], zero))
-                part_v = dot_rows(probs, jnp.where(mine, d_mixed[:, columns], zero))
-                if dq_pair is None:
-                    dq_pair, dk_pair, dv_pair = back[:, :LANES], part_k, part_v
-                else:
-                    dq_pair = dq_pair + back[:, :LANES]
-                    dk_pair = dk_pair + part_k
-                    dv_pair = dv_pair + part_v
-                d_relative = back[:, LANES:] if d_relative is None else d_relative + back[:, LANES:]
-            dq.append(dq_pair)
-            dk.append(dk_pair)
-            dv.append(dv_pair)
+        lefts.append(
+            [
+                jnp.concatenate([d_mixed[:, pair * LANES : (pair + 1) * LANES], inner], axis=1)
+                for pair in range(QUAD // 2)
+            ]
+        )
+    d_probs = [
+        dot_t(
+            lefts[slab][head >> 1],
+            jnp.concatenate([halves_of(values_in[slab], head), minus[head]], axis=1),
+        )
+        for slab, head in every
+    ]
+    parts_v = [
+        dot_rows(probs_in[slab, head], halves_of(d_mixed_in[slab], head)) for slab, head in every
+    ]
+    d_scores = [
+        (probs_in[slab, head].astype(F32) * item).astype(BF16)
+        for (slab, head), item in zip(every, d_probs)
+    ]
+    backs = [
+        dot(
+            item,
+            jnp.concatenate([halves_of(keys_in[slab], head), selectors[head]], axis=1),
+        )
+        for (slab, head), item in zip(every, d_scores)
+    ]
+    parts_k = [
+        dot_rows(item, halves_of(queries_in[slab], head))
+        for (slab, head), item in zip(every, d_scores)
+    ]
+    scale = HD**-0.5
+    joined = lambda items: jnp.concatenate(
+        [items[2 * pair] + items[2 * pair + 1] for pair in range(QUAD // 2)], axis=1
+    )
+    for slab in range(slabs):
+        mine = slice(slab * QUAD, (slab + 1) * QUAD)
+        d_relative = backs[slab * QUAD][:, LANES:]
+        for head in range(1, QUAD):
+            d_relative = d_relative + backs[slab * QUAD + head][:, LANES:]
         high = roll_rows(jnp.where(within < WIN, d_relative, 0.0), False)
-        wide = roll_rows(
-            jnp.where((within >= 16) & (within < 16 + WIN), d_relative, 0.0), True
-        )
+        wide = roll_rows(jnp.where((within >= 16) & (within < 16 + WIN), d_relative, 0.0), True)
         d_terms = jnp.concatenate([high, wide], axis=1).astype(BF16)
-        scale = HD**-0.5
-        dq = jnp.concatenate(dq, axis=1) * scale + dot_t(d_terms, tables[...])
-        table_grad[...] += dot_rows(queries, d_terms)
-        dq = dq.astype(BF16)
-        dk = (jnp.concatenate(dk, axis=1) * scale).astype(BF16)
-        dv = jnp.concatenate(dv, axis=1).astype(BF16)
+        dq = joined([item[:, :LANES] for item in backs[mine]]) * scale
+        dq = (dq + dot_t(d_terms, tables[...])).astype(BF16)
+        table_grad[...] += dot_rows(queries_in[slab], d_terms)
+        dk = (joined(parts_k[mine]) * scale).astype(BF16)
+        dv = joined(parts_v[mine]).astype(BF16)
         d_queries[slab] = dq
         d_keys[slab] = dk
         d_values[slab] = dv
         grads[slab] = jnp.concatenate([dq, dk, dv], axis=1)
-        return carry
-
-    lax.fori_loop(0, slabs, one_slab, 0)
+
     width = normed.shape[2]
     both = grads[...].reshape(slabs * ROWS, 3 * wide4)
     bias_grad[...] += jnp.sum(both.astype(F32), axis=0, keepdims=True)
@@ -838,7 +873,7 @@
 
     @pl.when(step == last)
     def _():
-        write_owned(acc, meta, keep, send)
+        write_owned(acc, meta, keep, send, across)
         masked = table_grad[...] * blocks[...].astype(F32)
         folded = masked[:HD]
         for head in range(1, QUAD):
@@ -851,7 +886,7 @@
             )
 
 
-def attend_back(quad, meta, normed, triple, probs, d_mixed, mixed, tables, selectors, sums):
+def attend_back(quad, across, meta, normed, triple, probs, d_mixed, mixed, tables, selectors, sums):
     slots, _, width = normed.shape
     slabs = group(slots)
     wide4 = QUAD * HD
@@ -864,7 +899,7 @@
     rows = slots * ROWS
     payload = (2, width // 4, 3 * wide4)
     return call(
-        functools.partial(attend_back_kernel, slabs),
+        functools.partial(attend_back_kernel, slabs, across),
         "attend_back",
         slots // slabs,
         (meta,),
@@ -902,8 +937,8 @@
 
 
 def first_kernel(slabs, meta, rows_in, d_middle, vectors, *rest):
-    grads, pieces = rest[:9], rest[9:15]
-    tokens_out, gain_grad, shift_grad, full, staged, weight, sems = rest[15:]
+    grads, pieces = rest[:9], rest[9:13]
+    tokens_out, gain_grad, shift_grad, full, staged, weight, sems = rest[13:]
     step = pl.program_id(0)
     last = pl.num_programs(0) - 1
 
@@ -916,18 +951,14 @@
 
     width = full.shape[2]
     count = slabs * ROWS
-    total = None
     wide4 = QUAD * HD
-    for index, grad in enumerate(grads):
-        part = dot_t(
-            grad[...].reshape(count, wide4), weight[:, index * wide4 : (index + 1) * wide4]
-        )
-        total = part if total is None else total + part
+    both = jnp.concatenate([grad[...].reshape(count, wide4) for grad in grads], axis=1)
+    total = dot_t(both, weight[...])
     unit, scale = normalize(rows_in[...].reshape(count, width).astype(F32))
     gain_grad[...] += jnp.sum(total * unit, axis=0, keepdims=True)
     shift_grad[...] += jnp.sum(total, axis=0, keepdims=True)
     back = normalize_back(unit, scale, total, vectors[FIRST_GAIN : FIRST_GAIN + 1])
-    full[...] = (d_middle[...] + back).reshape(slabs, ROWS, width)
+    full[...] = (d_middle[...].astype(F32) + back).reshape(slabs, ROWS, width)
     scatter_quarters(step == last, full, staged, tokens_out, step * slabs, slabs)
 
 
@@ -954,16 +985,13 @@
             pltpu.VMEM((slabs, ROWS, width), F32),
             pltpu.VMEM((parts * width // LANES, rows_dev * steps * slabs, LANES), F32),
             pltpu.VMEM((width, 3 * width), BF16),
-            pltpu.SemaphoreType.DMA((8,)),
+            pltpu.SemaphoreType.DMA((10,)),
         ],
         (6 * rows * width * width, rows * width * 14, 0),
     )
 
 
-def finish_kernel(unit, pairs, meta, *refs):
-    items, small, refs = refs[: 2 * pairs], refs[2 * pairs], refs[2 * pairs + 1 :]
-    (triple_out, output_out, expand_out, shrink_out), refs = refs[:4], refs[4:]
-    vectors, tables, staged = refs[:8], refs[8:10], refs[10:]
+def join_halves(meta, items, staged):
     upper = meta[1] > 0
     for number, both in enumerate(staged):
         mine, other = items[2 * number], items[2 * number + 1]
@@ -979,10 +1007,16 @@
             both[:half] = mine[...]
             both[half:] = other[...]
 
-    shard, width = output_out.shape
+
+def finish_feed_kernel(unit, pairs, meta, *refs):
+    items, (expand_out, shrink_out), staged = (
+        refs[: 2 * pairs], refs[2 * pairs : 2 * pairs + 2], refs[2 * pairs + 2 :]
+    )
+    join_halves(meta, items, staged)
+    shard, width = expand_out.shape[0], shrink_out.shape[1]
     third = shard // 3
     parts = width // shard
-    for number, both in enumerate(staged[:3]):
+    for number, both in enumerate(staged):
         here = number * unit
         shrink_out[here : here + unit, :] = both[:unit, :].astype(F32)
         for block in range(parts - 1):
@@ -995,9 +1029,17 @@
             expand_out[piece * third : (piece + 1) * third, start : start + unit] = both[
                 unit + shard :, piece * unit : (piece + 1) * unit
             ].astype(F32)
-    output_out[...] = staged[3][:shard, :].astype(F32)
+
+
+def finish_rest_kernel(pairs, meta, *refs):
+    items, small, refs = refs[: 2 * pairs], refs[2 * pairs], refs[2 * pairs + 1 :]
+    (triple_out, output_out), refs = refs[:2], refs[2:]
+    vectors, tables, staged = refs[:8], refs[8:10], refs[10:]
+    join_halves(meta, items, staged)
+    shard, width = output_out.shape
+    output_out[...] = staged[0][:shard, :].astype(F32)
     wide4 = QUAD * HD
-    for quad, both in enumerate(staged[3:]):
+    for quad, both in enumerate(staged):
         values = both[shard:, :] if quad == 0 else both[...]
         for part in range(3):
             start = part * width + quad * wide4
@@ -1015,16 +1057,15 @@
             item[9 * piece : 9 * piece + 9, :] = small[TABLES : TABLES + 9, start : start + HD]
 
 
-def finish(meta, shares, small, matrices, vectors, tables, unit):
+def finish(kernel, name, meta, shares, others, outs):
     items = [item for pair in shares for item in pair]
-    outs = [item.shape for item in (*matrices, *vectors, *tables)]
     return call(
-        functools.partial(finish_kernel, unit, len(shares)),
-        "finish",
+        kernel,
+        name,
         1,
         (meta,),
-        [(item, whole(*item.shape)) for item in (*items, small)],
-        [(like(shape, F32), whole(*shape)) for shape in outs],
+        [(item, whole(*item.shape)) for item in (*items, *others)],
+        [(like(item.shape, F32), whole(*item.shape)) for item in outs],
         [pltpu.VMEM((2 * mine.shape[0], mine.shape[1]), BF16) for mine, _ in shares],
         (0, sum(6 * item.size for item in items), 0),
     )
@@ -1035,6 +1076,17 @@
     return lax.ppermute(values, axis, [(n, n ^ bits) for n in range(count)])
 
 
+def swap_diagonal(values):
+    across = lax.axis_size("seq")
+    count = lax.axis_size("dp") * across
+    perm = [(n, (n // across ^ 1) * across + (n % across ^ 1)) for n in range(count)]
+    return lax.ppermute(values, ("dp", "seq"), perm)
+
+
+def spread(far):
+    return far, swap(far, "dp", 1), swap(far, "seq", 1), swap_diagonal(far)
+
+
 def exchange_windows(values):
     return lax.all_to_all(values, "tensor", split_axis=0, concat_axis=0, tiled=True)
 
@@ -1043,10 +1095,9 @@
     return lax.optimization_barrier((values, *others))[0]
 
 
-def far_half(packed):
-    bit = lax.axis_index("dp") & 1
-    mine = lax.dynamic_index_in_dim(packed, bit, axis=0, keepdims=False)
-    return swap(mine, "tensor", 2)
+def far_quarter(packed):
+    which = 2 * (lax.axis_index("dp") & 1) + (lax.axis_index("seq") & 1)
+    return lax.dynamic_index_in_dim(packed, which, axis=0, keepdims=False)
 
 
 def add(*items):
@@ -1064,43 +1115,62 @@
     return out
 
 
-def reduce_stages(payloads):
+def reduce_stages(payloads, plan):
+    bits_of = {"c": 1, "y": 2}
     totals = []
     while True:
         keep, send, more = payloads.pop(0)
-        (far,) = yield [(send, "tensor", 1)]
+        (far,) = yield [(send, "tensor", bits_of[plan[0]])]
         totals.append(add(keep, far))
         if not more:
             break
     total = totals[0] if len(totals) == 1 else jnp.concatenate(totals, axis=1)
     spot = lax.axis_index("dp")
-    for bit in halves("dp"):
-        size = total.shape[1] // 2
-        upper = (spot & bit) > 0
-        far = jnp.where(upper, total[:, :size], total[:, size:])
-        near = jnp.where(upper, total[:, size:], total[:, :size])
-        (far,) = yield [(far, "dp", bit)]
-        total = add(near, far)
-    (far,) = yield [(total[1], "tensor", 2)]
-    total = add(total[0], far)
-    for bit in halves("seq"):
-        (far,) = yield [(total, "seq", bit)]
-        total = add(total, far)
+    place = lax.axis_index("seq")
+
+    def split(values, upper):
+        size = values.shape[-2] // 2
+        low, high = values[..., :size, :], values[..., size:, :]
+        return jnp.where(upper, high, low), jnp.where(upper, low, high)
+
+    def join(mine, far, upper):
+        return jnp.concatenate([jnp.where(upper, far, mine), jnp.where(upper, mine, far)], axis=0)
+
+    for letter in plan[1:]:
+        if letter in bits_of:
+            (far,) = yield [(total[1], "tensor", bits_of[letter])]
+            total = add(total[0], far)
+        elif letter == "x":
+            for bit in halves("dp"):
+                near, far = split(total, (spot & bit) > 0)
+                (far,) = yield [(far, "dp", bit)]
+                total = add(near, far)
+        else:
+            if letter == "s":
+                near, far = split(total, (place & 1) > 0)
+                (far,) = yield [(far, "seq", 1)]
+                total = add(near, far)
+            for bit in halves("seq"):
+                if letter == "s" and bit == 1:
+                    continue
+                (far,) = yield [(total, "seq", bit)]
+                total = add(total, far)
+            if letter == "s":
+                (far,) = yield [(total, "seq", 1)]
+                total = join(total, far, (place & 1) > 0)
     for bit in reversed(halves("dp")):
-        upper = (spot & bit) > 0
         (far,) = yield [(total, "dp", bit)]
         if bit > 1:
-            total = jnp.concatenate(
-                [jnp.where(upper, far, total), jnp.where(upper, total, far)], axis=0
-            )
+            total = join(total, far, (spot & bit) > 0)
     return total, far
 
 
 def sum_stages(values):
-    for axis in ("tensor", "dp", "seq"):
-        for bit in halves(axis):
-            (far,) = yield [(values, axis, bit)]
-            values = values + far
+    steps = [(axis, bit) for axis in ("tensor", "dp", "seq") for bit in halves(axis)]
+    steps = [("tensor", 2)] + [item for item in steps if item != ("tensor", 2)]
+    for axis, bit in steps:
+        (far,) = yield [(values, axis, bit)]
+        values = values + far
     return (values,)
 
 
@@ -1112,13 +1182,14 @@
     def begin(self, name, stages):
         self.running.append([name, stages, None])
 
-    def step(self, token, meta, *extra):
+    def step(self, names, token, meta, *extra):
         asked, ended = [], []
-        arrived = [item for entry in self.running for item in (entry[2] or ())]
+        chosen = [entry for entry in self.running if names is None or entry[0] in names]
+        arrived = [item for entry in chosen for item in (entry[2] or ())]
         if token is not None and arrived:
             token, *arrived = lax.optimization_barrier((token, *arrived))
         arrived = iter(arrived)
-        for entry in list(self.running):
+        for entry in chosen:
             name, stages, waiting = entry
             mine = None if waiting is None else [next(arrived) for _ in waiting]
             try:
@@ -1143,7 +1214,7 @@
 
     def finish(self):
         while self.running:
-            self.step(None, None)
+            self.step(None, None, None)
 
 
 def local(
@@ -1172,7 +1243,10 @@
     chunks = 3
     unit = width // chunks
     bit = lax.axis_index("dp") & 1
-    meta = jnp.where(jnp.arange(2) == 0, mine, bit).astype(jnp.int32)
+    quarter = 2 * bit + (lax.axis_index("seq") & 1)
+    meta = jnp.where(
+        jnp.arange(3) == 0, mine, jnp.where(jnp.arange(3) == 1, bit, quarter)
+    ).astype(jnp.int32)
 
     by_image = lambda values: jnp.swapaxes(values, 2, 3).reshape(parts, rows_dev, slots, width)
     to_image = lambda values: jnp.swapaxes(
@@ -1180,17 +1254,23 @@
     )
     windows = slot_window.reshape(parts, slots)
 
-    packed = triple_weight.reshape(2, shard // 2, -1)
-    far = far_half(packed)
-    rows_in = exchange_windows(by_image(tokens))
-    near = swap(packed, "tensor", 1)
+    far = jnp.concatenate(
+        [
+            far_quarter(triple_weight.reshape(4, shard // 4, -1)),
+            far_quarter(output_weight.reshape(4, shard // 4, -1)),
+        ],
+        axis=1,
+    )
+    far = swap(far, "tensor", 2)
+    near_triple = swap(triple_weight, "tensor", 1)
+    near_output = swap(output_weight, "tensor", 1)
     vectors, packed_rest = prepare(
         chunks,
         (
             first_gain, first_shift, output_bias, second_gain, second_shift, shrink_bias,
             triple_bias, expand_bias,
         ),
-        (output_weight, expand_weight, shrink_weight),
+        (expand_weight, shrink_weight),
     )
     sums = np.zeros((QUAD * HD, LANES), np.float32)
     for head in range(QUAD):
@@ -1198,39 +1278,47 @@
     sums = jnp.asarray(sums, BF16)
     ahead = (height_table, width_table, table_places(False), head_blocks(False))
     behind = (height_table, width_table, table_places(True), head_blocks(True))
-    far, vectors, packed_rest, meta = lax.optimization_barrier((far, vectors, packed_rest, meta))
-    other = swap(far, "dp", 1)
-    triple_pieces = (
-        packed, near, far, other, swap(far, "tensor", 1), swap(other, "tensor", 1),
-    )
-
-    packed = after(packed_rest, rows_in, far)
-    far = far_half(packed)
+    far, vectors, packed_rest, meta, own_tokens = lax.optimization_barrier(
+        (far, vectors, packed_rest, meta, by_image(tokens))
+    )
+    rows_in = exchange_windows(own_tokens)
+    fetched = jnp.stack(spread(far))
+    crossed = swap(fetched, "tensor", 1)
+
+    packed, rows_in, fetched, crossed = lax.optimization_barrier(
+        (packed_rest, rows_in, fetched, crossed)
+    )
+    triple_pieces = (triple_weight, near_triple, fetched, crossed)
+    output_pieces = (output_weight, near_output, fetched, crossed)
+    far = swap(far_quarter(packed), "tensor", 2)
     near = swap(packed, "tensor", 1)
     steps = slots // group(slots)
-    early = max(1, steps // 2)
+    early = max(1, steps // 4)
     selectors = key_selectors(False)
     kept = attend(
         0, early, meta, windows, rows_in, vectors, ahead, selectors, triple_pieces, None
     )
     kept = list(kept)
     kept[4], far, own_grads = lax.optimization_barrier((kept[4], far, by_image(out_grad)))
-    meta, far, own_grads = lax.optimization_barrier((meta, far, own_grads))
-    other = swap(far, "dp", 1)
-    crossed = swap(far, "tensor", 1)
+    meta, far, near, own_grads = lax.optimization_barrier((meta, far, near, own_grads))
     grads_in = exchange_windows(own_grads)
+    fetched = spread(far)
+    crossed = (swap(far, "tensor", 1),)
     if early < steps:
         kept = attend(
             early, steps - early, meta, windows, rows_in, vectors, ahead, selectors,
             triple_pieces, kept,
         )
     full_rows, normed, triple, probs, attended = kept
-    attended, other = lax.optimization_barrier((attended, other))
-    rest_pieces = (packed, near, far, other, crossed, swap(other, "tensor", 1))
-
-    middle, normed2, branch, shrink_bias_grad = project(
-        meta, windows, attended, full_rows, grads_in, vectors, rest_pieces
-    )
+    attended, *others = lax.optimization_barrier((attended, *fetched[1:]))
+    meta, *others = lax.optimization_barrier((meta, *others))
+    crossed += tuple(swap(item, "tensor", 1) for item in others)
+    middle_stage = project(
+        meta, windows, attended, full_rows, grads_in, vectors, output_pieces
+    )
+    shrink_bias_grad = middle_stage[3]
+    rest_pieces = (packed, near, far, *others, *crossed)
+    middle, normed2, branch = middle_stage[:3]
     exchanges = Exchanges()
     kept = None
     expand_bias_grads = []
@@ -1238,33 +1326,35 @@
         *kept, keep, send, bias_grad = feed(
             number, chunks, meta, normed2, branch, vectors, rest_pieces, kept
         )
-        exchanges.begin(("feed", number), reduce_stages([(keep, send, False)]))
-        bias_grad, meta = exchanges.step(bias_grad, meta)
+        plan = ("cyxz", "cyxz", "cxyz")[number]
+        exchanges.begin(("feed", number), reduce_stages([(keep, send, False)], plan))
+        bias_grad, meta = exchanges.step(None, bias_grad, meta)
         expand_bias_grads.append(bias_grad)
 
     result, d_middle, d_attended, keep, send, output_bias_grad, gain2_grad, shift2_grad = (
         middle_back(
-            meta, windows, rows_dev, middle, *kept, branch, attended, vectors, rest_pieces
+            meta, windows, rows_dev, middle, *kept, branch, attended, vectors, output_pieces
         )
     )
     payloads = [(keep, send, True)]
-    exchanges.begin(("rest", 0), reduce_stages(payloads))
-    output_bias_grad, meta = exchanges.step(output_bias_grad, meta)
+    exchanges.begin(("rest", 0), reduce_stages(payloads, "cyxs"))
+    output_bias_grad, meta = exchanges.step(None, output_bias_grad, meta)
     result = exchange_windows(result)
 
     quad_grads, triple_bias_grads, table_grads = [], [], []
     for quad in range(HEADS // QUAD):
         dq, dk, dv, keep, send, bias_grad, table_grad = attend_back(
-            quad, meta, normed, triple, probs, d_attended, attended, behind, key_selectors(True), sums
+            quad, 2 if quad == 2 else 1, meta, normed, triple, probs, d_attended, attended, behind, key_selectors(True), sums
         )
         if quad == 0:
             payloads.append((keep, send, False))
         else:
-            exchanges.begin(("rest", quad), reduce_stages([(keep, send, False)]))
+            plan = "cyxz" if quad == 1 else "ycxz"
+            exchanges.begin(("rest", quad), reduce_stages([(keep, send, False)], plan))
         if quad == 1:
-            bias_grad, meta, result = exchanges.step(bias_grad, meta, result)
+            bias_grad, meta, result = exchanges.step(None, bias_grad, meta, result)
         else:
-            bias_grad, meta = exchanges.step(bias_grad, meta)
+            bias_grad, meta = exchanges.step(None, bias_grad, meta)
         quad_grads.append((dq, dk, dv))
         triple_bias_grads.append(bias_grad)
         table_grads.append(table_grad)
@@ -1273,9 +1363,8 @@
     token_grad, gain1_grad, shift1_grad = first_back(
         0, steps, meta, rows_dev, full_rows, d_middle, vectors, grads9, triple_pieces
     )
-    tokens_gradient = to_image(exchange_windows(token_grad))
     result = to_image(result)
-    gain1_grad, _ = exchanges.step(gain1_grad, None)
+    gain1_grad, _ = exchanges.step(None, gain1_grad, None)
     small = collect(
         (gain1_grad, shift1_grad, output_bias_grad, gain2_grad, shift2_grad, shrink_bias_grad),
         triple_bias_grads,
@@ -1283,22 +1372,30 @@
         table_grads,
     )
     exchanges.begin("small", sum_stages(small))
+    exchanges.step(["small"], None, None)
+    first_far = exchanges.running[-1][2][0]
+    tokens_gradient = to_image(exchange_windows(after(token_grad, first_far)))
     exchanges.finish()
     shares = [exchanges.done["feed", number] for number in range(chunks)]
-    shares += [exchanges.done["rest", number] for number in range(HEADS // QUAD)]
-    (
-        triple_gradient, output_gradient, expand_gradient, shrink_gradient, *outs, high, wide,
-    ) = finish(
+    expand_gradient, shrink_gradient = finish(
+        functools.partial(finish_feed_kernel, unit, chunks),
+        "finish_feed",
         meta,
         shares,
-        exchanges.done["small"][0],
-        (triple_weight, output_weight, expand_weight, shrink_weight),
+        (),
+        (expand_weight, shrink_weight),
+    )
+    shares = [exchanges.done["rest", number] for number in range(HEADS // QUAD)]
+    triple_gradient, output_gradient, *outs, high, wide = finish(
+        functools.partial(finish_rest_kernel, len(shares)),
+        "finish_rest",
+        meta,
+        shares,
+        exchanges.done["small"],
         (
-            first_gain, first_shift, output_bias, second_gain, second_shift, shrink_bias,
-            triple_bias, expand_bias,
+            triple_weight, output_weight, first_gain, first_shift, output_bias, second_gain,
+            second_shift, shrink_bias, triple_bias, expand_bias, height_table, width_table,
         ),
-        (height_table, width_table),
-        unit,
     )
     return (
         result,

time: 467 us -> 404 us (0.87)
  waiting for transfers between devices: 114 us -> 73.1 us
  Pallas kernels: 248 us -> 212 us
  starting transfers between devices: 63.7 us -> 73.8 us
  local copies, waits for them, and re-layouts: 15.9 us -> 22.2 us
    ppermute x52 -> x57, waiting for transfers between devices: 110 us -> 51.6 us  [swap(): return lax.ppermute(values, axis, [(n, n ^ bits) for n in range(count)])]
    pallas_call x14 -> x15, Pallas kernels: 248 us -> 212 us  [call(): pl.pallas_call(kernel, out_shape=tuple((item for item, _ in outs)), grid_...]
    all_to_all x4, waiting for transfers between devices: 4.02 us -> 18.6 us  [exchange_windows(): lax.all_to_all(values, 'tensor', split_axis=0, concat_axis=0, tiled=True)]
    unnamed x58 -> x80, local copies, waits for them, and re-layouts: 11.3 us -> 17.5 us
    ppermute x0 -> x2, starting transfers between devices: none -> 5.45 us  [swap_diagonal(): return lax.ppermute(values, ('dp', 'seq'), perm)]
    ppermute x52 -> x57, starting transfers between devices: 46.5 us -> 51.4 us  [swap(): return lax.ppermute(values, axis, [(n, n ^ bits) for n in range(count)])]
    convert_element_type x28 -> x30, other arithmetic: 14.5 us -> 10.1 us  [add(): return total.astype(BF16)]
  transfers between devices with their start and end apart: 56 -> 63, of which waited for: 13 -> 18; matrix products, arithmetic and copies ran while one was open for 3% -> 3% of each run, Pallas kernels for 45% -> 47%
where the time goes in v3:
time: 404 us; the launch traced here: 398 us
  Pallas kernels  212 us (52%)
  starting transfers between devices  73.8 us (18%)
  waiting for transfers between devices  73.1 us (18%)
  local copies, waits for them, and re-layouts  22.2 us (5%)
  other arithmetic  14.8 us (4%)
    pallas_call x15, Pallas kernels, call(): pl.pallas_call(kernel, out_shape=tuple((item for item, _ in outs)), grid_...  212 us
    ppermute x57, waiting for transfers between devices, swap(): return lax.ppermute(values, axis, [(n, n ^ bits) for n in range(count)])  51.6 us
    ppermute x57, starting transfers between devices, swap(): return lax.ppermute(values, axis, [(n, n ^ bits) for n in range(count)])  51.4 us
    all_to_all x4, waiting for transfers between devices, exchange_windows(): lax.all_to_all(values, 'tensor', split_axis=0, concat_axis=0, tiled=True)  18.6 us
    unnamed x80, local copies, waits for them, and re-layouts  17.5 us
    all_to_all x4, starting transfers between devices, exchange_windows(): lax.all_to_all(values, 'tensor', split_axis=0, concat_axis=0, tiled=True)  16.9 us
    convert_element_type x30, other arithmetic, add(): return total.astype(BF16)  10.1 us
  transfers between devices with their start and end apart: 63, of which 18 were waited for; matrix products, arithmetic and copies ran while one was open for 3% of the time, Pallas kernels for 47%

profile of v3, /device:TPU:0, one launch (start us, length us, event | category | flops | bytes accessed | tf_op | source)
XLA Modules:
  0.0 397.6 jit_solution(3825289967476520280)
XLA Ops:
  16.1 4.5 %all-to-all-start = ((bf16[4,49,8,768]{3,2,1,0:T(8,128)(2,1)}), bf16[4,49,8,768]{3,2,1,0:T(8,128)(2,1)}, u32[]{:S(2)}, u32[]{:S(2)}) async-start(bf16[4,49,8,768]{3,2,1,0:T(8,128)(2,1)} %bitcast.5), calls=%async_computation | async-start | bytes 4816896 | tf_op jit(solution)/shard_map/all_to_all | solution.py:1091
  23.5 4.5 %collective-permute-done.2 = bf16[48,3072]{1,0:T(8,128)(2,1)S(1)} collective-permute-done((bf16[48,3072]{1,0:T(8,128)(2,1)S(1)}, bf16[48,3072]{1,0:T(8,128)(2,1)S(1)}, u32[]{:S(2)}, u32[]{:S(2)}) %collective-permute-start.2) | collective-permute-done | bytes 294944 | tf_op jit(solution)/shard_map/ppermute | solution.py:1076
  31.1 18.6 %all-to-all-done.tokens = bf16[4,49,8,768]{3,2,1,0:T(8,128)(2,1)} async-done(((bf16[4,49,8,768]{3,2,1,0:T(8,128)(2,1)}), bf16[4,49,8,768]{3,2,1,0:T(8,128)(2,1)}, u32[]{:S(2)}, u32[]{:S(2)}) %all-to-all-start) | async-done | bytes 2408480 | tf_op jit(solution)/shard_map/all_to_all | solution.py:1091
  56.0 12.4 %attend.2 = (bf16[8,200,768]{2,1,0:T(8,128)(2,1)}, bf16[8,200,768]{2,1,0:T(8,128)(2,1)}, bf16[8,200,2304]{2,1,0:T(8,128)(2,1)}, bf16[8,12,200,200]{3,2,1,0:T(8,128)(2,1)}, bf16[8,200,768]{2,1,0:T(8,128)(2,1)}) custom-call(s32[3]{0:T(128)} %compare_select_fusion.1.meta, s32[4,8]{1,0:T(4,128)} %bitcast.75, bf16[4,49,8,768]{3,2,1,0:T(8,128)(2,1)} %all-to-all-done.tokens, ...), custom_call_target="tpu_custom_call" | custom-call | flops 2398617600 | bytes 10911744 | tf_op jit(solution)/shard_map/attend/pallas_call | solution.py:239
  69.2 4.1 %all-to-all-start.1 = ((bf16[4,49,8,768]{3,2,1,0:T(8,128)(2,1)}), bf16[4,49,8,768]{3,2,1,0:T(8,128)(2,1)S(1)}, u32[]{:S(2)}, u32[]{:S(2)}) async-start(bf16[4,49,8,768]{3,2,1,0:T(8,128)(2,1)} %bitcast.68), calls=%async_computation.1 | async-start | bytes 4816896 | tf_op jit(solution)/shard_map/all_to_all | solution.py:1091
  77.3 23.3 %attend.3 = (bf16[8,200,768]{2,1,0:T(8,128)(2,1)}, bf16[8,200,768]{2,1,0:T(8,128)(2,1)}, bf16[8,200,2304]{2,1,0:T(8,128)(2,1)}, bf16[8,12,200,200]{3,2,1,0:T(8,128)(2,1)}, bf16[8,200,768]{2,1,0:T(8,128)(2,1)}) custom-call(s32[3]{0:T(128)} %compare_select_fusion.1.meta, ...), custom_call_target="tpu_custom_call", output_to_operand_aliasing={{0}: (13, {}), {1}: (14, {}), {2}: (15, {}), {3}: (16, {}),... | custom-call | flops 7195852800 | bytes 25657344 | tf_op jit(solution)/shard_map/attend/pallas_call | solution.py:239
  107.9 11.9 %project.1 = (f32[1600,768]{1,0:T(8,128)}, bf16[1600,768]{1,0:T(8,128)(2,1)}, bf16[1600,768]{1,0:T(8,128)(2,1)}, f32[1,768]{1,0:T(1,128)}) custom-call(s32[3]{0:T(128)} %compare_select_fusion.1.meta, s32[4,8]{1,0:T(4,128)} %bitcast.77, bf16[8,200,768]{2,1,0:T(8,128)(2,1)} %get-tuple-element.209.attended.mixed_in, ...), custom_call_target="tpu_custom_call" | custom-call | flops 1887436800 | bytes 17203200 | tf_op jit(solution)/shard_map/project/pallas_call | solution.py:239
  119.9 25.2 %feed.3 = (bf16[1600,768]{1,0:T(8,128)(2,1)}, bf16[1600,768]{1,0:T(8,128)(2,1)}, bf16[2,512,768]{2,1,0:T(8,128)(2,1)}, bf16[2,512,768]{2,1,0:T(8,128)(2,1)}, f32[1,1024]{1,0:T(1,128)}) custom-call(s32[3]{0:T(128)} %compare_select_fusion.1.meta, bf16[1600,768]{1,0:T(8,128)(2,1)} %get-tuple-element.212.normed, bf16[1600,768]{1,0:T(8,128)(2,1)} %get-tuple-element.213.branch, ...), custom_call_target="tpu_custom_call" | custom-call | flops 15099494400 | bytes 21037056 | tf_op jit(solution)/shard_map/feed/pallas_call | solution.py:239
  145.6 25.6 %feed.4 = (bf16[1600,768]{1,0:T(8,128)(2,1)}, bf16[1600,768]{1,0:T(8,128)(2,1)}, bf16[2,512,768]{2,1,0:T(8,128)(2,1)}, bf16[2,512,768]{2,1,0:T(8,128)(2,1)}, f32[1,1024]{1,0:T(1,128)}) custom-call(s32[3]{0:T(128)} %compare_select_fusion.1.meta, bf16[1600,768]{1,0:T(8,128)(2,1)} %get-tuple-element.212.normed, ...), custom_call_target="tpu_custom_call", output_to_operand_aliasing={{0}: (14, {}), {1}: (15, {})} | custom-call | flops 15099494400 | bytes 21037056 | tf_op jit(solution)/shard_map/feed/pallas_call | solution.py:239
  174.7 25.7 %feed.5 = (bf16[1600,768]{1,0:T(8,128)(2,1)}, bf16[1600,768]{1,0:T(8,128)(2,1)}, bf16[2,512,768]{2,1,0:T(8,128)(2,1)}, bf16[2,512,768]{2,1,0:T(8,128)(2,1)}, f32[1,1024]{1,0:T(1,128)}) custom-call(s32[3]{0:T(128)} %compare_select_fusion.1.meta, bf16[1600,768]{1,0:T(8,128)(2,1)} %get-tuple-element.212.normed, ...), custom_call_target="tpu_custom_call", output_to_operand_aliasing={{0}: (14, {}), {1}: (15, {})} | custom-call | flops 15099494400 | bytes 21037056 | tf_op jit(solution)/shard_map/feed/pallas_call | solution.py:239
  204.8 18.6 %middle.1 = (bf16[4,49,8,768]{3,2,1,0:T(8,128)(2,1)}, bf16[1600,768]{1,0:T(8,128)(2,1)}, bf16[8,200,768]{2,1,0:T(8,128)(2,1)}, bf16[2,192,768]{2,1,0:T(8,128)(2,...) custom-call(s32[3]{0:T(128)} %compare_select_fusion.1.meta, ...), custom_call_target="tpu_custom_call" | custom-call | flops 3774873600 | bytes 22118400 | tf_op jit(solution)/shard_map/middle/pallas_call | solution.py:239
  229.7 4.7 %all-to-all-start.2 = ((bf16[4,49,8,768]{3,2,1,0:T(8,128)(2,1)}), bf16[4,49,8,768]{3,2,1,0:T(8,128)(2,1)}, u32[]{:S(2)}, u32[]{:S(2)}) async-start(bf16[4,49,8,768]{3,2,1,0:T(8,128)(2,1)} %get-tuple-element.278), calls=%async_computation.2 | async-start | bytes 4816896 | tf_op jit(solution)/shard_map/all_to_all | solution.py:1091
  237.5 13.0 %attend_back.3 = (bf16[8,200,256]{2,1,0:T(8,128)(2,1)}, bf16[8,200,256]{2,1,0:T(8,128)(2,1)}, bf16[8,200,256]{2,1,0:T(8,128)(2,1)}, bf16[2,192,768]{2,1,0:T(8,12...) custom-call(s32[3]{0:T(128)} %compare_select_fusion.1.meta, ...), custom_call_target="tpu_custom_call" | custom-call | flops 4508876800 | bytes 12288000 | tf_op jit(solution)/shard_map/attend_back/pallas_call | solution.py:239
  250.5 6.4 %collective-permute-done.23 = bf16[256,768]{1,0:T(8,128)(2,1)S(1)} collective-permute-done((bf16[256,768]{1,0:T(8,128)(2,1)}, bf16[256,768]{1,0:T(8,128)(2,1)S(1)}, u32[]{:S(2)}, u32[]{:S(2)}) %collective-permute-start.23) | collective-permute-done | bytes 393248 | tf_op jit(solution)/shard_map/ppermute | solution.py:1076
  266.6 13.1 %attend_back.4 = (bf16[8,200,256]{2,1,0:T(8,128)(2,1)}, bf16[8,200,256]{2,1,0:T(8,128)(2,1)}, bf16[8,200,256]{2,1,0:T(8,128)(2,1)}, bf16[2,192,768]{2,1,0:T(8,12...) custom-call(s32[3]{0:T(128)} %compare_select_fusion.1.meta, ...), custom_call_target="tpu_custom_call" | custom-call | flops 4508876800 | bytes 12288000 | tf_op jit(solution)/shard_map/attend_back/pallas_call | solution.py:239
  287.4 12.9 %attend_back.5 = (bf16[8,200,256]{2,1,0:T(8,128)(2,1)}, bf16[8,200,256]{2,1,0:T(8,128)(2,1)}, bf16[8,200,256]{2,1,0:T(8,128)(2,1)}, bf16[2,192,768]{2,1,0:T(8,12...) custom-call(s32[3]{0:T(128)} %compare_select_fusion.1.meta, ...), custom_call_target="tpu_custom_call" | custom-call | flops 4508876800 | bytes 12288000 | tf_op jit(solution)/shard_map/attend_back/pallas_call | solution.py:239
  300.4 3.8 collective-permute-done.31
  311.3 16.8 %first_back.1 = (bf16[4,49,8,768]{3,2,1,0:T(8,128)(2,1)}, f32[1,768]{1,0:T(1,128)}, f32[1,768]{1,0:T(1,128)}) custom-call(s32[3]{0:T(128)} %compare_select_fusion.1.meta, bf16[8,200,768]{2,1,0:T(8,128)(2,1)} %get-tuple-element.210.rows_in, bf16[1600,768]{1,0:T(8,128)(2,1)} %get-tuple-element.295.d_middle, f32[13,768]{1,0:T(8,128)} %get-tuple-element.190.vectors, ...), custom_call_target="tpu_custom_call" | custom-call | flops 5662310400 | bytes 17203200 | tf_op jit(solution)/shard_map/first_back/pallas_call | solution.py:239
  338.7 3.6 all-to-all-start.3
  358.6 4.2 %collective-permute-done.47 = bf16[96,768]{1,0:T(8,128)(2,1)S(1)} collective-permute-done((bf16[96,768]{1,0:T(8,128)(2,1)S(1)}, bf16[96,768]{1,0:T(8,128)(2,1)S(1)}, u32[]{:S(2)}, u32[]{:S(2)}) %collective-permute-start.47) | collective-permute-done | bytes 147488 | tf_op jit(solution)/shard_map/ppermute | solution.py:1076
  369.5 6.1 %collective-permute-done.52 = bf16[96,768]{1,0:T(8,128)(2,1)S(1)} collective-permute-done((bf16[96,768]{1,0:T(8,128)(2,1)S(1)}, bf16[96,768]{1,0:T(8,128)(2,1)S(1)}, u32[]{:S(2)}, u32[]{:S(2)}) %collective-permute-start.52) | collective-permute-done | bytes 147488 | tf_op jit(solution)/shard_map/ppermute | solution.py:1076
  377.0 5.2 %collective-permute-done.57 = f32[24,768]{1,0:T(8,128)S(1)} collective-permute-done((f32[24,768]{1,0:T(8,128)S(1)}, f32[24,768]{1,0:T(8,128)S(1)}, u32[]{:S(2)}, u32[]{:S(2)}) %collective-permute-start.57) | collective-permute-done | bytes 73760 | tf_op jit(solution)/shard_map/ppermute | solution.py:1076
  382.9 4.8 %finish_feed.1 = (f32[192,3072]{1,0:T(8,128)}, f32[768,768]{1,0:T(8,128)}) custom-call(s32[3]{0:T(128)} %compare_select_fusion.1.meta, bf16[256,768]{1,0:T(8,128)(2,1)} %copy-done.5, bf16[256,768]{1,0:T(8,128)(2,1)} %copy-done.26, bf16[256,768]{1,0:T(8,128)(2,1)} %copy-done.6, bf16[256,768]{1,0:T(8,128)(2,1)} %copy-done.27, bf16[256,768]{1,0:T(8,128)(2,1)} %copy-done.7, ...), custom_call_target="tpu_custom_call" | custom-call | bytes 7077888 | tf_op jit(solution)/shard_map/finish_feed/pallas_call | solution.py:239
  389.2 3.5 finish_rest.1
  (253 shorter events, 123.2 us)
Async XLA Ops:
  16.1 33.6 %all-to-all-start = ((bf16[4,49,8,768]{3,2,1,0:T(8,128)(2,1)}), bf16[4,49,8,768]{3,2,1,0:T(8,128)(2,1)}, u32[]{:S(2)}, u32[]{:S(2)}) async-start(bf16[4,49,8,768]{3,2,1,0:T(8,128)(2,1)} %bitcast.5), calls=%async_computation | async-start | bytes 4816896 | tf_op jit(solution)/shard_map/all_to_all | solution.py:1091
  69.2 37.2 %all-to-all-start.1 = ((bf16[4,49,8,768]{3,2,1,0:T(8,128)(2,1)}), bf16[4,49,8,768]{3,2,1,0:T(8,128)(2,1)S(1)}, u32[]{:S(2)}, u32[]{:S(2)}) async-start(bf16[4,49,8,768]{3,2,1,0:T(8,128)(2,1)} %bitcast.68), calls=%async_computation.1 | async-start | bytes 4816896 | tf_op jit(solution)/shard_map/all_to_all | solution.py:1091
  73.3 46.6 %collective-permute-start.12 = (bf16[384,768]{1,0:T(8,128)(2,1)S(1)}, bf16[384,768]{1,0:T(8,128)(2,1)}, u32[]{:S(2)}, u32[]{:S(2)}) collective-permute-start(bf16[384,768]{1,0:T(8,128)(2,1)S(1)} %copy-done.38), channel_id=1, source_target_pairs={{0,1},{1,0},{2,3},{3,2},{4,5},{5,4},{6,7},{7,6},{8,9},{9,8},{10,11... | collective-permute-start | bytes 1769480 | tf_op jit(solution)/shard_map/ppermute | solution.py:1076
  73.8 26.8 %collective-permute-start.10 = (bf16[384,768]{1,0:T(8,128)(2,1)S(1)}, bf16[384,768]{1,0:T(8,128)(2,1)}, u32[]{:S(2)}, u32[]{:S(2)}) collective-permute-start(bf16[384,768]{1,0:T(8,128)(2,1)S(1)} %copy-done.38), channel_id=1, source_target_pairs={{0,20},{4,16},{8,28},{12,24},{16,4},{20,0},{24,12},{28,8},{1,21},{... | collective-permute-start | bytes 1769480 | tf_op jit(solution)/shard_map/ppermute | solution.py:1083
  76.6 26.5 %collective-permute-start.9 = (bf16[384,768]{1,0:T(8,128)(2,1)S(1)}, bf16[384,768]{1,0:T(8,128)(2,1)}, u32[]{:S(2)}, u32[]{:S(2)}) collective-permute-start(bf16[384,768]{1,0:T(8,128)(2,1)S(1)} %copy-done.38), channel_id=1, source_target_pairs={{0,4},{4,0},{8,12},{12,8},{1,5},{5,1},{9,13},{13,9},{2,6},{6,2},{1... | collective-permute-start | bytes 1769480 | tf_op jit(solution)/shard_map/ppermute | solution.py:1076
  77.0 26.1 %collective-permute-start.8 = (bf16[384,768]{1,0:T(8,128)(2,1)S(1)}, bf16[384,768]{1,0:T(8,128)(2,1)}, u32[]{:S(2)}, u32[]{:S(2)}) collective-permute-start(bf16[384,768]{1,0:T(8,128)(2,1)S(1)} %copy-done.38), channel_id=1, source_target_pairs={{0,16},{16,0},{1,17},{17,1},{2,18},{18,2},{3,19},{19,3},{4,20},{20... | collective-permute-start | bytes 1769480 | tf_op jit(solution)/shard_map/ppermute | solution.py:1076
  145.2 26.0 %collective-permute-start.16 = (bf16[2,512,768]{2,1,0:T(8,128)(2,1)}, bf16[2,512,768]{2,1,0:T(8,128)(2,1)S(1)}, u32[]{:S(2)}, u32[]{:S(2)}) collective-permute-start(bf16[2,512,768]{2,1,0:T(8,128)(2,1)} %get-tuple-element.224), channel_id=1, source_target_pairs={{0,1},{1,0},{2,3},{3,2},{4,5},{5,4},{6,7},{7,6},{8,9},{9,8},{10,11... | collective-permute-start | bytes 4718600 | tf_op jit(solution)/shard_map/ppermute | solution.py:1076
  172.6 27.8 %collective-permute-start.18 = (bf16[2,512,768]{2,1,0:T(8,128)(2,1)}, bf16[2,512,768]{2,1,0:T(8,128)(2,1)S(1)}, u32[]{:S(2)}, u32[]{:S(2)}) collective-permute-start(bf16[2,512,768]{2,1,0:T(8,128)(2,1)} %get-tuple-element.232), channel_id=1, source_target_pairs={{0,1},{1,0},{2,3},{3,2},{4,5},{5,4},{6,7},{7,6},{8,9},{9,8},{10,11... | collective-permute-start | bytes 4718600 | tf_op jit(solution)/shard_map/ppermute | solution.py:1076
  172.7 27.6 %collective-permute-start.17 = (bf16[512,768]{1,0:T(8,128)(2,1)}, bf16[512,768]{1,0:T(8,128)(2,1)S(1)}, u32[]{:S(2)}, u32[]{:S(2)}) collective-permute-start(bf16[512,768]{1,0:T(8,128)(2,1)} %slice_bitcast_fusion.3), channel_id=1, source_target_pairs={{0,2},{1,3},{2,0},{3,1},{4,6},{5,7},{6,4},{7,5},{8,10},{9,11},{10,... | collective-permute-start | bytes 2359304 | tf_op jit(solution)/shard_map/ppermute | solution.py:1076
  203.0 20.4 %collective-permute-start.21 = (bf16[2,512,768]{2,1,0:T(8,128)(2,1)}, bf16[2,512,768]{2,1,0:T(8,128)(2,1)S(1)}, u32[]{:S(2)}, u32[]{:S(2)}) collective-permute-start(bf16[2,512,768]{2,1,0:T(8,128)(2,1)} %get-tuple-element.244), channel_id=1, source_target_pairs={{0,1},{1,0},{2,3},{3,2},{4,5},{5,4},{6,7},{7,6},{8,9},{9,8},{10,11... | collective-permute-start | bytes 4718600 | tf_op jit(solution)/shard_map/ppermute | solution.py:1076
  203.1 20.3 %collective-permute-start.20 = (bf16[512,768]{1,0:T(8,128)(2,1)S(1)}, bf16[512,768]{1,0:T(8,128)(2,1)S(1)}, u32[]{:S(2)}, u32[]{:S(2)}) collective-permute-start(bf16[512,768]{1,0:T(8,128)(2,1)S(1)} %slice_bitcast_fusion.1), channel_id=1, source_target_pairs={{0,2},{1,3},{2,0},{3,1},{4,6},{5,7},{6,4},{7,5},{8,10},{9,11},{10,... | collective-permute-start | bytes 2359304 | tf_op jit(solution)/shard_map/ppermute | solution.py:1076
  229.0 27.8 %collective-permute-start.24 = (bf16[2,256,768]{2,1,0:T(8,128)(2,1)S(1)}, bf16[2,256,768]{2,1,0:T(8,128)(2,1)}, u32[]{:S(2)}, u32[]{:S(2)}) collective-permute-start(bf16[2,256,768]{2,1,0:T(8,128)(2,1)S(1)} %broadcast_select_fusion), channel_id=1, source_target_pairs={{0,16},{16,0},{1,17},{17,1},{2,18},{18,2},{3,19},{19,3},{4,20},{20... | collective-permute-start | bytes 2359304 | tf_op jit(solution)/shard_map/ppermute | solution.py:1076
  229.7 27.2 %collective-permute-start.25 = (bf16[2,192,768]{2,1,0:T(8,128)(2,1)}, bf16[2,192,768]{2,1,0:T(8,128)(2,1)}, u32[]{:S(2)}, u32[]{:S(2)}) collective-permute-start(bf16[2,192,768]{2,1,0:T(8,128)(2,1)} %get-tuple-element.259), channel_id=1, source_target_pairs={{0,1},{1,0},{2,3},{3,2},{4,5},{5,4},{6,7},{7,6},{8,9},{9,8},{10,11... | collective-permute-start | bytes 1769480 | tf_op jit(solution)/shard_map/ppermute | solution.py:1076
  229.7 52.1 %all-to-all-start.2 = ((bf16[4,49,8,768]{3,2,1,0:T(8,128)(2,1)}), bf16[4,49,8,768]{3,2,1,0:T(8,128)(2,1)}, u32[]{:S(2)}, u32[]{:S(2)}) async-start(bf16[4,49,8,768]{3,2,1,0:T(8,128)(2,1)} %get-tuple-element.278), calls=%async_computation.2 | async-start | bytes 4816896 | tf_op jit(solution)/shard_map/all_to_all | solution.py:1091
  236.1 20.8 %collective-permute-start.23 = (bf16[256,768]{1,0:T(8,128)(2,1)}, bf16[256,768]{1,0:T(8,128)(2,1)S(1)}, u32[]{:S(2)}, u32[]{:S(2)}) collective-permute-start(bf16[256,768]{1,0:T(8,128)(2,1)} %broadcast_select_fusion.1), channel_id=1, source_target_pairs={{0,16},{16,0},{1,17},{17,1},{2,18},{18,2},{3,19},{19,3},{4,20},{20... | collective-permute-start | bytes 1179656 | tf_op jit(solution)/shard_map/ppermute | solution.py:1076
  281.8 22.4 %collective-permute-start.33 = (bf16[384,768]{1,0:T(8,128)(2,1)S(1)}, bf16[384,768]{1,0:T(8,128)(2,1)S(1)}, u32[]{:S(2)}, u32[]{:S(2)}) collective-permute-start(bf16[384,768]{1,0:T(8,128)(2,1)S(1)} %fusion.5), channel_id=1, source_target_pairs={{0,2},{1,3},{2,0},{3,1},{4,6},{5,7},{6,4},{7,5},{8,10},{9,11},{10,... | collective-permute-start | bytes 1769480 | tf_op jit(solution)/shard_map/ppermute | solution.py:1076
  283.1 21.1 %collective-permute-start.34 = (bf16[2,192,768]{2,1,0:T(8,128)(2,1)}, bf16[2,192,768]{2,1,0:T(8,128)(2,1)S(1)}, u32[]{:S(2)}, u32[]{:S(2)}) collective-permute-start(bf16[2,192,768]{2,1,0:T(8,128)(2,1)} %get-tuple-element.286), channel_id=1, source_target_pairs={{0,1},{1,0},{2,3},{3,2},{4,5},{5,4},{6,7},{7,6},{8,9},{9,8},{10,11... | collective-permute-start | bytes 1769480 | tf_op jit(solution)/shard_map/ppermute | solution.py:1076
  283.6 20.6 %collective-permute-start.31 = (bf16[256,768]{1,0:T(8,128)(2,1)S(1)}, bf16[256,768]{1,0:T(8,128)(2,1)S(1)}, u32[]{:S(2)}, u32[]{:S(2)}) collective-permute-start(bf16[256,768]{1,0:T(8,128)(2,1)S(1)} %add_convert_fusion.11), channel_id=1, source_target_pairs={{0,8},{4,12},{8,0},{12,4},{1,9},{5,13},{9,1},{13,5},{2,10},{6,14},... | collective-permute-start | bytes 1179656 | tf_op jit(solution)/shard_map/ppermute | solution.py:1076
  305.7 22.8 %collective-permute-start.39 = (bf16[2,192,768]{2,1,0:T(8,128)(2,1)}, bf16[2,192,768]{2,1,0:T(8,128)(2,1)S(1)}, u32[]{:S(2)}, u32[]{:S(2)}) collective-permute-start(bf16[2,192,768]{2,1,0:T(8,128)(2,1)} %get-tuple-element.311), channel_id=1, source_target_pairs={{0,2},{1,3},{2,0},{3,1},{4,6},{5,7},{6,4},{7,5},{8,10},{9,11},{10,... | collective-permute-start | bytes 1769480 | tf_op jit(solution)/shard_map/ppermute | solution.py:1076
  306.6 21.5 %collective-permute-start.37 = (bf16[192,768]{1,0:T(8,128)(2,1)S(1)}, bf16[192,768]{1,0:T(8,128)(2,1)S(1)}, u32[]{:S(2)}, u32[]{:S(2)}) collective-permute-start(bf16[192,768]{1,0:T(8,128)(2,1)S(1)} %broadcast_select_fusion.3), channel_id=1, source_target_pairs={{0,16},{16,0},{1,17},{17,1},{2,18},{18,2},{3,19},{19,3},{4,20},{20... | collective-permute-start | bytes 884744 | tf_op jit(solution)/shard_map/ppermute | solution.py:1076
  337.4 45.4 %collective-permute-start.58 = (bf16[256,768]{1,0:T(8,128)(2,1)S(1)}, bf16[256,768]{1,0:T(8,128)(2,1)}, u32[]{:S(2)}, u32[]{:S(2)}) collective-permute-start(bf16[256,768]{1,0:T(8,128)(2,1)S(1)} %add_convert_fusion.8.refs_4_), channel_id=1, source_target_pairs={{0,16},{16,0},{1,17},{17,1},{2,18},{18,2},{3,19},{19,3},{4,20},{20... | collective-permute-start | bytes 1179656 | tf_op jit(solution)/shard_map/ppermute | solution.py:1076
  338.7 54.0 %all-to-all-start.3 = ((bf16[4,49,8,768]{3,2,1,0:T(8,128)(2,1)}), bf16[4,49,8,768]{3,2,1,0:T(8,128)(2,1)S(1)}, u32[]{:S(2)}, u32[]{:S(2)}) async-start(bf16[4,49,8,768]{3,2,1,0:T(8,128)(2,1)} %get-tuple-element.327), calls=%async_computation.3 | async-start | bytes 4816896 | tf_op jit(solution)/shard_map/all_to_all | solution.py:1091
  350.1 26.8 %collective-permute-start.56 = (f32[24,768]{1,0:T(8,128)S(1)}, f32[24,768]{1,0:T(8,128)S(1)}, u32[]{:S(2)}, u32[]{:S(2)}) collective-permute-start(f32[24,768]{1,0:T(8,128)S(1)} %add.156), channel_id=1, source_target_pairs={{0,4},{4,0},{8,12},{12,8},{1,5},{5,1},{9,13},{13,9},{2,6},{6,2},{1... | collective-permute-start | bytes 221192 | tf_op jit(solution)/shard_map/ppermute | solution.py:1076
  362.8 25.0 %collective-permute-start.48 = (bf16[96,768]{1,0:T(8,128)(2,1)S(1)}, bf16[96,768]{1,0:T(8,128)(2,1)S(1)}, u32[]{:S(2)}, u32[]{:S(2)}) collective-permute-start(bf16[96,768]{1,0:T(8,128)(2,1)S(1)} %add_convert_fusion.20.refs_2_), channel_id=1, source_target_pairs={{0,16},{16,0},{1,17},{17,1},{2,18},{18,2},{3,19},{19,3},{4,20},{20... | collective-permute-start | bytes 442376 | tf_op jit(solution)/shard_map/ppermute | solution.py:1076
  (78 other events, 790.5 us)

commit v4 on v3

--- a/solution.py
+++ b/solution.py
@@ -1115,7 +1115,7 @@
     return out
 
 
-def reduce_stages(payloads, plan):
+def reduce_stages(payloads, plan, hook=None):
     bits_of = {"c": 1, "y": 2}
     totals = []
     while True:
@@ -1137,7 +1137,9 @@
         return jnp.concatenate([jnp.where(upper, far, mine), jnp.where(upper, mine, far)], axis=0)
 
     for letter in plan[1:]:
-        if letter in bits_of:
+        if letter == "w":
+            total = hook(total)
+        elif letter in bits_of:
             (far,) = yield [(total[1], "tensor", bits_of[letter])]
             total = add(total[0], far)
         elif letter == "x":
@@ -1212,9 +1214,9 @@
             self.done[name] = tuple(next(finished) for _ in pair)
         return (token, meta, *extra)
 
-    def finish(self):
-        while self.running:
-            self.step(None, None, None)
+    def finish(self, names):
+        while any(entry[0] in names for entry in self.running):
+            self.step(names, None, None)
 
 
 def local(
@@ -1278,19 +1280,25 @@
     sums = jnp.asarray(sums, BF16)
     ahead = (height_table, width_table, table_places(False), head_blocks(False))
     behind = (height_table, width_table, table_places(True), head_blocks(True))
-    far, vectors, packed_rest, meta, own_tokens = lax.optimization_barrier(
-        (far, vectors, packed_rest, meta, by_image(tokens))
+    first_rest = far_quarter(packed_rest)
+    far, vectors, packed_rest, first_rest, meta, own_tokens, near_triple, near_output = (
+        lax.optimization_barrier(
+            (
+                far, vectors, packed_rest, first_rest, meta, by_image(tokens), near_triple,
+                near_output,
+            )
+        )
     )
     rows_in = exchange_windows(own_tokens)
     fetched = jnp.stack(spread(far))
     crossed = swap(fetched, "tensor", 1)
 
-    packed, rows_in, fetched, crossed = lax.optimization_barrier(
-        (packed_rest, rows_in, fetched, crossed)
+    packed, first_rest, rows_in, fetched, crossed = lax.optimization_barrier(
+        (packed_rest, first_rest, rows_in, fetched, crossed)
     )
     triple_pieces = (triple_weight, near_triple, fetched, crossed)
     output_pieces = (output_weight, near_output, fetched, crossed)
-    far = swap(far_quarter(packed), "tensor", 2)
+    far = swap(first_rest, "tensor", 2)
     near = swap(packed, "tensor", 1)
     steps = slots // group(slots)
     early = max(1, steps // 4)
@@ -1349,8 +1357,9 @@
         if quad == 0:
             payloads.append((keep, send, False))
         else:
-            plan = "cyxz" if quad == 1 else "ycxz"
-            exchanges.begin(("rest", quad), reduce_stages([(keep, send, False)], plan))
+            plan = "cyxz" if quad == 1 else "ycxzw"
+            hook = lambda total: after(total, *feed_gradients)
+            exchanges.begin(("rest", quad), reduce_stages([(keep, send, False)], plan, hook))
         if quad == 1:
             bias_grad, meta, result = exchanges.step(None, bias_grad, meta, result)
         else:
@@ -1375,9 +1384,10 @@
     exchanges.step(["small"], None, None)
     first_far = exchanges.running[-1][2][0]
     tokens_gradient = to_image(exchange_windows(after(token_grad, first_far)))
-    exchanges.finish()
-    shares = [exchanges.done["feed", number] for number in range(chunks)]
-    expand_gradient, shrink_gradient = finish(
+    names = [("feed", number) for number in range(chunks)]
+    exchanges.finish(names)
+    shares = [exchanges.done[name] for name in names]
+    feed_gradients = finish(
         functools.partial(finish_feed_kernel, unit, chunks),
         "finish_feed",
         meta,
@@ -1385,6 +1395,8 @@
         (),
         (expand_weight, shrink_weight),
     )
+    expand_gradient, shrink_gradient = feed_gradients
+    exchanges.finish([("rest", number) for number in range(HEADS // QUAD)] + ["small"])
     shares = [exchanges.done["rest", number] for number in range(HEADS // QUAD)]
     triple_gradient, output_gradient, *outs, high, wide = finish(
         functools.partial(finish_rest_kernel, len(shares)),

time: 404 us -> 399 us (0.988)
  waiting for transfers between devices: 73.1 us -> 60.3 us
  starting transfers between devices: 73.8 us -> 81 us
    ppermute x57, waiting for transfers between devices: 51.6 us -> 39.5 us  [swap(): return lax.ppermute(values, axis, [(n, n ^ bits) for n in range(count)])]
    ppermute x57, starting transfers between devices: 51.4 us -> 58.7 us  [swap(): return lax.ppermute(values, axis, [(n, n ^ bits) for n in range(count)])]
    unnamed x80 -> x78, local copies, waits for them, and re-layouts: 17.5 us -> 15.7 us
  transfers between devices with their start and end apart: 63 -> 63, of which waited for: 18 -> 14; matrix products, arithmetic and copies ran while one was open for 3% -> 4% of each run, Pallas kernels for 47% -> 47%
where the time goes in v4:
time: 399 us; the launch traced here: 392 us
  Pallas kernels  212 us (53%)
  starting transfers between devices  81 us (20%)
  waiting for transfers between devices  60.3 us (15%)
  local copies, waits for them, and re-layouts  21.2 us (5%)
  other arithmetic  15.9 us (4%)
    pallas_call x15, Pallas kernels, call(): pl.pallas_call(kernel, out_shape=tuple((item for item, _ in outs)), grid_...  212 us
    ppermute x57, starting transfers between devices, swap(): return lax.ppermute(values, axis, [(n, n ^ bits) for n in range(count)])  58.7 us
    ppermute x57, waiting for transfers between devices, swap(): return lax.ppermute(values, axis, [(n, n ^ bits) for n in range(count)])  39.5 us
    all_to_all x4, waiting for transfers between devices, exchange_windows(): lax.all_to_all(values, 'tensor', split_axis=0, concat_axis=0, tiled=True)  17.9 us
    all_to_all x4, starting transfers between devices, exchange_windows(): lax.all_to_all(values, 'tensor', split_axis=0, concat_axis=0, tiled=True)  16.8 us
    unnamed x78, local copies, waits for them, and re-layouts  15.7 us
    convert_element_type x30, other arithmetic, add(): return total.astype(BF16)  11.3 us
  transfers between devices with their start and end apart: 63, of which 14 were waited for; matrix products, arithmetic and copies ran while one was open for 4% of the time, Pallas kernels for 47%

profile of v4, /device:TPU:0, one launch (start us, length us, event | category | flops | bytes accessed | tf_op | source)
XLA Modules:
  0.0 391.9 jit_solution(5675990708410238524)
XLA Ops:
  16.9 4.5 %all-to-all-start = ((bf16[4,49,8,768]{3,2,1,0:T(8,128)(2,1)}), bf16[4,49,8,768]{3,2,1,0:T(8,128)(2,1)}, u32[]{:S(2)}, u32[]{:S(2)}) async-start(bf16[4,49,8,768]{3,2,1,0:T(8,128)(2,1)} %bitcast.6), calls=%async_computation | async-start | bytes 4816896 | tf_op jit(solution)/shard_map/all_to_all | solution.py:1091
  24.2 5.3 %collective-permute-done.4 = bf16[48,3072]{1,0:T(8,128)(2,1)S(1)} collective-permute-done((bf16[48,3072]{1,0:T(8,128)(2,1)S(1)}, bf16[48,3072]{1,0:T(8,128)(2,1)S(1)}, u32[]{:S(2)}, u32[]{:S(2)}) %collective-permute-start.4) | collective-permute-done | bytes 294944 | tf_op jit(solution)/shard_map/ppermute | solution.py:1076
  32.6 17.9 %all-to-all-done.tokens = bf16[4,49,8,768]{3,2,1,0:T(8,128)(2,1)} async-done(((bf16[4,49,8,768]{3,2,1,0:T(8,128)(2,1)}), bf16[4,49,8,768]{3,2,1,0:T(8,128)(2,1)}, u32[]{:S(2)}, u32[]{:S(2)}) %all-to-all-start) | async-done | bytes 2408480 | tf_op jit(solution)/shard_map/all_to_all | solution.py:1091
  50.8 12.4 %attend.2 = (bf16[8,200,768]{2,1,0:T(8,128)(2,1)}, bf16[8,200,768]{2,1,0:T(8,128)(2,1)}, bf16[8,200,2304]{2,1,0:T(8,128)(2,1)}, bf16[8,12,200,200]{3,2,1,0:T(8,128)(2,1)}, bf16[8,200,768]{2,1,0:T(8,128)(2,1)}) custom-call(s32[3]{0:T(128)} %compare_select_fusion.1.meta, s32[4,8]{1,0:T(4,128)} %bitcast.75, bf16[4,49,8,768]{3,2,1,0:T(8,128)(2,1)} %all-to-all-done.tokens, ...), custom_call_target="tpu_custom_call" | custom-call | flops 2398617600 | bytes 10911744 | tf_op jit(solution)/shard_map/attend/pallas_call | solution.py:239
  66.2 3.9 %all-to-all-start.1 = ((bf16[4,49,8,768]{3,2,1,0:T(8,128)(2,1)}), bf16[4,49,8,768]{3,2,1,0:T(8,128)(2,1)S(1)}, u32[]{:S(2)}, u32[]{:S(2)}) async-start(bf16[4,49,8,768]{3,2,1,0:T(8,128)(2,1)} %bitcast.68), calls=%async_computation.1 | async-start | bytes 4816896 | tf_op jit(solution)/shard_map/all_to_all | solution.py:1091
  74.2 23.2 %attend.3 = (bf16[8,200,768]{2,1,0:T(8,128)(2,1)}, bf16[8,200,768]{2,1,0:T(8,128)(2,1)}, bf16[8,200,2304]{2,1,0:T(8,128)(2,1)}, bf16[8,12,200,200]{3,2,1,0:T(8,128)(2,1)}, bf16[8,200,768]{2,1,0:T(8,128)(2,1)}) custom-call(s32[3]{0:T(128)} %compare_select_fusion.1.meta, ...), custom_call_target="tpu_custom_call", output_to_operand_aliasing={{0}: (13, {}), {1}: (14, {}), {2}: (15, {}), {3}: (16, {}),... | custom-call | flops 7195852800 | bytes 25657344 | tf_op jit(solution)/shard_map/attend/pallas_call | solution.py:239
  101.9 11.9 %project.1 = (f32[1600,768]{1,0:T(8,128)}, bf16[1600,768]{1,0:T(8,128)(2,1)}, bf16[1600,768]{1,0:T(8,128)(2,1)}, f32[1,768]{1,0:T(1,128)}) custom-call(s32[3]{0:T(128)} %compare_select_fusion.1.meta, s32[4,8]{1,0:T(4,128)} %bitcast.77, bf16[8,200,768]{2,1,0:T(8,128)(2,1)} %get-tuple-element.217.attended.mixed_in, ...), custom_call_target="tpu_custom_call" | custom-call | flops 1887436800 | bytes 17203200 | tf_op jit(solution)/shard_map/project/pallas_call | solution.py:239
  113.8 25.2 %feed.3 = (bf16[1600,768]{1,0:T(8,128)(2,1)}, bf16[1600,768]{1,0:T(8,128)(2,1)}, bf16[2,512,768]{2,1,0:T(8,128)(2,1)}, bf16[2,512,768]{2,1,0:T(8,128)(2,1)}, f32[1,1024]{1,0:T(1,128)}) custom-call(s32[3]{0:T(128)} %compare_select_fusion.1.meta, bf16[1600,768]{1,0:T(8,128)(2,1)} %get-tuple-element.221.normed, bf16[1600,768]{1,0:T(8,128)(2,1)} %get-tuple-element.222.branch, ...), custom_call_target="tpu_custom_call" | custom-call | flops 15099494400 | bytes 21037056 | tf_op jit(solution)/shard_map/feed/pallas_call | solution.py:239
  139.7 25.6 %feed.4 = (bf16[1600,768]{1,0:T(8,128)(2,1)}, bf16[1600,768]{1,0:T(8,128)(2,1)}, bf16[2,512,768]{2,1,0:T(8,128)(2,1)}, bf16[2,512,768]{2,1,0:T(8,128)(2,1)}, f32[1,1024]{1,0:T(1,128)}) custom-call(s32[3]{0:T(128)} %compare_select_fusion.1.meta, bf16[1600,768]{1,0:T(8,128)(2,1)} %get-tuple-element.221.normed, ...), custom_call_target="tpu_custom_call", output_to_operand_aliasing={{0}: (14, {}), {1}: (15, {})} | custom-call | flops 15099494400 | bytes 21037056 | tf_op jit(solution)/shard_map/feed/pallas_call | solution.py:239
  168.7 25.7 %feed.5 = (bf16[1600,768]{1,0:T(8,128)(2,1)}, bf16[1600,768]{1,0:T(8,128)(2,1)}, bf16[2,512,768]{2,1,0:T(8,128)(2,1)}, bf16[2,512,768]{2,1,0:T(8,128)(2,1)}, f32[1,1024]{1,0:T(1,128)}) custom-call(s32[3]{0:T(128)} %compare_select_fusion.1.meta, bf16[1600,768]{1,0:T(8,128)(2,1)} %get-tuple-element.221.normed, ...), custom_call_target="tpu_custom_call", output_to_operand_aliasing={{0}: (14, {}), {1}: (15, {})} | custom-call | flops 15099494400 | bytes 21037056 | tf_op jit(solution)/shard_map/feed/pallas_call | solution.py:239
  198.9 18.6 %middle.1 = (bf16[4,49,8,768]{3,2,1,0:T(8,128)(2,1)}, bf16[1600,768]{1,0:T(8,128)(2,1)}, bf16[8,200,768]{2,1,0:T(8,128)(2,1)}, bf16[2,192,768]{2,1,0:T(8,128)(2,...) custom-call(s32[3]{0:T(128)} %compare_select_fusion.1.meta, ...), custom_call_target="tpu_custom_call" | custom-call | flops 3774873600 | bytes 22118400 | tf_op jit(solution)/shard_map/middle/pallas_call | solution.py:239
  223.8 4.7 %all-to-all-start.2 = ((bf16[4,49,8,768]{3,2,1,0:T(8,128)(2,1)}), bf16[4,49,8,768]{3,2,1,0:T(8,128)(2,1)}, u32[]{:S(2)}, u32[]{:S(2)}) async-start(bf16[4,49,8,768]{3,2,1,0:T(8,128)(2,1)} %get-tuple-element.287), calls=%async_computation.2 | async-start | bytes 4816896 | tf_op jit(solution)/shard_map/all_to_all | solution.py:1091
  231.6 13.0 %attend_back.3 = (bf16[8,200,256]{2,1,0:T(8,128)(2,1)}, bf16[8,200,256]{2,1,0:T(8,128)(2,1)}, bf16[8,200,256]{2,1,0:T(8,128)(2,1)}, bf16[2,192,768]{2,1,0:T(8,12...) custom-call(s32[3]{0:T(128)} %compare_select_fusion.1.meta, ...), custom_call_target="tpu_custom_call" | custom-call | flops 4508876800 | bytes 12288000 | tf_op jit(solution)/shard_map/attend_back/pallas_call | solution.py:239
  244.6 6.2 %collective-permute-done.23 = bf16[256,768]{1,0:T(8,128)(2,1)S(1)} collective-permute-done((bf16[256,768]{1,0:T(8,128)(2,1)}, bf16[256,768]{1,0:T(8,128)(2,1)S(1)}, u32[]{:S(2)}, u32[]{:S(2)}) %collective-permute-start.23) | collective-permute-done | bytes 393248 | tf_op jit(solution)/shard_map/ppermute | solution.py:1076
  260.6 13.1 %attend_back.4 = (bf16[8,200,256]{2,1,0:T(8,128)(2,1)}, bf16[8,200,256]{2,1,0:T(8,128)(2,1)}, bf16[8,200,256]{2,1,0:T(8,128)(2,1)}, bf16[2,192,768]{2,1,0:T(8,12...) custom-call(s32[3]{0:T(128)} %compare_select_fusion.1.meta, ...), custom_call_target="tpu_custom_call" | custom-call | flops 4508876800 | bytes 12288000 | tf_op jit(solution)/shard_map/attend_back/pallas_call | solution.py:239
  282.5 12.9 %attend_back.5 = (bf16[8,200,256]{2,1,0:T(8,128)(2,1)}, bf16[8,200,256]{2,1,0:T(8,128)(2,1)}, bf16[8,200,256]{2,1,0:T(8,128)(2,1)}, bf16[2,192,768]{2,1,0:T(8,12...) custom-call(s32[3]{0:T(128)} %compare_select_fusion.1.meta, ...), custom_call_target="tpu_custom_call" | custom-call | flops 4508876800 | bytes 12288000 | tf_op jit(solution)/shard_map/attend_back/pallas_call | solution.py:239
  295.4 3.9 collective-permute-done.31
  307.0 16.8 %first_back.1 = (bf16[4,49,8,768]{3,2,1,0:T(8,128)(2,1)}, f32[1,768]{1,0:T(1,128)}, f32[1,768]{1,0:T(1,128)}) custom-call(s32[3]{0:T(128)} %compare_select_fusion.1.meta, bf16[8,200,768]{2,1,0:T(8,128)(2,1)} %get-tuple-element.218.rows_in, bf16[1600,768]{1,0:T(8,128)(2,1)} %get-tuple-element.304.d_middle, f32[13,768]{1,0:T(8,128)} %get-tuple-element.196.vectors, ...), custom_call_target="tpu_custom_call" | custom-call | flops 5662310400 | bytes 17203200 | tf_op jit(solution)/shard_map/first_back/pallas_call | solution.py:239
  334.4 3.6 all-to-all-start.3
  352.2 4.8 %finish_feed.1 = (f32[192,3072]{1,0:T(8,128)}, f32[768,768]{1,0:T(8,128)}) custom-call(s32[3]{0:T(128)} %compare_select_fusion.1.meta, bf16[256,768]{1,0:T(8,128)(2,1)} %copy-done.5, bf16[256,768]{1,0:T(8,128)(2,1)} %copy-done.24, bf16[256,768]{1,0:T(8,128)(2,1)} %copy-done.6, bf16[256,768]{1,0:T(8,128)(2,1)} %copy-done.25, bf16[256,768]{1,0:T(8,128)(2,1)} %copy-done.7, ...), custom_call_target="tpu_custom_call" | custom-call | bytes 7077888 | tf_op jit(solution)/shard_map/finish_feed/pallas_call | solution.py:239
  359.3 4.2 %collective-permute-start.48 = (bf16[96,768]{1,0:T(8,128)(2,1)S(1)}, bf16[96,768]{1,0:T(8,128)(2,1)S(1)}, u32[]{:S(2)}, u32[]{:S(2)}) collective-permute-start(bf16[96,768]{1,0:T(8,128)(2,1)S(1)} %add_convert_fusion.20.refs_2_), channel_id=1, source_target_pairs={{0,16},{16,0},{1,17},{17,1},{2,18},{18,2},{3,19},{19,3},{4,20},{20... | collective-permute-start | bytes 442376 | tf_op jit(solution)/shard_map/ppermute | solution.py:1076
  367.3 4.5 %collective-permute-done.52 = bf16[96,768]{1,0:T(8,128)(2,1)S(1)} collective-permute-done((bf16[96,768]{1,0:T(8,128)(2,1)S(1)}, bf16[96,768]{1,0:T(8,128)(2,1)S(1)}, u32[]{:S(2)}, u32[]{:S(2)}) %collective-permute-start.52) | collective-permute-done | bytes 147488 | tf_op jit(solution)/shard_map/ppermute | solution.py:1076
  371.9 3.8 collective-permute-start.54
  375.8 5.6 %collective-permute-done.58 = f32[24,768]{1,0:T(8,128)S(1)} collective-permute-done((f32[24,768]{1,0:T(8,128)S(1)}, f32[24,768]{1,0:T(8,128)S(1)}, u32[]{:S(2)}, u32[]{:S(2)}) %collective-permute-start.58) | collective-permute-done | bytes 73760 | tf_op jit(solution)/shard_map/ppermute | solution.py:1076
  (251 shorter events, 118.7 us)
Async XLA Ops:
  16.9 33.6 %all-to-all-start = ((bf16[4,49,8,768]{3,2,1,0:T(8,128)(2,1)}), bf16[4,49,8,768]{3,2,1,0:T(8,128)(2,1)}, u32[]{:S(2)}, u32[]{:S(2)}) async-start(bf16[4,49,8,768]{3,2,1,0:T(8,128)(2,1)} %bitcast.6), calls=%async_computation | async-start | bytes 4816896 | tf_op jit(solution)/shard_map/all_to_all | solution.py:1091
  66.2 34.2 %all-to-all-start.1 = ((bf16[4,49,8,768]{3,2,1,0:T(8,128)(2,1)}), bf16[4,49,8,768]{3,2,1,0:T(8,128)(2,1)S(1)}, u32[]{:S(2)}, u32[]{:S(2)}) async-start(bf16[4,49,8,768]{3,2,1,0:T(8,128)(2,1)} %bitcast.68), calls=%async_computation.1 | async-start | bytes 4816896 | tf_op jit(solution)/shard_map/all_to_all | solution.py:1091
  70.2 43.6 %collective-permute-start.12 = (bf16[384,768]{1,0:T(8,128)(2,1)S(1)}, bf16[384,768]{1,0:T(8,128)(2,1)}, u32[]{:S(2)}, u32[]{:S(2)}) collective-permute-start(bf16[384,768]{1,0:T(8,128)(2,1)S(1)} %collective-permute-done.7.rest_2_), channel_id=1, source_target_pairs={{0,1},{1,0},{2,3},{3,2},{4,5},{5,4},{6,7},{7,6},{8,9},{9,8},{10,11... | collective-permute-start | bytes 1769480 | tf_op jit(solution)/shard_map/ppermute | solution.py:1076
  70.7 26.7 %collective-permute-start.11 = (bf16[384,768]{1,0:T(8,128)(2,1)S(1)}, bf16[384,768]{1,0:T(8,128)(2,1)}, u32[]{:S(2)}, u32[]{:S(2)}) collective-permute-start(bf16[384,768]{1,0:T(8,128)(2,1)S(1)} %collective-permute-done.7.rest_2_), channel_id=1, source_target_pairs={{0,20},{4,16},{8,28},{12,24},{16,4},{20,0},{24,12},{28,8},{1,21},{... | collective-permute-start | bytes 1769480 | tf_op jit(solution)/shard_map/ppermute | solution.py:1083
  73.4 26.5 %collective-permute-start.10 = (bf16[384,768]{1,0:T(8,128)(2,1)S(1)}, bf16[384,768]{1,0:T(8,128)(2,1)}, u32[]{:S(2)}, u32[]{:S(2)}) collective-permute-start(bf16[384,768]{1,0:T(8,128)(2,1)S(1)} %collective-permute-done.7.rest_2_), channel_id=1, source_target_pairs={{0,4},{4,0},{8,12},{12,8},{1,5},{5,1},{9,13},{13,9},{2,6},{6,2},{1... | collective-permute-start | bytes 1769480 | tf_op jit(solution)/shard_map/ppermute | solution.py:1076
  73.9 26.1 %collective-permute-start.9 = (bf16[384,768]{1,0:T(8,128)(2,1)S(1)}, bf16[384,768]{1,0:T(8,128)(2,1)}, u32[]{:S(2)}, u32[]{:S(2)}) collective-permute-start(bf16[384,768]{1,0:T(8,128)(2,1)S(1)} %collective-permute-done.7.rest_2_), channel_id=1, source_target_pairs={{0,16},{16,0},{1,17},{17,1},{2,18},{18,2},{3,19},{19,3},{4,20},{20... | collective-permute-start | bytes 1769480 | tf_op jit(solution)/shard_map/ppermute | solution.py:1076
  139.1 26.2 %collective-permute-start.16 = (bf16[2,512,768]{2,1,0:T(8,128)(2,1)}, bf16[2,512,768]{2,1,0:T(8,128)(2,1)S(1)}, u32[]{:S(2)}, u32[]{:S(2)}) collective-permute-start(bf16[2,512,768]{2,1,0:T(8,128)(2,1)} %get-tuple-element.233), channel_id=1, source_target_pairs={{0,1},{1,0},{2,3},{3,2},{4,5},{5,4},{6,7},{7,6},{8,9},{9,8},{10,11... | collective-permute-start | bytes 4718600 | tf_op jit(solution)/shard_map/ppermute | solution.py:1076
  166.7 27.7 %collective-permute-start.18 = (bf16[2,512,768]{2,1,0:T(8,128)(2,1)}, bf16[2,512,768]{2,1,0:T(8,128)(2,1)S(1)}, u32[]{:S(2)}, u32[]{:S(2)}) collective-permute-start(bf16[2,512,768]{2,1,0:T(8,128)(2,1)} %get-tuple-element.241), channel_id=1, source_target_pairs={{0,1},{1,0},{2,3},{3,2},{4,5},{5,4},{6,7},{7,6},{8,9},{9,8},{10,11... | collective-permute-start | bytes 4718600 | tf_op jit(solution)/shard_map/ppermute | solution.py:1076
  166.7 27.6 %collective-permute-start.17 = (bf16[512,768]{1,0:T(8,128)(2,1)}, bf16[512,768]{1,0:T(8,128)(2,1)S(1)}, u32[]{:S(2)}, u32[]{:S(2)}) collective-permute-start(bf16[512,768]{1,0:T(8,128)(2,1)} %slice_bitcast_fusion.3), channel_id=1, source_target_pairs={{0,2},{1,3},{2,0},{3,1},{4,6},{5,7},{6,4},{7,5},{8,10},{9,11},{10,... | collective-permute-start | bytes 2359304 | tf_op jit(solution)/shard_map/ppermute | solution.py:1076
  197.0 20.5 %collective-permute-start.21 = (bf16[2,512,768]{2,1,0:T(8,128)(2,1)}, bf16[2,512,768]{2,1,0:T(8,128)(2,1)S(1)}, u32[]{:S(2)}, u32[]{:S(2)}) collective-permute-start(bf16[2,512,768]{2,1,0:T(8,128)(2,1)} %get-tuple-element.253), channel_id=1, source_target_pairs={{0,1},{1,0},{2,3},{3,2},{4,5},{5,4},{6,7},{7,6},{8,9},{9,8},{10,11... | collective-permute-start | bytes 4718600 | tf_op jit(solution)/shard_map/ppermute | solution.py:1076
  197.2 20.3 %collective-permute-start.20 = (bf16[512,768]{1,0:T(8,128)(2,1)S(1)}, bf16[512,768]{1,0:T(8,128)(2,1)S(1)}, u32[]{:S(2)}, u32[]{:S(2)}) collective-permute-start(bf16[512,768]{1,0:T(8,128)(2,1)S(1)} %slice_bitcast_fusion.1), channel_id=1, source_target_pairs={{0,2},{1,3},{2,0},{3,1},{4,6},{5,7},{6,4},{7,5},{8,10},{9,11},{10,... | collective-permute-start | bytes 2359304 | tf_op jit(solution)/shard_map/ppermute | solution.py:1076
  223.1 27.7 %collective-permute-start.24 = (bf16[2,256,768]{2,1,0:T(8,128)(2,1)S(1)}, bf16[2,256,768]{2,1,0:T(8,128)(2,1)}, u32[]{:S(2)}, u32[]{:S(2)}) collective-permute-start(bf16[2,256,768]{2,1,0:T(8,128)(2,1)S(1)} %broadcast_select_fusion), channel_id=1, source_target_pairs={{0,16},{16,0},{1,17},{17,1},{2,18},{18,2},{3,19},{19,3},{4,20},{20... | collective-permute-start | bytes 2359304 | tf_op jit(solution)/shard_map/ppermute | solution.py:1076
  223.8 27.0 %collective-permute-start.25 = (bf16[2,192,768]{2,1,0:T(8,128)(2,1)}, bf16[2,192,768]{2,1,0:T(8,128)(2,1)}, u32[]{:S(2)}, u32[]{:S(2)}) collective-permute-start(bf16[2,192,768]{2,1,0:T(8,128)(2,1)} %get-tuple-element.268), channel_id=1, source_target_pairs={{0,1},{1,0},{2,3},{3,2},{4,5},{5,4},{6,7},{7,6},{8,9},{9,8},{10,11... | collective-permute-start | bytes 1769480 | tf_op jit(solution)/shard_map/ppermute | solution.py:1076
  223.8 53.1 %all-to-all-start.2 = ((bf16[4,49,8,768]{3,2,1,0:T(8,128)(2,1)}), bf16[4,49,8,768]{3,2,1,0:T(8,128)(2,1)}, u32[]{:S(2)}, u32[]{:S(2)}) async-start(bf16[4,49,8,768]{3,2,1,0:T(8,128)(2,1)} %get-tuple-element.287), calls=%async_computation.2 | async-start | bytes 4816896 | tf_op jit(solution)/shard_map/all_to_all | solution.py:1091
  230.2 20.6 %collective-permute-start.23 = (bf16[256,768]{1,0:T(8,128)(2,1)}, bf16[256,768]{1,0:T(8,128)(2,1)S(1)}, u32[]{:S(2)}, u32[]{:S(2)}) collective-permute-start(bf16[256,768]{1,0:T(8,128)(2,1)} %broadcast_select_fusion.1), channel_id=1, source_target_pairs={{0,16},{16,0},{1,17},{17,1},{2,18},{18,2},{3,19},{19,3},{4,20},{20... | collective-permute-start | bytes 1179656 | tf_op jit(solution)/shard_map/ppermute | solution.py:1076
  253.4 20.3 %collective-permute-start.26 = (bf16[256,768]{1,0:T(8,128)(2,1)S(1)}, bf16[256,768]{1,0:T(8,128)(2,1)S(1)}, u32[]{:S(2)}, u32[]{:S(2)}) collective-permute-start(bf16[256,768]{1,0:T(8,128)(2,1)S(1)} %get-tuple-element.275), channel_id=1, source_target_pairs={{0,8},{4,12},{8,0},{12,4},{1,9},{5,13},{9,1},{13,5},{2,10},{6,14},... | collective-permute-start | bytes 1179656 | tf_op jit(solution)/shard_map/ppermute | solution.py:1076
  276.9 22.4 %collective-permute-start.33 = (bf16[384,768]{1,0:T(8,128)(2,1)S(1)}, bf16[384,768]{1,0:T(8,128)(2,1)S(1)}, u32[]{:S(2)}, u32[]{:S(2)}) collective-permute-start(bf16[384,768]{1,0:T(8,128)(2,1)S(1)} %fusion.5), channel_id=1, source_target_pairs={{0,2},{1,3},{2,0},{3,1},{4,6},{5,7},{6,4},{7,5},{8,10},{9,11},{10,... | collective-permute-start | bytes 1769480 | tf_op jit(solution)/shard_map/ppermute | solution.py:1076
  278.1 21.2 %collective-permute-start.34 = (bf16[2,192,768]{2,1,0:T(8,128)(2,1)}, bf16[2,192,768]{2,1,0:T(8,128)(2,1)S(1)}, u32[]{:S(2)}, u32[]{:S(2)}) collective-permute-start(bf16[2,192,768]{2,1,0:T(8,128)(2,1)} %get-tuple-element.295), channel_id=1, source_target_pairs={{0,1},{1,0},{2,3},{3,2},{4,5},{5,4},{6,7},{7,6},{8,9},{9,8},{10,11... | collective-permute-start | bytes 1769480 | tf_op jit(solution)/shard_map/ppermute | solution.py:1076
  278.7 20.6 %collective-permute-start.31 = (bf16[256,768]{1,0:T(8,128)(2,1)S(1)}, bf16[256,768]{1,0:T(8,128)(2,1)S(1)}, u32[]{:S(2)}, u32[]{:S(2)}) collective-permute-start(bf16[256,768]{1,0:T(8,128)(2,1)S(1)} %add_convert_fusion.11), channel_id=1, source_target_pairs={{0,8},{4,12},{8,0},{12,4},{1,9},{5,13},{9,1},{13,5},{2,10},{6,14},... | collective-permute-start | bytes 1179656 | tf_op jit(solution)/shard_map/ppermute | solution.py:1076
  301.5 22.7 %collective-permute-start.39 = (bf16[2,192,768]{2,1,0:T(8,128)(2,1)}, bf16[2,192,768]{2,1,0:T(8,128)(2,1)S(1)}, u32[]{:S(2)}, u32[]{:S(2)}) collective-permute-start(bf16[2,192,768]{2,1,0:T(8,128)(2,1)} %get-tuple-element.320), channel_id=1, source_target_pairs={{0,2},{1,3},{2,0},{3,1},{4,6},{5,7},{6,4},{7,5},{8,10},{9,11},{10,... | collective-permute-start | bytes 1769480 | tf_op jit(solution)/shard_map/ppermute | solution.py:1076
  302.4 21.4 %collective-permute-start.37 = (bf16[192,768]{1,0:T(8,128)(2,1)S(1)}, bf16[192,768]{1,0:T(8,128)(2,1)S(1)}, u32[]{:S(2)}, u32[]{:S(2)}) collective-permute-start(bf16[192,768]{1,0:T(8,128)(2,1)S(1)} %broadcast_select_fusion.3), channel_id=1, source_target_pairs={{0,16},{16,0},{1,17},{17,1},{2,18},{18,2},{3,19},{19,3},{4,20},{20... | collective-permute-start | bytes 884744 | tf_op jit(solution)/shard_map/ppermute | solution.py:1076
  334.4 52.6 %all-to-all-start.3 = ((bf16[4,49,8,768]{3,2,1,0:T(8,128)(2,1)}), bf16[4,49,8,768]{3,2,1,0:T(8,128)(2,1)S(1)}, u32[]{:S(2)}, u32[]{:S(2)}) async-start(bf16[4,49,8,768]{3,2,1,0:T(8,128)(2,1)} %get-tuple-element.336), calls=%async_computation.3 | async-start | bytes 4816896 | tf_op jit(solution)/shard_map/all_to_all | solution.py:1091
  345.7 30.0 %collective-permute-start.57 = (f32[24,768]{1,0:T(8,128)S(1)}, f32[24,768]{1,0:T(8,128)S(1)}, u32[]{:S(2)}, u32[]{:S(2)}) collective-permute-start(f32[24,768]{1,0:T(8,128)S(1)} %add.157), channel_id=1, source_target_pairs={{0,4},{4,0},{8,12},{12,8},{1,5},{5,1},{9,13},{13,9},{2,6},{6,2},{1... | collective-permute-start | bytes 221192 | tf_op jit(solution)/shard_map/ppermute | solution.py:1076
  359.3 22.8 %collective-permute-start.48 = (bf16[96,768]{1,0:T(8,128)(2,1)S(1)}, bf16[96,768]{1,0:T(8,128)(2,1)S(1)}, u32[]{:S(2)}, u32[]{:S(2)}) collective-permute-start(bf16[96,768]{1,0:T(8,128)(2,1)S(1)} %add_convert_fusion.20.refs_2_), channel_id=1, source_target_pairs={{0,16},{16,0},{1,17},{17,1},{2,18},{18,2},{3,19},{19,3},{4,20},{20... | collective-permute-start | bytes 442376 | tf_op jit(solution)/shard_map/ppermute | solution.py:1076
  (77 other events, 730.7 us)

commit v5 on v4

--- a/solution.py
+++ b/solution.py
@@ -1009,10 +1009,11 @@
 
 
 def finish_feed_kernel(unit, pairs, meta, *refs):
-    items, (expand_out, shrink_out), staged = (
-        refs[: 2 * pairs], refs[2 * pairs : 2 * pairs + 2], refs[2 * pairs + 2 :]
+    items, (expand_out, shrink_out, output_out), staged = (
+        refs[: 2 * pairs], refs[2 * pairs : 2 * pairs + 3], refs[2 * pairs + 3 :]
     )
     join_halves(meta, items, staged)
+    output_out[...] = staged[-1][2 * unit :, :].astype(F32)
     shard, width = expand_out.shape[0], shrink_out.shape[1]
     third = shard // 3
     parts = width // shard
@@ -1027,20 +1028,19 @@
         start = (parts - 1) * width + here
         for piece in range(3):
             expand_out[piece * third : (piece + 1) * third, start : start + unit] = both[
-                unit + shard :, piece * unit : (piece + 1) * unit
+                unit + shard : 2 * unit, piece * unit : (piece + 1) * unit
             ].astype(F32)
 
 
 def finish_rest_kernel(pairs, meta, *refs):
     items, small, refs = refs[: 2 * pairs], refs[2 * pairs], refs[2 * pairs + 1 :]
-    (triple_out, output_out), refs = refs[:2], refs[2:]
+    triple_out, refs = refs[0], refs[1:]
     vectors, tables, staged = refs[:8], refs[8:10], refs[10:]
     join_halves(meta, items, staged)
-    shard, width = output_out.shape
-    output_out[...] = staged[0][:shard, :].astype(F32)
+    shard, width = triple_out.shape[0], small.shape[1]
     wide4 = QUAD * HD
-    for quad, both in enumerate(staged):
-        values = both[shard:, :] if quad == 0 else both[...]
+    quads = [both[n : n + shard, :] for both in staged for n in range(0, both.shape[0], shard)]
+    for quad, values in enumerate(quads):
         for part in range(3):
             start = part * width + quad * wide4
             triple_out[:, start : start + wide4] = values[
@@ -1334,8 +1334,9 @@
         *kept, keep, send, bias_grad = feed(
             number, chunks, meta, normed2, branch, vectors, rest_pieces, kept
         )
-        plan = ("cyxz", "cyxz", "cxyz")[number]
-        exchanges.begin(("feed", number), reduce_stages([(keep, send, False)], plan))
+        plan = ("cyxz", "cyxz", "cxys")[number]
+        payloads = [(keep, send, number == chunks - 1)]
+        exchanges.begin(("feed", number), reduce_stages(payloads, plan))
         bias_grad, meta = exchanges.step(None, bias_grad, meta)
         expand_bias_grads.append(bias_grad)
 
@@ -1344,22 +1345,23 @@
             meta, windows, rows_dev, middle, *kept, branch, attended, vectors, output_pieces
         )
     )
-    payloads = [(keep, send, True)]
-    exchanges.begin(("rest", 0), reduce_stages(payloads, "cyxs"))
+    payloads.append((keep, send, False))
     output_bias_grad, meta = exchanges.step(None, output_bias_grad, meta)
     result = exchange_windows(result)
 
     quad_grads, triple_bias_grads, table_grads = [], [], []
     for quad in range(HEADS // QUAD):
         dq, dk, dv, keep, send, bias_grad, table_grad = attend_back(
-            quad, 2 if quad == 2 else 1, meta, normed, triple, probs, d_attended, attended, behind, key_selectors(True), sums
+            quad, 1, meta, normed, triple, probs, d_attended, attended, behind, key_selectors(True), sums
         )
         if quad == 0:
+            payloads = [(keep, send, True)]
+            exchanges.begin(("rest", 0), reduce_stages(payloads, "cyxs"))
+        elif quad == 1:
             payloads.append((keep, send, False))
         else:
-            plan = "cyxz" if quad == 1 else "ycxzw"
             hook = lambda total: after(total, *feed_gradients)
-            exchanges.begin(("rest", quad), reduce_stages([(keep, send, False)], plan, hook))
+            exchanges.begin(("rest", 1), reduce_stages([(keep, send, False)], "cyxz", hook))
         if quad == 1:
             bias_grad, meta, result = exchanges.step(None, bias_grad, meta, result)
         else:
@@ -1393,20 +1395,20 @@
         meta,
         shares,
         (),
-        (expand_weight, shrink_weight),
-    )
-    expand_gradient, shrink_gradient = feed_gradients
-    exchanges.finish([("rest", number) for number in range(HEADS // QUAD)] + ["small"])
-    shares = [exchanges.done["rest", number] for number in range(HEADS // QUAD)]
-    triple_gradient, output_gradient, *outs, high, wide = finish(
+        (expand_weight, shrink_weight, output_weight),
+    )
+    expand_gradient, shrink_gradient, output_gradient = feed_gradients
+    exchanges.finish([("rest", number) for number in range(2)] + ["small"])
+    shares = [exchanges.done["rest", number] for number in range(2)]
+    triple_gradient, *outs, high, wide = finish(
         functools.partial(finish_rest_kernel, len(shares)),
         "finish_rest",
         meta,
         shares,
         exchanges.done["small"],
         (
-            triple_weight, output_weight, first_gain, first_shift, output_bias, second_gain,
-            second_shift, shrink_bias, triple_bias, expand_bias, height_table, width_table,
+            triple_weight, first_gain, first_shift, output_bias, second_gain, second_shift,
+            shrink_bias, triple_bias, expand_bias, height_table, width_table,
         ),
     )
     return (

time: 399 us -> 392 us (0.982)
  starting transfers between devices: 81 us -> 68.5 us
  waiting for transfers between devices: 60.3 us -> 69.1 us
    ppermute x57 -> x53, starting transfers between devices: 58.7 us -> 45.6 us  [swap(): return lax.ppermute(values, axis, [(n, n ^ bits) for n in range(count)])]
    ppermute x57 -> x53, waiting for transfers between devices: 39.5 us -> 45.3 us  [swap(): return lax.ppermute(values, axis, [(n, n ^ bits) for n in range(count)])]
    unnamed x78 -> x68, local copies, waits for them, and re-layouts: 15.7 us -> 12.8 us
    convert_element_type x30 -> x26, other arithmetic: 11.3 us -> 12.8 us  [add(): return total.astype(BF16)]
  transfers between devices with their start and end apart: 63 -> 59, of which waited for: 14 -> 18; matrix products, arithmetic and copies ran while one was open for 4% -> 4% of each run, Pallas kernels for 47% -> 48%
where the time goes in v5:
time: 392 us; the launch traced here: 386 us
  Pallas kernels  211 us (54%)
  waiting for transfers between devices  69.1 us (18%)
  starting transfers between devices  68.5 us (17%)
  local copies, waits for them, and re-layouts  18.4 us (5%)
  other arithmetic  17.2 us (4%)
    pallas_call x15, Pallas kernels, call(): pl.pallas_call(kernel, out_shape=tuple((item for item, _ in outs)), grid_...  211 us
    ppermute x53, starting transfers between devices, swap(): return lax.ppermute(values, axis, [(n, n ^ bits) for n in range(count)])  45.6 us
    ppermute x53, waiting for transfers between devices, swap(): return lax.ppermute(values, axis, [(n, n ^ bits) for n in range(count)])  45.3 us
    all_to_all x4, waiting for transfers between devices, exchange_windows(): lax.all_to_all(values, 'tensor', split_axis=0, concat_axis=0, tiled=True)  21 us
    all_to_all x4, starting transfers between devices, exchange_windows(): lax.all_to_all(values, 'tensor', split_axis=0, concat_axis=0, tiled=True)  17.4 us
    unnamed x68, local copies, waits for them, and re-layouts  12.8 us
    convert_element_type x26, other arithmetic, add(): return total.astype(BF16)  12.8 us
  transfers between devices with their start and end apart: 59, of which 18 were waited for; matrix products, arithmetic and copies ran while one was open for 4% of the time, Pallas kernels for 48%

profile of v5, /device:TPU:0, one launch (start us, length us, event | category | flops | bytes accessed | tf_op | source)
XLA Modules:
  0.0 385.9 jit_solution(12118214120058693829)
XLA Ops:
  5.8 3.3 prepare.1
  16.9 4.5 %all-to-all-start = ((bf16[4,49,8,768]{3,2,1,0:T(8,128)(2,1)}), bf16[4,49,8,768]{3,2,1,0:T(8,128)(2,1)}, u32[]{:S(2)}, u32[]{:S(2)}) async-start(bf16[4,49,8,768]{3,2,1,0:T(8,128)(2,1)} %bitcast.6), calls=%async_computation | async-start | bytes 4816896 | tf_op jit(solution)/shard_map/all_to_all | solution.py:1091
  24.2 5.3 %collective-permute-done.4 = bf16[48,3072]{1,0:T(8,128)(2,1)S(1)} collective-permute-done((bf16[48,3072]{1,0:T(8,128)(2,1)S(1)}, bf16[48,3072]{1,0:T(8,128)(2,1)S(1)}, u32[]{:S(2)}, u32[]{:S(2)}) %collective-permute-start.4) | collective-permute-done | bytes 294944 | tf_op jit(solution)/shard_map/ppermute | solution.py:1076
  32.6 17.9 %all-to-all-done.tokens = bf16[4,49,8,768]{3,2,1,0:T(8,128)(2,1)} async-done(((bf16[4,49,8,768]{3,2,1,0:T(8,128)(2,1)}), bf16[4,49,8,768]{3,2,1,0:T(8,128)(2,1)}, u32[]{:S(2)}, u32[]{:S(2)}) %all-to-all-start) | async-done | bytes 2408480 | tf_op jit(solution)/shard_map/all_to_all | solution.py:1091
  50.9 12.3 %attend.2 = (bf16[8,200,768]{2,1,0:T(8,128)(2,1)}, bf16[8,200,768]{2,1,0:T(8,128)(2,1)}, bf16[8,200,2304]{2,1,0:T(8,128)(2,1)}, bf16[8,12,200,200]{3,2,1,0:T(8,128)(2,1)}, bf16[8,200,768]{2,1,0:T(8,128)(2,1)}) custom-call(s32[3]{0:T(128)} %compare_select_fusion.1.meta, s32[4,8]{1,0:T(4,128)} %bitcast.68, bf16[4,49,8,768]{3,2,1,0:T(8,128)(2,1)} %all-to-all-done.tokens, ...), custom_call_target="tpu_custom_call" | custom-call | flops 2398617600 | bytes 10911744 | tf_op jit(solution)/shard_map/attend/pallas_call | solution.py:239
  66.2 4.2 %all-to-all-start.1 = ((bf16[4,49,8,768]{3,2,1,0:T(8,128)(2,1)}), bf16[4,49,8,768]{3,2,1,0:T(8,128)(2,1)S(1)}, u32[]{:S(2)}, u32[]{:S(2)}) async-start(bf16[4,49,8,768]{3,2,1,0:T(8,128)(2,1)} %bitcast.61), calls=%async_computation.1 | async-start | bytes 4816896 | tf_op jit(solution)/shard_map/all_to_all | solution.py:1091
  74.4 23.2 %attend.3 = (bf16[8,200,768]{2,1,0:T(8,128)(2,1)}, bf16[8,200,768]{2,1,0:T(8,128)(2,1)}, bf16[8,200,2304]{2,1,0:T(8,128)(2,1)}, bf16[8,12,200,200]{3,2,1,0:T(8,128)(2,1)}, bf16[8,200,768]{2,1,0:T(8,128)(2,1)}) custom-call(s32[3]{0:T(128)} %compare_select_fusion.1.meta, ...), custom_call_target="tpu_custom_call", output_to_operand_aliasing={{0}: (13, {}), {1}: (14, {}), {2}: (15, {}), {3}: (16, {}),... | custom-call | flops 7195852800 | bytes 25657344 | tf_op jit(solution)/shard_map/attend/pallas_call | solution.py:239
  102.1 11.9 %project.1 = (f32[1600,768]{1,0:T(8,128)}, bf16[1600,768]{1,0:T(8,128)(2,1)}, bf16[1600,768]{1,0:T(8,128)(2,1)}, f32[1,768]{1,0:T(1,128)}) custom-call(s32[3]{0:T(128)} %compare_select_fusion.1.meta, s32[4,8]{1,0:T(4,128)} %bitcast.70, bf16[8,200,768]{2,1,0:T(8,128)(2,1)} %get-tuple-element.210.attended.mixed_in, ...), custom_call_target="tpu_custom_call" | custom-call | flops 1887436800 | bytes 17203200 | tf_op jit(solution)/shard_map/project/pallas_call | solution.py:239
  114.1 24.9 %feed.3 = (bf16[1600,768]{1,0:T(8,128)(2,1)}, bf16[1600,768]{1,0:T(8,128)(2,1)}, bf16[2,512,768]{2,1,0:T(8,128)(2,1)}, bf16[2,512,768]{2,1,0:T(8,128)(2,1)}, f32[1,1024]{1,0:T(1,128)}) custom-call(s32[3]{0:T(128)} %compare_select_fusion.1.meta, bf16[1600,768]{1,0:T(8,128)(2,1)} %get-tuple-element.214.normed, bf16[1600,768]{1,0:T(8,128)(2,1)} %get-tuple-element.215.branch, ...), custom_call_target="tpu_custom_call" | custom-call | flops 15099494400 | bytes 21037056 | tf_op jit(solution)/shard_map/feed/pallas_call | solution.py:239
  139.5 25.6 %feed.4 = (bf16[1600,768]{1,0:T(8,128)(2,1)}, bf16[1600,768]{1,0:T(8,128)(2,1)}, bf16[2,512,768]{2,1,0:T(8,128)(2,1)}, bf16[2,512,768]{2,1,0:T(8,128)(2,1)}, f32[1,1024]{1,0:T(1,128)}) custom-call(s32[3]{0:T(128)} %compare_select_fusion.1.meta, bf16[1600,768]{1,0:T(8,128)(2,1)} %get-tuple-element.214.normed, ...), custom_call_target="tpu_custom_call", output_to_operand_aliasing={{0}: (14, {}), {1}: (15, {})} | custom-call | flops 15099494400 | bytes 21037056 | tf_op jit(solution)/shard_map/feed/pallas_call | solution.py:239
  168.5 25.7 %feed.5 = (bf16[1600,768]{1,0:T(8,128)(2,1)}, bf16[1600,768]{1,0:T(8,128)(2,1)}, bf16[2,512,768]{2,1,0:T(8,128)(2,1)}, bf16[2,512,768]{2,1,0:T(8,128)(2,1)}, f32[1,1024]{1,0:T(1,128)}) custom-call(s32[3]{0:T(128)} %compare_select_fusion.1.meta, bf16[1600,768]{1,0:T(8,128)(2,1)} %get-tuple-element.214.normed, ...), custom_call_target="tpu_custom_call", output_to_operand_aliasing={{0}: (14, {}), {1}: (15, {})} | custom-call | flops 15099494400 | bytes 21037056 | tf_op jit(solution)/shard_map/feed/pallas_call | solution.py:239
  198.8 18.6 %middle.1 = (bf16[4,49,8,768]{3,2,1,0:T(8,128)(2,1)}, bf16[1600,768]{1,0:T(8,128)(2,1)}, bf16[8,200,768]{2,1,0:T(8,128)(2,1)}, bf16[2,192,768]{2,1,0:T(8,128)(2,...) custom-call(s32[3]{0:T(128)} %compare_select_fusion.1.meta, ...), custom_call_target="tpu_custom_call" | custom-call | flops 3774873600 | bytes 22118400 | tf_op jit(solution)/shard_map/middle/pallas_call | solution.py:239
  222.3 13.1 %attend_back.3 = (bf16[8,200,256]{2,1,0:T(8,128)(2,1)}, bf16[8,200,256]{2,1,0:T(8,128)(2,1)}, bf16[8,200,256]{2,1,0:T(8,128)(2,1)}, bf16[2,192,768]{2,1,0:T(8,12...) custom-call(s32[3]{0:T(128)} %compare_select_fusion.1.meta, ...), custom_call_target="tpu_custom_call" | custom-call | flops 4508876800 | bytes 12288000 | tf_op jit(solution)/shard_map/attend_back/pallas_call | solution.py:239
  238.5 4.9 %all-to-all-start.2 = ((bf16[4,49,8,768]{3,2,1,0:T(8,128)(2,1)}), bf16[4,49,8,768]{3,2,1,0:T(8,128)(2,1)}, u32[]{:S(2)}, u32[]{:S(2)}) async-start(bf16[4,49,8,768]{3,2,1,0:T(8,128)(2,1)} %get-tuple-element.276), calls=%async_computation.2 | async-start | bytes 4816896 | tf_op jit(solution)/shard_map/all_to_all | solution.py:1091
  247.0 12.9 %attend_back.4 = (bf16[8,200,256]{2,1,0:T(8,128)(2,1)}, bf16[8,200,256]{2,1,0:T(8,128)(2,1)}, bf16[8,200,256]{2,1,0:T(8,128)(2,1)}, bf16[2,192,768]{2,1,0:T(8,12...) custom-call(s32[3]{0:T(128)} %compare_select_fusion.1.meta, ...), custom_call_target="tpu_custom_call" | custom-call | flops 4508876800 | bytes 12288000 | tf_op jit(solution)/shard_map/attend_back/pallas_call | solution.py:239
  259.9 4.4 %collective-permute-done.25 = bf16[256,768]{1,0:T(8,128)(2,1)S(1)} collective-permute-done((bf16[256,768]{1,0:T(8,128)(2,1)S(1)}, bf16[256,768]{1,0:T(8,128)(2,1)S(1)}, u32[]{:S(2)}, u32[]{:S(2)}) %collective-permute-start.25) | collective-permute-done | bytes 393248 | tf_op jit(solution)/shard_map/ppermute | solution.py:1076
  277.3 13.0 %attend_back.5 = (bf16[8,200,256]{2,1,0:T(8,128)(2,1)}, bf16[8,200,256]{2,1,0:T(8,128)(2,1)}, bf16[8,200,256]{2,1,0:T(8,128)(2,1)}, bf16[2,192,768]{2,1,0:T(8,12...) custom-call(s32[3]{0:T(128)} %compare_select_fusion.1.meta, ...), custom_call_target="tpu_custom_call" | custom-call | flops 4508876800 | bytes 12288000 | tf_op jit(solution)/shard_map/attend_back/pallas_call | solution.py:239
  298.6 16.5 %first_back.1 = (bf16[4,49,8,768]{3,2,1,0:T(8,128)(2,1)}, f32[1,768]{1,0:T(1,128)}, f32[1,768]{1,0:T(1,128)}) custom-call(s32[3]{0:T(128)} %compare_select_fusion.1.meta, bf16[8,200,768]{2,1,0:T(8,128)(2,1)} %get-tuple-element.211.rows_in, bf16[1600,768]{1,0:T(8,128)(2,1)} %get-tuple-element.293.d_middle, f32[13,768]{1,0:T(8,128)} %get-tuple-element.189.vectors, ...), custom_call_target="tpu_custom_call" | custom-call | flops 5662310400 | bytes 17203200 | tf_op jit(solution)/shard_map/first_back/pallas_call | solution.py:239
  326.9 3.8 all-to-all-start.3
  343.3 3.7 collective-permute-done.39
  349.2 5.5 %collective-permute-done.40 = bf16[96,768]{1,0:T(8,128)(2,1)S(1)} collective-permute-done((bf16[96,768]{1,0:T(8,128)(2,1)S(1)}, bf16[96,768]{1,0:T(8,128)(2,1)S(1)}, u32[]{:S(2)}, u32[]{:S(2)}) %collective-permute-start.40) | collective-permute-done | bytes 147488 | tf_op jit(solution)/shard_map/ppermute | solution.py:1076
  358.0 3.3 collective-permute-done.41
  365.7 4.2 %collective-permute-done.51 = f32[24,768]{1,0:T(8,128)S(1)} collective-permute-done((f32[24,768]{1,0:T(8,128)S(1)}, f32[24,768]{1,0:T(8,128)S(1)}, u32[]{:S(2)}, u32[]{:S(2)}) %collective-permute-start.51) | collective-permute-done | bytes 73760 | tf_op jit(solution)/shard_map/ppermute | solution.py:1076
  376.0 5.1 %finish_feed.1 = (f32[192,3072]{1,0:T(8,128)}, f32[768,768]{1,0:T(8,128)}, f32[192,768]{1,0:T(8,128)}) custom-call(s32[3]{0:T(128)} %compare_select_fusion.1.meta, bf16[256,768]{1,0:T(8,128)(2,1)} %copy-done.8, bf16[256,768]{1,0:T(8,128)(2,1)} %copy-done.27, bf16[256,768]{1,0:T(8,128)(2,1)} %copy-done.9, bf16[256,768]{1,0:T(8,128)(2,1)} %copy-done.28, ...), custom_call_target="tpu_custom_call" | custom-call | bytes 7962624 | tf_op jit(solution)/shard_map/finish_feed/pallas_call | solution.py:239
  (230 shorter events, 116.5 us)
Async XLA Ops:
  16.9 33.6 %all-to-all-start = ((bf16[4,49,8,768]{3,2,1,0:T(8,128)(2,1)}), bf16[4,49,8,768]{3,2,1,0:T(8,128)(2,1)}, u32[]{:S(2)}, u32[]{:S(2)}) async-start(bf16[4,49,8,768]{3,2,1,0:T(8,128)(2,1)} %bitcast.6), calls=%async_computation | async-start | bytes 4816896 | tf_op jit(solution)/shard_map/all_to_all | solution.py:1091
  66.2 34.5 %all-to-all-start.1 = ((bf16[4,49,8,768]{3,2,1,0:T(8,128)(2,1)}), bf16[4,49,8,768]{3,2,1,0:T(8,128)(2,1)S(1)}, u32[]{:S(2)}, u32[]{:S(2)}) async-start(bf16[4,49,8,768]{3,2,1,0:T(8,128)(2,1)} %bitcast.61), calls=%async_computation.1 | async-start | bytes 4816896 | tf_op jit(solution)/shard_map/all_to_all | solution.py:1091
  70.4 43.6 %collective-permute-start.12 = (bf16[384,768]{1,0:T(8,128)(2,1)S(1)}, bf16[384,768]{1,0:T(8,128)(2,1)}, u32[]{:S(2)}, u32[]{:S(2)}) collective-permute-start(bf16[384,768]{1,0:T(8,128)(2,1)S(1)} %collective-permute-done.7.rest_2_), channel_id=1, source_target_pairs={{0,1},{1,0},{2,3},{3,2},{4,5},{5,4},{6,7},{7,6},{8,9},{9,8},{10,11... | collective-permute-start | bytes 1769480 | tf_op jit(solution)/shard_map/ppermute | solution.py:1076
  70.9 26.7 %collective-permute-start.11 = (bf16[384,768]{1,0:T(8,128)(2,1)S(1)}, bf16[384,768]{1,0:T(8,128)(2,1)}, u32[]{:S(2)}, u32[]{:S(2)}) collective-permute-start(bf16[384,768]{1,0:T(8,128)(2,1)S(1)} %collective-permute-done.7.rest_2_), channel_id=1, source_target_pairs={{0,20},{4,16},{8,28},{12,24},{16,4},{20,0},{24,12},{28,8},{1,21},{... | collective-permute-start | bytes 1769480 | tf_op jit(solution)/shard_map/ppermute | solution.py:1083
  73.7 26.5 %collective-permute-start.10 = (bf16[384,768]{1,0:T(8,128)(2,1)S(1)}, bf16[384,768]{1,0:T(8,128)(2,1)}, u32[]{:S(2)}, u32[]{:S(2)}) collective-permute-start(bf16[384,768]{1,0:T(8,128)(2,1)S(1)} %collective-permute-done.7.rest_2_), channel_id=1, source_target_pairs={{0,4},{4,0},{8,12},{12,8},{1,5},{5,1},{9,13},{13,9},{2,6},{6,2},{1... | collective-permute-start | bytes 1769480 | tf_op jit(solution)/shard_map/ppermute | solution.py:1076
  74.1 26.1 %collective-permute-start.9 = (bf16[384,768]{1,0:T(8,128)(2,1)S(1)}, bf16[384,768]{1,0:T(8,128)(2,1)}, u32[]{:S(2)}, u32[]{:S(2)}) collective-permute-start(bf16[384,768]{1,0:T(8,128)(2,1)S(1)} %collective-permute-done.7.rest_2_), channel_id=1, source_target_pairs={{0,16},{16,0},{1,17},{17,1},{2,18},{18,2},{3,19},{19,3},{4,20},{20... | collective-permute-start | bytes 1769480 | tf_op jit(solution)/shard_map/ppermute | solution.py:1076
  138.9 26.2 %collective-permute-start.16 = (bf16[2,512,768]{2,1,0:T(8,128)(2,1)}, bf16[2,512,768]{2,1,0:T(8,128)(2,1)S(1)}, u32[]{:S(2)}, u32[]{:S(2)}) collective-permute-start(bf16[2,512,768]{2,1,0:T(8,128)(2,1)} %get-tuple-element.226), channel_id=1, source_target_pairs={{0,1},{1,0},{2,3},{3,2},{4,5},{5,4},{6,7},{7,6},{8,9},{9,8},{10,11... | collective-permute-start | bytes 4718600 | tf_op jit(solution)/shard_map/ppermute | solution.py:1076
  166.5 27.7 %collective-permute-start.18 = (bf16[2,512,768]{2,1,0:T(8,128)(2,1)}, bf16[2,512,768]{2,1,0:T(8,128)(2,1)S(1)}, u32[]{:S(2)}, u32[]{:S(2)}) collective-permute-start(bf16[2,512,768]{2,1,0:T(8,128)(2,1)} %get-tuple-element.234), channel_id=1, source_target_pairs={{0,1},{1,0},{2,3},{3,2},{4,5},{5,4},{6,7},{7,6},{8,9},{9,8},{10,11... | collective-permute-start | bytes 4718600 | tf_op jit(solution)/shard_map/ppermute | solution.py:1076
  166.6 27.7 %collective-permute-start.17 = (bf16[512,768]{1,0:T(8,128)(2,1)}, bf16[512,768]{1,0:T(8,128)(2,1)S(1)}, u32[]{:S(2)}, u32[]{:S(2)}) collective-permute-start(bf16[512,768]{1,0:T(8,128)(2,1)} %slice_bitcast_fusion.3), channel_id=1, source_target_pairs={{0,2},{1,3},{2,0},{3,1},{4,6},{5,7},{6,4},{7,5},{8,10},{9,11},{10,... | collective-permute-start | bytes 2359304 | tf_op jit(solution)/shard_map/ppermute | solution.py:1076
  196.9 20.5 %collective-permute-start.21 = (bf16[2,512,768]{2,1,0:T(8,128)(2,1)}, bf16[2,512,768]{2,1,0:T(8,128)(2,1)S(1)}, u32[]{:S(2)}, u32[]{:S(2)}) collective-permute-start(bf16[2,512,768]{2,1,0:T(8,128)(2,1)} %get-tuple-element.246), channel_id=1, source_target_pairs={{0,1},{1,0},{2,3},{3,2},{4,5},{5,4},{6,7},{7,6},{8,9},{9,8},{10,11... | collective-permute-start | bytes 4718600 | tf_op jit(solution)/shard_map/ppermute | solution.py:1076
  197.1 20.3 %collective-permute-start.20 = (bf16[512,768]{1,0:T(8,128)(2,1)S(1)}, bf16[512,768]{1,0:T(8,128)(2,1)S(1)}, u32[]{:S(2)}, u32[]{:S(2)}) collective-permute-start(bf16[512,768]{1,0:T(8,128)(2,1)S(1)} %slice_bitcast_fusion.1), channel_id=1, source_target_pairs={{0,2},{1,3},{2,0},{3,1},{4,6},{5,7},{6,4},{7,5},{8,10},{9,11},{10,... | collective-permute-start | bytes 2359304 | tf_op jit(solution)/shard_map/ppermute | solution.py:1076
  197.4 20.0 %collective-permute-start.19 = (bf16[256,768]{1,0:T(8,128)(2,1)}, bf16[256,768]{1,0:T(8,128)(2,1)S(1)}, u32[]{:S(2)}, u32[]{:S(2)}) collective-permute-start(bf16[256,768]{1,0:T(8,128)(2,1)} %broadcast_select_fusion.2), channel_id=1, source_target_pairs={{0,16},{16,0},{1,17},{17,1},{2,18},{18,2},{3,19},{19,3},{4,20},{20... | collective-permute-start | bytes 1179656 | tf_op jit(solution)/shard_map/ppermute | solution.py:1076
  237.1 28.6 %collective-permute-start.27 = (bf16[2,352,768]{2,1,0:T(8,128)(2,1)}, bf16[2,352,768]{2,1,0:T(8,128)(2,1)}, u32[]{:S(2)}, u32[]{:S(2)}) collective-permute-start(bf16[2,352,768]{2,1,0:T(8,128)(2,1)} %broadcast_select_fusion), channel_id=1, source_target_pairs={{0,16},{16,0},{1,17},{17,1},{2,18},{18,2},{3,19},{19,3},{4,20},{20... | collective-permute-start | bytes 3244040 | tf_op jit(solution)/shard_map/ppermute | solution.py:1076
  238.5 34.0 %all-to-all-start.2 = ((bf16[4,49,8,768]{3,2,1,0:T(8,128)(2,1)}), bf16[4,49,8,768]{3,2,1,0:T(8,128)(2,1)}, u32[]{:S(2)}, u32[]{:S(2)}) async-start(bf16[4,49,8,768]{3,2,1,0:T(8,128)(2,1)} %get-tuple-element.276), calls=%async_computation.2 | async-start | bytes 4816896 | tf_op jit(solution)/shard_map/all_to_all | solution.py:1091
  243.4 22.3 %collective-permute-start.28 = (bf16[2,192,768]{2,1,0:T(8,128)(2,1)}, bf16[2,192,768]{2,1,0:T(8,128)(2,1)S(1)}, u32[]{:S(2)}, u32[]{:S(2)}) collective-permute-start(bf16[2,192,768]{2,1,0:T(8,128)(2,1)} %get-tuple-element.271), channel_id=1, source_target_pairs={{0,1},{1,0},{2,3},{3,2},{4,5},{5,4},{6,7},{7,6},{8,9},{9,8},{10,11... | collective-permute-start | bytes 1769480 | tf_op jit(solution)/shard_map/ppermute | solution.py:1076
  244.0 20.4 %collective-permute-start.25 = (bf16[256,768]{1,0:T(8,128)(2,1)S(1)}, bf16[256,768]{1,0:T(8,128)(2,1)S(1)}, u32[]{:S(2)}, u32[]{:S(2)}) collective-permute-start(bf16[256,768]{1,0:T(8,128)(2,1)S(1)} %get-tuple-element.268), channel_id=1, source_target_pairs={{0,8},{4,12},{8,0},{12,4},{1,9},{5,13},{9,1},{13,5},{2,10},{6,14},... | collective-permute-start | bytes 1179656 | tf_op jit(solution)/shard_map/ppermute | solution.py:1076
  246.5 19.2 %collective-permute-start.26 = (bf16[256,768]{1,0:T(8,128)(2,1)S(1)}, bf16[256,768]{1,0:T(8,128)(2,1)S(1)}, u32[]{:S(2)}, u32[]{:S(2)}) collective-permute-start(bf16[256,768]{1,0:T(8,128)(2,1)S(1)} %get-tuple-element.269), channel_id=1, source_target_pairs={{0,4},{4,0},{8,12},{12,8},{1,5},{5,1},{9,13},{13,9},{2,6},{6,2},{1... | collective-permute-start | bytes 1179656 | tf_op jit(solution)/shard_map/ppermute | solution.py:1076
  273.1 19.6 %collective-permute-start.30 = (bf16[256,768]{1,0:T(8,128)(2,1)S(1)}, bf16[256,768]{1,0:T(8,128)(2,1)S(1)}, u32[]{:S(2)}, u32[]{:S(2)}) collective-permute-start(bf16[256,768]{1,0:T(8,128)(2,1)S(1)} %add_convert_fusion.9), channel_id=1, source_target_pairs={{0,8},{4,12},{8,0},{12,4},{1,9},{5,13},{9,1},{13,5},{2,10},{6,14},... | collective-permute-start | bytes 1179656 | tf_op jit(solution)/shard_map/ppermute | solution.py:1076
  296.5 18.7 %collective-permute-start.35 = (bf16[384,768]{1,0:T(8,128)(2,1)S(1)}, bf16[384,768]{1,0:T(8,128)(2,1)S(1)}, u32[]{:S(2)}, u32[]{:S(2)}) collective-permute-start(bf16[384,768]{1,0:T(8,128)(2,1)S(1)} %fusion.5), channel_id=1, source_target_pairs={{0,2},{1,3},{2,0},{3,1},{4,6},{5,7},{6,4},{7,5},{8,10},{9,11},{10,... | collective-permute-start | bytes 1769480 | tf_op jit(solution)/shard_map/ppermute | solution.py:1076
  297.2 18.1 %collective-permute-start.36 = (bf16[2,192,768]{2,1,0:T(8,128)(2,1)}, bf16[2,192,768]{2,1,0:T(8,128)(2,1)S(1)}, u32[]{:S(2)}, u32[]{:S(2)}) collective-permute-start(bf16[2,192,768]{2,1,0:T(8,128)(2,1)} %get-tuple-element.308), channel_id=1, source_target_pairs={{0,1},{1,0},{2,3},{3,2},{4,5},{5,4},{6,7},{7,6},{8,9},{9,8},{10,11... | collective-permute-start | bytes 1769480 | tf_op jit(solution)/shard_map/ppermute | solution.py:1076
  297.2 18.0 %collective-permute-start.33 = (bf16[256,768]{1,0:T(8,128)(2,1)S(1)}, bf16[256,768]{1,0:T(8,128)(2,1)S(1)}, u32[]{:S(2)}, u32[]{:S(2)}) collective-permute-start(bf16[256,768]{1,0:T(8,128)(2,1)S(1)} %add_convert_fusion.8.refs_2_), channel_id=1, source_target_pairs={{0,16},{16,0},{1,17},{17,1},{2,18},{18,2},{3,19},{19,3},{4,20},{20... | collective-permute-start | bytes 1179656 | tf_op jit(solution)/shard_map/ppermute | solution.py:1076
  326.9 54.2 %all-to-all-start.3 = ((bf16[4,49,8,768]{3,2,1,0:T(8,128)(2,1)}), bf16[4,49,8,768]{3,2,1,0:T(8,128)(2,1)S(1)}, u32[]{:S(2)}, u32[]{:S(2)}) async-start(bf16[4,49,8,768]{3,2,1,0:T(8,128)(2,1)} %get-tuple-element.324), calls=%async_computation.3 | async-start | bytes 4816896 | tf_op jit(solution)/shard_map/all_to_all | solution.py:1091
  330.7 33.7 %collective-permute-start.50 = (f32[24,768]{1,0:T(8,128)S(1)}, f32[24,768]{1,0:T(8,128)S(1)}, u32[]{:S(2)}, u32[]{:S(2)}) collective-permute-start(f32[24,768]{1,0:T(8,128)S(1)} %add.139), channel_id=1, source_target_pairs={{0,4},{4,0},{8,12},{12,8},{1,5},{5,1},{9,13},{13,9},{2,6},{6,2},{1... | collective-permute-start | bytes 221192 | tf_op jit(solution)/shard_map/ppermute | solution.py:1076
  348.5 26.6 %collective-permute-start.54 = (bf16[352,768]{1,0:T(8,128)(2,1)S(1)}, bf16[352,768]{1,0:T(8,128)(2,1)S(1)}, u32[]{:S(2)}, u32[]{:S(2)}) collective-permute-start(bf16[352,768]{1,0:T(8,128)(2,1)S(1)} %pad_maximum_fusion.3.refs_4_), channel_id=1, source_target_pairs={{0,16},{16,0},{1,17},{17,1},{2,18},{18,2},{3,19},{19,3},{4,20},{20... | collective-permute-start | bytes 1622024 | tf_op jit(solution)/shard_map/ppermute | solution.py:1076
  (68 other events, 638.9 us)

commit v6 on v5

--- a/solution.py
+++ b/solution.py
@@ -1167,11 +1167,13 @@
     return total, far
 
 
-def sum_stages(values):
+def sum_stages(values, hook):
     steps = [(axis, bit) for axis in ("tensor", "dp", "seq") for bit in halves(axis)]
     steps = [("tensor", 2)] + [item for item in steps if item != ("tensor", 2)]
-    for axis, bit in steps:
+    for number, (axis, bit) in enumerate(steps):
         (far,) = yield [(values, axis, bit)]
+        if number == len(steps) - 1:
+            far = hook(far)
         values = values + far
     return (values,)
 
@@ -1382,7 +1384,8 @@
         expand_bias_grads,
         table_grads,
     )
-    exchanges.begin("small", sum_stages(small))
+    hook = lambda far: after(far, *feed_gradients)
+    exchanges.begin("small", sum_stages(small, hook))
     exchanges.step(["small"], None, None)
     first_far = exchanges.running[-1][2][0]
     tokens_gradient = to_image(exchange_windows(after(token_grad, first_far)))

time: 392 us -> 390 us (level)
  transfers between devices with their start and end apart: 59 -> 59, of which waited for: 18 -> 17; matrix products, arithmetic and copies ran while one was open for 4% -> 4% of each run, Pallas kernels for 48% -> 48%
where the time goes in v6:
time: 390 us; the launch traced here: 383 us
  Pallas kernels  211 us (54%)
  starting transfers between devices  69.6 us (18%)
  waiting for transfers between devices  65.5 us (17%)
  local copies, waits for them, and re-layouts  18.3 us (5%)
  other arithmetic  17.2 us (4%)
    pallas_call x15, Pallas kernels, call(): pl.pallas_call(kernel, out_shape=tuple((item for item, _ in outs)), grid_...  211 us
    ppermute x53, starting transfers between devices, swap(): return lax.ppermute(values, axis, [(n, n ^ bits) for n in range(count)])  46.7 us
    ppermute x53, waiting for transfers between devices, swap(): return lax.ppermute(values, axis, [(n, n ^ bits) for n in range(count)])  41.7 us
    all_to_all x4, waiting for transfers between devices, exchange_windows(): lax.all_to_all(values, 'tensor', split_axis=0, concat_axis=0, tiled=True)  21 us
    all_to_all x4, starting transfers between devices, exchange_windows(): lax.all_to_all(values, 'tensor', split_axis=0, concat_axis=0, tiled=True)  17.4 us
    convert_element_type x26, other arithmetic, add(): return total.astype(BF16)  12.8 us
    unnamed x68, local copies, waits for them, and re-layouts  12.7 us
  transfers between devices with their start and end apart: 59, of which 17 were waited for; matrix products, arithmetic and copies ran while one was open for 4% of the time, Pallas kernels for 48%

profile of v6, /device:TPU:0, one launch (start us, length us, event | category | flops | bytes accessed | tf_op | source)
XLA Modules:
  0.0 383.1 jit_solution(14440081650800017175)
XLA Ops:
  5.8 3.3 prepare.1
  16.9 4.5 %all-to-all-start = ((bf16[4,49,8,768]{3,2,1,0:T(8,128)(2,1)}), bf16[4,49,8,768]{3,2,1,0:T(8,128)(2,1)}, u32[]{:S(2)}, u32[]{:S(2)}) async-start(bf16[4,49,8,768]{3,2,1,0:T(8,128)(2,1)} %bitcast.6), calls=%async_computation | async-start | bytes 4816896 | tf_op jit(solution)/shard_map/all_to_all | solution.py:1091
  24.2 5.3 %collective-permute-done.4 = bf16[48,3072]{1,0:T(8,128)(2,1)S(1)} collective-permute-done((bf16[48,3072]{1,0:T(8,128)(2,1)S(1)}, bf16[48,3072]{1,0:T(8,128)(2,1)S(1)}, u32[]{:S(2)}, u32[]{:S(2)}) %collective-permute-start.4) | collective-permute-done | bytes 294944 | tf_op jit(solution)/shard_map/ppermute | solution.py:1076
  32.6 17.9 %all-to-all-done.tokens = bf16[4,49,8,768]{3,2,1,0:T(8,128)(2,1)} async-done(((bf16[4,49,8,768]{3,2,1,0:T(8,128)(2,1)}), bf16[4,49,8,768]{3,2,1,0:T(8,128)(2,1)}, u32[]{:S(2)}, u32[]{:S(2)}) %all-to-all-start) | async-done | bytes 2408480 | tf_op jit(solution)/shard_map/all_to_all | solution.py:1091
  50.9 12.3 %attend.2 = (bf16[8,200,768]{2,1,0:T(8,128)(2,1)}, bf16[8,200,768]{2,1,0:T(8,128)(2,1)}, bf16[8,200,2304]{2,1,0:T(8,128)(2,1)}, bf16[8,12,200,200]{3,2,1,0:T(8,128)(2,1)}, bf16[8,200,768]{2,1,0:T(8,128)(2,1)}) custom-call(s32[3]{0:T(128)} %compare_select_fusion.1.meta, s32[4,8]{1,0:T(4,128)} %bitcast.68, bf16[4,49,8,768]{3,2,1,0:T(8,128)(2,1)} %all-to-all-done.tokens, ...), custom_call_target="tpu_custom_call" | custom-call | flops 2398617600 | bytes 10911744 | tf_op jit(solution)/shard_map/attend/pallas_call | solution.py:239
  66.2 4.2 %all-to-all-start.1 = ((bf16[4,49,8,768]{3,2,1,0:T(8,128)(2,1)}), bf16[4,49,8,768]{3,2,1,0:T(8,128)(2,1)S(1)}, u32[]{:S(2)}, u32[]{:S(2)}) async-start(bf16[4,49,8,768]{3,2,1,0:T(8,128)(2,1)} %bitcast.61), calls=%async_computation.1 | async-start | bytes 4816896 | tf_op jit(solution)/shard_map/all_to_all | solution.py:1091
  74.4 23.2 %attend.3 = (bf16[8,200,768]{2,1,0:T(8,128)(2,1)}, bf16[8,200,768]{2,1,0:T(8,128)(2,1)}, bf16[8,200,2304]{2,1,0:T(8,128)(2,1)}, bf16[8,12,200,200]{3,2,1,0:T(8,128)(2,1)}, bf16[8,200,768]{2,1,0:T(8,128)(2,1)}) custom-call(s32[3]{0:T(128)} %compare_select_fusion.1.meta, ...), custom_call_target="tpu_custom_call", output_to_operand_aliasing={{0}: (13, {}), {1}: (14, {}), {2}: (15, {}), {3}: (16, {}),... | custom-call | flops 7195852800 | bytes 25657344 | tf_op jit(solution)/shard_map/attend/pallas_call | solution.py:239
  102.1 11.9 %project.1 = (f32[1600,768]{1,0:T(8,128)}, bf16[1600,768]{1,0:T(8,128)(2,1)}, bf16[1600,768]{1,0:T(8,128)(2,1)}, f32[1,768]{1,0:T(1,128)}) custom-call(s32[3]{0:T(128)} %compare_select_fusion.1.meta, s32[4,8]{1,0:T(4,128)} %bitcast.70, bf16[8,200,768]{2,1,0:T(8,128)(2,1)} %get-tuple-element.211.attended.mixed_in, ...), custom_call_target="tpu_custom_call" | custom-call | flops 1887436800 | bytes 17203200 | tf_op jit(solution)/shard_map/project/pallas_call | solution.py:239
  114.1 24.9 %feed.3 = (bf16[1600,768]{1,0:T(8,128)(2,1)}, bf16[1600,768]{1,0:T(8,128)(2,1)}, bf16[2,512,768]{2,1,0:T(8,128)(2,1)}, bf16[2,512,768]{2,1,0:T(8,128)(2,1)}, f32[1,1024]{1,0:T(1,128)}) custom-call(s32[3]{0:T(128)} %compare_select_fusion.1.meta, bf16[1600,768]{1,0:T(8,128)(2,1)} %get-tuple-element.215.normed, bf16[1600,768]{1,0:T(8,128)(2,1)} %get-tuple-element.216.branch, ...), custom_call_target="tpu_custom_call" | custom-call | flops 15099494400 | bytes 21037056 | tf_op jit(solution)/shard_map/feed/pallas_call | solution.py:239
  139.5 25.6 %feed.4 = (bf16[1600,768]{1,0:T(8,128)(2,1)}, bf16[1600,768]{1,0:T(8,128)(2,1)}, bf16[2,512,768]{2,1,0:T(8,128)(2,1)}, bf16[2,512,768]{2,1,0:T(8,128)(2,1)}, f32[1,1024]{1,0:T(1,128)}) custom-call(s32[3]{0:T(128)} %compare_select_fusion.1.meta, bf16[1600,768]{1,0:T(8,128)(2,1)} %get-tuple-element.215.normed, ...), custom_call_target="tpu_custom_call", output_to_operand_aliasing={{0}: (14, {}), {1}: (15, {})} | custom-call | flops 15099494400 | bytes 21037056 | tf_op jit(solution)/shard_map/feed/pallas_call | solution.py:239
  168.5 25.7 %feed.5 = (bf16[1600,768]{1,0:T(8,128)(2,1)}, bf16[1600,768]{1,0:T(8,128)(2,1)}, bf16[2,512,768]{2,1,0:T(8,128)(2,1)}, bf16[2,512,768]{2,1,0:T(8,128)(2,1)}, f32[1,1024]{1,0:T(1,128)}) custom-call(s32[3]{0:T(128)} %compare_select_fusion.1.meta, bf16[1600,768]{1,0:T(8,128)(2,1)} %get-tuple-element.215.normed, ...), custom_call_target="tpu_custom_call", output_to_operand_aliasing={{0}: (14, {}), {1}: (15, {})} | custom-call | flops 15099494400 | bytes 21037056 | tf_op jit(solution)/shard_map/feed/pallas_call | solution.py:239
  198.8 18.6 %middle.1 = (bf16[4,49,8,768]{3,2,1,0:T(8,128)(2,1)}, bf16[1600,768]{1,0:T(8,128)(2,1)}, bf16[8,200,768]{2,1,0:T(8,128)(2,1)}, bf16[2,192,768]{2,1,0:T(8,128)(2,...) custom-call(s32[3]{0:T(128)} %compare_select_fusion.1.meta, ...), custom_call_target="tpu_custom_call" | custom-call | flops 3774873600 | bytes 22118400 | tf_op jit(solution)/shard_map/middle/pallas_call | solution.py:239
  222.3 13.1 %attend_back.3 = (bf16[8,200,256]{2,1,0:T(8,128)(2,1)}, bf16[8,200,256]{2,1,0:T(8,128)(2,1)}, bf16[8,200,256]{2,1,0:T(8,128)(2,1)}, bf16[2,192,768]{2,1,0:T(8,12...) custom-call(s32[3]{0:T(128)} %compare_select_fusion.1.meta, ...), custom_call_target="tpu_custom_call" | custom-call | flops 4508876800 | bytes 12288000 | tf_op jit(solution)/shard_map/attend_back/pallas_call | solution.py:239
  238.5 4.9 %all-to-all-start.2 = ((bf16[4,49,8,768]{3,2,1,0:T(8,128)(2,1)}), bf16[4,49,8,768]{3,2,1,0:T(8,128)(2,1)}, u32[]{:S(2)}, u32[]{:S(2)}) async-start(bf16[4,49,8,768]{3,2,1,0:T(8,128)(2,1)} %get-tuple-element.277), calls=%async_computation.2 | async-start | bytes 4816896 | tf_op jit(solution)/shard_map/all_to_all | solution.py:1091
  247.0 12.9 %attend_back.4 = (bf16[8,200,256]{2,1,0:T(8,128)(2,1)}, bf16[8,200,256]{2,1,0:T(8,128)(2,1)}, bf16[8,200,256]{2,1,0:T(8,128)(2,1)}, bf16[2,192,768]{2,1,0:T(8,12...) custom-call(s32[3]{0:T(128)} %compare_select_fusion.1.meta, ...), custom_call_target="tpu_custom_call" | custom-call | flops 4508876800 | bytes 12288000 | tf_op jit(solution)/shard_map/attend_back/pallas_call | solution.py:239
  259.9 4.4 %collective-permute-done.25 = bf16[256,768]{1,0:T(8,128)(2,1)S(1)} collective-permute-done((bf16[256,768]{1,0:T(8,128)(2,1)S(1)}, bf16[256,768]{1,0:T(8,128)(2,1)S(1)}, u32[]{:S(2)}, u32[]{:S(2)}) %collective-permute-start.25) | collective-permute-done | bytes 393248 | tf_op jit(solution)/shard_map/ppermute | solution.py:1076
  277.3 13.0 %attend_back.5 = (bf16[8,200,256]{2,1,0:T(8,128)(2,1)}, bf16[8,200,256]{2,1,0:T(8,128)(2,1)}, bf16[8,200,256]{2,1,0:T(8,128)(2,1)}, bf16[2,192,768]{2,1,0:T(8,12...) custom-call(s32[3]{0:T(128)} %compare_select_fusion.1.meta, ...), custom_call_target="tpu_custom_call" | custom-call | flops 4508876800 | bytes 12288000 | tf_op jit(solution)/shard_map/attend_back/pallas_call | solution.py:239
  298.6 16.5 %first_back.1 = (bf16[4,49,8,768]{3,2,1,0:T(8,128)(2,1)}, f32[1,768]{1,0:T(1,128)}, f32[1,768]{1,0:T(1,128)}) custom-call(s32[3]{0:T(128)} %compare_select_fusion.1.meta, bf16[8,200,768]{2,1,0:T(8,128)(2,1)} %get-tuple-element.212.rows_in, bf16[1600,768]{1,0:T(8,128)(2,1)} %get-tuple-element.294.d_middle, f32[13,768]{1,0:T(8,128)} %get-tuple-element.190.vectors, ...), custom_call_target="tpu_custom_call" | custom-call | flops 5662310400 | bytes 17203200 | tf_op jit(solution)/shard_map/first_back/pallas_call | solution.py:239
  327.2 3.8 all-to-all-start.3
  344.2 3.7 collective-permute-done.39
  350.1 5.4 %collective-permute-done.40 = bf16[96,768]{1,0:T(8,128)(2,1)S(1)} collective-permute-done((bf16[96,768]{1,0:T(8,128)(2,1)S(1)}, bf16[96,768]{1,0:T(8,128)(2,1)S(1)}, u32[]{:S(2)}, u32[]{:S(2)}) %collective-permute-start.40) | collective-permute-done | bytes 147488 | tf_op jit(solution)/shard_map/ppermute | solution.py:1076
  355.8 3.5 collective-permute-start.46
  361.6 3.7 collective-permute-done.46
  367.9 5.1 %finish_feed.1 = (f32[192,3072]{1,0:T(8,128)}, f32[768,768]{1,0:T(8,128)}, f32[192,768]{1,0:T(8,128)}) custom-call(s32[3]{0:T(128)} %compare_select_fusion.1.meta, bf16[256,768]{1,0:T(8,128)(2,1)} %copy-done.8, bf16[256,768]{1,0:T(8,128)(2,1)} %copy-done.27, bf16[256,768]{1,0:T(8,128)(2,1)} %copy-done.9, bf16[256,768]{1,0:T(8,128)(2,1)} %copy-done.28, ...), custom_call_target="tpu_custom_call" | custom-call | bytes 7962624 | tf_op jit(solution)/shard_map/finish_feed/pallas_call | solution.py:239
  (230 shorter events, 114.0 us)
Async XLA Ops:
  16.9 33.6 %all-to-all-start = ((bf16[4,49,8,768]{3,2,1,0:T(8,128)(2,1)}), bf16[4,49,8,768]{3,2,1,0:T(8,128)(2,1)}, u32[]{:S(2)}, u32[]{:S(2)}) async-start(bf16[4,49,8,768]{3,2,1,0:T(8,128)(2,1)} %bitcast.6), calls=%async_computation | async-start | bytes 4816896 | tf_op jit(solution)/shard_map/all_to_all | solution.py:1091
  66.2 34.5 %all-to-all-start.1 = ((bf16[4,49,8,768]{3,2,1,0:T(8,128)(2,1)}), bf16[4,49,8,768]{3,2,1,0:T(8,128)(2,1)S(1)}, u32[]{:S(2)}, u32[]{:S(2)}) async-start(bf16[4,49,8,768]{3,2,1,0:T(8,128)(2,1)} %bitcast.61), calls=%async_computation.1 | async-start | bytes 4816896 | tf_op jit(solution)/shard_map/all_to_all | solution.py:1091
  70.4 43.6 %collective-permute-start.12 = (bf16[384,768]{1,0:T(8,128)(2,1)S(1)}, bf16[384,768]{1,0:T(8,128)(2,1)}, u32[]{:S(2)}, u32[]{:S(2)}) collective-permute-start(bf16[384,768]{1,0:T(8,128)(2,1)S(1)} %collective-permute-done.7.rest_2_), channel_id=1, source_target_pairs={{0,1},{1,0},{2,3},{3,2},{4,5},{5,4},{6,7},{7,6},{8,9},{9,8},{10,11... | collective-permute-start | bytes 1769480 | tf_op jit(solution)/shard_map/ppermute | solution.py:1076
  70.9 26.7 %collective-permute-start.11 = (bf16[384,768]{1,0:T(8,128)(2,1)S(1)}, bf16[384,768]{1,0:T(8,128)(2,1)}, u32[]{:S(2)}, u32[]{:S(2)}) collective-permute-start(bf16[384,768]{1,0:T(8,128)(2,1)S(1)} %collective-permute-done.7.rest_2_), channel_id=1, source_target_pairs={{0,20},{4,16},{8,28},{12,24},{16,4},{20,0},{24,12},{28,8},{1,21},{... | collective-permute-start | bytes 1769480 | tf_op jit(solution)/shard_map/ppermute | solution.py:1083
  73.7 26.5 %collective-permute-start.10 = (bf16[384,768]{1,0:T(8,128)(2,1)S(1)}, bf16[384,768]{1,0:T(8,128)(2,1)}, u32[]{:S(2)}, u32[]{:S(2)}) collective-permute-start(bf16[384,768]{1,0:T(8,128)(2,1)S(1)} %collective-permute-done.7.rest_2_), channel_id=1, source_target_pairs={{0,4},{4,0},{8,12},{12,8},{1,5},{5,1},{9,13},{13,9},{2,6},{6,2},{1... | collective-permute-start | bytes 1769480 | tf_op jit(solution)/shard_map/ppermute | solution.py:1076
  74.1 26.1 %collective-permute-start.9 = (bf16[384,768]{1,0:T(8,128)(2,1)S(1)}, bf16[384,768]{1,0:T(8,128)(2,1)}, u32[]{:S(2)}, u32[]{:S(2)}) collective-permute-start(bf16[384,768]{1,0:T(8,128)(2,1)S(1)} %collective-permute-done.7.rest_2_), channel_id=1, source_target_pairs={{0,16},{16,0},{1,17},{17,1},{2,18},{18,2},{3,19},{19,3},{4,20},{20... | collective-permute-start | bytes 1769480 | tf_op jit(solution)/shard_map/ppermute | solution.py:1076
  138.9 26.2 %collective-permute-start.16 = (bf16[2,512,768]{2,1,0:T(8,128)(2,1)}, bf16[2,512,768]{2,1,0:T(8,128)(2,1)S(1)}, u32[]{:S(2)}, u32[]{:S(2)}) collective-permute-start(bf16[2,512,768]{2,1,0:T(8,128)(2,1)} %get-tuple-element.227), channel_id=1, source_target_pairs={{0,1},{1,0},{2,3},{3,2},{4,5},{5,4},{6,7},{7,6},{8,9},{9,8},{10,11... | collective-permute-start | bytes 4718600 | tf_op jit(solution)/shard_map/ppermute | solution.py:1076
  166.5 27.7 %collective-permute-start.18 = (bf16[2,512,768]{2,1,0:T(8,128)(2,1)}, bf16[2,512,768]{2,1,0:T(8,128)(2,1)S(1)}, u32[]{:S(2)}, u32[]{:S(2)}) collective-permute-start(bf16[2,512,768]{2,1,0:T(8,128)(2,1)} %get-tuple-element.235), channel_id=1, source_target_pairs={{0,1},{1,0},{2,3},{3,2},{4,5},{5,4},{6,7},{7,6},{8,9},{9,8},{10,11... | collective-permute-start | bytes 4718600 | tf_op jit(solution)/shard_map/ppermute | solution.py:1076
  166.6 27.7 %collective-permute-start.17 = (bf16[512,768]{1,0:T(8,128)(2,1)}, bf16[512,768]{1,0:T(8,128)(2,1)S(1)}, u32[]{:S(2)}, u32[]{:S(2)}) collective-permute-start(bf16[512,768]{1,0:T(8,128)(2,1)} %slice_bitcast_fusion.3), channel_id=1, source_target_pairs={{0,2},{1,3},{2,0},{3,1},{4,6},{5,7},{6,4},{7,5},{8,10},{9,11},{10,... | collective-permute-start | bytes 2359304 | tf_op jit(solution)/shard_map/ppermute | solution.py:1076
  196.9 20.5 %collective-permute-start.21 = (bf16[2,512,768]{2,1,0:T(8,128)(2,1)}, bf16[2,512,768]{2,1,0:T(8,128)(2,1)S(1)}, u32[]{:S(2)}, u32[]{:S(2)}) collective-permute-start(bf16[2,512,768]{2,1,0:T(8,128)(2,1)} %get-tuple-element.247), channel_id=1, source_target_pairs={{0,1},{1,0},{2,3},{3,2},{4,5},{5,4},{6,7},{7,6},{8,9},{9,8},{10,11... | collective-permute-start | bytes 4718600 | tf_op jit(solution)/shard_map/ppermute | solution.py:1076
  197.1 20.3 %collective-permute-start.20 = (bf16[512,768]{1,0:T(8,128)(2,1)S(1)}, bf16[512,768]{1,0:T(8,128)(2,1)S(1)}, u32[]{:S(2)}, u32[]{:S(2)}) collective-permute-start(bf16[512,768]{1,0:T(8,128)(2,1)S(1)} %slice_bitcast_fusion.1), channel_id=1, source_target_pairs={{0,2},{1,3},{2,0},{3,1},{4,6},{5,7},{6,4},{7,5},{8,10},{9,11},{10,... | collective-permute-start | bytes 2359304 | tf_op jit(solution)/shard_map/ppermute | solution.py:1076
  197.4 20.0 %collective-permute-start.19 = (bf16[256,768]{1,0:T(8,128)(2,1)}, bf16[256,768]{1,0:T(8,128)(2,1)S(1)}, u32[]{:S(2)}, u32[]{:S(2)}) collective-permute-start(bf16[256,768]{1,0:T(8,128)(2,1)} %broadcast_select_fusion.2), channel_id=1, source_target_pairs={{0,16},{16,0},{1,17},{17,1},{2,18},{18,2},{3,19},{19,3},{4,20},{20... | collective-permute-start | bytes 1179656 | tf_op jit(solution)/shard_map/ppermute | solution.py:1076
  237.1 28.6 %collective-permute-start.27 = (bf16[2,352,768]{2,1,0:T(8,128)(2,1)}, bf16[2,352,768]{2,1,0:T(8,128)(2,1)}, u32[]{:S(2)}, u32[]{:S(2)}) collective-permute-start(bf16[2,352,768]{2,1,0:T(8,128)(2,1)} %broadcast_select_fusion), channel_id=1, source_target_pairs={{0,16},{16,0},{1,17},{17,1},{2,18},{18,2},{3,19},{19,3},{4,20},{20... | collective-permute-start | bytes 3244040 | tf_op jit(solution)/shard_map/ppermute | solution.py:1076
  238.5 34.0 %all-to-all-start.2 = ((bf16[4,49,8,768]{3,2,1,0:T(8,128)(2,1)}), bf16[4,49,8,768]{3,2,1,0:T(8,128)(2,1)}, u32[]{:S(2)}, u32[]{:S(2)}) async-start(bf16[4,49,8,768]{3,2,1,0:T(8,128)(2,1)} %get-tuple-element.277), calls=%async_computation.2 | async-start | bytes 4816896 | tf_op jit(solution)/shard_map/all_to_all | solution.py:1091
  243.4 22.3 %collective-permute-start.28 = (bf16[2,192,768]{2,1,0:T(8,128)(2,1)}, bf16[2,192,768]{2,1,0:T(8,128)(2,1)S(1)}, u32[]{:S(2)}, u32[]{:S(2)}) collective-permute-start(bf16[2,192,768]{2,1,0:T(8,128)(2,1)} %get-tuple-element.272), channel_id=1, source_target_pairs={{0,1},{1,0},{2,3},{3,2},{4,5},{5,4},{6,7},{7,6},{8,9},{9,8},{10,11... | collective-permute-start | bytes 1769480 | tf_op jit(solution)/shard_map/ppermute | solution.py:1076
  244.0 20.4 %collective-permute-start.25 = (bf16[256,768]{1,0:T(8,128)(2,1)S(1)}, bf16[256,768]{1,0:T(8,128)(2,1)S(1)}, u32[]{:S(2)}, u32[]{:S(2)}) collective-permute-start(bf16[256,768]{1,0:T(8,128)(2,1)S(1)} %get-tuple-element.269), channel_id=1, source_target_pairs={{0,8},{4,12},{8,0},{12,4},{1,9},{5,13},{9,1},{13,5},{2,10},{6,14},... | collective-permute-start | bytes 1179656 | tf_op jit(solution)/shard_map/ppermute | solution.py:1076
  246.5 19.2 %collective-permute-start.26 = (bf16[256,768]{1,0:T(8,128)(2,1)S(1)}, bf16[256,768]{1,0:T(8,128)(2,1)S(1)}, u32[]{:S(2)}, u32[]{:S(2)}) collective-permute-start(bf16[256,768]{1,0:T(8,128)(2,1)S(1)} %get-tuple-element.270), channel_id=1, source_target_pairs={{0,4},{4,0},{8,12},{12,8},{1,5},{5,1},{9,13},{13,9},{2,6},{6,2},{1... | collective-permute-start | bytes 1179656 | tf_op jit(solution)/shard_map/ppermute | solution.py:1076
  273.1 19.6 %collective-permute-start.30 = (bf16[256,768]{1,0:T(8,128)(2,1)S(1)}, bf16[256,768]{1,0:T(8,128)(2,1)S(1)}, u32[]{:S(2)}, u32[]{:S(2)}) collective-permute-start(bf16[256,768]{1,0:T(8,128)(2,1)S(1)} %add_convert_fusion.9), channel_id=1, source_target_pairs={{0,8},{4,12},{8,0},{12,4},{1,9},{5,13},{9,1},{13,5},{2,10},{6,14},... | collective-permute-start | bytes 1179656 | tf_op jit(solution)/shard_map/ppermute | solution.py:1076
  296.5 18.7 %collective-permute-start.35 = (bf16[384,768]{1,0:T(8,128)(2,1)S(1)}, bf16[384,768]{1,0:T(8,128)(2,1)S(1)}, u32[]{:S(2)}, u32[]{:S(2)}) collective-permute-start(bf16[384,768]{1,0:T(8,128)(2,1)S(1)} %fusion.5), channel_id=1, source_target_pairs={{0,2},{1,3},{2,0},{3,1},{4,6},{5,7},{6,4},{7,5},{8,10},{9,11},{10,... | collective-permute-start | bytes 1769480 | tf_op jit(solution)/shard_map/ppermute | solution.py:1076
  297.2 18.1 %collective-permute-start.36 = (bf16[2,192,768]{2,1,0:T(8,128)(2,1)}, bf16[2,192,768]{2,1,0:T(8,128)(2,1)S(1)}, u32[]{:S(2)}, u32[]{:S(2)}) collective-permute-start(bf16[2,192,768]{2,1,0:T(8,128)(2,1)} %get-tuple-element.309), channel_id=1, source_target_pairs={{0,1},{1,0},{2,3},{3,2},{4,5},{5,4},{6,7},{7,6},{8,9},{9,8},{10,11... | collective-permute-start | bytes 1769480 | tf_op jit(solution)/shard_map/ppermute | solution.py:1076
  297.2 18.0 %collective-permute-start.34 = (bf16[176,768]{1,0:T(8,128)(2,1)S(1)}, bf16[176,768]{1,0:T(8,128)(2,1)S(1)}, u32[]{:S(2)}, u32[]{:S(2)}) collective-permute-start(bf16[176,768]{1,0:T(8,128)(2,1)S(1)} %broadcast_select_fusion.6), channel_id=1, source_target_pairs={{0,4},{4,0},{8,12},{12,8},{1,5},{5,1},{9,13},{13,9},{2,6},{6,2},{1... | collective-permute-start | bytes 811016 | tf_op jit(solution)/shard_map/ppermute | solution.py:1076
  297.2 18.0 %collective-permute-start.33 = (bf16[256,768]{1,0:T(8,128)(2,1)S(1)}, bf16[256,768]{1,0:T(8,128)(2,1)S(1)}, u32[]{:S(2)}, u32[]{:S(2)}) collective-permute-start(bf16[256,768]{1,0:T(8,128)(2,1)S(1)} %add_convert_fusion.8.refs_2_), channel_id=1, source_target_pairs={{0,16},{16,0},{1,17},{17,1},{2,18},{18,2},{3,19},{19,3},{4,20},{20... | collective-permute-start | bytes 1179656 | tf_op jit(solution)/shard_map/ppermute | solution.py:1076
  327.2 51.0 %all-to-all-start.3 = ((bf16[4,49,8,768]{3,2,1,0:T(8,128)(2,1)}), bf16[4,49,8,768]{3,2,1,0:T(8,128)(2,1)S(1)}, u32[]{:S(2)}, u32[]{:S(2)}) async-start(bf16[4,49,8,768]{3,2,1,0:T(8,128)(2,1)} %get-tuple-element.325), calls=%async_computation.3 | async-start | bytes 4816896 | tf_op jit(solution)/shard_map/all_to_all | solution.py:1091
  331.1 35.0 %collective-permute-start.50 = (f32[24,768]{1,0:T(8,128)S(1)}, f32[24,768]{1,0:T(8,128)S(1)}, u32[]{:S(2)}, u32[]{:S(2)}) collective-permute-start(f32[24,768]{1,0:T(8,128)S(1)} %add.139), channel_id=1, source_target_pairs={{0,4},{4,0},{8,12},{12,8},{1,5},{5,1},{9,13},{13,9},{2,6},{6,2},{1... | collective-permute-start | bytes 221192 | tf_op jit(solution)/shard_map/ppermute | solution.py:1076
  (68 other events, 639.3 us)

commit v7 on v6

--- a/solution.py
+++ b/solution.py
@@ -510,7 +510,7 @@
         + vectors[OUTPUT_BIAS : OUTPUT_BIAS + 1]
     )
     unit, _ = normalize(middle)
-    middle_out[...] = middle
+    middle_out[...] = middle.astype(BF16)
     normed = unit * vectors[SECOND_GAIN : SECOND_GAIN + 1] + vectors[SECOND_SHIFT : SECOND_SHIFT + 1]
     normed_out[...] = normed.astype(BF16)
     gather_quarters(step == 0, grads, staged, full, step * slabs, slabs)
@@ -536,7 +536,7 @@
         + [(item, whole(*item.shape)) for item in (grads, vectors)]
         + [(item, ANY) for item in pieces],
         [
-            (like((rows, width), F32), flat),
+            (like((rows, width), BF16), flat),
             (like((rows, width), BF16), flat),
             (like((rows, width), BF16), flat),
             (like((1, width), F32), whole(1, width)),
@@ -707,7 +707,7 @@
 
     width = full.shape[2]
     count = slabs * ROWS
-    rows = middle[...]
+    rows = middle[...].astype(F32)
     result = rows + out_acc[...].astype(F32) + vectors[SHRINK_BIAS : SHRINK_BIAS + 1]
     full[...] = result.reshape(slabs, ROWS, width)
     scatter_quarters(step == last, full, staged, result_out, step * slabs, slabs)

time: 390 us -> 389 us (level)
  no operation moved by 1% of the time
where the time goes in v7:
time: 389 us; the launch traced here: 383 us
  Pallas kernels  211 us (54%)
  starting transfers between devices  69.6 us (18%)
  waiting for transfers between devices  65.4 us (17%)
  local copies, waits for them, and re-layouts  18.3 us (5%)
  other arithmetic  17.2 us (4%)
    pallas_call x15, Pallas kernels, call(): pl.pallas_call(kernel, out_shape=tuple((item for item, _ in outs)), grid_...  211 us
    ppermute x53, starting transfers between devices, swap(): return lax.ppermute(values, axis, [(n, n ^ bits) for n in range(count)])  46.7 us
    ppermute x53, waiting for transfers between devices, swap(): return lax.ppermute(values, axis, [(n, n ^ bits) for n in range(count)])  41.6 us
    all_to_all x4, waiting for transfers between devices, exchange_windows(): lax.all_to_all(values, 'tensor', split_axis=0, concat_axis=0, tiled=True)  21 us
    all_to_all x4, starting transfers between devices, exchange_windows(): lax.all_to_all(values, 'tensor', split_axis=0, concat_axis=0, tiled=True)  17.4 us
    convert_element_type x26, other arithmetic, add(): return total.astype(BF16)  12.8 us
    unnamed x68, local copies, waits for them, and re-layouts  12.7 us
  transfers between devices with their start and end apart: 59, of which 17 were waited for; matrix products, arithmetic and copies ran while one was open for 4% of the time, Pallas kernels for 48%

profile of v7, /device:TPU:0, one launch (start us, length us, event | category | flops | bytes accessed | tf_op | source)
XLA Modules:
  0.0 382.8 jit_solution(2017283454673415661)
XLA Ops:
  5.8 3.3 prepare.1
  16.9 4.5 %all-to-all-start = ((bf16[4,49,8,768]{3,2,1,0:T(8,128)(2,1)}), bf16[4,49,8,768]{3,2,1,0:T(8,128)(2,1)}, u32[]{:S(2)}, u32[]{:S(2)}) async-start(bf16[4,49,8,768]{3,2,1,0:T(8,128)(2,1)} %bitcast.6), calls=%async_computation | async-start | bytes 4816896 | tf_op jit(solution)/shard_map/all_to_all | solution.py:1091
  24.2 5.3 %collective-permute-done.4 = bf16[48,3072]{1,0:T(8,128)(2,1)S(1)} collective-permute-done((bf16[48,3072]{1,0:T(8,128)(2,1)S(1)}, bf16[48,3072]{1,0:T(8,128)(2,1)S(1)}, u32[]{:S(2)}, u32[]{:S(2)}) %collective-permute-start.4) | collective-permute-done | bytes 294944 | tf_op jit(solution)/shard_map/ppermute | solution.py:1076
  32.6 17.9 %all-to-all-done.tokens = bf16[4,49,8,768]{3,2,1,0:T(8,128)(2,1)} async-done(((bf16[4,49,8,768]{3,2,1,0:T(8,128)(2,1)}), bf16[4,49,8,768]{3,2,1,0:T(8,128)(2,1)}, u32[]{:S(2)}, u32[]{:S(2)}) %all-to-all-start) | async-done | bytes 2408480 | tf_op jit(solution)/shard_map/all_to_all | solution.py:1091
  50.9 12.4 %attend.2 = (bf16[8,200,768]{2,1,0:T(8,128)(2,1)}, bf16[8,200,768]{2,1,0:T(8,128)(2,1)}, bf16[8,200,2304]{2,1,0:T(8,128)(2,1)}, bf16[8,12,200,200]{3,2,1,0:T(8,128)(2,1)}, bf16[8,200,768]{2,1,0:T(8,128)(2,1)}) custom-call(s32[3]{0:T(128)} %compare_select_fusion.1.meta, s32[4,8]{1,0:T(4,128)} %bitcast.68, bf16[4,49,8,768]{3,2,1,0:T(8,128)(2,1)} %all-to-all-done.tokens, ...), custom_call_target="tpu_custom_call" | custom-call | flops 2398617600 | bytes 10911744 | tf_op jit(solution)/shard_map/attend/pallas_call | solution.py:239
  66.2 4.2 %all-to-all-start.1 = ((bf16[4,49,8,768]{3,2,1,0:T(8,128)(2,1)}), bf16[4,49,8,768]{3,2,1,0:T(8,128)(2,1)S(1)}, u32[]{:S(2)}, u32[]{:S(2)}) async-start(bf16[4,49,8,768]{3,2,1,0:T(8,128)(2,1)} %bitcast.61), calls=%async_computation.1 | async-start | bytes 4816896 | tf_op jit(solution)/shard_map/all_to_all | solution.py:1091
  74.4 23.2 %attend.3 = (bf16[8,200,768]{2,1,0:T(8,128)(2,1)}, bf16[8,200,768]{2,1,0:T(8,128)(2,1)}, bf16[8,200,2304]{2,1,0:T(8,128)(2,1)}, bf16[8,12,200,200]{3,2,1,0:T(8,128)(2,1)}, bf16[8,200,768]{2,1,0:T(8,128)(2,1)}) custom-call(s32[3]{0:T(128)} %compare_select_fusion.1.meta, ...), custom_call_target="tpu_custom_call", output_to_operand_aliasing={{0}: (13, {}), {1}: (14, {}), {2}: (15, {}), {3}: (16, {}),... | custom-call | flops 7195852800 | bytes 25657344 | tf_op jit(solution)/shard_map/attend/pallas_call | solution.py:239
  102.1 11.7 %project.1 = (bf16[1600,768]{1,0:T(8,128)(2,1)}, bf16[1600,768]{1,0:T(8,128)(2,1)}, bf16[1600,768]{1,0:T(8,128)(2,1)}, f32[1,768]{1,0:T(1,128)}) custom-call(s32[3]{0:T(128)} %compare_select_fusion.1.meta, s32[4,8]{1,0:T(4,128)} %bitcast.70, bf16[8,200,768]{2,1,0:T(8,128)(2,1)} %get-tuple-element.211.attended.mixed_in, ...), custom_call_target="tpu_custom_call" | custom-call | flops 1887436800 | bytes 17203200 | tf_op jit(solution)/shard_map/project/pallas_call | solution.py:239
  113.9 24.9 %feed.3 = (bf16[1600,768]{1,0:T(8,128)(2,1)}, bf16[1600,768]{1,0:T(8,128)(2,1)}, bf16[2,512,768]{2,1,0:T(8,128)(2,1)}, bf16[2,512,768]{2,1,0:T(8,128)(2,1)}, f32[1,1024]{1,0:T(1,128)}) custom-call(s32[3]{0:T(128)} %compare_select_fusion.1.meta, bf16[1600,768]{1,0:T(8,128)(2,1)} %get-tuple-element.215.normed, bf16[1600,768]{1,0:T(8,128)(2,1)} %get-tuple-element.216.branch, ...), custom_call_target="tpu_custom_call" | custom-call | flops 15099494400 | bytes 21037056 | tf_op jit(solution)/shard_map/feed/pallas_call | solution.py:239
  139.3 25.5 %feed.4 = (bf16[1600,768]{1,0:T(8,128)(2,1)}, bf16[1600,768]{1,0:T(8,128)(2,1)}, bf16[2,512,768]{2,1,0:T(8,128)(2,1)}, bf16[2,512,768]{2,1,0:T(8,128)(2,1)}, f32[1,1024]{1,0:T(1,128)}) custom-call(s32[3]{0:T(128)} %compare_select_fusion.1.meta, bf16[1600,768]{1,0:T(8,128)(2,1)} %get-tuple-element.215.normed, ...), custom_call_target="tpu_custom_call", output_to_operand_aliasing={{0}: (14, {}), {1}: (15, {})} | custom-call | flops 15099494400 | bytes 21037056 | tf_op jit(solution)/shard_map/feed/pallas_call | solution.py:239
  168.2 25.6 %feed.5 = (bf16[1600,768]{1,0:T(8,128)(2,1)}, bf16[1600,768]{1,0:T(8,128)(2,1)}, bf16[2,512,768]{2,1,0:T(8,128)(2,1)}, bf16[2,512,768]{2,1,0:T(8,128)(2,1)}, f32[1,1024]{1,0:T(1,128)}) custom-call(s32[3]{0:T(128)} %compare_select_fusion.1.meta, bf16[1600,768]{1,0:T(8,128)(2,1)} %get-tuple-element.215.normed, ...), custom_call_target="tpu_custom_call", output_to_operand_aliasing={{0}: (14, {}), {1}: (15, {})} | custom-call | flops 15099494400 | bytes 21037056 | tf_op jit(solution)/shard_map/feed/pallas_call | solution.py:239
  198.4 18.6 %middle.1 = (bf16[4,49,8,768]{3,2,1,0:T(8,128)(2,1)}, bf16[1600,768]{1,0:T(8,128)(2,1)}, bf16[8,200,768]{2,1,0:T(8,128)(2,1)}, bf16[2,192,768]{2,1,0:T(8,128)(2,...) custom-call(s32[3]{0:T(128)} %compare_select_fusion.1.meta, ...), custom_call_target="tpu_custom_call" | custom-call | flops 3774873600 | bytes 22118400 | tf_op jit(solution)/shard_map/middle/pallas_call | solution.py:239
  221.9 13.1 %attend_back.3 = (bf16[8,200,256]{2,1,0:T(8,128)(2,1)}, bf16[8,200,256]{2,1,0:T(8,128)(2,1)}, bf16[8,200,256]{2,1,0:T(8,128)(2,1)}, bf16[2,192,768]{2,1,0:T(8,12...) custom-call(s32[3]{0:T(128)} %compare_select_fusion.1.meta, ...), custom_call_target="tpu_custom_call" | custom-call | flops 4508876800 | bytes 12288000 | tf_op jit(solution)/shard_map/attend_back/pallas_call | solution.py:239
  238.1 4.9 %all-to-all-start.2 = ((bf16[4,49,8,768]{3,2,1,0:T(8,128)(2,1)}), bf16[4,49,8,768]{3,2,1,0:T(8,128)(2,1)}, u32[]{:S(2)}, u32[]{:S(2)}) async-start(bf16[4,49,8,768]{3,2,1,0:T(8,128)(2,1)} %get-tuple-element.277), calls=%async_computation.2 | async-start | bytes 4816896 | tf_op jit(solution)/shard_map/all_to_all | solution.py:1091
  246.6 12.9 %attend_back.4 = (bf16[8,200,256]{2,1,0:T(8,128)(2,1)}, bf16[8,200,256]{2,1,0:T(8,128)(2,1)}, bf16[8,200,256]{2,1,0:T(8,128)(2,1)}, bf16[2,192,768]{2,1,0:T(8,12...) custom-call(s32[3]{0:T(128)} %compare_select_fusion.1.meta, ...), custom_call_target="tpu_custom_call" | custom-call | flops 4508876800 | bytes 12288000 | tf_op jit(solution)/shard_map/attend_back/pallas_call | solution.py:239
  259.6 4.4 %collective-permute-done.25 = bf16[256,768]{1,0:T(8,128)(2,1)S(1)} collective-permute-done((bf16[256,768]{1,0:T(8,128)(2,1)S(1)}, bf16[256,768]{1,0:T(8,128)(2,1)S(1)}, u32[]{:S(2)}, u32[]{:S(2)}) %collective-permute-start.25) | collective-permute-done | bytes 393248 | tf_op jit(solution)/shard_map/ppermute | solution.py:1076
  276.9 13.0 %attend_back.5 = (bf16[8,200,256]{2,1,0:T(8,128)(2,1)}, bf16[8,200,256]{2,1,0:T(8,128)(2,1)}, bf16[8,200,256]{2,1,0:T(8,128)(2,1)}, bf16[2,192,768]{2,1,0:T(8,12...) custom-call(s32[3]{0:T(128)} %compare_select_fusion.1.meta, ...), custom_call_target="tpu_custom_call" | custom-call | flops 4508876800 | bytes 12288000 | tf_op jit(solution)/shard_map/attend_back/pallas_call | solution.py:239
  298.3 16.5 %first_back.1 = (bf16[4,49,8,768]{3,2,1,0:T(8,128)(2,1)}, f32[1,768]{1,0:T(1,128)}, f32[1,768]{1,0:T(1,128)}) custom-call(s32[3]{0:T(128)} %compare_select_fusion.1.meta, bf16[8,200,768]{2,1,0:T(8,128)(2,1)} %get-tuple-element.212.rows_in, bf16[1600,768]{1,0:T(8,128)(2,1)} %get-tuple-element.294.d_middle, f32[13,768]{1,0:T(8,128)} %get-tuple-element.190.vectors, ...), custom_call_target="tpu_custom_call" | custom-call | flops 5662310400 | bytes 17203200 | tf_op jit(solution)/shard_map/first_back/pallas_call | solution.py:239
  326.9 3.8 all-to-all-start.3
  343.9 3.7 collective-permute-done.39
  349.8 5.4 %collective-permute-done.40 = bf16[96,768]{1,0:T(8,128)(2,1)S(1)} collective-permute-done((bf16[96,768]{1,0:T(8,128)(2,1)S(1)}, bf16[96,768]{1,0:T(8,128)(2,1)S(1)}, u32[]{:S(2)}, u32[]{:S(2)}) %collective-permute-start.40) | collective-permute-done | bytes 147488 | tf_op jit(solution)/shard_map/ppermute | solution.py:1076
  355.5 3.5 collective-permute-start.46
  361.3 3.7 collective-permute-done.46
  367.6 5.1 %finish_feed.1 = (f32[192,3072]{1,0:T(8,128)}, f32[768,768]{1,0:T(8,128)}, f32[192,768]{1,0:T(8,128)}) custom-call(s32[3]{0:T(128)} %compare_select_fusion.1.meta, bf16[256,768]{1,0:T(8,128)(2,1)} %copy-done.8, bf16[256,768]{1,0:T(8,128)(2,1)} %copy-done.27, bf16[256,768]{1,0:T(8,128)(2,1)} %copy-done.9, bf16[256,768]{1,0:T(8,128)(2,1)} %copy-done.28, ...), custom_call_target="tpu_custom_call" | custom-call | bytes 7962624 | tf_op jit(solution)/shard_map/finish_feed/pallas_call | solution.py:239
  (230 shorter events, 113.9 us)
Async XLA Ops:
  16.9 33.6 %all-to-all-start = ((bf16[4,49,8,768]{3,2,1,0:T(8,128)(2,1)}), bf16[4,49,8,768]{3,2,1,0:T(8,128)(2,1)}, u32[]{:S(2)}, u32[]{:S(2)}) async-start(bf16[4,49,8,768]{3,2,1,0:T(8,128)(2,1)} %bitcast.6), calls=%async_computation | async-start | bytes 4816896 | tf_op jit(solution)/shard_map/all_to_all | solution.py:1091
  66.2 34.5 %all-to-all-start.1 = ((bf16[4,49,8,768]{3,2,1,0:T(8,128)(2,1)}), bf16[4,49,8,768]{3,2,1,0:T(8,128)(2,1)S(1)}, u32[]{:S(2)}, u32[]{:S(2)}) async-start(bf16[4,49,8,768]{3,2,1,0:T(8,128)(2,1)} %bitcast.61), calls=%async_computation.1 | async-start | bytes 4816896 | tf_op jit(solution)/shard_map/all_to_all | solution.py:1091
  70.4 43.4 %collective-permute-start.12 = (bf16[384,768]{1,0:T(8,128)(2,1)S(1)}, bf16[384,768]{1,0:T(8,128)(2,1)}, u32[]{:S(2)}, u32[]{:S(2)}) collective-permute-start(bf16[384,768]{1,0:T(8,128)(2,1)S(1)} %collective-permute-done.7.rest_2_), channel_id=1, source_target_pairs={{0,1},{1,0},{2,3},{3,2},{4,5},{5,4},{6,7},{7,6},{8,9},{9,8},{10,11... | collective-permute-start | bytes 1769480 | tf_op jit(solution)/shard_map/ppermute | solution.py:1076
  70.9 26.7 %collective-permute-start.11 = (bf16[384,768]{1,0:T(8,128)(2,1)S(1)}, bf16[384,768]{1,0:T(8,128)(2,1)}, u32[]{:S(2)}, u32[]{:S(2)}) collective-permute-start(bf16[384,768]{1,0:T(8,128)(2,1)S(1)} %collective-permute-done.7.rest_2_), channel_id=1, source_target_pairs={{0,20},{4,16},{8,28},{12,24},{16,4},{20,0},{24,12},{28,8},{1,21},{... | collective-permute-start | bytes 1769480 | tf_op jit(solution)/shard_map/ppermute | solution.py:1083
  73.7 26.5 %collective-permute-start.10 = (bf16[384,768]{1,0:T(8,128)(2,1)S(1)}, bf16[384,768]{1,0:T(8,128)(2,1)}, u32[]{:S(2)}, u32[]{:S(2)}) collective-permute-start(bf16[384,768]{1,0:T(8,128)(2,1)S(1)} %collective-permute-done.7.rest_2_), channel_id=1, source_target_pairs={{0,4},{4,0},{8,12},{12,8},{1,5},{5,1},{9,13},{13,9},{2,6},{6,2},{1... | collective-permute-start | bytes 1769480 | tf_op jit(solution)/shard_map/ppermute | solution.py:1076
  74.1 26.1 %collective-permute-start.9 = (bf16[384,768]{1,0:T(8,128)(2,1)S(1)}, bf16[384,768]{1,0:T(8,128)(2,1)}, u32[]{:S(2)}, u32[]{:S(2)}) collective-permute-start(bf16[384,768]{1,0:T(8,128)(2,1)S(1)} %collective-permute-done.7.rest_2_), channel_id=1, source_target_pairs={{0,16},{16,0},{1,17},{17,1},{2,18},{18,2},{3,19},{19,3},{4,20},{20... | collective-permute-start | bytes 1769480 | tf_op jit(solution)/shard_map/ppermute | solution.py:1076
  138.8 26.1 %collective-permute-start.16 = (bf16[2,512,768]{2,1,0:T(8,128)(2,1)}, bf16[2,512,768]{2,1,0:T(8,128)(2,1)S(1)}, u32[]{:S(2)}, u32[]{:S(2)}) collective-permute-start(bf16[2,512,768]{2,1,0:T(8,128)(2,1)} %get-tuple-element.227), channel_id=1, source_target_pairs={{0,1},{1,0},{2,3},{3,2},{4,5},{5,4},{6,7},{7,6},{8,9},{9,8},{10,11... | collective-permute-start | bytes 4718600 | tf_op jit(solution)/shard_map/ppermute | solution.py:1076
  166.2 27.6 %collective-permute-start.18 = (bf16[2,512,768]{2,1,0:T(8,128)(2,1)}, bf16[2,512,768]{2,1,0:T(8,128)(2,1)S(1)}, u32[]{:S(2)}, u32[]{:S(2)}) collective-permute-start(bf16[2,512,768]{2,1,0:T(8,128)(2,1)} %get-tuple-element.235), channel_id=1, source_target_pairs={{0,1},{1,0},{2,3},{3,2},{4,5},{5,4},{6,7},{7,6},{8,9},{9,8},{10,11... | collective-permute-start | bytes 4718600 | tf_op jit(solution)/shard_map/ppermute | solution.py:1076
  166.3 27.6 %collective-permute-start.17 = (bf16[512,768]{1,0:T(8,128)(2,1)}, bf16[512,768]{1,0:T(8,128)(2,1)S(1)}, u32[]{:S(2)}, u32[]{:S(2)}) collective-permute-start(bf16[512,768]{1,0:T(8,128)(2,1)} %slice_bitcast_fusion.3), channel_id=1, source_target_pairs={{0,2},{1,3},{2,0},{3,1},{4,6},{5,7},{6,4},{7,5},{8,10},{9,11},{10,... | collective-permute-start | bytes 2359304 | tf_op jit(solution)/shard_map/ppermute | solution.py:1076
  196.5 20.6 %collective-permute-start.21 = (bf16[2,512,768]{2,1,0:T(8,128)(2,1)}, bf16[2,512,768]{2,1,0:T(8,128)(2,1)S(1)}, u32[]{:S(2)}, u32[]{:S(2)}) collective-permute-start(bf16[2,512,768]{2,1,0:T(8,128)(2,1)} %get-tuple-element.247), channel_id=1, source_target_pairs={{0,1},{1,0},{2,3},{3,2},{4,5},{5,4},{6,7},{7,6},{8,9},{9,8},{10,11... | collective-permute-start | bytes 4718600 | tf_op jit(solution)/shard_map/ppermute | solution.py:1076
  196.7 20.3 %collective-permute-start.20 = (bf16[512,768]{1,0:T(8,128)(2,1)S(1)}, bf16[512,768]{1,0:T(8,128)(2,1)S(1)}, u32[]{:S(2)}, u32[]{:S(2)}) collective-permute-start(bf16[512,768]{1,0:T(8,128)(2,1)S(1)} %slice_bitcast_fusion.1), channel_id=1, source_target_pairs={{0,2},{1,3},{2,0},{3,1},{4,6},{5,7},{6,4},{7,5},{8,10},{9,11},{10,... | collective-permute-start | bytes 2359304 | tf_op jit(solution)/shard_map/ppermute | solution.py:1076
  197.0 20.0 %collective-permute-start.19 = (bf16[256,768]{1,0:T(8,128)(2,1)}, bf16[256,768]{1,0:T(8,128)(2,1)S(1)}, u32[]{:S(2)}, u32[]{:S(2)}) collective-permute-start(bf16[256,768]{1,0:T(8,128)(2,1)} %broadcast_select_fusion.2), channel_id=1, source_target_pairs={{0,16},{16,0},{1,17},{17,1},{2,18},{18,2},{3,19},{19,3},{4,20},{20... | collective-permute-start | bytes 1179656 | tf_op jit(solution)/shard_map/ppermute | solution.py:1076
  236.7 28.6 %collective-permute-start.27 = (bf16[2,352,768]{2,1,0:T(8,128)(2,1)}, bf16[2,352,768]{2,1,0:T(8,128)(2,1)}, u32[]{:S(2)}, u32[]{:S(2)}) collective-permute-start(bf16[2,352,768]{2,1,0:T(8,128)(2,1)} %broadcast_select_fusion), channel_id=1, source_target_pairs={{0,16},{16,0},{1,17},{17,1},{2,18},{18,2},{3,19},{19,3},{4,20},{20... | collective-permute-start | bytes 3244040 | tf_op jit(solution)/shard_map/ppermute | solution.py:1076
  238.1 34.0 %all-to-all-start.2 = ((bf16[4,49,8,768]{3,2,1,0:T(8,128)(2,1)}), bf16[4,49,8,768]{3,2,1,0:T(8,128)(2,1)}, u32[]{:S(2)}, u32[]{:S(2)}) async-start(bf16[4,49,8,768]{3,2,1,0:T(8,128)(2,1)} %get-tuple-element.277), calls=%async_computation.2 | async-start | bytes 4816896 | tf_op jit(solution)/shard_map/all_to_all | solution.py:1091
  243.0 22.3 %collective-permute-start.28 = (bf16[2,192,768]{2,1,0:T(8,128)(2,1)}, bf16[2,192,768]{2,1,0:T(8,128)(2,1)S(1)}, u32[]{:S(2)}, u32[]{:S(2)}) collective-permute-start(bf16[2,192,768]{2,1,0:T(8,128)(2,1)} %get-tuple-element.272), channel_id=1, source_target_pairs={{0,1},{1,0},{2,3},{3,2},{4,5},{5,4},{6,7},{7,6},{8,9},{9,8},{10,11... | collective-permute-start | bytes 1769480 | tf_op jit(solution)/shard_map/ppermute | solution.py:1076
  243.6 20.4 %collective-permute-start.25 = (bf16[256,768]{1,0:T(8,128)(2,1)S(1)}, bf16[256,768]{1,0:T(8,128)(2,1)S(1)}, u32[]{:S(2)}, u32[]{:S(2)}) collective-permute-start(bf16[256,768]{1,0:T(8,128)(2,1)S(1)} %get-tuple-element.269), channel_id=1, source_target_pairs={{0,8},{4,12},{8,0},{12,4},{1,9},{5,13},{9,1},{13,5},{2,10},{6,14},... | collective-permute-start | bytes 1179656 | tf_op jit(solution)/shard_map/ppermute | solution.py:1076
  246.2 19.2 %collective-permute-start.26 = (bf16[256,768]{1,0:T(8,128)(2,1)S(1)}, bf16[256,768]{1,0:T(8,128)(2,1)S(1)}, u32[]{:S(2)}, u32[]{:S(2)}) collective-permute-start(bf16[256,768]{1,0:T(8,128)(2,1)S(1)} %get-tuple-element.270), channel_id=1, source_target_pairs={{0,4},{4,0},{8,12},{12,8},{1,5},{5,1},{9,13},{13,9},{2,6},{6,2},{1... | collective-permute-start | bytes 1179656 | tf_op jit(solution)/shard_map/ppermute | solution.py:1076
  272.7 19.6 %collective-permute-start.30 = (bf16[256,768]{1,0:T(8,128)(2,1)S(1)}, bf16[256,768]{1,0:T(8,128)(2,1)S(1)}, u32[]{:S(2)}, u32[]{:S(2)}) collective-permute-start(bf16[256,768]{1,0:T(8,128)(2,1)S(1)} %add_convert_fusion.9), channel_id=1, source_target_pairs={{0,8},{4,12},{8,0},{12,4},{1,9},{5,13},{9,1},{13,5},{2,10},{6,14},... | collective-permute-start | bytes 1179656 | tf_op jit(solution)/shard_map/ppermute | solution.py:1076
  296.1 18.8 %collective-permute-start.35 = (bf16[384,768]{1,0:T(8,128)(2,1)S(1)}, bf16[384,768]{1,0:T(8,128)(2,1)S(1)}, u32[]{:S(2)}, u32[]{:S(2)}) collective-permute-start(bf16[384,768]{1,0:T(8,128)(2,1)S(1)} %fusion.5), channel_id=1, source_target_pairs={{0,2},{1,3},{2,0},{3,1},{4,6},{5,7},{6,4},{7,5},{8,10},{9,11},{10,... | collective-permute-start | bytes 1769480 | tf_op jit(solution)/shard_map/ppermute | solution.py:1076
  296.8 18.1 %collective-permute-start.36 = (bf16[2,192,768]{2,1,0:T(8,128)(2,1)}, bf16[2,192,768]{2,1,0:T(8,128)(2,1)S(1)}, u32[]{:S(2)}, u32[]{:S(2)}) collective-permute-start(bf16[2,192,768]{2,1,0:T(8,128)(2,1)} %get-tuple-element.309), channel_id=1, source_target_pairs={{0,1},{1,0},{2,3},{3,2},{4,5},{5,4},{6,7},{7,6},{8,9},{9,8},{10,11... | collective-permute-start | bytes 1769480 | tf_op jit(solution)/shard_map/ppermute | solution.py:1076
  296.8 18.0 %collective-permute-start.34 = (bf16[176,768]{1,0:T(8,128)(2,1)S(1)}, bf16[176,768]{1,0:T(8,128)(2,1)S(1)}, u32[]{:S(2)}, u32[]{:S(2)}) collective-permute-start(bf16[176,768]{1,0:T(8,128)(2,1)S(1)} %broadcast_select_fusion.6), channel_id=1, source_target_pairs={{0,4},{4,0},{8,12},{12,8},{1,5},{5,1},{9,13},{13,9},{2,6},{6,2},{1... | collective-permute-start | bytes 811016 | tf_op jit(solution)/shard_map/ppermute | solution.py:1076
  296.8 18.0 %collective-permute-start.33 = (bf16[256,768]{1,0:T(8,128)(2,1)S(1)}, bf16[256,768]{1,0:T(8,128)(2,1)S(1)}, u32[]{:S(2)}, u32[]{:S(2)}) collective-permute-start(bf16[256,768]{1,0:T(8,128)(2,1)S(1)} %add_convert_fusion.8.refs_2_), channel_id=1, source_target_pairs={{0,16},{16,0},{1,17},{17,1},{2,18},{18,2},{3,19},{19,3},{4,20},{20... | collective-permute-start | bytes 1179656 | tf_op jit(solution)/shard_map/ppermute | solution.py:1076
  326.9 50.9 %all-to-all-start.3 = ((bf16[4,49,8,768]{3,2,1,0:T(8,128)(2,1)}), bf16[4,49,8,768]{3,2,1,0:T(8,128)(2,1)S(1)}, u32[]{:S(2)}, u32[]{:S(2)}) async-start(bf16[4,49,8,768]{3,2,1,0:T(8,128)(2,1)} %get-tuple-element.325), calls=%async_computation.3 | async-start | bytes 4816896 | tf_op jit(solution)/shard_map/all_to_all | solution.py:1091
  330.8 35.0 %collective-permute-start.50 = (f32[24,768]{1,0:T(8,128)S(1)}, f32[24,768]{1,0:T(8,128)S(1)}, u32[]{:S(2)}, u32[]{:S(2)}) collective-permute-start(f32[24,768]{1,0:T(8,128)S(1)} %add.139), channel_id=1, source_target_pairs={{0,4},{4,0},{8,12},{12,8},{1,5},{5,1},{9,13},{13,9},{2,6},{6,2},{1... | collective-permute-start | bytes 221192 | tf_op jit(solution)/shard_map/ppermute | solution.py:1076
  (68 other events, 638.7 us)
